TPU v7x, 32 devices: a whole 2x2x4 slice. The times are simulated.
32 devices in a mesh: gx: 4 (over y, x), gy: 8 (over z, core).
Axes of the slice: x: 2, y: 2, z: 4, core: 2. Of those that a mesh axis runs over, the one named last changes fastest.
Arguments:
- layer_in: bfloat16 [16384, 768], P(('gx', 'gy')), may hold values from -6 to 6
- doc_ids: int32 [32, 512], P('gx'), may hold values from 0 to 7, never falling along the last dimension, each value on 1 to 128 neighbouring positions
- mix_gain: bfloat16 [768], P(('gx', 'gy')), may hold values from 0.5 to 1.5
- value_weight: bfloat16 [768, 768], P('gx', 'gy'), may hold values from -0.21875 to 0.21875
- mixing: bfloat16 [12, 512, 512], P(None, 'gy', 'gx'), may hold values from -9 to 9
- output_weight: bfloat16 [768, 768], P('gy', 'gx'), may hold values from -0.875 to 0.875
- ffn_gain: bfloat16 [768], P(('gx', 'gy')), may hold values from 0.5 to 1.5
- up_weight: bfloat16 [768, 3072], P('gx', 'gy'), may hold values from -0.21875 to 0.21875
- down_weight: bfloat16 [3072, 768], P('gy', 'gx'), may hold values from -0.109375 to 0.109375
- cotangent: bfloat16 [16384, 768], P(('gx', 'gy')), may hold values from -6 to 6
Outputs:
- layer_out: bfloat16 [16384, 768], P(('gx', 'gy'))
- grad_in: float32 [16384, 768], P(('gx', 'gy'))
- grad_mix_gain: float32 [768], P(('gx', 'gy'))
- grad_value: float32 [768, 768], P('gx', 'gy')
- grad_mixing: float32 [12, 512, 512], P(None, 'gy', 'gx')
- grad_output: float32 [768, 768], P('gy', 'gx')
- grad_ffn_gain: float32 [768], P(('gx', 'gy'))
- grad_up: float32 [768, 3072], P('gx', 'gy')
- grad_down: float32 [3072, 768], P('gy', 'gx')
Inputs may be any that keep to these rules, and one draw needn't show every extreme that they name: `doc_ids`: each row packs documents: ids never fall along the row, every id from 0 to 7 holds 1 to 128 tokens, and one document holds exactly 128.
All inputs are finite; a program needn't handle non-finite values.
Results may differ from a plain program's by a relative error of at most 0.025.
Values may be sent and summed in bfloat16 or wider, within the bound.
No kernel may reach another device: no remote copies, remote signals or barrier semaphores. Data moves between devices by JAX's collectives and lax.ppermute only.
A program may use at most 320 MiB of HBM per device.

v0:
```python
import math

import jax
import jax.numpy as jnp
from jax import lax
from jax.sharding import PartitionSpec as P

HS = 64


EPS = 1e-05
NEG = -1e30


def layer_norm(tok_rows, norm_gain):
    average = jnp.mean(tok_rows, axis=-1, keepdims=True)
    centred = tok_rows - average
    spread = jnp.mean(centred * centred, axis=-1, keepdims=True)
    return centred * lax.rsqrt(spread + EPS) * norm_gain


def gelu_tanh(up_vals):
    return jax.nn.gelu(up_vals, approximate=True)


def matmul(left, right):
    return jnp.dot(left, right, preferred_element_type=jnp.float32)


def matmul_nt(left, right):
    return lax.dot_general(
        left, right, (((1,), (1,)), ((), ())), preferred_element_type=jnp.float32
    )


def matmul_tn(left, right):
    return lax.dot_general(
        left, right, (((0,), (0,)), ((), ())), preferred_element_type=jnp.float32
    )


def masked_scores(doc_rows, heads_mix):
    same_doc = doc_rows[:, :, None] == doc_rows[:, None, :]
    return jnp.where(same_doc[:, None], heads_mix[None], NEG)


def to_groups(columns, select):
    return columns[:, None, :] * select[None]


def from_groups(grouped):
    return jnp.sum(grouped, axis=1)


def column_heads(col_width, head_total, head_size):
    col_start = lax.axis_index("gy") * col_width
    head_count = min(head_total, (col_width - 1) // head_size + 2)
    head_start = jnp.minimum(col_start // head_size, head_total - head_count)
    owner = (col_start + jnp.arange(col_width, dtype=jnp.int32)) // head_size - head_start
    select = (owner[None, :] == jnp.arange(head_count, dtype=jnp.int32)[:, None]).astype(
        jnp.bfloat16
    )
    return (head_start, head_count, select)


def mixer_forward(grouped, doc_rows, heads_mix):
    seq_count, length = doc_rows.shape
    groups, group_width = (grouped.shape[1], grouped.shape[2])
    per_block = math.gcd(seq_count, 8)
    blocks = seq_count // per_block
    vals_blocks = grouped.reshape(blocks, per_block, length, groups, group_width)
    doc_blocks = doc_rows.reshape(blocks, per_block, length)

    def block_fn(block_item):
        block_docs, block_vals = block_item
        scores = masked_scores(block_docs, heads_mix)
        row_top = jnp.max(scores, axis=-1, keepdims=True)
        expo_vals = jnp.exp(scores - row_top)
        row_total = jnp.sum(expo_vals, axis=-1, keepdims=True)
        mix_probs = (expo_vals / row_total).astype(jnp.bfloat16)
        mix_out = jnp.einsum(
            "sgqk,skgw->sqgw", mix_probs, block_vals, preferred_element_type=jnp.float32
        )
        return (mix_out, (row_top + jnp.log(row_total))[..., 0])

    mix_out, log_sums = lax.map(block_fn, (doc_blocks, vals_blocks))
    return (mix_out.reshape(seq_count * length, groups, group_width), log_sums)


def mixer_backward(grouped, grad_groups, doc_rows, log_sums, heads_mix):
    seq_count, length = doc_rows.shape
    groups, group_width = (grouped.shape[1], grouped.shape[2])
    per_block = math.gcd(seq_count, 8)
    blocks = seq_count // per_block
    vals_blocks = grouped.reshape(blocks, per_block, length, groups, group_width)
    grad_blocks = grad_groups.reshape(blocks, per_block, length, groups, group_width)
    doc_blocks = doc_rows.reshape(blocks, per_block, length)

    def block_fn(mix_acc, block_item):
        block_docs, block_vals, block_grads, block_sums = block_item
        scores = masked_scores(block_docs, heads_mix)
        mix_probs = jnp.exp(scores - block_sums[..., None])
        vals_grad = jnp.einsum(
            "sgqk,sqgw->skgw",
            mix_probs.astype(jnp.bfloat16),
            block_grads,
            preferred_element_type=jnp.float32,
        )
        probs_grad = jnp.einsum(
            "sqgw,skgw->sgqk", block_grads, block_vals, preferred_element_type=jnp.float32
        )
        score_grad = mix_probs * (
            probs_grad - jnp.sum(mix_probs * probs_grad, axis=-1, keepdims=True)
        )
        return (mix_acc + jnp.sum(score_grad, axis=0), vals_grad)

    mix_init = jnp.zeros(heads_mix.shape, jnp.float32)
    mix_grad, vals_grad = lax.scan(
        block_fn, mix_init, (doc_blocks, vals_blocks, grad_blocks, log_sums)
    )
    return (vals_grad.reshape(seq_count * length, groups, group_width), mix_grad)


def shards(
    layer_in,
    doc_ids,
    mix_gain,
    value_weight,
    mixing,
    output_weight,
    ffn_gain,
    up_weight,
    down_weight,
    cotangent,
):
    mixing_part, gain_one_part, gain_two_part = (
        lax.all_gather(mixing, "gy", axis=1, tiled=True),
        lax.all_gather(mix_gain, "gy", axis=0, tiled=True),
        lax.all_gather(ffn_gain, "gy", axis=0, tiled=True),
    )
    value_cols, up_cols, output_rows, down_rows, mix_full, gain_one, gain_two = (
        lax.all_gather(value_weight, "gx", axis=0, tiled=True),
        lax.all_gather(up_weight, "gx", axis=0, tiled=True),
        lax.all_gather(output_weight, "gx", axis=1, tiled=True),
        lax.all_gather(down_weight, "gx", axis=1, tiled=True),
        lax.all_gather(mixing_part, "gx", axis=2, tiled=True),
        lax.all_gather(gain_one_part, "gx", axis=0, tiled=True),
        lax.all_gather(gain_two_part, "gx", axis=0, tiled=True),
    )
    gain_one = gain_one.astype(jnp.float32)
    gain_two = gain_two.astype(jnp.float32)
    layer_vals = layer_in.astype(jnp.float32)
    cot_vals = cotangent.astype(jnp.float32)
    normed_low = layer_norm(layer_vals, gain_one).astype(jnp.bfloat16)
    normed_all = lax.all_gather(normed_low, "gy", axis=0, tiled=True)
    head_start, head_count, select = column_heads(value_cols.shape[1], mix_full.shape[0], HS)
    heads_mix = lax.dynamic_slice_in_dim(mix_full, head_start, head_count, 0).astype(jnp.float32)
    value_low = matmul(normed_all, value_cols).astype(jnp.bfloat16)
    grouped = to_groups(value_low, select)
    mix_out, log_sums = mixer_forward(grouped, doc_ids, heads_mix)
    mixed_low = from_groups(mix_out).astype(jnp.bfloat16)
    middle = layer_vals + lax.psum_scatter(
        matmul(mixed_low, output_rows), "gy", scatter_dimension=0, tiled=True
    )
    normed_two = layer_norm(middle, gain_two).astype(jnp.bfloat16)
    normed_two_all = lax.all_gather(normed_two, "gy", axis=0, tiled=True)
    up_vals = matmul(normed_two_all, up_cols)
    act_low = gelu_tanh(up_vals).astype(jnp.bfloat16)
    layer_out = (
        middle
        + lax.psum_scatter(
            matmul(act_low, down_rows).astype(jnp.bfloat16), "gy", scatter_dimension=0, tiled=True
        ).astype(jnp.float32)
    ).astype(jnp.bfloat16)
    cot_all = lax.all_gather(cotangent, "gy", axis=0, tiled=True)
    down_grad = matmul_tn(act_low, cot_all)
    act_grad = matmul_nt(cot_all, down_rows)
    gelu_out, gelu_back = jax.vjp(gelu_tanh, up_vals)
    up_grad_low = gelu_back(act_grad)[0].astype(jnp.bfloat16)
    up_weight_grad = matmul_tn(normed_two_all, up_grad_low)
    normed_two_grad = lax.psum_scatter(
        matmul_nt(up_grad_low, up_cols).astype(jnp.bfloat16), "gy", scatter_dimension=0, tiled=True
    ).astype(jnp.float32)
    norm_out, norm_back = jax.vjp(layer_norm, middle, gain_two)
    mid_norm_grad, gain_two_grad = norm_back(normed_two_grad)
    mid_grad = cot_vals + mid_norm_grad
    branch_low = mid_grad.astype(jnp.bfloat16)
    branch_all = lax.all_gather(branch_low, "gy", axis=0, tiled=True)
    output_grad = matmul_tn(mixed_low, branch_all)
    mixed_grad_low = matmul_nt(branch_all, output_rows).astype(jnp.bfloat16)
    vals_grad, mix_grad_local = mixer_backward(
        grouped, to_groups(mixed_grad_low, select), doc_ids, log_sums, heads_mix
    )
    value_grad_low = from_groups(vals_grad).astype(jnp.bfloat16)
    value_grad = matmul_tn(normed_all, value_grad_low)
    normed_one_grad = lax.psum_scatter(
        matmul_nt(value_grad_low, value_cols).astype(jnp.bfloat16),
        "gy",
        scatter_dimension=0,
        tiled=True,
    ).astype(jnp.float32)
    mix_grad_full = lax.dynamic_update_slice_in_dim(
        jnp.zeros(mix_full.shape, jnp.float32), mix_grad_local, head_start, 0
    )
    first_out, first_back = jax.vjp(layer_norm, layer_vals, gain_one)
    in_norm_grad, gain_one_grad = first_back(normed_one_grad)
    grad_in = mid_grad + in_norm_grad
    (
        value_grad,
        up_weight_grad,
        output_grad,
        down_grad,
        mix_grad_part,
        gain_one_part_grad,
        gain_two_part_grad,
    ) = (
        lax.psum_scatter(
            value_grad.astype(jnp.bfloat16), "gx", scatter_dimension=0, tiled=True
        ).astype(jnp.float32),
        lax.psum_scatter(
            up_weight_grad.astype(jnp.bfloat16), "gx", scatter_dimension=0, tiled=True
        ).astype(jnp.float32),
        lax.psum_scatter(
            output_grad.astype(jnp.bfloat16), "gx", scatter_dimension=1, tiled=True
        ).astype(jnp.float32),
        lax.psum_scatter(
            down_grad.astype(jnp.bfloat16), "gx", scatter_dimension=1, tiled=True
        ).astype(jnp.float32),
        lax.psum_scatter(
            mix_grad_full.astype(jnp.bfloat16), "gx", scatter_dimension=2, tiled=True
        ).astype(jnp.float32),
        lax.psum_scatter(
            gain_one_grad.astype(jnp.bfloat16), "gx", scatter_dimension=0, tiled=True
        ).astype(jnp.float32),
        lax.psum_scatter(
            gain_two_grad.astype(jnp.bfloat16), "gx", scatter_dimension=0, tiled=True
        ).astype(jnp.float32),
    )
    mix_grad_out, gain_one_out, gain_two_out = (
        lax.psum_scatter(
            mix_grad_part.astype(jnp.bfloat16), "gy", scatter_dimension=1, tiled=True
        ).astype(jnp.float32),
        lax.psum_scatter(
            gain_one_part_grad.astype(jnp.bfloat16), "gy", scatter_dimension=0, tiled=True
        ).astype(jnp.float32),
        lax.psum_scatter(
            gain_two_part_grad.astype(jnp.bfloat16), "gy", scatter_dimension=0, tiled=True
        ).astype(jnp.float32),
    )
    return (
        layer_out,
        grad_in,
        gain_one_out,
        value_grad,
        mix_grad_out,
        output_grad,
        gain_two_out,
        up_weight_grad,
        down_grad,
    )


def solution(mesh):
    in_specs = (
        P(("gx", "gy"), None),
        P("gx", None),
        P(("gx", "gy")),
        P("gx", "gy"),
        P(None, "gy", "gx"),
        P("gy", "gx"),
        P(("gx", "gy")),
        P("gx", "gy"),
        P("gy", "gx"),
        P(("gx", "gy"), None),
    )
    out_specs = (
        P(("gx", "gy"), None),
        P(("gx", "gy"), None),
        P(("gx", "gy")),
        P("gx", "gy"),
        P(None, "gy", "gx"),
        P("gy", "gx"),
        P(("gx", "gy")),
        P("gx", "gy"),
        P("gy", "gx"),
    )
    return jax.shard_map(shards, mesh=mesh, in_specs=in_specs, out_specs=out_specs, check_vma=False)
```

profile of v0, /device:TPU:0, one launch (start us, length us, event | category | flops | bytes accessed | tf_op | source)
XLA Modules:
  0.0 1063.8 jit_solution(16108159190764218038)
XLA Ops:
  12.4 18.4 %all-reduce.9 = (bf16[192]{0:T(256)(128)(2,1)S(1)}, bf16[192]{0:T(256)(128)(2,1)S(1)}) all-reduce(bf16[192]{0:T(256)(128)(2,1)S(1)} %dynamic-update-slice, bf16[192]{0:T(256)(128)(2,1)S(1)} %dynamic-update-slice.2), channel_id=1, replica_groups=mesh['gx'=4,'gy'=8] {'gy'}, use_global_device_ids=true, to_apply=%add | all-reduce | flops 384 | bytes 1536
  31.2 9.9 all-reduce.11
  47.3 8.2 all_gather.48
  55.5 8.3 all_gather.47
  65.2 42.3 %all-gather.11.cloned.1.call-done = bf16[4096,768]{1,0:T(8,128)(2,1)} async-done(((bf16[512,768]{1,0:T(8,128)(2,1)}), bf16[4096,768]{1,0:T(8,128)(2,1)}) %all-gather.11.cloned.1.call-update) | async-done | bytes 6291472 | tf_op jit(solution)/shard_map/all_gather | solution.py:155
  113.4 64.7 %all-gather.9.cloned.1.call-done = bf16[12,512,512]{2,1,0:T(8,128)(2,1)} async-done(((bf16[12,512,128]{2,1,0:T(8,128)(2,1)}), bf16[12,512,512]{2,1,0:T(8,128)(2,1)}) %all-gather.9.cloned.1.call-update) | async-done | bytes 6291472 | tf_op jit(solution)/shard_map/all_gather | solution.py:146
  209.1 128.7 %reduce-scatter.15.cloned.1.call-done = f32[512,768]{1,0:T(8,128)} async-done(((f32[4096,768]{1,0:T(8,128)}), f32[512,768]{1,0:T(8,128)}) %reduce-scatter.15.cloned.1.call-update) | async-done | bytes 1572880 | tf_op jit(solution)/shard_map/reduce_scatter | solution.py:162
  341.1 11.7 %all_gather.52 = bf16[768,384]{1,0:T(8,128)(2,1)} all-gather(bf16[192,384]{1,0:T(8,128)(2,1)S(1)} %copy-done.14), channel_id=1, replica_groups=mesh['gx'=4,'gy'=8] {'gx'}, dimensions={0}, use_global_device_ids=true | all-gather | bytes 737280 | tf_op jit(solution)/shard_map/all_gather | solution.py:143
  352.9 10.3 all_gather.53
  363.2 39.3 %all-gather.15.cloned.1.call-done = bf16[4096,768]{1,0:T(8,128)(2,1)} async-done(((bf16[512,768]{1,0:T(8,128)(2,1)}), bf16[4096,768]{1,0:T(8,128)(2,1)}) %all-gather.15.cloned.1.call-update) | async-done | bytes 6291472 | tf_op jit(solution)/shard_map/all_gather | solution.py:175
  402.5 8.9 fusion.104
  411.4 56.7 %all-gather.13.cloned.1.call-done = bf16[4096,768]{1,0:T(8,128)(2,1)} async-done(((bf16[512,768]{1,0:T(8,128)(2,1)}), bf16[4096,768]{1,0:T(8,128)(2,1)}) %all-gather.13.cloned.1.call-update) | async-done | bytes 6291472 | tf_op jit(solution)/shard_map/all_gather | solution.py:166
  468.0 13.9 %fusion.31 = (bf16[4096,384]{1,0:T(8,128)(2,1)S(1)}, f32[4096,384]{1,0:T(8,128)}) fusion(f32[4096,384]{1,0:T(8,128)} %fusion.104, bf16[4096,768]{1,0:T(8,128)(2,1)} %all-gather.13.cloned.1.call-done, bf16[768,384]{1,0:T(8,128)(2,1)} %all_gather.52), kind=kOutput, calls=%fused_computation.36 | convolution fusion | flops 2447376384 | bytes 22609920 | tf_op jit(solution)/shard_map/dot_general | solution.py:27
  489.0 9.9 convolution_convert_fusion.2
  499.0 58.6 %reduce-scatter.19.cloned.1.call-done = bf16[512,768]{1,0:T(8,128)(2,1)} async-done(((bf16[4096,768]{1,0:T(8,128)(2,1)}), bf16[512,768]{1,0:T(8,128)(2,1)}) %reduce-scatter.19.cloned.1.call-update) | async-done | bytes 786448 | tf_op jit(solution)/shard_map/reduce_scatter | solution.py:181
  559.4 68.6 %reduce-scatter.17.cloned.1.call-done = bf16[512,768]{1,0:T(8,128)(2,1)} async-done(((bf16[4096,768]{1,0:T(8,128)(2,1)}), bf16[512,768]{1,0:T(8,128)(2,1)}) %reduce-scatter.17.cloned.1.call-update) | async-done | bytes 786448 | tf_op jit(solution)/shard_map/reduce_scatter | solution.py:171
  633.6 63.0 %all-gather.17.cloned.1.call-done = bf16[4096,768]{1,0:T(8,128)(2,1)} async-done(((bf16[512,768]{1,0:T(8,128)(2,1)}), bf16[4096,768]{1,0:T(8,128)(2,1)}) %all-gather.17.cloned.1.call-update) | async-done | bytes 6291472 | tf_op jit(solution)/shard_map/all_gather | solution.py:188
  702.5 16.4 %fusion = f32[8,3,512,512]{2,3,1,0:T(8,128)} fusion(f32[8,3,512]{2,1,0:T(4,128)S(1)} %log_add_fusion, f32[3,512,512]{1,2,0:T(8,128)} %copy.31, pred[8,512,512]{1,2,0:T(8,128)(4,1)S(1)} %copy-done.5, bf16[8,512,96]{1,2,0:T(8,128)(2,1)} %bitcast.68, bf16[3,96]{1,0:T(4,128)(2,1)S(1)} %fusion.92, bf16[8,512,96]{1,2,0:T(8,128)(2,1)} %bitcast.65), kind=kOutput, calls=%fused_computation | convolution fusion | flops 1229206016 | bytes 32031296 | tf_op jit(solution)/shard_map/while/body/eval_jaxpr/sub | solution.py:113
  718.8 15.5 %fusion.9 = bf16[3,512,512]{1,2,0:T(8,128)(2,1)} fusion(f32[8,3,512,512]{2,3,1,0:T(8,128)} %fusion, f32[8,3,512]{2,1,0:T(4,128)S(1)} %log_add_fusion, f32[3,512,512]{1,2,0:T(8,128)} %copy.31, pred[8,512,512]{1,2,0:T(8,128)(4,1)S(1)} %copy-done.5, bf16[3,96]{1,0:T(4,128)(2,1)S(1)} %fusion.92, bf16[8,512,96]{1,2,0:T(8,128)(2,1)} %bitcast.66, ...), kind=kOutput, calls=%fused_computation.12 | convolution fusion | flops 1240989696 | bytes 33604160 | tf_op jit(solution)/shard_map/while/body/eval_jaxpr/sqgw,skgw->sgqk/dot_general | solution.py:109
  741.5 14.6 %copy.44 = bf16[12,512,512]{1,0,2:T(8,128)(2,1)} copy(bf16[12,512,512]{2,1,0:T(8,128)(2,1)} %constant_dynamic-update-slice_fusion) | data formatting | bytes 12582912
  756.1 13.4 %copy.52 = bf16[64,8,12,512]{3,1,2,0:T(8,128)(2,1)} copy(bf16[64,8,12,512]{3,2,1,0:T(8,128)(2,1)} %bitcast.56) | data formatting | bytes 12582912
  769.6 8.9 convolution_convert_fusion.5
  779.0 8.0 convolution_convert_fusion.6
  792.2 9.2 fusion.67
  813.0 25.6 %reduce-scatter.31.cloned.1.call-done = bf16[128,6144]{1,0:T(8,128)(2,1)} async-done(((bf16[512,6144]{1,0:T(8,128)(2,1)}), bf16[128,6144]{1,0:T(8,128)(2,1)}) %reduce-scatter.31.cloned.1.call-update) | async-done | bytes 1572880
  845.8 20.7 %reduce-scatter.29.cloned.1.call-done = bf16[384,192]{0,1:T(8,128)(2,1)} async-done(((bf16[384,768]{0,1:T(8,128)(2,1)}), bf16[384,192]{0,1:T(8,128)(2,1)}) %reduce-scatter.29.cloned.1.call-update) | async-done | bytes 147472 | tf_op jit(solution)/shard_map/reduce_scatter | solution.py:226
  868.1 26.4 %reduce-scatter.27.cloned.1.call-done = bf16[192,384]{1,0:T(8,128)(2,1)} async-done(((bf16[768,384]{1,0:T(8,128)(2,1)}), bf16[192,384]{1,0:T(8,128)(2,1)}) %reduce-scatter.27.cloned.1.call-update) | async-done | bytes 147472 | tf_op jit(solution)/shard_map/reduce_scatter | solution.py:220
  896.2 25.1 %reduce-scatter.33.cloned.1.call-done = bf16[192,96]{1,0:T(8,128)(2,1)} async-done(((bf16[768,96]{1,0:T(8,128)(2,1)}), bf16[192,96]{1,0:T(8,128)(2,1)}) %reduce-scatter.33.cloned.1.call-update) | async-done | bytes 36880
  922.9 25.6 %reduce-scatter.23.cloned.1.call-done = bf16[192,96]{1,0:T(8,128)(2,1)} async-done(((bf16[768,96]{1,0:T(8,128)(2,1)}), bf16[192,96]{1,0:T(8,128)(2,1)}) %reduce-scatter.23.cloned.1.call-update) | async-done | bytes 36880 | tf_op jit(solution)/shard_map/reduce_scatter | solution.py:217
  950.0 70.5 %reduce-scatter.21.cloned.1.call-done = bf16[512,768]{1,0:T(8,128)(2,1)} async-done(((bf16[4096,768]{1,0:T(8,128)(2,1)}), bf16[512,768]{1,0:T(8,128)(2,1)}) %reduce-scatter.21.cloned.1.call-update) | async-done | bytes 786448 | tf_op jit(solution)/shard_map/reduce_scatter | solution.py:196
  1024.3 9.9 all-reduce.10
  1034.3 13.7 %all-reduce.8 = (bf16[192]{0:T(256)(128)(2,1)S(1)}, bf16[192]{0:T(256)(128)(2,1)S(1)}) all-reduce(bf16[192]{0:T(256)(128)(2,1)S(1)} %dynamic-slice.6, bf16[192]{0:T(256)(128)(2,1)S(1)} %dynamic-slice.10), channel_id=7, replica_groups=mesh['gx'=4,'gy'=8] {'gy'}, use_global_device_ids=true, to_apply=%region_16.17.clone | all-reduce | flops 384 | bytes 1536
  (158 shorter events, 121.5 us)
Async XLA Ops:
  7.2 40.0 %copy-start.21 = (bf16[96,192]{1,0:T(8,128)(2,1)S(1)}, bf16[96,192]{1,0:T(8,128)(2,1)}, u32[]{:S(2)}) copy-start(bf16[96,192]{1,0:T(8,128)(2,1)} %param.15) | copy-start | bytes 110596
  7.2 48.3 %copy-start.22 = (bf16[192,96]{1,0:T(8,128)(2,1)S(1)}, bf16[192,96]{1,0:T(8,128)(2,1)}, u32[]{:S(2)}) copy-start(bf16[192,96]{1,0:T(8,128)(2,1)} %param.13) | copy-start | bytes 110596
  7.2 39.2 %all-gather.7.cloned.1.call-start = ((), (), s32[]{:S(2)}) async-start(), calls=%async_computation.10 | async-start | bytes 1769472 | tf_op jit(solution)/shard_map/all_gather | solution.py:137
  7.9 55.8 %copy-start.20 = (s32[8,512]{1,0:T(8,128)S(1)}, s32[8,512]{1,0:T(8,128)}, u32[]{:S(2)}) copy-start(s32[8,512]{1,0:T(8,128)} %param.11) | copy-start | bytes 49156
  7.9 99.6 %all-gather.11.cloned.1.call-start = ((), (), s32[]{:S(2)}) async-start(), calls=%async_computation.12 | async-start | bytes 7077888 | tf_op jit(solution)/shard_map/all_gather | solution.py:155
  46.3 131.8 %all-gather.9.cloned.1.call-start = ((), (), s32[]{:S(2)}) async-start(), calls=%async_computation.11 | async-start | bytes 7864320 | tf_op jit(solution)/shard_map/all_gather | solution.py:146
  47.0 290.9 %reduce-scatter.15.cloned.1.call-start = ((), (), s32[]{:S(2)}) async-start(), calls=%async_computation.13 | async-start | bytes 14155776 | tf_op jit(solution)/shard_map/reduce_scatter | solution.py:162
  63.7 48.6 %copy-start.10 = (bf16[768,96]{1,0:T(8,128)(2,1)}, bf16[768,96]{1,0:T(8,128)(2,1)S(1)}, u32[]{:S(2)}) copy-start(bf16[768,96]{1,0:T(8,128)(2,1)S(1)} %all_gather.47) | copy-start | bytes 442372
  65.2 129.2 %copy-start.4 = (pred[8,512,512]{1,2,0:T(8,128)(4,1)}, pred[8,512,512]{1,2,0:T(8,128)(4,1)S(1)}, u32[]{:S(2)}) copy-start(pred[8,512,512]{1,2,0:T(8,128)(4,1)S(1)} %broadcast_compare_fusion) | copy-start | bytes 6291460
  208.5 129.4 %copy-start = (bf16[512,768]{1,0:T(8,128)(2,1)S(1)}, bf16[512,768]{1,0:T(8,128)(2,1)}, u32[]{:S(2)}) copy-start(bf16[512,768]{1,0:T(8,128)(2,1)} %param.10) | copy-start | bytes 2359300
  208.5 194.0 %all-gather.15.cloned.1.call-start = ((), (), s32[]{:S(2)}) async-start(), calls=%async_computation.16 | async-start | bytes 7077888 | tf_op jit(solution)/shard_map/all_gather | solution.py:175
  209.1 258.9 %all-gather.13.cloned.1.call-start = ((), (), s32[]{:S(2)}) async-start(), calls=%async_computation.14 | async-start | bytes 7077888 | tf_op jit(solution)/shard_map/all_gather | solution.py:166
  339.5 13.3 %copy-start.15 = (bf16[384,192]{0,1:T(8,128)(2,1)S(1)}, bf16[384,192]{0,1:T(8,128)(2,1)}, u32[]{:S(2)}) copy-start(bf16[384,192]{0,1:T(8,128)(2,1)} %param.18) | copy-start | bytes 442372
  341.0 216.5 %reduce-scatter.19.cloned.1.call-start = ((), (), s32[]{:S(2)}) async-start(), calls=%async_computation.17 | async-start | bytes 7077888 | tf_op jit(solution)/shard_map/reduce_scatter | solution.py:181
  468.0 15.5 %copy-start.13 = (bf16[768,384]{1,0:T(8,128)(2,1)S(1)}, bf16[768,384]{1,0:T(8,128)(2,1)}, u32[]{:S(2)}) copy-start(bf16[768,384]{1,0:T(8,128)(2,1)} %all_gather.52) | copy-start | bytes 1769476
  488.9 139.1 %reduce-scatter.17.cloned.1.call-start = ((), (), s32[]{:S(2)}) async-start(), calls=%async_computation.15 | async-start | bytes 7077888 | tf_op jit(solution)/shard_map/reduce_scatter | solution.py:171
  498.9 197.7 %all-gather.17.cloned.1.call-start = ((), (), s32[]{:S(2)}) async-start(), calls=%async_computation.18 | async-start | bytes 7077888 | tf_op jit(solution)/shard_map/all_gather | solution.py:188
  559.4 72.8 %copy-start.8 = (bf16[512,768]{1,0:T(8,128)(2,1)S(1)}, bf16[512,768]{1,0:T(8,128)(2,1)}, u32[]{:S(2)}) copy-start(bf16[512,768]{1,0:T(8,128)(2,1)} %param.19) | copy-start | bytes 2359300
  633.3 205.2 %reduce-scatter.31.cloned.1.call-start = ((), (), s32[]{:S(2)}) async-start(), calls=%async_computation.24 | async-start | bytes 7864320
  633.6 68.9 %copy-start.5 = (pred[8,512,512]{1,2,0:T(8,128)(4,1)S(1)}, pred[8,512,512]{1,2,0:T(8,128)(4,1)}, u32[]{:S(2)}) copy-start(pred[8,512,512]{1,2,0:T(8,128)(4,1)} %copy-done.4) | copy-start | bytes 6291460
  769.6 96.9 %reduce-scatter.29.cloned.1.call-start = ((), (), s32[]{:S(2)}) async-start(), calls=%async_computation.23 | async-start | bytes 737280 | tf_op jit(solution)/shard_map/reduce_scatter | solution.py:226
  778.6 116.0 %reduce-scatter.27.cloned.1.call-start = ((), (), s32[]{:S(2)}) async-start(), calls=%async_computation.22 | async-start | bytes 737280 | tf_op jit(solution)/shard_map/reduce_scatter | solution.py:220
  787.0 134.3 %reduce-scatter.33.cloned.1.call-start = ((), (), s32[]{:S(2)}) async-start(), calls=%async_computation.25 | async-start | bytes 245760
  802.6 145.9 %reduce-scatter.23.cloned.1.call-start = ((), (), s32[]{:S(2)}) async-start(), calls=%async_computation.20 | async-start | bytes 245760 | tf_op jit(solution)/shard_map/reduce_scatter | solution.py:217
  808.2 212.3 %reduce-scatter.21.cloned.1.call-start = ((), (), s32[]{:S(2)}) async-start(), calls=%async_computation.19 | async-start | bytes 7077888 | tf_op jit(solution)/shard_map/reduce_scatter | solution.py:196
  812.9 242.5 %reduce-scatter.25.cloned.1.call-start = ((), (), s32[]{:S(2)}) async-start(), calls=%async_computation.21 | async-start | bytes 1769472 | tf_op jit(solution)/shard_map/reduce_scatter | solution.py:240
  841.4 179.1 %copy-start.17 = (f32[768]{0:T(1024)S(1)}, f32[768]{0:T(1024)}, u32[]{:S(2)}) copy-start(f32[768]{0:T(1024)} %copy-done.16) | copy-start | bytes 9220
  841.4 179.1 %copy-start.19 = (f32[512]{0:T(512)S(1)}, f32[512]{0:T(512)}, u32[]{:S(2)}) copy-start(f32[512]{0:T(512)} %copy-done.18) | copy-start | bytes 6148
  841.4 180.8 %copy-start.26 = (f32[512]{0:T(512)S(1)}, f32[512]{0:T(512)}, u32[]{:S(2)}) copy-start(f32[512]{0:T(512)} %copy-done.25) | copy-start | bytes 6148
  844.3 177.9 %copy-start.24 = (f32[512]{0:T(512)S(1)}, f32[512]{0:T(512)}, u32[]{:S(2)}) copy-start(f32[512]{0:T(512)} %copy-done.23) | copy-start | bytes 6148
  844.3 204.9 %copy-start.2 = (f32[512,768]{1,0:T(8,128)S(1)}, f32[512,768]{1,0:T(8,128)}, u32[]{:S(2)}) copy-start(f32[512,768]{1,0:T(8,128)} %copy-done.1) | copy-start | bytes 4718596
  1020.5 28.7 %copy-start.7 = (bf16[512,768]{1,0:T(8,128)(2,1)S(1)}, bf16[512,768]{1,0:T(8,128)(2,1)}, u32[]{:S(2)}) copy-start(bf16[512,768]{1,0:T(8,128)(2,1)} %reduce-scatter.21.cloned.1.call-done) | copy-start | bytes 2359300
  (12 other events, 45.9 us)
Sparse Core Ops, SparseCore 0:
  9.6 27.8 all-gather.6
  46.4 61.0 all-gather.10
  109.4 68.6 all-gather.8
  208.6 129.2 reduce-scatter.14
  339.4 63.0 all-gather.14
  404.6 63.3 all-gather.12
  489.0 68.4 reduce-scatter.18
  559.8 68.1 reduce-scatter.16
  633.4 63.1 all-gather.16
  769.7 68.8 reduce-scatter.30
  841.4 25.0 reduce-scatter.28
  869.5 25.0 reduce-scatter.26
  897.3 23.9 reduce-scatter.32
  924.5 23.9 reduce-scatter.22
  950.7 69.7 reduce-scatter.20
  1022.7 32.6 reduce-scatter.24
where the time goes:
time: 1070 us; the launch traced here: 1060 us
  waiting for transfers between devices  721 us (67%)
  matrix products  134 us (13%)
  blocking collectives  90.4 us (8%)
  local copies, waits for them, and re-layouts  56.2 us (5%)
  other arithmetic  43.4 us (4%)
  between operations  17.3 us (2%)
    reduce_scatter x1, waiting for transfers between devices, shards(): lax.psum_scatter(matmul(mixed_low, output_rows), 'gy', scatter_dimension=...  129 us
    reduce_scatter x1, waiting for transfers between devices, shards(): lax.psum_scatter(matmul_nt(value_grad_low, value_cols).astype(jnp.bfloat1...  70.5 us
    reduce_scatter x1, waiting for transfers between devices, shards(): lax.psum_scatter(matmul(act_low, down_rows).astype(jnp.bfloat16), 'gy', s...  68.6 us
    all_gather x1, waiting for transfers between devices, shards(): lax.all_gather(mixing_part, 'gx', axis=2, tiled=True)  64.7 us
    all_gather x1, waiting for transfers between devices, shards(): branch_all = lax.all_gather(branch_low, 'gy', axis=0, tiled=True)  63 us
    reduce_scatter x1, waiting for transfers between devices, shards(): lax.psum_scatter(matmul_nt(up_grad_low, up_cols).astype(jnp.bfloat16), 'g...  58.6 us
    all_gather x1, waiting for transfers between devices, shards(): normed_two_all = lax.all_gather(normed_two, 'gy', axis=0, tiled=True)  56.7 us
    unnamed x18, waiting for transfers between devices  52.8 us
  transfers between devices with their start and end apart: 16, of which 15 were waited for; matrix products, arithmetic and copies ran while one was open for 10% of the time, Pallas kernels for 0%

commit v1 on v0

v1 whole, which is shorter than its diff:
```python
import functools

import jax
import jax.numpy as jnp
from jax import lax
from jax.experimental import pallas as pl
from jax.experimental.pallas import tpu as pltpu
from jax.sharding import PartitionSpec as P

D = 768
H = 12
HS = 64
FF = 3072
L = 512
EPS = 1e-05
G = 4
Z = 4
DB = D // G
CB = D // (2 * Z)
FB = FF // (2 * Z)
QB = L // (2 * Z)
KB = L // G
LN = 128
GW = 2 * LN
TM = 128
WIN = 3
HZ = H // Z
GC = 0.7978845608
GA = 0.044715
VMEM_LIMIT = 52 * 1024 * 1024

F32 = jnp.float32
BF16 = jnp.bfloat16


def dot(a, b, ca, cb):
    return lax.dot_general(a, b, (((ca,), (cb,)), ((), ())), preferred_element_type=F32)


def call(body, grid, in_specs, out_specs, out_shape, scratch=(), flops=0, nbytes=0):
    return pl.pallas_call(
        body,
        grid_spec=pltpu.PrefetchScalarGridSpec(
            num_scalar_prefetch=1,
            grid=grid,
            in_specs=in_specs,
            out_specs=out_specs,
            scratch_shapes=list(scratch),
        ),
        out_shape=out_shape,
        compiler_params=pltpu.CompilerParams(
            dimension_semantics=("arbitrary",) * len(grid), vmem_limit_bytes=VMEM_LIMIT
        ),
        cost_estimate=pl.CostEstimate(flops=flops, bytes_accessed=nbytes, transcendentals=0),
    )


def whole(shape):
    zeros = (0,) * len(shape)
    return pl.BlockSpec(shape, lambda i, t: zeros, pipeline_mode=pl.Buffered(1))


def rows(width):
    return pl.BlockSpec((TM, width), lambda i, t: (i, 0))


def out_whole(shape):
    zeros = (0,) * len(shape)
    return pl.BlockSpec(shape, lambda i, t: zeros)


def tab_a(t, g):
    return t[1 + g]


def tab_b(t, g):
    return t[1 + G + g]


def tab_z(t, z):
    return t[1 + 2 * G + z]


def norm_stats(x):
    mean = jnp.mean(x, axis=-1, keepdims=True)
    cen = x - mean
    rstd = lax.rsqrt(jnp.mean(cen * cen, axis=-1, keepdims=True) + EPS)
    return cen, rstd


def weight_z(ref, t, z):
    return jnp.concatenate([ref[tab_a(t, g), tab_z(t, z)] for g in range(G)], axis=0)


def head_masks(nrows):
    lane = lax.broadcasted_iota(jnp.int32, (nrows, GW), 1)
    col = jnp.where(lane < LN, lane, lane - (LN - CB))
    junk = jnp.logical_or(
        jnp.logical_and(lane >= CB, lane < LN), lane >= LN + CB
    )
    col = jnp.where(junk, -1, col)
    return [jnp.logical_and(col >= HS * i, col < HS * (i + 1)) for i in range(HZ)]


def halves(ref, off, core, axis0=None):
    lo = pl.multiple_of(off + core * QB, QB)
    hi = pl.multiple_of(off + (1 - core) * QB, QB)
    if axis0 is None:
        return jnp.concatenate([ref[pl.ds(lo, QB), :], ref[pl.ds(hi, QB), :]], axis=0)
    return jnp.concatenate(
        [ref[axis0, pl.ds(lo, QB), :], ref[axis0, pl.ds(hi, QB), :]], axis=0
    )


def put_halves(ref, off, core, val, axis0=None):
    lo = pl.multiple_of(off + core * QB, QB)
    hi = pl.multiple_of(off + (1 - core) * QB, QB)
    if axis0 is None:
        ref[pl.ds(lo, QB), :] = val[:QB]
        ref[pl.ds(hi, QB), :] = val[QB:]
    else:
        ref[axis0, pl.ds(lo, QB), :] = val[:QB]
        ref[axis0, pl.ds(hi, QB), :] = val[QB:]


def exp_scores(own, oth, t, m, start, head, mask):
    parts = [
        jnp.concatenate(
            [
                own[tab_b(t, start + i), tab_z(t, m), head],
                oth[tab_b(t, start + i), tab_z(t, m), head],
            ],
            axis=0,
        )
        for i in range(WIN)
    ]
    scores = jnp.concatenate(parts, axis=1).astype(F32)
    return jnp.where(mask, jnp.exp(scores), 0.0)


def window(m):
    return jnp.clip(m - 1, 0, G - WIN)


def values_body(t, x_ref, g_ref, v_ref, n_ref, val_ref):
    cen, rstd = norm_stats(x_ref[...].astype(F32))
    low = (cen * rstd * g_ref[...]).astype(BF16)
    n_ref[...] = low
    for z in range(Z):
        val_ref[z] = dot(low, weight_z(v_ref, t, z), 1, 0).astype(BF16)


def mixer_body(t, x_ref, g_ref, dq_ref, dk_ref, val_ref, own_ref, oth_ref, o_ref, mix_ref, mid_ref, n_ref):
    m = pl.program_id(0)
    core = t[0]
    start = window(m)
    k0 = pl.multiple_of(start * KB, KB)
    mask = halves(dq_ref, 0, core) == dk_ref[:, pl.ds(k0, WIN * KB)]
    heads = head_masks(TM)
    acc = halves(x_ref, 0, core).astype(F32)
    for z in range(Z):
        win = val_ref[z, pl.ds(k0, WIN * KB), :]
        out = jnp.zeros((TM, GW), F32)
        for i in range(HZ):
            e = exp_scores(own_ref, oth_ref, t, m, start, HZ * z + i, mask)
            inv = 1.0 / jnp.sum(e, axis=-1, keepdims=True)
            part = dot((e * inv).astype(BF16), win, 1, 0)
            out = jnp.where(heads[i], part, out)
        low = out.astype(BF16)
        put_halves(mix_ref, 0, core, low, z)
        acc = acc + dot(low, weight_z(o_ref, t, z), 1, 1)
    put_halves(mid_ref, 0, core, acc)
    cen, rstd = norm_stats(acc)
    put_halves(n_ref, 0, core, (cen * rstd * g_ref[...]).astype(BF16))


def ffn_body(first, last, t, n_ref, c_ref, u_ref, d_ref, *refs):
    refs = list(refs)
    if not first:
        ia_ref, ib_ref = refs[:2]
        refs = refs[2:]
    if last:
        mid_ref = refs[0]
        refs = refs[1:]
    gu_ref, gd_ref, b_ref, a_ref = refs[:4]
    j = pl.program_id(0)
    n = n_ref[...]
    cot = c_ref[...]
    up_w = jnp.concatenate([u_ref[tab_b(t, g), 0] for g in range(G)], axis=0)
    dn_w = jnp.concatenate([d_ref[tab_a(t, g), 0] for g in range(G)], axis=0)

    @pl.when(j == 0)
    def _():
        if first:
            a_ref[...] = jnp.zeros_like(a_ref)
            b_ref[...] = jnp.zeros_like(b_ref)
        else:
            a_ref[...] = ia_ref[...]
            b_ref[...] = ib_ref[...]

    up = dot(n, up_w, 1, 0)
    sq = up * up
    th = jnp.tanh(GC * up * (1.0 + GA * sq))
    half = 0.5 + 0.5 * th
    act = (up * half).astype(BF16)
    slope = half + (0.5 * GC) * up * (1.0 - th * th) * (1.0 + (3.0 * GA) * sq)
    a_ref[...] += dot(act, dn_w, 1, 1)
    gd = dot(cot, act, 0, 0).astype(BF16)
    up_g = (dot(cot, dn_w, 1, 0) * slope).astype(BF16)
    gu = dot(n, up_g, 0, 0).astype(BF16)
    b_ref[...] += dot(up_g, up_w, 1, 1)
    for g in range(G):
        gu_ref[tab_b(t, g), 0] = gu[g * DB : (g + 1) * DB]
        gd_ref[tab_a(t, g), 0] = gd[g * DB : (g + 1) * DB]
    if last:
        lo_ref = refs[4]

        @pl.when(j == Z - 1)
        def _():
            lo_ref[...] = (mid_ref[...] + a_ref[...]).astype(BF16)


def norm_back(cen, rstd, gain, dn):
    xhat = cen * rstd
    e = dn * gain
    dv = (
        e
        - jnp.mean(e, axis=-1, keepdims=True)
        - xhat * jnp.mean(e * xhat, axis=-1, keepdims=True)
    ) * rstd
    return dv, jnp.sum(dn * xhat, axis=0, keepdims=True)


def mixer_back_body(
    t, dn_ref, mid_ref, c_ref, g_ref, dq_ref, dk_ref, mix_ref, val_ref, own_ref, oth_ref, o_ref,
    mg_ref, keep_ref, send_ref, go_ref, vg_ref, dg_ref, go_acc, vg_acc,
):
    m = pl.program_id(0)
    core = t[0]
    start = window(m)
    k0 = pl.multiple_of(start * KB, KB)

    @pl.when(m == 0)
    def _():
        go_acc[...] = jnp.zeros_like(go_acc)
        vg_acc[...] = jnp.zeros_like(vg_acc)
        dg_ref[...] = jnp.zeros_like(dg_ref)

    cen, rstd = norm_stats(halves(mid_ref, 0, core))
    dv, dg = norm_back(cen, rstd, g_ref[...], halves(dn_ref, 0, core))
    dg_ref[...] += dg
    mid_grad = halves(c_ref, 0, core).astype(F32) + dv
    put_halves(mg_ref, 0, core, mid_grad)
    branch = mid_grad.astype(BF16)
    mask = halves(dq_ref, 0, core) == dk_ref[:, pl.ds(k0, WIN * KB)]
    heads = head_masks(TM)
    rest = jnp.where(start == 0, G - 1, 0)
    keep_ref[tab_b(t, rest), 0] = jnp.zeros((H, QB, KB), BF16)
    send_ref[tab_b(t, rest), 0] = jnp.zeros((H, QB, KB), BF16)
    for z in range(Z):
        go_acc[z] += dot(branch, halves(mix_ref, 0, core, z), 0, 0)
        grad = dot(branch, weight_z(o_ref, t, z), 1, 0)
        grad = grad.astype(BF16).astype(F32)
        win = val_ref[z, pl.ds(k0, WIN * KB), :]
        total = jnp.zeros((WIN * KB, GW), F32)
        for i in range(HZ):
            e = exp_scores(own_ref, oth_ref, t, m, start, HZ * z + i, mask)
            inv = 1.0 / jnp.sum(e, axis=-1, keepdims=True)
            prob = e * inv
            mine = jnp.where(heads[i], grad, 0.0).astype(BF16)
            total = total + dot(prob.astype(BF16), mine, 0, 0)
            dp = dot(mine, win, 1, 1)
            pd = prob * dp
            ds = (pd - prob * jnp.sum(pd, axis=-1, keepdims=True)).astype(BF16)
            for k in range(WIN):
                blk = ds[:, k * KB : (k + 1) * KB]
                keep_ref[tab_b(t, start + k), 0, HZ * z + i] = blk[:QB]
                send_ref[tab_b(t, start + k), 0, HZ * z + i] = blk[QB:]
        vg_acc[z, pl.ds(k0, WIN * KB), :] += total

    @pl.when(m == Z - 1)
    def _():
        vg_ref[...] = vg_acc[...].astype(BF16)
        for z in range(Z):
            for g in range(G):
                go_ref[tab_a(t, g), tab_z(t, z)] = go_acc[z, g * DB : (g + 1) * DB].astype(BF16)


def last_body(t, x_ref, g_ref, n_ref, vg_ref, v_ref, mg_ref, gi_ref, gv_ref, dg_ref, gv_acc):
    m = pl.program_id(0)

    @pl.when(m == 0)
    def _():
        gv_acc[...] = jnp.zeros_like(gv_acc)
        dg_ref[...] = jnp.zeros_like(dg_ref)

    low = n_ref[...]
    dn = jnp.zeros((TM, D), F32)
    for z in range(Z):
        vg = vg_ref[z]
        gv_acc[z] += dot(low, vg, 0, 0)
        dn = dn + dot(vg, weight_z(v_ref, t, z), 1, 1)
    cen, rstd = norm_stats(x_ref[...].astype(F32))
    dv, dg = norm_back(cen, rstd, g_ref[...], dn)
    dg_ref[...] += dg
    gi_ref[...] = mg_ref[...] + dv

    @pl.when(m == Z - 1)
    def _():
        for z in range(Z):
            for g in range(G):
                gv_ref[tab_a(t, g), tab_z(t, z)] = gv_acc[z, g * DB : (g + 1) * DB].astype(BF16)


def sds(shape, dtype):
    return jax.ShapeDtypeStruct(shape, dtype)


W_SHAPE = (G, Z, DB, GW)
M_SHAPE = (G, Z, H, QB, KB)
F_SHAPE = (G, Z, DB, FB)


def run_values(tab, x, gain, v_w):
    return call(
        values_body,
        (L // TM,),
        [rows(D), whole((1, D)), whole(W_SHAPE)],
        [rows(D), pl.BlockSpec((Z, TM, GW), lambda i, t: (0, i, 0))],
        [sds((L, D), BF16), sds((Z, L, GW), BF16)],
        flops=2 * L * D * Z * GW,
        nbytes=6 << 20,
    )(tab, x, gain, v_w)


def run_mixer(tab, x, gain, dq, dk, vals, own, oth, o_w):
    return call(
        mixer_body,
        (L // TM,),
        [
            rows(D), whole((1, D)), rows(1), whole((1, L)), whole((Z, L, GW)),
            whole(M_SHAPE), whole(M_SHAPE), whole(W_SHAPE),
        ],
        [pl.BlockSpec((Z, TM, GW), lambda i, t: (0, i, 0)), rows(D), rows(D)],
        [sds((Z, L, GW), BF16), sds((L, D), F32), sds((L, D), BF16)],
        flops=2 * L * D * Z * GW + 2 * H * L * WIN * KB * GW,
        nbytes=14 << 20,
    )(tab, x, gain, dq, dk, vals, own, oth, o_w)


def run_ffn(tab, n, cot, u_w, d_w, acc=None, mid=None):
    first, last = acc is None, mid is not None
    blk = pl.BlockSpec((G, 1, DB, FB), lambda i, t: (0, i, 0, 0))
    in_specs = [whole((L, D)), whole((L, D)), blk, blk]
    args = [tab, n, cot, u_w, d_w]
    if not first:
        in_specs += [whole((L, D)), whole((L, D))]
        args += list(acc)
    if last:
        in_specs += [whole((L, D))]
        args += [mid]
    out_specs = [blk, blk, out_whole((L, D))]
    outs = [sds(F_SHAPE, BF16), sds(F_SHAPE, BF16), sds((L, D), F32)]
    scratch = ()
    if last:
        scratch = (pltpu.VMEM((L, D), F32),)
        out_specs += [out_whole((L, D))]
        outs += [sds((L, D), BF16)]
    else:
        out_specs += [out_whole((L, D))]
        outs += [sds((L, D), F32)]

    def body(t, *refs):
        if last:
            refs = list(refs)
            refs = refs[:-2] + [refs[-1], refs[-2]]
        ffn_body(first, last, t, *refs)

    return call(
        body, (Z,), in_specs, out_specs, outs, scratch, flops=6 * L * D * FF, nbytes=20 << 20
    )(*args)


def run_mixer_back(tab, dn, mid, cot, gain, dq, dk, mixed, vals, own, oth, o_w):
    blk = pl.BlockSpec((G, 1, H, QB, KB), lambda i, t: (0, t[1 + 2 * G + i], 0, 0, 0))
    return call(
        mixer_back_body,
        (L // TM,),
        [
            rows(D), rows(D), rows(D), whole((1, D)), rows(1), whole((1, L)),
            pl.BlockSpec((Z, TM, GW), lambda i, t: (0, i, 0)), whole((Z, L, GW)),
            whole(M_SHAPE), whole(M_SHAPE), whole(W_SHAPE),
        ],
        [rows(D), blk, blk, out_whole(W_SHAPE), out_whole((Z, L, GW)), out_whole((1, D))],
        [
            sds((L, D), F32), sds(M_SHAPE, BF16), sds(M_SHAPE, BF16), sds(W_SHAPE, BF16),
            sds((Z, L, GW), BF16), sds((1, D), F32),
        ],
        scratch=(pltpu.VMEM((Z, D, GW), F32), pltpu.VMEM((Z, L, GW), F32)),
        flops=4 * L * D * Z * GW + 6 * H * L * WIN * KB * GW,
        nbytes=28 << 20,
    )(tab, dn, mid, cot, gain, dq, dk, mixed, vals, own, oth, o_w)


def run_last(tab, x, gain, low, vg, v_w, mid_grad):
    return call(
        last_body,
        (L // TM,),
        [
            rows(D), whole((1, D)), rows(D), pl.BlockSpec((Z, TM, GW), lambda i, t: (0, i, 0)),
            whole(W_SHAPE), rows(D),
        ],
        [rows(D), out_whole(W_SHAPE), out_whole((1, D))],
        [sds((L, D), F32), sds(W_SHAPE, BF16), sds((1, D), F32)],
        scratch=(pltpu.VMEM((Z, D, GW), F32),),
        flops=4 * L * D * Z * GW,
        nbytes=12 << 20,
    )(tab, x, gain, low, vg, v_w, mid_grad)


def cols_in(mat):
    mat = mat.reshape(G, DB, Z, 2, CB).transpose(0, 2, 1, 3, 4)
    return jnp.pad(mat, ((0, 0),) * 4 + ((0, LN - CB),)).reshape(W_SHAPE)


def cols_out(mat):
    mat = mat.reshape(G, Z, DB, 2, LN)[..., :CB]
    return mat.transpose(0, 2, 1, 3, 4).reshape(D, D)


def shards(layer_in, doc_ids, mix_gain, value_w, mixing, output_w, ffn_gain, up_w, down_w, cot):
    ax = ("gx", "gy")
    me = lax.axis_index("gy")

    def gather(arr, d0, d1):
        arr = lax.all_gather(arr, "gx", axis=d0, tiled=True)
        return lax.all_gather(arr, "gy", axis=d1, tiled=True)

    def scatter(arr, d0, d1):
        arr = lax.psum_scatter(arr, "gx", scatter_dimension=d0, tiled=True)
        return lax.psum_scatter(arr, "gy", scatter_dimension=d1, tiled=True).astype(F32)

    gains = lax.all_gather(jnp.stack([mix_gain, ffn_gain]), ax, axis=1, tiled=True).astype(F32)
    gain_one, gain_two = gains[:1], gains[1:]
    v_full = cols_in(gather(value_w, 0, 1))
    o_full = cols_in(gather(output_w.T, 0, 1))
    mix_full = gather(mixing, 2, 1).reshape(H, Z, 2, QB, G, KB).transpose(2, 4, 1, 0, 3, 5)
    up_full = gather(up_w, 0, 1).reshape(G, DB, Z, 2, FB).transpose(3, 0, 2, 1, 4)
    dn_full = gather(down_w.T, 0, 1).reshape(G, DB, Z, 2, FB).transpose(3, 0, 2, 1, 4)
    tab = jnp.array([0] + [0, 1, 2, 3] * 3, jnp.int32)

    docs = lax.dynamic_slice_in_dim(doc_ids, me, 1, 0)
    dq, dk = docs.reshape(L, 1), docs
    low, vals = run_values(tab, layer_in, gain_one, v_full)
    mixed, mid, n_two = run_mixer(
        tab, layer_in, gain_two, dq, dk, vals, mix_full[0], mix_full[1], o_full
    )
    gu0, gd0, *acc = run_ffn(tab, n_two, cot, up_full[0], dn_full[0])
    acc = (acc[1], acc[0])
    gu1, gd1, n_grad, layer_out = run_ffn(tab, n_two, cot, up_full[1], dn_full[1], acc, mid)
    mid_grad, gm0, gm1, go, vg, dg_two = run_mixer_back(
        tab, n_grad, mid, cot, gain_two, dq, dk, mixed, vals, mix_full[0], mix_full[1], o_full
    )
    grad_in, gv, dg_one = run_last(tab, layer_in, gain_one, low, vg, v_full, mid_grad)

    def ffn_out(a, b):
        return jnp.stack([a, b]).transpose(1, 3, 2, 0, 4).reshape(D, FF)

    grad_up = scatter(ffn_out(gu0, gu1), 0, 1)
    grad_down = scatter(ffn_out(gd0, gd1), 0, 1).T
    grad_value = scatter(cols_out(gv), 0, 1)
    grad_output = scatter(cols_out(go), 0, 1).T
    gm = jnp.stack([gm0, gm1]).transpose(3, 2, 0, 4, 1, 5).reshape(H, L, L)
    grad_mixing = scatter(gm, 2, 1)
    dgs = jnp.concatenate([dg_one, dg_two], axis=0)
    dgs = lax.psum_scatter(dgs, ax, scatter_dimension=1, tiled=True)
    return (
        layer_out, grad_in, dgs[0], grad_value, grad_mixing, grad_output, dgs[1], grad_up, grad_down,
    )


def solution(mesh):
    tok = P(("gx", "gy"), None)
    vec = P(("gx", "gy"))
    wgt = P("gx", "gy")
    twg = P("gy", "gx")
    mix = P(None, "gy", "gx")
    in_specs = (tok, P("gx", None), vec, wgt, mix, twg, vec, wgt, twg, tok)
    out_specs = (tok, tok, vec, wgt, mix, twg, vec, wgt, twg)
    return jax.shard_map(shards, mesh=mesh, in_specs=in_specs, out_specs=out_specs, check_vma=False)
```

time: 1070 us -> 778 us (0.73)
  waiting for transfers between devices: 721 us -> 293 us
  local copies, waits for them, and re-layouts: 56.2 us -> 223 us
  matrix products: 134 us -> 0 us
  Pallas kernels: 0 us -> 80.5 us
  blocking collectives: 90.4 us -> 133 us
  other arithmetic: 43.4 us -> 19.7 us
    reduce_scatter x8 -> x5, waiting for transfers between devices: 402 us -> 86.4 us  [the longest x2 49 us: scatter(): lax.psum_scatter(arr, 'gy', scatter_dimension=d1, tiled=True).astype(F32)]
    all_gather x6 -> x5, waiting for transfers between devices: 266 us -> 69.7 us  [gather(): return lax.all_gather(arr, 'gy', axis=d1, tiled=True)]
    dot_general x15 -> x0, matrix products: 117 us -> none  [the longest x4 35 us: matmul(): return jnp.dot(left, right, preferred_element_type=jnp.float32)]
    reshape x0 -> x19, local copies, waits for them, and re-layouts: none -> 91 us  [the longest x2 22.5 us: ffn_out(): return jnp.stack([a, b]).transpose(1, 3, 2, 0, 4).reshape(D, FF)]
    unnamed x18 -> x20, waiting for transfers between devices: 52.8 us -> 137 us
    pallas_call x0 -> x6, Pallas kernels: none -> 80.5 us  [the longest x2 34.1 us: run_ffn(): call(body, (Z,), in_specs, out_specs, outs, scratch, flops=6 * L * D * FF...]
    all_gather x4 -> x6, blocking collectives: 38.5 us -> 93.6 us  [the longest x5 52.5 us: gather(): arr = lax.all_gather(arr, 'gx', axis=d0, tiled=True)]
    unnamed x74 -> x42, local copies, waits for them, and re-layouts: 42.1 us -> 95.7 us
  transfers between devices with their start and end apart: 16 -> 15, of which waited for: 15 -> 8; matrix products, arithmetic and copies ran while one was open for 10% -> 28% of each run, Pallas kernels for 0% -> 1%
where the time goes in v1:
time: 778 us; the launch traced here: 766 us
  waiting for transfers between devices  293 us (38%)
  local copies, waits for them, and re-layouts  223 us (29%)
  blocking collectives  133 us (17%)
  Pallas kernels  80.5 us (10%)
  other arithmetic  19.7 us (3%)
  between operations  14.8 us (2%)
    unnamed x20, waiting for transfers between devices  137 us
    unnamed x42, local copies, waits for them, and re-layouts  95.7 us
    all_gather x5, waiting for transfers between devices, gather(): return lax.all_gather(arr, 'gy', axis=d1, tiled=True)  69.7 us
    all_gather x5, blocking collectives, gather(): arr = lax.all_gather(arr, 'gx', axis=d0, tiled=True)  52.5 us
    reduce_scatter x2, waiting for transfers between devices, scatter(): lax.psum_scatter(arr, 'gy', scatter_dimension=d1, tiled=True).astype(F32)  49 us
    all_gather x1, blocking collectives, shards(): lax.all_gather(jnp.stack([mix_gain, ffn_gain]), ax, axis=1, tiled=True)  41.1 us
    unnamed x1, blocking collectives  39.5 us
    reduce_scatter x3, waiting for transfers between devices, scatter(): arr = lax.psum_scatter(arr, 'gx', scatter_dimension=d0, tiled=True)  37.4 us
  transfers between devices with their start and end apart: 15, of which 8 were waited for; matrix products, arithmetic and copies ran while one was open for 28% of the time, Pallas kernels for 1%

profile of v1, /device:TPU:0, one launch (start us, length us, event | category | flops | bytes accessed | tf_op | source)
XLA Modules:
  0.0 765.6 jit_solution(6086787188753511185)
XLA Ops:
  7.3 10.6 %all_gather.34 = bf16[768,96]{1,0:T(8,128)(2,1)S(1)} all-gather(bf16[192,96]{1,0:T(8,128)(2,1)} %param.14), channel_id=1, replica_groups=mesh['gx'=4,'gy'=8] {'gx'}, dimensions={0}, use_global_device_ids=true | all-gather | bytes 184320 | tf_op jit(solution)/shard_map/all_gather | solution.py:436
  19.6 8.5 %all_gather.38 = bf16[768,96]{1,0:T(8,128)(2,1)S(1)} all-gather(bf16[192,96]{1,0:T(8,128)(2,1)S(1)} %bitcast.102), channel_id=1, replica_groups=mesh['gx'=4,'gy'=8] {'gx'}, dimensions={0}, use_global_device_ids=true | all-gather | bytes 184320 | tf_op jit(solution)/shard_map/all_gather | solution.py:436
  29.0 11.8 %all_gather.42 = bf16[768,384]{1,0:T(8,128)(2,1)} all-gather(bf16[192,384]{1,0:T(8,128)(2,1)} %bitcast.103), channel_id=1, replica_groups=mesh['gx'=4,'gy'=8] {'gx'}, dimensions={0}, use_global_device_ids=true | all-gather | bytes 737280 | tf_op jit(solution)/shard_map/all_gather | solution.py:436
  40.8 10.2 %all_gather.40 = bf16[768,384]{1,0:T(8,128)(2,1)} all-gather(bf16[192,384]{1,0:T(8,128)(2,1)S(1)} %copy-done.10), channel_id=1, replica_groups=mesh['gx'=4,'gy'=8] {'gx'}, dimensions={0}, use_global_device_ids=true | all-gather | bytes 737280 | tf_op jit(solution)/shard_map/all_gather | solution.py:436
  51.1 11.5 %all_gather.36 = bf16[12,64,512]{2,1,0:T(8,128)(2,1)} all-gather(bf16[12,64,128]{2,1,0:T(8,128)(2,1)S(1)} %copy-done.9), channel_id=1, replica_groups=mesh['gx'=4,'gy'=8] {'gx'}, dimensions={2}, use_global_device_ids=true | all-gather | bytes 983040 | tf_op jit(solution)/shard_map/all_gather | solution.py:436
  62.9 41.1 %all-gather = bf16[32,24,2]{1,2,0:T(2,128)(2,1)S(1)} all-gather(bf16[1,24,2]{1,2,0:T(2,128)(2,1)S(1)} %maximum_bitcast_fusion.3), channel_id=1, replica_groups=mesh['gx'=4,'gy'=8] {'gx','gy'}, dimensions={0}, use_global_device_ids=true | all-gather | bytes 3168 | tf_op jit(solution)/shard_map/all_gather | solution.py:443
  124.6 5.2 shard_map.178
  129.8 11.6 %reshape.70 = bf16[4,192,4,2,384]{4,3,2,1,0:T(2,128)(2,1)} reshape(bf16[768,3072]{1,0:T(8,128)(2,1)} %all-gather.15.cloned.1.call-done) | data formatting | bytes 9437184 | tf_op jit(solution)/shard_map/reshape | solution.py:449
  141.4 5.4 copy.107
  146.9 24.3 %all-gather.13.cloned.1.call-done = bf16[768,3072]{1,0:T(8,128)(2,1)} async-done(((bf16[768,384]{1,0:T(8,128)(2,1)}), bf16[768,3072]{1,0:T(8,128)(2,1)}) %all-gather.13.cloned.1.call-update) | async-done | bytes 4718608 | tf_op jit(solution)/shard_map/all_gather | solution.py:437
  171.2 11.9 %reshape.69 = bf16[4,192,4,2,384]{4,3,2,1,0:T(2,128)(2,1)} reshape(bf16[768,3072]{1,0:T(8,128)(2,1)} %all-gather.13.cloned.1.call-done) | data formatting | bytes 9437184 | tf_op jit(solution)/shard_map/reshape | solution.py:448
  190.7 45.3 %all-gather.9.cloned.1.call-done = bf16[12,512,512]{2,1,0:T(8,128)(2,1)} async-done(((bf16[12,64,512]{2,1,0:T(8,128)(2,1)}), bf16[12,512,512]{2,1,0:T(8,128)(2,1)}) %all-gather.9.cloned.1.call-update) | async-done | bytes 6291472 | tf_op jit(solution)/shard_map/all_gather | solution.py:437
  236.1 9.8 %reshape.66 = bf16[12,4,2,64,4,128]{5,4,3,2,1,0:T(4,128)(2,1)} reshape(bf16[12,512,512]{2,1,0:T(8,128)(2,1)} %all-gather.9.cloned.1.call-done) | data formatting | bytes 12582912 | tf_op jit(solution)/shard_map/reshape | solution.py:447
  254.4 12.5 %shard_map.179 = (bf16[4,512,256]{2,1,0:T(8,128)(2,1)}, f32[512,768]{1,0:T(8,128)}, bf16[512,768]{1,0:T(8,128)(2,1)S(1)}) custom-call(s32[13]{0:T(128)S(1)} %copy-done.3, bf16[512,768]{1,0:T(8,128)(2,1)S(1)} %copy-done.2, f32[1,768]{1,0:T(1,128)S(1)} %get-tuple-element.60.g_ref, s32[512,1]{1,0:T(8,128)S(1)} %copy.77.dq_ref, ...), custom_call_target="tpu_custom_call" | custom-call | flops 2013265920 | bytes 14680064 | tf_op jit(solution)/shard_map/pallas_call | solution.py:337
  266.9 16.1 %shard_map.180 = (bf16[4,4,192,384]{3,2,1,0:T(8,128)(2,1)}, bf16[4,4,192,384]{3,2,1,0:T(8,128)(2,1)}, f32[512,768]{1,0:T(8,128)}, f32[512,768]{1,0:T(8,128)}) custom-call(s32[13]{0:T(128)S(1)} %copy-done.3, bf16[512,768]{1,0:T(8,128)(2,1)S(1)} %get-tuple-element.32.refs_0_, bf16[512,768]{1,0:T(8,128)(2,1)S(1)} %copy-done.4, ...), custom_call_target="tpu_custom_call" | custom-call | flops 7247757312 | bytes 20971520 | tf_op jit(solution)/shard_map/pallas_call | solution.py:379
  283.1 18.0 %shard_map.181 = (bf16[4,4,192,384]{3,2,1,0:T(8,128)(2,1)}, bf16[4,4,192,384]{3,2,1,0:T(8,128)(2,1)}, f32[512,768]{1,0:T(8,128)}, bf16[512,768]{1,0:T(8,128)(2,1)}) custom-call(s32[13]{0:T(128)S(1)} %copy-done.3, bf16[512,768]{1,0:T(8,128)(2,1)S(1)} %get-tuple-element.32.refs_0_, bf16[512,768]{1,0:T(8,128)(2,1)S(1)} %copy-done.4, ...), custom_call_target="tpu_custom_call" | custom-call | flops 7247757312 | bytes 20971520 | tf_op jit(solution)/shard_map/pallas_call | solution.py:379
  301.1 20.1 %shard_map.182 = (f32[512,768]{1,0:T(8,128)}, bf16[4,4,12,64,128]{4,3,2,1,0:T(8,128)(2,1)}, bf16[4,4,12,64,128]{4,3,2,1,0:T(8,128)(2,1)}, bf16[4,4,192,256]{3,2,...) custom-call(s32[13]{0:T(128)S(1)} %copy-done.3, f32[512,768]{1,0:T(8,128)} %get-tuple-element.38.dn_ref, ...), custom_call_target="tpu_custom_call" | custom-call | flops 5234491392 | bytes 29360128 | tf_op jit(solution)/shard_map/pallas_call | solution.py:386
  321.2 8.6 %shard_map.183 = (f32[512,768]{1,0:T(8,128)}, bf16[4,4,192,256]{3,2,1,0:T(8,128)(2,1)}, f32[1,768]{1,0:T(1,128)S(1)}) custom-call(s32[13]{0:T(128)S(1)} %copy-done.3, bf16[512,768]{1,0:T(8,128)(2,1)S(1)} %copy-done.2, f32[1,768]{1,0:T(1,128)S(1)} %get-tuple-element.59.g_ref, bf16[512,768]{1,0:T(8,128)(2,1)S(1)} %get-tuple-element.37.n_ref, ...), custom_call_target="tpu_custom_call" | custom-call | flops 1610612736 | bytes 12582912 | tf_op jit(solution)/shard_map/pallas_call | solution.py:406
  346.8 9.5 %copy.85 = bf16[4,192,4,2,384]{4,3,2,1,0:T(2,128)(2,1)} copy(bf16[4,192,4,2,384]{4,1,2,0,3:T(8,128)(2,1)} %maximum_bitcast_fusion.2) | data formatting | bytes 9437184 | tf_op jit(solution)/shard_map/transpose | solution.py:467
  356.3 11.3 %reshape.77 = bf16[768,3072]{1,0:T(8,128)(2,1)} reshape(bf16[4,192,4,2,384]{4,3,2,1,0:T(2,128)(2,1)} %copy.85) | data formatting | bytes 9437184 | tf_op jit(solution)/shard_map/reshape | solution.py:467
  373.6 9.4 %copy.84 = bf16[4,192,4,2,384]{4,3,2,1,0:T(2,128)(2,1)} copy(bf16[4,192,4,2,384]{4,1,2,0,3:T(8,128)(2,1)} %maximum_bitcast_fusion.1) | data formatting | bytes 9437184 | tf_op jit(solution)/shard_map/transpose | solution.py:467
  383.0 11.3 %reshape.76 = bf16[768,3072]{1,0:T(8,128)(2,1)} reshape(bf16[4,192,4,2,384]{4,3,2,1,0:T(2,128)(2,1)} %copy.84) | data formatting | bytes 9437184 | tf_op jit(solution)/shard_map/reshape | solution.py:467
  401.3 30.9 %copy.98 = bf16[12,4,2,64,4,128]{3,2,1,0,5,4:T(2,128)(2,1)} copy(bf16[12,4,2,64,4,128]{5,3,0,1,4,2:T(8,128)(2,1)} %maximum_bitcast_fusion) | data formatting | bytes 12582912
  432.2 26.2 %reshape.93 = bf16[12,512,512]{1,0,2:T(8,128)(2,1)} reshape(bf16[12,4,2,64,4,128]{3,2,1,0,5,4:T(2,128)(2,1)} %copy.98) | data formatting | bytes 12582912
  458.3 13.3 %copy.102 = bf16[64,8,12,512]{3,1,2,0:T(8,128)(2,1)} copy(bf16[64,8,12,512]{3,2,1,0:T(8,128)(2,1)} %bitcast.83) | data formatting | bytes 12582912
  478.4 37.3 %reduce-scatter.28.cloned.1.call-done = bf16[192,3072]{1,0:T(8,128)(2,1)} async-done(((bf16[768,3072]{1,0:T(8,128)(2,1)}), bf16[192,3072]{1,0:T(8,128)(2,1)}) %reduce-scatter.28.cloned.1.call-update) | async-done | bytes 1179664 | tf_op jit(solution)/shard_map/reduce_scatter | solution.py:440
  518.3 70.5 %reduce-scatter.34.cloned.1.call-done = bf16[128,6144]{1,0:T(8,128)(2,1)} async-done(((bf16[512,6144]{1,0:T(8,128)(2,1)}), bf16[128,6144]{1,0:T(8,128)(2,1)}) %reduce-scatter.34.cloned.1.call-update) | async-done | bytes 1572880
  594.6 39.5 %all-reduce.2 = f32[2,768]{1,0:T(2,128)S(1)} all-reduce(f32[2,768]{1,0:T(2,128)S(1)} %pad_maximum_fusion), channel_id=2, replica_groups=mesh['gx'=4,'gy'=8] {'gx','gy'}, use_global_device_ids=true, to_apply=%region_0.1.clone | all-reduce | flops 1536 | bytes 12288
  636.2 17.2 %reduce-scatter.26.cloned.1.call-done = bf16[192,96]{0,1:T(8,128)(2,1)} async-done(((bf16[192,768]{0,1:T(8,128)(2,1)}), bf16[192,96]{0,1:T(8,128)(2,1)}) %reduce-scatter.26.cloned.1.call-update) | async-done | bytes 36880 | tf_op jit(solution)/shard_map/reduce_scatter | solution.py:441
  654.8 33.4 %reduce-scatter.40.cloned.1.call-done = bf16[384,192]{1,0:T(8,128)(2,1)} async-done(((bf16[3072,192]{1,0:T(8,128)(2,1)}), bf16[384,192]{1,0:T(8,128)(2,1)}) %reduce-scatter.40.cloned.1.call-update) | async-done | bytes 147472
  689.3 33.2 %reduce-scatter.38.cloned.1.call-done = bf16[384,192]{1,0:T(8,128)(2,1)} async-done(((bf16[3072,192]{1,0:T(8,128)(2,1)}), bf16[384,192]{1,0:T(8,128)(2,1)}) %reduce-scatter.38.cloned.1.call-update) | async-done | bytes 147472
  725.1 31.8 %reduce-scatter.24.cloned.1.call-done = bf16[12,64,128]{2,1,0:T(8,128)(2,1)} async-done(((bf16[12,512,128]{2,1,0:T(8,128)(2,1)}), bf16[12,64,128]{2,1,0:T(8,128)(2,1)}) %reduce-scatter.24.cloned.1.call-update) | async-done | bytes 196624 | tf_op jit(solution)/shard_map/reduce_scatter | solution.py:441
  (114 shorter events, 93.6 us)
Async XLA Ops:
  7.2 55.5 %copy-start = (s32[8,512]{1,0:T(8,128)S(1)}, s32[8,512]{1,0:T(8,128)}, u32[]{:S(2)}) copy-start(s32[8,512]{1,0:T(8,128)} %param.12) | copy-start | bytes 49156
  7.2 33.6 %copy-start.10 = (bf16[192,384]{1,0:T(8,128)(2,1)S(1)}, bf16[192,384]{1,0:T(8,128)(2,1)}, u32[]{:S(2)}) copy-start(bf16[192,384]{1,0:T(8,128)(2,1)} %param.18) | copy-start | bytes 442372
  7.2 43.9 %copy-start.9 = (bf16[12,64,128]{2,1,0:T(8,128)(2,1)S(1)}, bf16[12,64,128]{2,1,0:T(8,128)(2,1)}, u32[]{:S(2)}) copy-start(bf16[12,64,128]{2,1,0:T(8,128)(2,1)} %param.15) | copy-start | bytes 589828
  7.2 97.1 %all-gather.7.cloned.1.call-start = ((), (), s32[]{:S(2)}) async-start(), calls=%async_computation.10 | async-start | bytes 1327104 | tf_op jit(solution)/shard_map/all_gather | solution.py:437
  18.6 95.9 %all-gather.11.cloned.1.call-start = ((), (), s32[]{:S(2)}) async-start(), calls=%async_computation.12 | async-start | bytes 1327104 | tf_op jit(solution)/shard_map/all_gather | solution.py:437
  28.9 100.9 %all-gather.15.cloned.1.call-start = ((), (), s32[]{:S(2)}) async-start(), calls=%async_computation.14 | async-start | bytes 5308416 | tf_op jit(solution)/shard_map/all_gather | solution.py:437
  28.9 33.9 %copy-start.11 = (bf16[24]{0:T(256)(128)(2,1)S(1)}, bf16[24]{0:T(256)(128)(2,1)}, u32[]{:S(2)}) copy-start(bf16[24]{0:T(256)(128)(2,1)} %param.17) | copy-start | bytes 148
  29.0 33.9 %copy-start.12 = (bf16[24]{0:T(256)(128)(2,1)S(1)}, bf16[24]{0:T(256)(128)(2,1)}, u32[]{:S(2)}) copy-start(bf16[24]{0:T(256)(128)(2,1)} %param.13) | copy-start | bytes 148
  40.8 130.4 %all-gather.13.cloned.1.call-start = ((), (), s32[]{:S(2)}) async-start(), calls=%async_computation.13 | async-start | bytes 5308416 | tf_op jit(solution)/shard_map/all_gather | solution.py:437
  51.1 185.0 %all-gather.9.cloned.1.call-start = ((), (), s32[]{:S(2)}) async-start(), calls=%async_computation.11 | async-start | bytes 7077888 | tf_op jit(solution)/shard_map/all_gather | solution.py:437
  62.6 409.1 %reduce-scatter.22.cloned.1.call-start = ((), (), s32[]{:S(2)}) async-start(), calls=%async_computation.15 | async-start | bytes 1474560 | tf_op jit(solution)/shard_map/reduce_scatter | solution.py:440
  122.3 2.3 copy-start.2
  122.4 2.3 copy-start.3
  183.1 3.8 copy-start.5
  254.4 12.5 %copy-start.4 = (bf16[512,768]{1,0:T(8,128)(2,1)S(1)}, bf16[512,768]{1,0:T(8,128)(2,1)}, u32[]{:S(2)}) copy-start(bf16[512,768]{1,0:T(8,128)(2,1)} %c_ref.1) | copy-start | bytes 2359300
  334.4 2.2 copy-start.8
  336.6 137.2 %reduce-scatter.36.cloned.1.call-start = ((), (), s32[]{:S(2)}) async-start(), calls=%async_computation.22 | async-start | bytes 1474560
  341.7 134.1 %reduce-scatter.30.cloned.1.call-start = ((), (), s32[]{:S(2)}) async-start(), calls=%async_computation.19 | async-start | bytes 5898240 | tf_op jit(solution)/shard_map/reduce_scatter | solution.py:440
  367.6 1.7 copy-start.7
  367.6 148.1 %reduce-scatter.28.cloned.1.call-start = ((), (), s32[]{:S(2)}) async-start(), calls=%async_computation.18 | async-start | bytes 5898240 | tf_op jit(solution)/shard_map/reduce_scatter | solution.py:440
  394.3 1.9 copy-start.6
  394.3 194.5 %reduce-scatter.34.cloned.1.call-start = ((), (), s32[]{:S(2)}) async-start(), calls=%async_computation.21 | async-start | bytes 7864320
  471.7 163.0 %reduce-scatter.32.cloned.1.call-start = ((), (), s32[]{:S(2)}) async-start(), calls=%async_computation.20 | async-start | bytes 442368
  473.7 179.7 %reduce-scatter.26.cloned.1.call-start = ((), (), s32[]{:S(2)}) async-start(), calls=%async_computation.17 | async-start | bytes 442368 | tf_op jit(solution)/shard_map/reduce_scatter | solution.py:441
  475.7 212.6 %reduce-scatter.40.cloned.1.call-start = ((), (), s32[]{:S(2)}) async-start(), calls=%async_computation.24 | async-start | bytes 1769472
  478.4 244.2 %reduce-scatter.38.cloned.1.call-start = ((), (), s32[]{:S(2)}) async-start(), calls=%async_computation.23 | async-start | bytes 1769472
  518.3 238.6 %reduce-scatter.24.cloned.1.call-start = ((), (), s32[]{:S(2)}) async-start(), calls=%async_computation.16 | async-start | bytes 1769472 | tf_op jit(solution)/shard_map/reduce_scatter | solution.py:441
  591.7 166.9 %copy-start.1 = (s32[8,512]{1,0:T(8,128)S(1)}, s32[8,512]{1,0:T(8,128)}, u32[]{:S(2)}) copy-start(s32[8,512]{1,0:T(8,128)} %param.12) | copy-start | bytes 49156
Sparse Core Ops, SparseCore 0:
  18.8 22.9 all-gather.6
  43.9 22.4 all-gather.10
  68.0 51.3 all-gather.14
  120.9 50.2 all-gather.12
  172.7 63.3 all-gather.8
  336.7 27.2 reduce-scatter.21
  366.9 28.5 reduce-scatter.35
  398.5 57.0 reduce-scatter.29
  458.6 57.0 reduce-scatter.27
  518.6 70.1 reduce-scatter.33
  591.6 30.7 reduce-scatter.31
  624.7 28.6 reduce-scatter.25
  655.7 32.4 reduce-scatter.39
  690.4 32.0 reduce-scatter.37
  724.7 32.1 reduce-scatter.23

commit v2 on v1

v2 whole, which is shorter than its diff:
```python
import functools

import jax
import jax.numpy as jnp
from jax import lax
from jax.experimental import pallas as pl
from jax.experimental.pallas import tpu as pltpu
from jax.sharding import PartitionSpec as P

D = 768
H = 12
HS = 64
FF = 3072
L = 512
EPS = 1e-05
G = 4
Z = 4
DB = D // G
CB = D // (2 * Z)
FB = FF // (2 * Z)
QB = L // (2 * Z)
KB = L // G
LN = 128
GW = 2 * LN
GN = CB // 4
HA = H // 2
HR = HA * QB
TM = 128
WIN = 3
HZ = H // Z
GC = 0.7978845608
GA = 0.044715
VMEM_LIMIT = 52 * 1024 * 1024

F32 = jnp.float32
BF16 = jnp.bfloat16


def dot(a, b, ca, cb):
    return lax.dot_general(a, b, (((ca,), (cb,)), ((), ())), preferred_element_type=F32)


def call(body, grid, in_specs, out_specs, out_shape, scratch=(), flops=0, nbytes=0):
    return pl.pallas_call(
        body,
        grid_spec=pltpu.PrefetchScalarGridSpec(
            num_scalar_prefetch=1,
            grid=grid,
            in_specs=in_specs,
            out_specs=out_specs,
            scratch_shapes=list(scratch),
        ),
        out_shape=out_shape,
        compiler_params=pltpu.CompilerParams(
            dimension_semantics=("arbitrary",) * len(grid), vmem_limit_bytes=VMEM_LIMIT
        ),
        cost_estimate=pl.CostEstimate(flops=flops, bytes_accessed=nbytes, transcendentals=0),
    )


def whole(shape):
    zeros = (0,) * len(shape)
    return pl.BlockSpec(shape, lambda i, t: zeros, pipeline_mode=pl.Buffered(1))


def rows(width):
    return pl.BlockSpec((TM, width), lambda i, t: (i, 0))


def out_whole(shape):
    zeros = (0,) * len(shape)
    return pl.BlockSpec(shape, lambda i, t: zeros)


def tab_a(t, g):
    return t[1 + g]


def tab_b(t, g):
    return t[1 + G + g]


def tab_z(t, z):
    return t[1 + 2 * G + z]


def norm_stats(x):
    mean = jnp.mean(x, axis=-1, keepdims=True)
    cen = x - mean
    rstd = lax.rsqrt(jnp.mean(cen * cen, axis=-1, keepdims=True) + EPS)
    return cen, rstd


def weight_z(own, oth, t, z, base):
    parts = [
        jnp.concatenate(
            [ref[tab_a(t, g), tab_z(t, z), base : base + DB, :] for g in range(G)], axis=0
        )
        for ref in (own, oth)
    ]
    return jnp.concatenate(parts, axis=1)


def head_masks(core, nrows):
    lane = lax.broadcasted_iota(jnp.int32, (nrows, GW), 1)
    tile = lane // LN
    place = lane - tile * LN
    side = jnp.where(core == 0, tile, 1 - tile)
    col = jnp.where(place < CB, side * CB + place, -1)
    return [jnp.logical_and(col >= HS * i, col < HS * (i + 1)) for i in range(HZ)]


def halves(ref, core, lead=None):
    lo = pl.multiple_of(core * QB, QB)
    hi = pl.multiple_of((1 - core) * QB, QB)
    if lead is None:
        return jnp.concatenate([ref[pl.ds(lo, QB), :], ref[pl.ds(hi, QB), :]], axis=0)
    return jnp.concatenate([ref[lead, pl.ds(lo, QB), :], ref[lead, pl.ds(hi, QB), :]], axis=0)


def put_halves(ref, core, val, lead=None):
    lo = pl.multiple_of(core * QB, QB)
    hi = pl.multiple_of((1 - core) * QB, QB)
    if lead is None:
        ref[pl.ds(lo, QB), :] = val[:QB]
        ref[pl.ds(hi, QB), :] = val[QB:]
    else:
        ref[lead, pl.ds(lo, QB), :] = val[:QB]
        ref[lead, pl.ds(hi, QB), :] = val[QB:]


def window(m):
    return jnp.clip(m - 1, 0, G - WIN)


def exp_scores(a_own, a_oth, b_own, b_oth, t, m, head, mask):
    parts = []
    for i in range(WIN):
        both = []
        for a, b in ((a_own, b_own), (a_oth, b_oth)):
            if head < HA:
                both.append(a[tab_b(t, window(m) + i), tab_z(t, m), head * QB : (head + 1) * QB, :])
            else:
                h = head - HA
                both.append(b[tab_z(t, m), i, h * QB : (h + 1) * QB, :])
        parts.append(jnp.concatenate(both, axis=0))
    scores = jnp.concatenate(parts, axis=1).astype(F32)
    return jnp.where(mask, jnp.exp(scores), 0.0)


def gain_spots():
    for g in range(G):
        for z in range(Z):
            for c in range(2):
                yield g, z, c, DB * g + (2 * GN) * z + GN * c


def pick(core, c, own, oth):
    return jnp.where(core == c, own, oth)


def gains_row(own, oth, t, base):
    lane = lax.broadcasted_iota(jnp.int32, (1, LN), 1)
    tiles = [jnp.zeros((1, LN), F32) for _ in range(D // LN)]
    for g, z, c, at in gain_spots():
        a, b = (r[tab_a(t, g), tab_z(t, z), base : base + 16, :].astype(F32)[:1] for r in (own, oth))
        row = pick(t[0], c, a, b)
        tile, off = at // LN, at % LN
        row = pltpu.roll(row, (off - CB) % LN, 1)
        tiles[tile] = jnp.where(jnp.logical_and(lane >= off, lane < off + GN), row, tiles[tile])
        if off + GN > LN:
            tiles[tile + 1] = jnp.where(lane < off + GN - LN, row, tiles[tile + 1])
    return jnp.concatenate(tiles, axis=1)


def put_weight_grads(acc, dg, t, keep, send):
    lane = lax.broadcasted_iota(jnp.int32, (1, LN), 1)
    top = lax.broadcasted_iota(jnp.int32, (16, LN), 0) == 0
    spot = jnp.logical_and(top, jnp.logical_and(lane >= CB, lane < CB + GN))
    rows_of = {}
    for g, z, c, at in gain_spots():
        tile, off = at // LN, at % LN
        row = dg[:, tile * LN : (tile + 1) * LN]
        if off + GN > LN:
            row = jnp.where(lane < off, dg[:, (tile + 1) * LN : (tile + 2) * LN], row)
        rows_of[g, z, c] = pltpu.roll(row, (CB - off) % LN, 1)
    for g in range(G):
        for z in range(Z):
            for p, ref in ((0, keep), (1, send)):
                blk = acc[z, g * DB : (g + 1) * DB, p * LN : (p + 1) * LN]
                row = pick(t[0], p, rows_of[g, z, 0], rows_of[g, z, 1])
                ref[tab_a(t, g), tab_z(t, z)] = blk.astype(BF16)
                ref[tab_a(t, g), tab_z(t, z), 0:16, :] = jnp.where(spot, row, blk[:16]).astype(BF16)


def values_body(t, x_ref, own_ref, oth_ref, n_ref, val_ref, gain_ref):
    @pl.when(pl.program_id(0) == 0)
    def _():
        gain_ref[0:1, :] = gains_row(own_ref, oth_ref, t, 0)
        gain_ref[1:2, :] = gains_row(own_ref, oth_ref, t, DB)

    cen, rstd = norm_stats(x_ref[...].astype(F32))
    low = (cen * rstd * gain_ref[0:1, :]).astype(BF16)
    n_ref[...] = low
    for z in range(Z):
        val_ref[z] = dot(low, weight_z(own_ref, oth_ref, t, z, 0), 1, 0).astype(BF16)


def mixer_body(
    t, x_ref, gain_ref, dq_ref, dk_ref, val_ref, a_own, a_oth, b_own, b_oth, w_own, w_oth,
    mix_ref, mid_ref, n_ref,
):
    m = pl.program_id(0)
    core = t[0]
    k0 = pl.multiple_of(window(m) * KB, KB)
    mask = halves(dq_ref, core) == dk_ref[:, pl.ds(k0, WIN * KB)]
    heads = head_masks(core, TM)
    acc = halves(x_ref, core).astype(F32)
    for z in range(Z):
        win = val_ref[z, pl.ds(k0, WIN * KB), :]
        out = jnp.zeros((TM, GW), F32)
        for i in range(HZ):
            e = exp_scores(a_own, a_oth, b_own, b_oth, t, m, HZ * z + i, mask)
            inv = 1.0 / jnp.sum(e, axis=-1, keepdims=True)
            part = dot((e * inv).astype(BF16), win, 1, 0)
            out = jnp.where(heads[i], part, out)
        low = out.astype(BF16)
        put_halves(mix_ref, core, low, z)
        acc = acc + dot(low, weight_z(w_own, w_oth, t, z, DB), 1, 1)
    put_halves(mid_ref, core, acc)
    cen, rstd = norm_stats(acc)
    put_halves(n_ref, core, (cen * rstd * gain_ref[1:2, :]).astype(BF16))


def ffn_body(first, last, t, n_ref, c_ref, u_ref, d_ref, *refs):
    refs = list(refs)
    if not first:
        ia_ref, ib_ref = refs[:2]
        refs = refs[2:]
    if last:
        mid_ref = refs[0]
        refs = refs[1:]
    gu_ref, gd_ref, b_ref, a_ref = refs[:4]
    j = pl.program_id(0)
    n = n_ref[...]
    cot = c_ref[...]
    up_w = jnp.concatenate([u_ref[tab_b(t, g), 0] for g in range(G)], axis=0)
    dn_w = jnp.concatenate([d_ref[tab_a(t, g), 0] for g in range(G)], axis=0)

    @pl.when(j == 0)
    def _():
        if first:
            a_ref[...] = jnp.zeros_like(a_ref)
            b_ref[...] = jnp.zeros_like(b_ref)
        else:
            a_ref[...] = ia_ref[...]
            b_ref[...] = ib_ref[...]

    up = dot(n, up_w, 1, 0)
    sq = up * up
    th = jnp.tanh(GC * up * (1.0 + GA * sq))
    half = 0.5 + 0.5 * th
    act = (up * half).astype(BF16)
    slope = half + (0.5 * GC) * up * (1.0 - th * th) * (1.0 + (3.0 * GA) * sq)
    a_ref[...] += dot(act, dn_w, 1, 1)
    gd = dot(cot, act, 0, 0).astype(BF16)
    up_g = (dot(cot, dn_w, 1, 0) * slope).astype(BF16)
    gu = dot(n, up_g, 0, 0).astype(BF16)
    b_ref[...] += dot(up_g, up_w, 1, 1)
    for g in range(G):
        gu_ref[tab_b(t, g), 0] = gu[g * DB : (g + 1) * DB]
        gd_ref[tab_a(t, g), 0] = gd[g * DB : (g + 1) * DB]
    if last:
        lo_ref = refs[4]

        @pl.when(j == Z - 1)
        def _():
            lo_ref[...] = (mid_ref[...] + a_ref[...]).astype(BF16)


def norm_back(cen, rstd, gain, dn):
    xhat = cen * rstd
    e = dn * gain
    dv = (
        e
        - jnp.mean(e, axis=-1, keepdims=True)
        - xhat * jnp.mean(e * xhat, axis=-1, keepdims=True)
    ) * rstd
    return dv, jnp.sum(dn * xhat, axis=0, keepdims=True)


def mixer_back_body(
    t, dn_ref, mid_ref, c_ref, gain_ref, dq_ref, dk_ref, mix_ref, val_ref,
    a_own, a_oth, b_own, b_oth, w_own, w_oth,
    mg_ref, ka_ref, sa_ref, kb_ref, sb_ref, ko_ref, so_ref, vg_ref, dg_acc, go_acc, vg_acc,
):
    m = pl.program_id(0)
    core = t[0]
    start = window(m)
    k0 = pl.multiple_of(start * KB, KB)

    @pl.when(m == 0)
    def _():
        go_acc[...] = jnp.zeros_like(go_acc)
        vg_acc[...] = jnp.zeros_like(vg_acc)
        dg_acc[...] = jnp.zeros_like(dg_acc)

    cen, rstd = norm_stats(halves(mid_ref, core))
    dv, dg = norm_back(cen, rstd, gain_ref[1:2, :], halves(dn_ref, core))
    dg_acc[0:1, :] += dg
    mid_grad = halves(c_ref, core).astype(F32) + dv
    put_halves(mg_ref, core, mid_grad)
    branch = mid_grad.astype(BF16)
    mask = halves(dq_ref, core) == dk_ref[:, pl.ds(k0, WIN * KB)]
    heads = head_masks(core, TM)
    rest = tab_b(t, jnp.where(start == 0, G - 1, 0))
    ka_ref[rest, 0] = jnp.zeros((HR, KB), BF16)
    sa_ref[rest, 0] = jnp.zeros((HR, KB), BF16)
    for z in range(Z):
        go_acc[z] += dot(branch, halves(mix_ref, core, z), 0, 0)
        grad = dot(branch, weight_z(w_own, w_oth, t, z, DB), 1, 0)
        grad = grad.astype(BF16).astype(F32)
        win = val_ref[z, pl.ds(k0, WIN * KB), :]
        total = jnp.zeros((WIN * KB, GW), F32)
        for i in range(HZ):
            head = HZ * z + i
            e = exp_scores(a_own, a_oth, b_own, b_oth, t, m, head, mask)
            inv = 1.0 / jnp.sum(e, axis=-1, keepdims=True)
            prob = e * inv
            mine = jnp.where(heads[i], grad, 0.0).astype(BF16)
            total = total + dot(prob.astype(BF16), mine, 0, 0)
            dp = dot(mine, win, 1, 1)
            pd = prob * dp
            ds = (pd - prob * jnp.sum(pd, axis=-1, keepdims=True)).astype(BF16)
            for k in range(WIN):
                for p, (ra, rb) in enumerate(((ka_ref, kb_ref), (sa_ref, sb_ref))):
                    blk = ds[p * QB : (p + 1) * QB, k * KB : (k + 1) * KB]
                    if head < HA:
                        ra[tab_b(t, start + k), 0, head * QB : (head + 1) * QB, :] = blk
                    else:
                        h = head - HA
                        rb[0, k, h * QB : (h + 1) * QB, :] = blk
        vg_acc[z, pl.ds(k0, WIN * KB), :] += total

    @pl.when(m == Z - 1)
    def _():
        vg_ref[...] = vg_acc[...].astype(BF16)
        put_weight_grads(go_acc, dg_acc[0:1, :], t, ko_ref, so_ref)


def last_body(
    t, x_ref, gain_ref, n_ref, vg_ref, w_own, w_oth, mg_ref, gi_ref, kv_ref, sv_ref, dg_acc, gv_acc
):
    m = pl.program_id(0)

    @pl.when(m == 0)
    def _():
        gv_acc[...] = jnp.zeros_like(gv_acc)
        dg_acc[...] = jnp.zeros_like(dg_acc)

    low = n_ref[...]
    dn = jnp.zeros((TM, D), F32)
    for z in range(Z):
        vg = vg_ref[z]
        gv_acc[z] += dot(low, vg, 0, 0)
        dn = dn + dot(vg, weight_z(w_own, w_oth, t, z, 0), 1, 1)
    cen, rstd = norm_stats(x_ref[...].astype(F32))
    dv, dg = norm_back(cen, rstd, gain_ref[0:1, :], dn)
    dg_acc[0:1, :] += dg
    gi_ref[...] = mg_ref[...] + dv

    @pl.when(m == Z - 1)
    def _():
        put_weight_grads(gv_acc, dg_acc[0:1, :], t, kv_ref, sv_ref)


def sds(shape, dtype):
    return jax.ShapeDtypeStruct(shape, dtype)


W_SHAPE = (G, Z, 2 * DB, LN)
V_SHAPE = (G, Z, DB, LN)
A_SHAPE = (G, Z, HR, KB)
B_SHAPE = (Z, WIN, HR, KB)
F_SHAPE = (G, Z, DB, FB)
Z_ROWS = pl.BlockSpec((Z, TM, GW), lambda i, t: (0, i, 0))


def run_values(tab, x, w):
    return call(
        values_body,
        (L // TM,),
        [rows(D), whole(W_SHAPE), whole(W_SHAPE)],
        [rows(D), Z_ROWS, out_whole((8, D))],
        [sds((L, D), BF16), sds((Z, L, GW), BF16), sds((8, D), F32)],
        flops=2 * L * D * Z * GW,
        nbytes=6 << 20,
    )(tab, x, *w)


def run_mixer(tab, x, gain, dq, dk, vals, a, b, w):
    return call(
        mixer_body,
        (L // TM,),
        [
            rows(D), whole((8, D)), rows(1), whole((1, L)), whole((Z, L, GW)),
            whole(A_SHAPE), whole(A_SHAPE), whole(B_SHAPE), whole(B_SHAPE),
            whole(W_SHAPE), whole(W_SHAPE),
        ],
        [Z_ROWS, rows(D), rows(D)],
        [sds((Z, L, GW), BF16), sds((L, D), F32), sds((L, D), BF16)],
        flops=2 * L * D * Z * GW + 2 * H * L * WIN * KB * GW,
        nbytes=14 << 20,
    )(tab, x, gain, dq, dk, vals, *a, *b, *w)

def run_ffn(tab, n, cot, u_w, d_w, acc=None, mid=None):
    first, last = acc is None, mid is not None
    blk = pl.BlockSpec((G, 1, DB, FB), lambda i, t: (0, i, 0, 0))
    in_specs = [whole((L, D)), whole((L, D)), blk, blk]
    args = [tab, n, cot, u_w, d_w]
    if not first:
        in_specs += [whole((L, D)), whole((L, D))]
        args += list(acc)
    if last:
        in_specs += [whole((L, D))]
        args += [mid]
    out_specs = [blk, blk, out_whole((L, D))]
    outs = [sds(F_SHAPE, BF16), sds(F_SHAPE, BF16), sds((L, D), F32)]
    scratch = ()
    if last:
        scratch = (pltpu.VMEM((L, D), F32),)
        out_specs += [out_whole((L, D))]
        outs += [sds((L, D), BF16)]
    else:
        out_specs += [out_whole((L, D))]
        outs += [sds((L, D), F32)]

    def body(t, *refs):
        if last:
            refs = list(refs)
            refs = refs[:-2] + [refs[-1], refs[-2]]
        ffn_body(first, last, t, *refs)

    return call(
        body, (Z,), in_specs, out_specs, outs, scratch, flops=6 * L * D * FF, nbytes=20 << 20
    )(*args)


def run_mixer_back(tab, dn, mid, cot, gain, dq, dk, mixed, vals, a, b, w):
    blk_a = pl.BlockSpec((G, 1, HR, KB), lambda i, t: (0, tab_z(t, i), 0, 0))
    blk_b = pl.BlockSpec((1, WIN, HR, KB), lambda i, t: (tab_z(t, i), 0, 0, 0))
    return call(
        mixer_back_body,
        (L // TM,),
        [
            rows(D), rows(D), rows(D), whole((8, D)), rows(1), whole((1, L)), Z_ROWS,
            whole((Z, L, GW)), whole(A_SHAPE), whole(A_SHAPE), whole(B_SHAPE), whole(B_SHAPE),
            whole(W_SHAPE), whole(W_SHAPE),
        ],
        [rows(D), blk_a, blk_a, blk_b, blk_b, out_whole(V_SHAPE), out_whole(V_SHAPE), out_whole((Z, L, GW))],
        [
            sds((L, D), F32), sds(A_SHAPE, BF16), sds(A_SHAPE, BF16), sds(B_SHAPE, BF16),
            sds(B_SHAPE, BF16), sds(V_SHAPE, BF16), sds(V_SHAPE, BF16), sds((Z, L, GW), BF16),
        ],
        scratch=(pltpu.VMEM((8, D), F32), pltpu.VMEM((Z, D, GW), F32), pltpu.VMEM((Z, L, GW), F32)),
        flops=4 * L * D * Z * GW + 6 * H * L * WIN * KB * GW,
        nbytes=28 << 20,
    )(tab, dn, mid, cot, gain, dq, dk, mixed, vals, *a, *b, *w)


def run_last(tab, x, gain, low, vg, w, mid_grad):
    return call(
        last_body,
        (L // TM,),
        [rows(D), whole((8, D)), rows(D), Z_ROWS, whole(W_SHAPE), whole(W_SHAPE), rows(D)],
        [rows(D), out_whole(V_SHAPE), out_whole(V_SHAPE)],
        [sds((L, D), F32), sds(V_SHAPE, BF16), sds(V_SHAPE, BF16)],
        scratch=(pltpu.VMEM((8, D), F32), pltpu.VMEM((Z, D, GW), F32)),
        flops=4 * L * D * Z * GW,
        nbytes=12 << 20,
    )(tab, x, gain, low, vg, *w, mid_grad)


def add_up(terms):
    total = terms[0].astype(F32)
    for term in terms[1:]:
        total = total + term.astype(F32)
    return total


class Grid:
    def __init__(self, gx, gy):
        self.gy = gy
        self.size = {"y": gx // 2, "x": 2, "z": gy // 2, "c": 2}
        i, j = lax.axis_index("gx"), lax.axis_index("gy")
        self.at = {"y": i // 2, "x": i % 2, "z": j // 2, "c": j % 2}

    def fetch(self, val, axis, k):
        sizes = self.size
        pairs = []
        for y in range(sizes["y"]):
            for x in range(sizes["x"]):
                for z in range(sizes["z"]):
                    for c in range(sizes["c"]):
                        src = {"y": y, "x": x, "z": z, "c": c}
                        dst = dict(src)
                        dst[axis] = (src[axis] + k) % sizes[axis]
                        pairs.append(tuple((p["y"] * 2 + p["x"]) * self.gy + p["z"] * 2 + p["c"] for p in (src, dst)))
        return lax.ppermute(val, ("gx", "gy"), pairs)

    def rel(self, axis, v):
        return (self.at[axis] - v) % self.size[axis]

    def spread(self, val, axis):
        return jnp.stack([val] + [self.fetch(val, axis, k) for k in range(1, self.size[axis])])

    def reduce(self, terms, axis):
        got = [
            self.fetch(add_up([t[k] for t in terms]).astype(BF16), axis, -k)
            for k in range(1, self.size[axis])
        ]
        return [t[0] for t in terms] + got


def compute(tab, x, docs, cot, a, b, w, u, d):
    dq, dk = docs.reshape(L, 1), docs
    low, vals, gain = run_values(tab, x, w)
    mixed, mid, n_two = run_mixer(tab, x, gain, dq, dk, vals, a, b, w)
    gu0, gd0, acc_b, acc_a = run_ffn(tab, n_two, cot, u[0], d[0])
    gu1, gd1, n_grad, layer_out = run_ffn(tab, n_two, cot, u[1], d[1], (acc_a, acc_b), mid)
    mid_grad, ka, sa, kb, sb, ko, so, vg = run_mixer_back(
        tab, n_grad, mid, cot, gain, dq, dk, mixed, vals, a, b, w
    )
    grad_in, kv, sv = run_last(tab, x, gain, low, vg, w, mid_grad)
    return layer_out, grad_in, (gu0, gu1), (gd0, gd1), (ka, sa), (kb, sb), (ko, so), (kv, sv)


def lane_pad(mat, gains):
    row = jnp.pad(gains.reshape(1, GN), ((0, DB - 1), (0, LN - CB - GN)))
    return jnp.concatenate([mat, row], axis=1)


def small_shards(layer_in, doc_ids, mix_gain, value_w, mixing, output_w, ffn_gain, up_w, down_w, cot):
    grid = Grid(G, 2 * Z)
    at = grid.at
    order_a = [grid.rel("x", g % 2) * 2 + grid.rel("y", g // 2) for g in range(G)]
    order_b = [grid.rel("y", g // 2) * 2 + grid.rel("x", g % 2) for g in range(G)]
    order_z = [grid.rel("z", z) for z in range(Z)]
    tab = jnp.stack([at["c"]] + order_a + order_b + order_z).astype(jnp.int32)
    docs = lax.dynamic_slice_in_dim(doc_ids, lax.axis_index("gy"), 1, 0)

    mix = mixing.reshape(2, HR, KB)
    wts = jnp.concatenate([lane_pad(value_w, mix_gain), lane_pad(output_w.T, ffn_gain)], axis=0)
    first = jnp.concatenate([mix[0], wts], axis=0)
    first = grid.spread(first, "z")
    a = grid.spread(grid.spread(first[:, :HR], "x"), "y").reshape(A_SHAPE)
    w = grid.spread(grid.spread(first[:, HR:], "y"), "x").reshape(W_SHAPE)
    b = grid.spread(grid.spread(mix[1], "x"), "y").reshape(G, HR, KB)
    start = window(at["z"])
    order = jnp.stack(order_b)
    b = jnp.stack([lax.dynamic_index_in_dim(b, order[start + i], 0, False) for i in range(WIN)])
    b = grid.spread(b, "z")
    ffn = grid.spread(jnp.stack([up_w, down_w.T]), "z")
    u = grid.spread(grid.spread(ffn[:, 0], "x"), "y").reshape(F_SHAPE)
    d = grid.spread(grid.spread(ffn[:, 1], "y"), "x").reshape(F_SHAPE)
    a, b, w, u, d = ((v, grid.fetch(v, "c", 1)) for v in (a, b, w, u, d))

    layer_out, grad_in, gu, gd, ga, gb, go, gv = compute(
        tab, layer_in, docs, cot, a, b, w, u, d
    )

    def core_sum(pair):
        return [pair[0], grid.fetch(pair[1], "c", 1)]

    def split(vals, *lead):
        return [v.reshape(lead + v.shape[-3:]) for v in vals]

    up = grid.reduce(grid.reduce(split(core_sum(gu), 2, 2), "y"), "x")
    dn = grid.reduce(grid.reduce(split(core_sum(gd), 2, 2), "x"), "y")
    both = [jnp.stack([p, q], axis=1) for p, q in zip(up, dn)]
    ffn = add_up(grid.reduce(both, "z"))
    gb = core_sum(gb)
    gb = grid.reduce(gb, "z")
    wide = []
    for v in gb:
        blocks = []
        for k in range(G):
            y = (at["y"] - k // 2) % 2
            x = (at["x"] - k % 2) % 2
            spot = y * 2 + x - start
            blk = lax.dynamic_index_in_dim(v, jnp.clip(spot, 0, WIN - 1), 0, False)
            ok = jnp.logical_and(spot >= 0, spot < WIN)
            blocks.append(jnp.where(ok, blk, jnp.zeros_like(blk)))
        wide.append(jnp.stack(blocks).reshape(2, 2, HR, KB))
    gb = add_up(grid.reduce(grid.reduce(wide, "y"), "x"))
    ga = split(core_sum(ga), 2, 2)
    ga = add_up(grid.reduce(grid.reduce(grid.reduce(ga, "y"), "x"), "z"))
    go, gv = core_sum(go), core_sum(gv)
    gw = split([jnp.concatenate([p, q], axis=2) for p, q in zip(gv, go)], 2, 2)
    gw = add_up(grid.reduce(grid.reduce(grid.reduce(gw, "x"), "y"), "z"))

    grad_mixing = jnp.concatenate([ga, gb], axis=0).reshape(H, QB, KB)
    return (
        layer_out, grad_in, gw[0, CB : CB + GN], gw[:DB, :CB], grad_mixing, gw[DB:, :CB].T,
        gw[DB, CB : CB + GN], ffn[0], ffn[1].T,
    )


def cols_in(v, o, gains):
    def blocks(mat, gain):
        mat = mat.reshape(G, DB, Z, 2, CB).transpose(3, 0, 2, 1, 4)
        gain = gain.reshape(G, Z, 2, 1, GN).transpose(2, 0, 1, 3, 4)
        gain = jnp.pad(gain, ((0, 0),) * 3 + ((0, DB - 1), (0, LN - CB - GN)))
        return jnp.concatenate([mat, gain], axis=-1)

    return jnp.concatenate([blocks(v, gains[0]), blocks(o, gains[1])], axis=3)


def cols_out(keep, send):
    mat = jnp.stack([keep, send])
    dg = mat[:, :, :, 0, CB : CB + GN].transpose(1, 2, 0, 3).reshape(D)
    return mat[..., :CB].transpose(1, 3, 2, 0, 4).reshape(D, D), dg


def any_shards(layer_in, doc_ids, mix_gain, value_w, mixing, output_w, ffn_gain, up_w, down_w, cot):
    ax = ("gx", "gy")
    seqs = layer_in.shape[0] // L
    me = lax.axis_index("gy") * seqs

    def gather(arr, d0, d1):
        arr = lax.all_gather(arr, "gx", axis=d0, tiled=True)
        return lax.all_gather(arr, "gy", axis=d1, tiled=True)

    def scatter(arr, d0, d1):
        arr = lax.psum_scatter(arr, "gx", scatter_dimension=d0, tiled=True)
        return lax.psum_scatter(arr, "gy", scatter_dimension=d1, tiled=True).astype(F32)

    gains = lax.all_gather(jnp.stack([mix_gain, ffn_gain]), ax, axis=1, tiled=True)
    w = cols_in(gather(value_w, 0, 1), gather(output_w.T, 0, 1), gains)
    mix_full = gather(mixing, 2, 1).reshape(2, HA, Z, 2, QB, G, KB).transpose(0, 3, 5, 2, 1, 4, 6)
    mix_full = mix_full.reshape(2, 2, G, Z, HR, KB)
    a = mix_full[0]
    starts = [min(max(m - 1, 0), G - WIN) for m in range(Z)]
    b = jnp.stack([mix_full[1][:, s : s + WIN, m] for m, s in enumerate(starts)], axis=1)
    u = gather(up_w, 0, 1).reshape(G, DB, Z, 2, FB).transpose(3, 0, 2, 1, 4)
    d = gather(down_w.T, 0, 1).reshape(G, DB, Z, 2, FB).transpose(3, 0, 2, 1, 4)
    tab = jnp.array([0] + [0, 1, 2, 3] * 3, jnp.int32)

    rows_out, grads = [], None
    for s in range(seqs):
        docs = lax.dynamic_slice_in_dim(doc_ids, me + s, 1, 0)
        part = slice(s * L, (s + 1) * L)
        out, g_in, *rest = compute(tab, layer_in[part], docs, cot[part], a, b, w, u, d)
        rows_out.append((out, g_in))
        rest = jax.tree.map(lambda v: v.astype(F32), rest) if seqs > 1 else rest
        grads = rest if grads is None else jax.tree.map(jnp.add, grads, rest)
    layer_out = jnp.concatenate([r[0] for r in rows_out], axis=0)
    grad_in = jnp.concatenate([r[1] for r in rows_out], axis=0)
    gu, gd, ga, gb, go, gv = jax.tree.map(lambda v: v.astype(BF16), grads)

    def ffn_out(pair):
        return jnp.stack(pair).transpose(1, 3, 2, 0, 4).reshape(D, FF)

    value_full, dg_one = cols_out(*gv)
    output_full, dg_two = cols_out(*go)
    ga, gb = jnp.stack(ga), jnp.stack(gb)
    gb = jnp.stack(
        [
            jnp.pad(gb[:, m], ((0, 0), (s, G - WIN - s), (0, 0), (0, 0)))
            for m, s in enumerate(starts)
        ],
        axis=2,
    )
    gm = jnp.stack([ga, gb]).reshape(2, 2, G, Z, HA, QB, KB).transpose(0, 4, 3, 1, 5, 2, 6)
    dgs = jnp.stack([dg_one, dg_two]).astype(F32)
    dgs = lax.psum_scatter(dgs, ax, scatter_dimension=1, tiled=True)
    return (
        layer_out, grad_in, dgs[0], scatter(value_full, 0, 1), scatter(gm.reshape(H, L, L), 2, 1),
        scatter(output_full, 0, 1).T, dgs[1], scatter(ffn_out(gu), 0, 1), scatter(ffn_out(gd), 0, 1).T,
    )


def solution(mesh):
    tok = P(("gx", "gy"), None)
    vec = P(("gx", "gy"))
    wgt = P("gx", "gy")
    twg = P("gy", "gx")
    mix = P(None, "gy", "gx")
    in_specs = (tok, P("gx", None), vec, wgt, mix, twg, vec, wgt, twg, tok)
    out_specs = (tok, tok, vec, wgt, mix, twg, vec, wgt, twg)

    def run(*args):
        small = (mesh.shape["gx"], mesh.shape["gy"], args[0].shape[0]) == (G, 2 * Z, L)
        return (small_shards if small else any_shards)(*args)

    return jax.shard_map(run, mesh=mesh, in_specs=in_specs, out_specs=out_specs, check_vma=False)
```

time: 778 us -> 377 us (0.48); the launches traced: 766 us -> 372 us
  local copies, waits for them, and re-layouts: 223 us -> 15.1 us
  blocking collectives: 133 us -> 0 us
  waiting for transfers between devices: 293 us -> 180 us
  starting transfers between devices: 1.09 us -> 54.2 us
  other arithmetic: 19.7 us -> 34.6 us
    ppermute x0 -> x52, waiting for transfers between devices: none -> 180 us  [fetch(): return lax.ppermute(val, ('gx', 'gy'), pairs)]
    unnamed x20 -> x0, waiting for transfers between devices: 137 us -> none
    all_gather x6 -> x0, blocking collectives: 93.6 us -> none  [the longest x5 52.5 us: gather(): arr = lax.all_gather(arr, 'gx', axis=d0, tiled=True)]
    unnamed x42 -> x40, local copies, waits for them, and re-layouts: 95.7 us -> 4.82 us
    reshape x19 -> x2, local copies, waits for them, and re-layouts: 91 us -> 0.15 us  [compute(): dq, dk = (docs.reshape(L, 1), docs)]
    reduce_scatter x5 -> x0, waiting for transfers between devices: 86.4 us -> none  [the longest x2 49 us: scatter(): lax.psum_scatter(arr, 'gy', scatter_dimension=d1, tiled=True).astype(F32)]
    all_gather x5 -> x0, waiting for transfers between devices: 69.7 us -> none  [gather(): return lax.all_gather(arr, 'gy', axis=d1, tiled=True)]
    ppermute x0 -> x52, starting transfers between devices: none -> 54.2 us  [fetch(): return lax.ppermute(val, ('gx', 'gy'), pairs)]
  transfers between devices with their start and end apart: 15 -> 52, of which waited for: 8 -> 23; matrix products, arithmetic and copies ran while one was open for 28% -> 12% of each run, Pallas kernels for 1% -> 9%
where the time goes in v2:
time: 377 us; the launch traced here: 372 us
  waiting for transfers between devices  180 us (48%)
  Pallas kernels  81.8 us (22%)
  starting transfers between devices  54.2 us (14%)
  other arithmetic  34.6 us (9%)
  local copies, waits for them, and re-layouts  15.1 us (4%)
  between operations  7.03 us (2%)
    ppermute x52, waiting for transfers between devices, fetch(): return lax.ppermute(val, ('gx', 'gy'), pairs)  180 us
    ppermute x52, starting transfers between devices, fetch(): return lax.ppermute(val, ('gx', 'gy'), pairs)  54.2 us
    pallas_call x2, Pallas kernels, run_ffn(): call(body, (Z,), in_specs, out_specs, outs, scratch, flops=6 * L * D * FF...  33.7 us
    pallas_call x1, Pallas kernels, run_mixer_back(): call(mixer_back_body, (L // TM,), [rows(D), rows(D), rows(D), whole((8, D...  20.3 us
    another operation x16, other arithmetic, spread(): jnp.stack([val] + [self.fetch(val, axis, k) for k in range(1, self.size[a...  17.7 us
    pallas_call x1, Pallas kernels, run_mixer(): call(mixer_body, (L // TM,), [rows(D), whole((8, D)), rows(1), whole((1,...  12.6 us
    convert_element_type x13, other arithmetic, reduce(): add_up([t[k] for t in terms]).astype(BF16)  11.7 us
    pallas_call x1, Pallas kernels, run_last(): call(last_body, (L // TM,), [rows(D), whole((8, D)), rows(D), Z_ROWS, who...  9.28 us
  transfers between devices with their start and end apart: 52, of which 23 were waited for; matrix products, arithmetic and copies ran while one was open for 12% of the time, Pallas kernels for 9%

profile of v2, /device:TPU:0, one launch (start us, length us, event | category | flops | bytes accessed | tf_op | source)
XLA Modules:
  0.0 372.5 jit_solution(3619038935444314296)
XLA Ops:
  4.2 5.1 %collective-permute-start.2 = (bf16[768,128]{1,0:T(8,128)(2,1)S(1)}, bf16[768,128]{1,0:T(8,128)(2,1)S(1)}, u32[]{:S(2)}, u32[]{:S(2)}) collective-permute-start(bf16[768,128]{1,0:T(8,128)(2,1)S(1)} %fusion.34), channel_id=1, source_target_pairs={{0,6},{1,7},{2,0},{3,1},{4,2},{5,3},{6,4},{7,5},{8,14},{9,15},{10,... | collective-permute-start | bytes 589832 | tf_op jit(solution)/shard_map/ppermute | solution.py:509
  11.3 2.9 collective-permute-start.17
  16.0 11.0 %collective-permute-done.1 = bf16[768,128]{1,0:T(8,128)(2,1)S(1)} collective-permute-done((bf16[768,128]{1,0:T(8,128)(2,1)S(1)}, bf16[768,128]{1,0:T(8,128)(2,1)S(1)}, u32[]{:S(2)}, u32[]{:S(2)}) %collective-permute-start.1) | collective-permute-done | bytes 196640 | tf_op jit(solution)/shard_map/ppermute | solution.py:509
  27.1 2.4 collective-permute-done.17
  29.4 21.9 %collective-permute-done.16 = bf16[2,192,384]{2,1,0:T(8,128)(2,1)S(1)} collective-permute-done((bf16[2,192,384]{2,1,0:T(8,128)(2,1)S(1)}, bf16[2,192,384]{2,1,0:T(8,128)(2,1)S(1)}, u32[]{:S(2)}, u32[]{:S(2)}) %collective-permute-start.16) | collective-permute-done | bytes 294944 | tf_op jit(solution)/shard_map/ppermute | solution.py:509
  57.7 8.0 %collective-permute-done.3 = bf16[4,384,128]{2,1,0:T(8,128)(2,1)S(1)} collective-permute-done((bf16[4,384,128]{2,1,0:T(8,128)(2,1)S(1)}, bf16[4,384,128]{2,1,0:T(8,128)(2,1)S(1)}, u32[]{:S(2)}, u32[]{:S(2)}) %collective-permute-start.3) | collective-permute-done | bytes 393248 | tf_op jit(solution)/shard_map/ppermute | solution.py:509
  70.8 7.5 %collective-permute-done.21 = bf16[4,192,384]{2,1,0:T(8,128)(2,1)S(1)} collective-permute-done((bf16[4,192,384]{2,1,0:T(8,128)(2,1)S(1)}, bf16[4,192,384]{2,1,0:T(8,128)(2,1)S(1)}, u32[]{:S(2)}, u32[]{:S(2)}) %collective-permute-start.21) | collective-permute-done | bytes 589856 | tf_op jit(solution)/shard_map/ppermute | solution.py:509
  90.4 32.1 %collective-permute-done.10 = bf16[2,384,128]{2,1,0:T(8,128)(2,1)S(1)} collective-permute-done((bf16[2,384,128]{2,1,0:T(8,128)(2,1)S(1)}, bf16[2,384,128]{2,1,0:T(8,128)(2,1)S(1)}, u32[]{:S(2)}, u32[]{:S(2)}) %collective-permute-start.10) | collective-permute-done | bytes 196640 | tf_op jit(solution)/shard_map/ppermute | solution.py:509
  122.7 2.9 collective-permute-start.12
  129.0 2.4 pad_maximum_fusion.3
  131.5 3.0 pad_maximum_fusion
  135.0 3.0 pad_maximum_fusion.1
  138.0 11.7 %collective-permute-done.12 = bf16[3,384,128]{2,1,0:T(8,128)(2,1)S(1)} collective-permute-done((bf16[3,384,128]{2,1,0:T(8,128)(2,1)S(1)}, bf16[3,384,128]{2,1,0:T(8,128)(2,1)S(1)}, u32[]{:S(2)}, u32[]{:S(2)}) %collective-permute-start.12) | collective-permute-done | bytes 294944 | tf_op jit(solution)/shard_map/ppermute | solution.py:509
  151.8 5.9 %shard_map.169 = (bf16[512,768]{1,0:T(8,128)(2,1)S(1)}, bf16[4,512,256]{2,1,0:T(8,128)(2,1)}, f32[8,768]{1,0:T(8,128)S(1)}) custom-call(s32[13]{0:T(128)S(1)} %stack.256.t, bf16[512,768]{1,0:T(8,128)(2,1)S(1)} %copy-done.2, bf16[4,4,384,128]{3,2,1,0:T(8,128)(2,1)} %bitcast.250, bf16[4,4,384,128]{3,2,1,0:T(8,128)(2,1)} %collective-permute-done.5.oth_ref.w_oth), custom_call_target="tpu_custom_call" | custom-call | flops 805306368 | bytes 6291456 | tf_op jit(solution)/shard_map/pallas_call | solution.py:390
  157.7 12.6 %shard_map.170 = (bf16[4,512,256]{2,1,0:T(8,128)(2,1)}, f32[512,768]{1,0:T(8,128)}, bf16[512,768]{1,0:T(8,128)(2,1)S(1)}) custom-call(s32[13]{0:T(128)S(1)} %stack.256.t, bf16[512,768]{1,0:T(8,128)(2,1)S(1)} %copy-done.2, f32[8,768]{1,0:T(8,128)S(1)} %get-tuple-element.34.gain_ref, s32[512,1]{1,0:T(8,128)S(1)} %copy.29.dq_ref, ...), custom_call_target="tpu_custom_call" | custom-call | flops 2013265920 | bytes 14680064 | tf_op jit(solution)/shard_map/pallas_call | solution.py:402
  170.3 16.1 %shard_map.171 = (bf16[4,4,192,384]{3,2,1,0:T(8,128)(2,1)}, bf16[4,4,192,384]{3,2,1,0:T(8,128)(2,1)}, f32[512,768]{1,0:T(8,128)}, f32[512,768]{1,0:T(8,128)}) custom-call(s32[13]{0:T(128)S(1)} %stack.256.t, bf16[512,768]{1,0:T(8,128)(2,1)S(1)} %get-tuple-element.36.refs_0_, bf16[512,768]{1,0:T(8,128)(2,1)S(1)} %copy-done.4, ...), custom_call_target="tpu_custom_call" | custom-call | flops 7247757312 | bytes 20971520 | tf_op jit(solution)/shard_map/pallas_call | solution.py:444
  186.5 17.6 %shard_map.172 = (bf16[4,4,192,384]{3,2,1,0:T(8,128)(2,1)}, bf16[4,4,192,384]{3,2,1,0:T(8,128)(2,1)}, f32[512,768]{1,0:T(8,128)}, bf16[512,768]{1,0:T(8,128)(2,1)}) custom-call(s32[13]{0:T(128)S(1)} %stack.256.t, bf16[512,768]{1,0:T(8,128)(2,1)S(1)} %get-tuple-element.36.refs_0_, bf16[512,768]{1,0:T(8,128)(2,1)S(1)} %copy-done.4, ...), custom_call_target="tpu_custom_call" | custom-call | flops 7247757312 | bytes 20971520 | tf_op jit(solution)/shard_map/pallas_call | solution.py:444
  204.1 20.3 %shard_map.173 = (f32[512,768]{1,0:T(8,128)}, bf16[4,4,384,128]{3,2,1,0:T(8,128)(2,1)}, bf16[4,4,384,128]{3,2,1,0:T(8,128)(2,1)}, bf16[4,3,384,128]{3,2,1,0:T(8,...) custom-call(s32[13]{0:T(128)S(1)} %stack.256.t, ...), custom_call_target="tpu_custom_call" | custom-call | flops 5234491392 | bytes 29360128 | tf_op jit(solution)/shard_map/pallas_call | solution.py:452
  224.4 9.3 %shard_map.174 = (f32[512,768]{1,0:T(8,128)}, bf16[4,4,192,128]{3,2,1,0:T(8,128)(2,1)S(1)}, bf16[4,4,192,128]{3,2,1,0:T(8,128)(2,1)S(1)}) custom-call(s32[13]{0:T(128)S(1)} %stack.256.t, bf16[512,768]{1,0:T(8,128)(2,1)} %x_ref.5, f32[8,768]{1,0:T(8,128)S(1)} %get-tuple-element.34.gain_ref, bf16[512,768]{1,0:T(8,128)(2,1)} %copy-done.3, ...), custom_call_target="tpu_custom_call" | custom-call | flops 1610612736 | bytes 12582912 | tf_op jit(solution)/shard_map/pallas_call | solution.py:472
  237.3 2.2 collective-permute-done.25
  246.3 7.3 %collective-permute-done.38 = bf16[3,384,128]{2,1,0:T(8,128)(2,1)S(1)} collective-permute-done((bf16[3,384,128]{2,1,0:T(8,128)(2,1)S(1)}, bf16[3,384,128]{2,1,0:T(8,128)(2,1)S(1)}, u32[]{:S(2)}, u32[]{:S(2)}) %collective-permute-start.38) | collective-permute-done | bytes 294944 | tf_op jit(solution)/shard_map/ppermute | solution.py:509
  253.6 16.1 %collective-permute-done.39 = bf16[3,384,128]{2,1,0:T(8,128)(2,1)S(1)} collective-permute-done((bf16[3,384,128]{2,1,0:T(8,128)(2,1)S(1)}, bf16[3,384,128]{2,1,0:T(8,128)(2,1)S(1)}, u32[]{:S(2)}, u32[]{:S(2)}) %collective-permute-start.39) | collective-permute-done | bytes 294944 | tf_op jit(solution)/shard_map/ppermute | solution.py:509
  273.5 4.2 %collective-permute-done.41 = bf16[2,384,128]{2,1,0:T(8,128)(2,1)S(1)} collective-permute-done((bf16[2,384,128]{2,1,0:T(8,128)(2,1)S(1)}, bf16[2,384,128]{2,1,0:T(8,128)(2,1)S(1)}, u32[]{:S(2)}, u32[]{:S(2)}) %collective-permute-start.41) | collective-permute-done | bytes 196640 | tf_op jit(solution)/shard_map/ppermute | solution.py:509
  278.7 7.1 %collective-permute-done.27 = bf16[4,384,128]{2,1,0:T(8,128)(2,1)S(1)} collective-permute-done((bf16[4,384,128]{2,1,0:T(8,128)(2,1)S(1)}, bf16[4,384,128]{2,1,0:T(8,128)(2,1)S(1)}, u32[]{:S(2)}, u32[]{:S(2)}) %collective-permute-start.27) | collective-permute-done | bytes 393248 | tf_op jit(solution)/shard_map/ppermute | solution.py:509
  288.5 2.8 collective-permute-start.28
  306.8 7.5 %collective-permute-done.32 = bf16[2,4,384,128]{3,2,1,0:T(8,128)(2,1)} collective-permute-done((bf16[2,4,384,128]{3,2,1,0:T(8,128)(2,1)}, bf16[2,4,384,128]{3,2,1,0:T(8,128)(2,1)}, u32[]{:S(2)}, u32[]{:S(2)}) %collective-permute-start.32) | collective-permute-done | bytes 786464 | tf_op jit(solution)/shard_map/ppermute | solution.py:509
  317.5 12.9 %collective-permute-done.46 = bf16[2,4,192,384]{3,2,1,0:T(8,128)(2,1)S(1)} collective-permute-done((bf16[2,4,192,384]{3,2,1,0:T(8,128)(2,1)S(1)}, bf16[2,4,192,384]{3,2,1,0:T(8,128)(2,1)S(1)}, u32[]{:S(2)}, u32[]{:S(2)}) %collective-permute-start.46) | collective-permute-done | bytes 1179680 | tf_op jit(solution)/shard_map/ppermute | solution.py:509
  333.3 6.2 %collective-permute-done.45 = bf16[2,4,192,384]{3,2,1,0:T(8,128)(2,1)S(1)} collective-permute-done((bf16[2,4,192,384]{3,2,1,0:T(8,128)(2,1)S(1)}, bf16[2,4,192,384]{3,2,1,0:T(8,128)(2,1)S(1)}, u32[]{:S(2)}, u32[]{:S(2)}) %collective-permute-start.45) | collective-permute-done | bytes 1179680 | tf_op jit(solution)/shard_map/ppermute | solution.py:509
  344.5 2.8 collective-permute-start.34
  353.5 2.5 collective-permute-start.49
  357.9 4.9 %collective-permute-done.51 = bf16[2,192,384]{2,1,0:T(8,128)(2,1)S(1)} collective-permute-done((bf16[2,192,384]{2,1,0:T(8,128)(2,1)S(1)}, bf16[2,192,384]{2,1,0:T(8,128)(2,1)S(1)}, u32[]{:S(2)}, u32[]{:S(2)}) %collective-permute-start.51) | collective-permute-done | bytes 294944 | tf_op jit(solution)/shard_map/ppermute | solution.py:509
  362.8 8.6 %collective-permute-done.50 = bf16[2,192,384]{2,1,0:T(8,128)(2,1)S(1)} collective-permute-done((bf16[2,192,384]{2,1,0:T(8,128)(2,1)S(1)}, bf16[2,192,384]{2,1,0:T(8,128)(2,1)S(1)}, u32[]{:S(2)}, u32[]{:S(2)}) %collective-permute-start.50) | collective-permute-done | bytes 294944 | tf_op jit(solution)/shard_map/ppermute | solution.py:509
  (184 shorter events, 84.7 us)
Async XLA Ops:
  9.3 17.7 %collective-permute-start.1 = (bf16[768,128]{1,0:T(8,128)(2,1)S(1)}, bf16[768,128]{1,0:T(8,128)(2,1)S(1)}, u32[]{:S(2)}, u32[]{:S(2)}) collective-permute-start(bf16[768,128]{1,0:T(8,128)(2,1)S(1)} %fusion.34), channel_id=1, source_target_pairs={{0,4},{1,5},{2,6},{3,7},{4,0},{5,1},{6,2},{7,3},{8,12},{9,13},{10,... | collective-permute-start | bytes 589832 | tf_op jit(solution)/shard_map/ppermute | solution.py:509
  9.3 17.7 %collective-permute-start = (bf16[768,128]{1,0:T(8,128)(2,1)S(1)}, bf16[768,128]{1,0:T(8,128)(2,1)S(1)}, u32[]{:S(2)}, u32[]{:S(2)}) collective-permute-start(bf16[768,128]{1,0:T(8,128)(2,1)S(1)} %fusion.34), channel_id=1, source_target_pairs={{0,2},{1,3},{2,4},{3,5},{4,6},{5,7},{6,0},{7,1},{8,10},{9,11},{10,... | collective-permute-start | bytes 589832 | tf_op jit(solution)/shard_map/ppermute | solution.py:509
  11.3 18.1 %collective-permute-start.17 = (bf16[2,192,384]{2,1,0:T(8,128)(2,1)S(1)}, bf16[2,192,384]{2,1,0:T(8,128)(2,1)S(1)}, u32[]{:S(2)}, u32[]{:S(2)}) collective-permute-start(bf16[2,192,384]{2,1,0:T(8,128)(2,1)S(1)} %get-tuple-element.120), channel_id=1, source_target_pairs={{0,6},{1,7},{2,0},{3,1},{4,2},{5,3},{6,4},{7,5},{8,14},{9,15},{10,... | collective-permute-start | bytes 884744 | tf_op jit(solution)/shard_map/ppermute | solution.py:509
  14.2 37.1 %collective-permute-start.16 = (bf16[2,192,384]{2,1,0:T(8,128)(2,1)S(1)}, bf16[2,192,384]{2,1,0:T(8,128)(2,1)S(1)}, u32[]{:S(2)}, u32[]{:S(2)}) collective-permute-start(bf16[2,192,384]{2,1,0:T(8,128)(2,1)S(1)} %get-tuple-element.120), channel_id=1, source_target_pairs={{0,4},{1,5},{2,6},{3,7},{4,0},{5,1},{6,2},{7,3},{8,12},{9,13},{10,... | collective-permute-start | bytes 884744 | tf_op jit(solution)/shard_map/ppermute | solution.py:509
  15.3 36.0 %collective-permute-start.15 = (bf16[2,192,384]{2,1,0:T(8,128)(2,1)S(1)}, bf16[2,192,384]{2,1,0:T(8,128)(2,1)S(1)}, u32[]{:S(2)}, u32[]{:S(2)}) collective-permute-start(bf16[2,192,384]{2,1,0:T(8,128)(2,1)S(1)} %get-tuple-element.120), channel_id=1, source_target_pairs={{0,2},{1,3},{2,4},{3,5},{4,6},{5,7},{6,0},{7,1},{8,10},{9,11},{10,... | collective-permute-start | bytes 884744 | tf_op jit(solution)/shard_map/ppermute | solution.py:509
  51.7 16.3 %collective-permute-start.18 = (bf16[4,192,384]{2,1,0:T(8,128)(2,1)S(1)}, bf16[4,192,384]{2,1,0:T(8,128)(2,1)S(1)}, u32[]{:S(2)}, u32[]{:S(2)}) collective-permute-start(bf16[4,192,384]{2,1,0:T(8,128)(2,1)S(1)} %get-tuple-element.91), channel_id=1, source_target_pairs={{0,8},{1,9},{2,10},{3,11},{4,12},{5,13},{6,14},{7,15},{8,0},{9,1},... | collective-permute-start | bytes 1769480 | tf_op jit(solution)/shard_map/ppermute | solution.py:509
  55.1 23.2 %collective-permute-start.21 = (bf16[4,192,384]{2,1,0:T(8,128)(2,1)S(1)}, bf16[4,192,384]{2,1,0:T(8,128)(2,1)S(1)}, u32[]{:S(2)}, u32[]{:S(2)}) collective-permute-start(bf16[4,192,384]{2,1,0:T(8,128)(2,1)S(1)} %get-tuple-element.92), channel_id=1, source_target_pairs={{0,16},{1,17},{2,18},{3,19},{4,20},{5,21},{6,22},{7,23},{8,24},{9,... | collective-permute-start | bytes 1769480 | tf_op jit(solution)/shard_map/ppermute | solution.py:509
  55.6 27.7 %collective-permute-start.9 = (bf16[384,128]{1,0:T(8,128)(2,1)S(1)}, bf16[384,128]{1,0:T(8,128)(2,1)S(1)}, u32[]{:S(2)}, u32[]{:S(2)}) collective-permute-start(bf16[384,128]{1,0:T(8,128)(2,1)S(1)} %bitcast.268), channel_id=1, source_target_pairs={{0,8},{1,9},{2,10},{3,11},{4,12},{5,13},{6,14},{7,15},{8,0},{9,1},... | collective-permute-start | bytes 294920 | tf_op jit(solution)/shard_map/ppermute | solution.py:509
  56.2 24.4 %collective-permute-start.6 = (bf16[4,384,128]{2,1,0:T(8,128)(2,1)S(1)}, bf16[4,384,128]{2,1,0:T(8,128)(2,1)S(1)}, u32[]{:S(2)}, u32[]{:S(2)}) collective-permute-start(bf16[4,384,128]{2,1,0:T(8,128)(2,1)S(1)} %get-tuple-element.100), channel_id=1, source_target_pairs={{0,8},{1,9},{2,10},{3,11},{4,12},{5,13},{6,14},{7,15},{8,0},{9,1},... | collective-permute-start | bytes 1179656 | tf_op jit(solution)/shard_map/ppermute | solution.py:509
  66.6 56.1 %collective-permute-start.4 = (bf16[2,4,384,128]{3,2,1,0:T(8,128)(2,1)}, bf16[2,4,384,128]{3,2,1,0:T(8,128)(2,1)}, u32[]{:S(2)}, u32[]{:S(2)}) collective-permute-start(bf16[2,4,384,128]{3,2,1,0:T(8,128)(2,1)} %get-tuple-element.103), channel_id=1, source_target_pairs={{0,8},{1,9},{2,10},{3,11},{4,12},{5,13},{6,14},{7,15},{8,0},{9,1},... | collective-permute-start | bytes 2359304 | tf_op jit(solution)/shard_map/ppermute | solution.py:509
  69.3 62.2 %collective-permute-start.19 = (bf16[2,4,192,384]{3,2,1,0:T(8,128)(2,1)}, bf16[2,4,192,384]{3,2,1,0:T(8,128)(2,1)}, u32[]{:S(2)}, u32[]{:S(2)}) collective-permute-start(bf16[2,4,192,384]{3,2,1,0:T(8,128)(2,1)} %get-tuple-element.95), channel_id=1, source_target_pairs={{0,16},{1,17},{2,18},{3,19},{4,20},{5,21},{6,22},{7,23},{8,24},{9,... | collective-permute-start | bytes 3538952 | tf_op jit(solution)/shard_map/ppermute | solution.py:509
  80.0 54.4 %collective-permute-start.22 = (bf16[2,4,192,384]{3,2,1,0:T(8,128)(2,1)}, bf16[2,4,192,384]{3,2,1,0:T(8,128)(2,1)}, u32[]{:S(2)}, u32[]{:S(2)}) collective-permute-start(bf16[2,4,192,384]{3,2,1,0:T(8,128)(2,1)} %get-tuple-element.89), channel_id=1, source_target_pairs={{0,8},{1,9},{2,10},{3,11},{4,12},{5,13},{6,14},{7,15},{8,0},{9,1},... | collective-permute-start | bytes 3538952 | tf_op jit(solution)/shard_map/ppermute | solution.py:509
  81.8 45.2 %collective-permute-start.7 = (bf16[2,4,384,128]{3,2,1,0:T(8,128)(2,1)}, bf16[2,4,384,128]{3,2,1,0:T(8,128)(2,1)}, u32[]{:S(2)}, u32[]{:S(2)}) collective-permute-start(bf16[2,4,384,128]{3,2,1,0:T(8,128)(2,1)} %get-tuple-element.97), channel_id=1, source_target_pairs={{0,16},{1,17},{2,18},{3,19},{4,20},{5,21},{6,22},{7,23},{8,24},{9,... | collective-permute-start | bytes 2359304 | tf_op jit(solution)/shard_map/ppermute | solution.py:509
  83.4 39.1 %collective-permute-start.10 = (bf16[2,384,128]{2,1,0:T(8,128)(2,1)S(1)}, bf16[2,384,128]{2,1,0:T(8,128)(2,1)S(1)}, u32[]{:S(2)}, u32[]{:S(2)}) collective-permute-start(bf16[2,384,128]{2,1,0:T(8,128)(2,1)S(1)} %get-tuple-element.128), channel_id=1, source_target_pairs={{0,16},{1,17},{2,18},{3,19},{4,20},{5,21},{6,22},{7,23},{8,24},{9,... | collective-permute-start | bytes 589832 | tf_op jit(solution)/shard_map/ppermute | solution.py:509
  122.7 27.1 %collective-permute-start.12 = (bf16[3,384,128]{2,1,0:T(8,128)(2,1)S(1)}, bf16[3,384,128]{2,1,0:T(8,128)(2,1)S(1)}, u32[]{:S(2)}, u32[]{:S(2)}) collective-permute-start(bf16[3,384,128]{2,1,0:T(8,128)(2,1)S(1)} %get-tuple-element.122), channel_id=1, source_target_pairs={{0,4},{1,5},{2,6},{3,7},{4,0},{5,1},{6,2},{7,3},{8,12},{9,13},{10,... | collective-permute-start | bytes 884744 | tf_op jit(solution)/shard_map/ppermute | solution.py:509
  127.0 22.8 %collective-permute-start.11 = (bf16[3,384,128]{2,1,0:T(8,128)(2,1)S(1)}, bf16[3,384,128]{2,1,0:T(8,128)(2,1)S(1)}, u32[]{:S(2)}, u32[]{:S(2)}) collective-permute-start(bf16[3,384,128]{2,1,0:T(8,128)(2,1)S(1)} %get-tuple-element.122), channel_id=1, source_target_pairs={{0,2},{1,3},{2,4},{3,5},{4,6},{5,7},{6,0},{7,1},{8,10},{9,11},{10,... | collective-permute-start | bytes 884744 | tf_op jit(solution)/shard_map/ppermute | solution.py:509
  131.4 20.4 %collective-permute-start.5 = (bf16[4,4,384,128]{3,2,1,0:T(8,128)(2,1)S(1)}, bf16[4,4,384,128]{3,2,1,0:T(8,128)(2,1)}, u32[]{:S(2)}, u32[]{:S(2)}) collective-permute-start(bf16[4,4,384,128]{3,2,1,0:T(8,128)(2,1)S(1)} %bitcast.249), channel_id=1, source_target_pairs={{0,1},{1,0},{2,3},{3,2},{4,5},{5,4},{6,7},{7,6},{8,9},{9,8},{10,11... | collective-permute-start | bytes 4718600 | tf_op jit(solution)/shard_map/ppermute | solution.py:509
  134.5 23.2 %collective-permute-start.8 = (bf16[4,4,384,128]{3,2,1,0:T(8,128)(2,1)}, bf16[4,4,384,128]{3,2,1,0:T(8,128)(2,1)}, u32[]{:S(2)}, u32[]{:S(2)}) collective-permute-start(bf16[4,4,384,128]{3,2,1,0:T(8,128)(2,1)} %bitcast.31.a_own), channel_id=1, source_target_pairs={{0,1},{1,0},{2,3},{3,2},{4,5},{5,4},{6,7},{7,6},{8,9},{9,8},{10,11... | collective-permute-start | bytes 4718600 | tf_op jit(solution)/shard_map/ppermute | solution.py:509
  138.0 48.5 %collective-permute-start.20 = (bf16[4,4,192,384]{3,2,1,0:T(8,128)(2,1)}, bf16[4,4,192,384]{3,2,1,0:T(8,128)(2,1)}, u32[]{:S(2)}, u32[]{:S(2)}) collective-permute-start(bf16[4,4,192,384]{3,2,1,0:T(8,128)(2,1)} %bitcast.57.refs_2_), channel_id=1, source_target_pairs={{0,1},{1,0},{2,3},{3,2},{4,5},{5,4},{6,7},{7,6},{8,9},{9,8},{10,11... | collective-permute-start | bytes 7077896 | tf_op jit(solution)/shard_map/ppermute | solution.py:509
  149.8 36.7 %collective-permute-start.23 = (bf16[4,4,192,384]{3,2,1,0:T(8,128)(2,1)}, bf16[4,4,192,384]{3,2,1,0:T(8,128)(2,1)}, u32[]{:S(2)}, u32[]{:S(2)}) collective-permute-start(bf16[4,4,192,384]{3,2,1,0:T(8,128)(2,1)} %bitcast.63.refs_3_), channel_id=1, source_target_pairs={{0,1},{1,0},{2,3},{3,2},{4,5},{5,4},{6,7},{7,6},{8,9},{9,8},{10,11... | collective-permute-start | bytes 7077896 | tf_op jit(solution)/shard_map/ppermute | solution.py:509
  234.2 38.0 %collective-permute-start.31 = (bf16[4,4,384,128]{3,2,1,0:T(8,128)(2,1)}, bf16[4,4,384,128]{3,2,1,0:T(8,128)(2,1)S(1)}, u32[]{:S(2)}, u32[]{:S(2)}) collective-permute-start(bf16[4,4,384,128]{3,2,1,0:T(8,128)(2,1)} %get-tuple-element.52), channel_id=1, source_target_pairs={{0,1},{1,0},{2,3},{3,2},{4,5},{5,4},{6,7},{7,6},{8,9},{9,8},{10,11... | collective-permute-start | bytes 4718600 | tf_op jit(solution)/shard_map/ppermute | solution.py:509
  240.9 30.6 %collective-permute-start.26 = (bf16[2,4,384,128]{3,2,1,0:T(8,128)(2,1)S(1)}, bf16[2,4,384,128]{3,2,1,0:T(8,128)(2,1)S(1)}, u32[]{:S(2)}, u32[]{:S(2)}) collective-permute-start(bf16[2,4,384,128]{3,2,1,0:T(8,128)(2,1)S(1)} %add_convert_fusion.3), channel_id=1, source_target_pairs={{0,8},{1,9},{2,10},{3,11},{4,12},{5,13},{6,14},{7,15},{8,0},{9,1},... | collective-permute-start | bytes 2359304 | tf_op jit(solution)/shard_map/ppermute | solution.py:509
  244.8 54.9 %collective-permute-start.44 = (bf16[4,4,192,384]{3,2,1,0:T(8,128)(2,1)}, bf16[4,4,192,384]{3,2,1,0:T(8,128)(2,1)S(1)}, u32[]{:S(2)}, u32[]{:S(2)}) collective-permute-start(bf16[4,4,192,384]{3,2,1,0:T(8,128)(2,1)} %get-tuple-element.58), channel_id=1, source_target_pairs={{0,1},{1,0},{2,3},{3,2},{4,5},{5,4},{6,7},{7,6},{8,9},{9,8},{10,11... | collective-permute-start | bytes 7077896 | tf_op jit(solution)/shard_map/ppermute | solution.py:509
  245.0 24.7 %collective-permute-start.39 = (bf16[3,384,128]{2,1,0:T(8,128)(2,1)S(1)}, bf16[3,384,128]{2,1,0:T(8,128)(2,1)S(1)}, u32[]{:S(2)}, u32[]{:S(2)}) collective-permute-start(bf16[3,384,128]{2,1,0:T(8,128)(2,1)S(1)} %get-tuple-element.86), channel_id=1, source_target_pairs={{0,4},{1,5},{2,6},{3,7},{4,0},{5,1},{6,2},{7,3},{8,12},{9,13},{10,... | collective-permute-start | bytes 884744 | tf_op jit(solution)/shard_map/ppermute | solution.py:509
  269.7 32.5 %collective-permute-start.43 = (bf16[4,4,192,384]{3,2,1,0:T(8,128)(2,1)}, bf16[4,4,192,384]{3,2,1,0:T(8,128)(2,1)}, u32[]{:S(2)}, u32[]{:S(2)}) collective-permute-start(bf16[4,4,192,384]{3,2,1,0:T(8,128)(2,1)} %get-tuple-element.57), channel_id=1, source_target_pairs={{0,1},{1,0},{2,3},{3,2},{4,5},{5,4},{6,7},{7,6},{8,9},{9,8},{10,11... | collective-permute-start | bytes 7077896 | tf_op jit(solution)/shard_map/ppermute | solution.py:509
  293.5 20.8 %collective-permute-start.32 = (bf16[2,4,384,128]{3,2,1,0:T(8,128)(2,1)}, bf16[2,4,384,128]{3,2,1,0:T(8,128)(2,1)}, u32[]{:S(2)}, u32[]{:S(2)}) collective-permute-start(bf16[2,4,384,128]{3,2,1,0:T(8,128)(2,1)} %add_convert_fusion.2), channel_id=1, source_target_pairs={{0,16},{1,17},{2,18},{3,19},{4,20},{5,21},{6,22},{7,23},{8,24},{9,... | collective-permute-start | bytes 2359304 | tf_op jit(solution)/shard_map/ppermute | solution.py:509
  301.4 29.0 %collective-permute-start.46 = (bf16[2,4,192,384]{3,2,1,0:T(8,128)(2,1)S(1)}, bf16[2,4,192,384]{3,2,1,0:T(8,128)(2,1)S(1)}, u32[]{:S(2)}, u32[]{:S(2)}) collective-permute-start(bf16[2,4,192,384]{3,2,1,0:T(8,128)(2,1)S(1)} %add_convert_fusion), channel_id=1, source_target_pairs={{0,8},{1,9},{2,10},{3,11},{4,12},{5,13},{6,14},{7,15},{8,0},{9,1},... | collective-permute-start | bytes 3538952 | tf_op jit(solution)/shard_map/ppermute | solution.py:509
  303.9 35.6 %collective-permute-start.45 = (bf16[2,4,192,384]{3,2,1,0:T(8,128)(2,1)S(1)}, bf16[2,4,192,384]{3,2,1,0:T(8,128)(2,1)S(1)}, u32[]{:S(2)}, u32[]{:S(2)}) collective-permute-start(bf16[2,4,192,384]{3,2,1,0:T(8,128)(2,1)S(1)} %add_convert_fusion.1), channel_id=1, source_target_pairs={{0,16},{1,17},{2,18},{3,19},{4,20},{5,21},{6,22},{7,23},{8,24},{9,... | collective-permute-start | bytes 3538952 | tf_op jit(solution)/shard_map/ppermute | solution.py:509
  315.5 26.2 %collective-permute-start.33 = (bf16[4,384,128]{2,1,0:T(8,128)(2,1)S(1)}, bf16[4,384,128]{2,1,0:T(8,128)(2,1)S(1)}, u32[]{:S(2)}, u32[]{:S(2)}) collective-permute-start(bf16[4,384,128]{2,1,0:T(8,128)(2,1)S(1)} %fusion.6), channel_id=1, source_target_pairs={{0,8},{1,9},{2,10},{3,11},{4,12},{5,13},{6,14},{7,15},{8,0},{9,1},... | collective-permute-start | bytes 1179656 | tf_op jit(solution)/shard_map/ppermute | solution.py:509
  331.7 17.1 %collective-permute-start.48 = (bf16[4,192,384]{2,1,0:T(8,128)(2,1)S(1)}, bf16[4,192,384]{2,1,0:T(8,128)(2,1)S(1)}, u32[]{:S(2)}, u32[]{:S(2)}) collective-permute-start(bf16[4,192,384]{2,1,0:T(8,128)(2,1)S(1)} %fusion.1), channel_id=1, source_target_pairs={{0,16},{1,17},{2,18},{3,19},{4,20},{5,21},{6,22},{7,23},{8,24},{9,... | collective-permute-start | bytes 1769480 | tf_op jit(solution)/shard_map/ppermute | solution.py:509
  351.8 19.6 %collective-permute-start.50 = (bf16[2,192,384]{2,1,0:T(8,128)(2,1)S(1)}, bf16[2,192,384]{2,1,0:T(8,128)(2,1)S(1)}, u32[]{:S(2)}, u32[]{:S(2)}) collective-permute-start(bf16[2,192,384]{2,1,0:T(8,128)(2,1)S(1)} %get-tuple-element.78), channel_id=1, source_target_pairs={{0,4},{1,5},{2,6},{3,7},{4,0},{5,1},{6,2},{7,3},{8,12},{9,13},{10,... | collective-permute-start | bytes 884744 | tf_op jit(solution)/shard_map/ppermute | solution.py:509
  353.5 17.8 %collective-permute-start.49 = (bf16[2,192,384]{2,1,0:T(8,128)(2,1)S(1)}, bf16[2,192,384]{2,1,0:T(8,128)(2,1)S(1)}, u32[]{:S(2)}, u32[]{:S(2)}) collective-permute-start(bf16[2,192,384]{2,1,0:T(8,128)(2,1)S(1)} %get-tuple-element.77), channel_id=1, source_target_pairs={{0,6},{1,7},{2,0},{3,1},{4,2},{5,3},{6,4},{7,5},{8,14},{9,15},{10,... | collective-permute-start | bytes 884744 | tf_op jit(solution)/shard_map/ppermute | solution.py:509
  (38 other events, 488.5 us)

commit v3 on v2

v3 whole, which is shorter than its diff:
```python
import functools

import jax
import jax.numpy as jnp
from jax import lax
from jax.experimental import pallas as pl
from jax.experimental.pallas import tpu as pltpu
from jax.sharding import PartitionSpec as P

D = 768
H = 12
HS = 64
FF = 3072
L = 512
EPS = 1e-05
G = 4
Z = 4
DB = D // G
CB = D // (2 * Z)
FB = FF // (2 * Z)
QB = L // (2 * Z)
KB = L // G
LN = 128
GW = 2 * LN
GN = CB // 4
HA = H // 2
HR = HA * QB
TM = 128
WIN = 3
HZ = H // Z
GC = 0.7978845608
GA = 0.044715
VMEM_LIMIT = 52 * 1024 * 1024
COST = 1 << 36

F32 = jnp.float32
BF16 = jnp.bfloat16


def dot(a, b, ca, cb):
    return lax.dot_general(a, b, (((ca,), (cb,)), ((), ())), preferred_element_type=F32)


def call(body, grid, in_specs, out_specs, out_shape, scratch=(), flops=0, nbytes=0):
    return pl.pallas_call(
        body,
        grid_spec=pltpu.PrefetchScalarGridSpec(
            num_scalar_prefetch=1,
            grid=grid,
            in_specs=in_specs,
            out_specs=out_specs,
            scratch_shapes=list(scratch),
        ),
        out_shape=out_shape,
        compiler_params=pltpu.CompilerParams(
            dimension_semantics=("arbitrary",) * len(grid), vmem_limit_bytes=VMEM_LIMIT
        ),
        cost_estimate=pl.CostEstimate(flops=COST, bytes_accessed=nbytes, transcendentals=0),
    )


def whole(shape):
    zeros = (0,) * len(shape)
    return pl.BlockSpec(shape, lambda i, t: zeros, pipeline_mode=pl.Buffered(1))


def rows(width):
    return pl.BlockSpec((TM, width), lambda i, t: (i, 0))


def out_whole(shape):
    zeros = (0,) * len(shape)
    return pl.BlockSpec(shape, lambda i, t: zeros)


def tab_a(t, g):
    return t[1 + g]


def tab_b(t, g):
    return t[1 + G + g]


def tab_z(t, z):
    return t[1 + 2 * G + z]


def norm_stats(x):
    mean = jnp.mean(x, axis=-1, keepdims=True)
    cen = x - mean
    rstd = lax.rsqrt(jnp.mean(cen * cen, axis=-1, keepdims=True) + EPS)
    return cen, rstd


def weight_z(own, oth, t, z, base, tab=tab_a):
    parts = [
        jnp.concatenate(
            [ref[tab(t, g), tab_z(t, z), base : base + DB, :] for g in range(G)], axis=0
        )
        for ref in (own, oth)
    ]
    return jnp.concatenate(parts, axis=1)


def head_masks(core, nrows):
    lane = lax.broadcasted_iota(jnp.int32, (nrows, GW), 1)
    tile = lane // LN
    place = lane - tile * LN
    side = jnp.where(core == 0, tile, 1 - tile)
    col = jnp.where(place < CB, side * CB + place, -1)
    return [jnp.logical_and(col >= HS * i, col < HS * (i + 1)) for i in range(HZ)]


def halves(ref, core, lead=None):
    lo = pl.multiple_of(core * QB, QB)
    hi = pl.multiple_of((1 - core) * QB, QB)
    if lead is None:
        return jnp.concatenate([ref[pl.ds(lo, QB), :], ref[pl.ds(hi, QB), :]], axis=0)
    return jnp.concatenate([ref[lead, pl.ds(lo, QB), :], ref[lead, pl.ds(hi, QB), :]], axis=0)


def put_halves(ref, core, val, lead=None):
    lo = pl.multiple_of(core * QB, QB)
    hi = pl.multiple_of((1 - core) * QB, QB)
    if lead is None:
        ref[pl.ds(lo, QB), :] = val[:QB]
        ref[pl.ds(hi, QB), :] = val[QB:]
    else:
        ref[lead, pl.ds(lo, QB), :] = val[:QB]
        ref[lead, pl.ds(hi, QB), :] = val[QB:]


def window(m):
    return jnp.clip(m - 1, 0, G - WIN)


def block_at(banded, tab, t, m, i):
    return (tab_z(t, m), i) if banded else (tab(t, window(m) + i), tab_z(t, m))


def exp_scores(banded, own, oth, t, m, local, mask):
    parts = []
    for i in range(WIN):
        at = block_at(banded, tab_b, t, m, i) + (slice(local * QB, (local + 1) * QB),)
        parts.append(jnp.concatenate([own[at], oth[at]], axis=0))
    scores = jnp.concatenate(parts, axis=1).astype(F32)
    return jnp.where(mask, jnp.exp(scores), 0.0)


def gain_spots():
    for g in range(G):
        for z in range(Z):
            for c in range(2):
                yield g, z, c, DB * g + (2 * GN) * z + GN * c


def pick(core, c, own, oth):
    return jnp.where(core == c, own, oth)


def gains_row(own, oth, t, base):
    lane = lax.broadcasted_iota(jnp.int32, (1, LN), 1)
    tiles = [jnp.zeros((1, LN), F32) for _ in range(D // LN)]
    for g, z, c, at in gain_spots():
        a, b = (r[tab_a(t, g), tab_z(t, z), base : base + 16, :].astype(F32)[:1] for r in (own, oth))
        row = pick(t[0], c, a, b)
        tile, off = at // LN, at % LN
        row = pltpu.roll(row, (off - CB) % LN, 1)
        tiles[tile] = jnp.where(jnp.logical_and(lane >= off, lane < off + GN), row, tiles[tile])
        if off + GN > LN:
            tiles[tile + 1] = jnp.where(lane < off + GN - LN, row, tiles[tile + 1])
    return jnp.concatenate(tiles, axis=1)


def put_weight_grads(acc, dg, t, keep, send, tab):
    lane = lax.broadcasted_iota(jnp.int32, (1, LN), 1)
    top = lax.broadcasted_iota(jnp.int32, (16, LN), 0) == 0
    spot = jnp.logical_and(top, jnp.logical_and(lane >= CB, lane < CB + GN))
    rows_of = {}
    for g, z, c, at in gain_spots():
        tile, off = at // LN, at % LN
        row = dg[:, tile * LN : (tile + 1) * LN]
        if off + GN > LN:
            row = jnp.where(lane < off, dg[:, (tile + 1) * LN : (tile + 2) * LN], row)
        rows_of[g, z, c] = pltpu.roll(row, (CB - off) % LN, 1)
    for g in range(G):
        for z in range(Z):
            for p, ref in ((0, keep), (1, send)):
                blk = acc[z, g * DB : (g + 1) * DB, p * LN : (p + 1) * LN]
                row = pick(t[0], p, rows_of[g, z, 0], rows_of[g, z, 1])
                ref[tab(t, g), tab_z(t, z)] = blk.astype(BF16)
                ref[tab(t, g), tab_z(t, z), 0:16, :] = jnp.where(spot, row, blk[:16]).astype(BF16)


def values_body(t, x_ref, own_ref, oth_ref, n_ref, val_ref, gain_ref):
    @pl.when(pl.program_id(0) == 0)
    def _():
        gain_ref[0:1, :] = gains_row(own_ref, oth_ref, t, 0)
        gain_ref[1:2, :] = gains_row(own_ref, oth_ref, t, DB)

    cen, rstd = norm_stats(x_ref[...].astype(F32))
    low = (cen * rstd * gain_ref[0:1, :]).astype(BF16)
    n_ref[...] = low
    for z in range(Z):
        val_ref[z] = dot(low, weight_z(own_ref, oth_ref, t, z, 0), 1, 0).astype(BF16)


def mixer_body(last, t, x_ref, gain_ref, dq_ref, dk_ref, val_ref, own, oth, *refs):
    if last:
        first_ref, w_own, w_oth, mix_ref, mid_ref, n_ref = refs
    else:
        (mix_ref,) = refs
    m = pl.program_id(0)
    core = t[0]
    k0 = pl.multiple_of(window(m) * KB, KB)
    mask = halves(dq_ref, core) == dk_ref[:, pl.ds(k0, WIN * KB)]
    heads = head_masks(core, TM)
    lows = []
    for j in range(Z // 2):
        win = val_ref[j, pl.ds(k0, WIN * KB), :]
        out = jnp.zeros((TM, GW), F32)
        for i in range(HZ):
            e = exp_scores(last, own, oth, t, m, HZ * j + i, mask)
            inv = 1.0 / jnp.sum(e, axis=-1, keepdims=True)
            part = dot((e * inv).astype(BF16), win, 1, 0)
            out = jnp.where(heads[i], part, out)
        low = out.astype(BF16)
        put_halves(mix_ref, core, low, j)
        lows.append(low)
    if last:
        acc = halves(x_ref, core).astype(F32)
        lows = [halves(first_ref, core, j) for j in range(Z // 2)] + lows
        for z in range(Z):
            acc = acc + dot(lows[z], weight_z(w_own, w_oth, t, z, DB), 1, 1)
        put_halves(mid_ref, core, acc)
        cen, rstd = norm_stats(acc)
        put_halves(n_ref, core, (cen * rstd * gain_ref[1:2, :]).astype(BF16))


def ffn_body(first, last, tab, t, n_ref, c_ref, own, oth, *refs):
    refs = list(refs)
    if not first:
        ia_ref, ib_ref = refs[:2]
        refs = refs[2:]
    if last:
        mid_ref = refs[0]
        refs = refs[1:]
    keep, send, a_ref, b_ref = refs[:4]
    j = pl.program_id(0)
    n = n_ref[...]
    cot = c_ref[...]

    def weights(base):
        return jnp.concatenate(
            [
                jnp.concatenate([r[tab(t, g), 0, base : base + DB, :] for g in range(G)], axis=0)
                for r in (own, oth)
            ],
            axis=1,
        )

    up_w, dn_w = weights(0), weights(DB)

    @pl.when(j == 0)
    def _():
        if first:
            a_ref[...] = jnp.zeros_like(a_ref)
            b_ref[...] = jnp.zeros_like(b_ref)
        else:
            a_ref[...] = ia_ref[...]
            b_ref[...] = ib_ref[...]

    up = dot(n, up_w, 1, 0)
    sq = up * up
    th = jnp.tanh(GC * up * (1.0 + GA * sq))
    half = 0.5 + 0.5 * th
    act = (up * half).astype(BF16)
    slope = half + (0.5 * GC) * up * (1.0 - th * th) * (1.0 + (3.0 * GA) * sq)
    a_ref[...] += dot(act, dn_w, 1, 1)
    gd = dot(cot, act, 0, 0).astype(BF16)
    up_g = (dot(cot, dn_w, 1, 0) * slope).astype(BF16)
    gu = dot(n, up_g, 0, 0).astype(BF16)
    b_ref[...] += dot(up_g, up_w, 1, 1)
    for p, ref in ((0, keep), (1, send)):
        for g in range(G):
            part = slice(g * DB, (g + 1) * DB), slice(p * LN, (p + 1) * LN)
            ref[tab(t, g), 0, 0:DB, :] = gu[part]
            ref[tab(t, g), 0, DB : 2 * DB, :] = gd[part]
    if last:
        lo_ref = refs[4]

        @pl.when(j == Z - 1)
        def _():
            lo_ref[...] = (mid_ref[...] + a_ref[...]).astype(BF16)


def norm_back(cen, rstd, gain, dn):
    xhat = cen * rstd
    e = dn * gain
    dv = (
        e
        - jnp.mean(e, axis=-1, keepdims=True)
        - xhat * jnp.mean(e * xhat, axis=-1, keepdims=True)
    ) * rstd
    return dv, jnp.sum(dn * xhat, axis=0, keepdims=True)


def branch_body(
    t, dn_ref, mid_ref, c_ref, gain_ref, mixa_ref, mixb_ref, w_own, w_oth,
    mg_ref, grad_ref, keep, send, dg_acc, go_acc,
):
    m = pl.program_id(0)

    @pl.when(m == 0)
    def _():
        go_acc[...] = jnp.zeros_like(go_acc)
        dg_acc[...] = jnp.zeros_like(dg_acc)

    cen, rstd = norm_stats(mid_ref[...])
    dv, dg = norm_back(cen, rstd, gain_ref[1:2, :], dn_ref[...])
    dg_acc[0:1, :] += dg
    mid_grad = c_ref[...].astype(F32) + dv
    mg_ref[...] = mid_grad
    branch = mid_grad.astype(BF16)
    for z in range(Z):
        mix = mixa_ref[z] if z < Z // 2 else mixb_ref[z - Z // 2]
        go_acc[z] += dot(branch, mix, 0, 0)
        grad_ref[z] = dot(branch, weight_z(w_own, w_oth, t, z, DB), 1, 0).astype(BF16)

    @pl.when(m == Z - 1)
    def _():
        put_weight_grads(go_acc, dg_acc[0:1, :], t, keep, send, tab_a)


def mixer_back_body(banded, t, grad_ref, dq_ref, dk_ref, val_ref, own, oth, keep, send, vg_ref, vg_acc):
    m = pl.program_id(0)
    core = t[0]
    start = window(m)
    k0 = pl.multiple_of(start * KB, KB)

    @pl.when(m == 0)
    def _():
        vg_acc[...] = jnp.zeros_like(vg_acc)

    mask = halves(dq_ref, core) == dk_ref[:, pl.ds(k0, WIN * KB)]
    heads = head_masks(core, TM)
    if not banded:
        rest = tab_b(t, jnp.where(start == 0, G - 1, 0))
        keep[rest, 0] = jnp.zeros((HR, KB), BF16)
        send[rest, 0] = jnp.zeros((HR, KB), BF16)
    for j in range(Z // 2):
        grad = halves(grad_ref, core, j)
        win = val_ref[j, pl.ds(k0, WIN * KB), :]
        total = jnp.zeros((WIN * KB, GW), F32)
        for i in range(HZ):
            local = HZ * j + i
            e = exp_scores(banded, own, oth, t, m, local, mask)
            inv = 1.0 / jnp.sum(e, axis=-1, keepdims=True)
            prob = e * inv
            mine = jnp.where(heads[i], grad, jnp.zeros_like(grad))
            total = total + dot(prob.astype(BF16), mine, 0, 0)
            dp = dot(mine, win, 1, 1)
            pd = prob * dp
            ds = (pd - prob * jnp.sum(pd, axis=-1, keepdims=True)).astype(BF16)
            for k in range(WIN):
                at = (0, k) if banded else (tab_b(t, start + k), 0)
                at = at + (slice(local * QB, (local + 1) * QB),)
                for p, ref in ((0, keep), (1, send)):
                    ref[at] = ds[p * QB : (p + 1) * QB, k * KB : (k + 1) * KB]
        vg_acc[j, pl.ds(k0, WIN * KB), :] += total

    @pl.when(m == Z - 1)
    def _():
        vg_ref[...] = vg_acc[...].astype(BF16)


def last_body(
    t, x_ref, gain_ref, n_ref, vga_ref, vgb_ref, w_own, w_oth, mg_ref, gi_ref, keep, send, dg_acc, gv_acc
):
    m = pl.program_id(0)

    @pl.when(m == 0)
    def _():
        gv_acc[...] = jnp.zeros_like(gv_acc)
        dg_acc[...] = jnp.zeros_like(dg_acc)

    low = n_ref[...]
    dn = jnp.zeros((TM, D), F32)
    for z in range(Z):
        vg = vga_ref[z] if z < Z // 2 else vgb_ref[z - Z // 2]
        gv_acc[z] += dot(low, vg, 0, 0)
        dn = dn + dot(vg, weight_z(w_own, w_oth, t, z, 0), 1, 1)
    cen, rstd = norm_stats(x_ref[...].astype(F32))
    dv, dg = norm_back(cen, rstd, gain_ref[0:1, :], dn)
    dg_acc[0:1, :] += dg
    gi_ref[...] = mg_ref[...] + dv

    @pl.when(m == Z - 1)
    def _():
        put_weight_grads(gv_acc, dg_acc[0:1, :], t, keep, send, tab_a)


def sds(shape, dtype):
    return jax.ShapeDtypeStruct(shape, dtype)


U_SHAPE = (G, Z, 2 * DB, LN)
V_SHAPE = (G, Z, DB, LN)
B_SHAPE = (Z, WIN, HR, KB)
H_SHAPE = (Z // 2, L, GW)
Z_ROWS = pl.BlockSpec((Z, TM, GW), lambda i, t: (0, i, 0))
H_ROWS = pl.BlockSpec((Z // 2, TM, GW), lambda i, t: (0, i, 0))


def half(i):
    return pl.BlockSpec(H_SHAPE, lambda j, t: (i, 0, 0), pipeline_mode=pl.Buffered(1))


def half_rows(i):
    return pl.BlockSpec((Z // 2, TM, GW), lambda j, t: (i, j, 0))


def run_values(tab, x, w):
    return call(
        values_body,
        (L // TM,),
        [rows(D), whole(U_SHAPE), whole(U_SHAPE)],
        [rows(D), Z_ROWS, out_whole((8, D))],
        [sds((L, D), BF16), sds((Z, L, GW), BF16), sds((8, D), F32)],
        flops=2 * L * D * Z * GW,
        nbytes=6 << 20,
    )(tab, x, *w)


def run_mixer(tab, i, x, gain, dq, dk, vals, unit, first=None, w=None):
    last = first is not None
    shape = B_SHAPE if last else U_SHAPE
    in_specs = [
        rows(D), whole((8, D)), rows(1), whole((1, L)), half(i), whole(shape), whole(shape),
    ]
    args = [tab, x, gain, dq, dk, vals, *unit]
    out_specs, outs = [H_ROWS], [sds(H_SHAPE, BF16)]
    if last:
        in_specs += [H_ROWS, whole(U_SHAPE), whole(U_SHAPE)]
        args += [first, *w]
        out_specs += [rows(D), rows(D)]
        outs += [sds((L, D), F32), sds((L, D), BF16)]
    return call(
        functools.partial(mixer_body, last),
        (L // TM,),
        in_specs,
        out_specs,
        outs,
        flops=H * L * WIN * KB * GW,
        nbytes=9 << 20,
    )(*args)


def run_ffn(tab, order, n, cot, unit, acc=None, mid=None):
    first, last = acc is None, mid is not None
    blk = pl.BlockSpec((G, 1, 2 * DB, LN), lambda i, t: (0, i, 0, 0))
    in_specs = [whole((L, D)), whole((L, D)), blk, blk]
    args = [tab, n, cot, *unit]
    if not first:
        in_specs += [whole((L, D)), whole((L, D))]
        args += list(acc)
    if last:
        in_specs += [whole((L, D))]
        args += [mid]
    out_specs = [blk, blk, out_whole((L, D)), out_whole((L, D))]
    outs = [sds(U_SHAPE, BF16), sds(U_SHAPE, BF16), sds((L, D), F32), sds((L, D), F32)]
    if last:
        out_specs += [out_whole((L, D))]
        outs += [sds((L, D), BF16)]
    return call(
        functools.partial(ffn_body, first, last, order), (Z,), in_specs, out_specs, outs,
        flops=4 * L * D * FF, nbytes=14 << 20,
    )(*args)


def run_branch(tab, dn, mid, cot, gain, mixed_a, mixed_b, w):
    return call(
        branch_body,
        (L // TM,),
        [
            rows(D), rows(D), rows(D), whole((8, D)), H_ROWS, H_ROWS,
            whole(U_SHAPE), whole(U_SHAPE),
        ],
        [rows(D), Z_ROWS, out_whole(V_SHAPE), out_whole(V_SHAPE)],
        [sds((L, D), F32), sds((Z, L, GW), BF16), sds(V_SHAPE, BF16), sds(V_SHAPE, BF16)],
        scratch=(pltpu.VMEM((8, D), F32), pltpu.VMEM((Z, D, GW), F32)),
        flops=4 * L * D * Z * GW,
        nbytes=12 << 20,
    )(tab, dn, mid, cot, gain, mixed_a, mixed_b, *w)


def run_mixer_back(tab, banded, grad, dq, dk, vals, unit):
    i = int(banded)
    shape = B_SHAPE if banded else U_SHAPE
    if banded:
        blk = pl.BlockSpec((1, WIN, HR, KB), lambda j, t: (tab_z(t, j), 0, 0, 0))
    else:
        blk = pl.BlockSpec((G, 1, HR, KB), lambda j, t: (0, tab_z(t, j), 0, 0))
    return call(
        functools.partial(mixer_back_body, banded),
        (L // TM,),
        [half_rows(i), rows(1), whole((1, L)), half(i), whole(shape), whole(shape)],
        [blk, blk, out_whole(H_SHAPE)],
        [sds(shape, BF16), sds(shape, BF16), sds(H_SHAPE, BF16)],
        scratch=(pltpu.VMEM(H_SHAPE, F32),),
        flops=3 * H * L * WIN * KB * GW,
        nbytes=10 << 20,
    )(tab, grad, dq, dk, vals, *unit)


def run_last(tab, x, gain, low, vga, vgb, w, mid_grad):
    return call(
        last_body,
        (L // TM,),
        [rows(D), whole((8, D)), rows(D), H_ROWS, H_ROWS, whole(U_SHAPE), whole(U_SHAPE), rows(D)],
        [rows(D), out_whole(V_SHAPE), out_whole(V_SHAPE)],
        [sds((L, D), F32), sds(V_SHAPE, BF16), sds(V_SHAPE, BF16)],
        scratch=(pltpu.VMEM((8, D), F32), pltpu.VMEM((Z, D, GW), F32)),
        flops=4 * L * D * Z * GW,
        nbytes=12 << 20,
    )(tab, x, gain, low, vga, vgb, *w, mid_grad)


def add_up(terms):
    total = terms[0].astype(F32)
    for term in terms[1:]:
        total = total + term.astype(F32)
    return total


def after(val, *deps):
    return lax.optimization_barrier((val, deps))[0]


class Grid:
    def __init__(self, gx, gy):
        self.gy = gy
        self.size = {"y": gx // 2, "x": 2, "z": gy // 2, "c": 2}
        i, j = lax.axis_index("gx"), lax.axis_index("gy")
        self.at = {"y": i // 2, "x": i % 2, "z": j // 2, "c": j % 2}

    def fetch(self, val, axis, k):
        sizes = self.size
        pairs = []
        for y in range(sizes["y"]):
            for x in range(sizes["x"]):
                for z in range(sizes["z"]):
                    for c in range(sizes["c"]):
                        src = {"y": y, "x": x, "z": z, "c": c}
                        dst = dict(src)
                        dst[axis] = (src[axis] + k) % sizes[axis]
                        pairs.append(tuple((p["y"] * 2 + p["x"]) * self.gy + p["z"] * 2 + p["c"] for p in (src, dst)))
        return lax.ppermute(val, ("gx", "gy"), pairs)

    def rel(self, axis, v):
        return (self.at[axis] - v) % self.size[axis]

    def spread(self, val, axis):
        return jnp.stack([val] + [self.fetch(val, axis, k) for k in range(1, self.size[axis])])

    def reduce(self, terms, axis):
        got = [
            self.fetch(add_up([t[k] for t in terms]).astype(BF16), axis, -k)
            for k in range(1, self.size[axis])
        ]
        return [t[0] for t in terms] + got


def lane_pad(mat, gains):
    row = jnp.pad(gains.reshape(1, GN), ((0, DB - 1), (0, LN - CB - GN)))
    return jnp.concatenate([mat, row], axis=1)


def small_shards(layer_in, doc_ids, mix_gain, value_w, mixing, output_w, ffn_gain, up_w, down_w, cot):
    grid = Grid(G, 2 * Z)
    at = grid.at
    fetch, spread = grid.fetch, grid.spread
    order_a = [grid.rel("x", g % 2) * 2 + grid.rel("y", g // 2) for g in range(G)]
    order_b = [grid.rel("y", g // 2) * 2 + grid.rel("x", g % 2) for g in range(G)]
    order_z = [grid.rel("z", z) for z in range(Z)]
    tab = jnp.stack([at["c"]] + order_a + order_b + order_z).astype(jnp.int32)
    docs = lax.dynamic_slice_in_dim(doc_ids, lax.axis_index("gy"), 1, 0)
    dq, dk = docs.reshape(L, 1), docs

    mix = mixing.reshape(2, HR, KB)
    wts = jnp.concatenate([lane_pad(value_w, mix_gain), lane_pad(output_w.T, ffn_gain)], axis=0)
    down_t = down_w.T
    ffn = [
        jnp.concatenate([m[:, i * LN : (i + 1) * LN] for m in (up_w, down_t)], axis=0)
        for i in range(FB // LN)
    ]

    def cross(p, q, *deps):
        p, q = after((p, q), *deps)
        p, q = spread(p, "x"), spread(q, "y")
        return spread(p, "y").reshape(U_SHAPE), spread(q, "x").reshape(U_SHAPE)

    def both(val, *deps):
        return val, fetch(after(val, *deps), "c", 1)

    def tail_to(vals, *deps):
        return list(after(tuple(vals), *deps))

    c1 = spread(jnp.stack([mix[0], wts]), "z")
    b = spread(spread(mix[1], "x"), "y").reshape(G, HR, KB)
    start = window(at["z"])
    order = jnp.stack(order_b)
    b = jnp.stack([lax.dynamic_index_in_dim(b, order[start + i], 0, False) for i in range(WIN)])
    a, w = cross(c1[:, 0], c1[:, 1])
    b = spread(after(b, c1), "z")
    w = both(w)
    a = both(a)
    low, vals, gain = run_values(tab, layer_in, w)
    f1 = spread(after(ffn[0], b), "z")
    b = both(b)
    f1 = spread(after(f1, a[0], w[0]), "y")
    mixed_a = run_mixer(tab, 0, layer_in, gain, dq, dk, vals, a)[0]
    f23 = spread(after(jnp.stack([ffn[1], ffn[2]]), f1, low), "z")
    f1 = spread(f1, "x").reshape(U_SHAPE)
    f2, f3 = cross(f23[:, 0], f23[:, 1], mixed_a)
    mixed_b, mid, n_two = run_mixer(tab, 1, layer_in, gain, dq, dk, vals, b, mixed_a, w)
    f1 = both(f1)
    f2, f3 = both(f2, n_two), both(f3, n_two)

    def split(*pair):
        return [v.reshape((2, 2) + v.shape[1:]) for v in pair]

    k1, s1, *acc = run_ffn(tab, tab_a, n_two, cot, f1)
    r1 = fetch(s1, "c", 1)
    k2, s2, *acc = run_ffn(tab, tab_b, n_two, cot, f2, acc)
    g1 = grid.reduce(tail_to(split(k1, r1), s2), "x")
    r2 = fetch(s2, "c", 1)
    k3, s3, _, n_grad, layer_out = run_ffn(tab, tab_a, after(n_two, r1), cot, f3, acc, mid)
    n_grad = after(n_grad, g1, r2)
    g1 = grid.reduce(tail_to(g1, s3), "y")
    g2 = grid.reduce(tail_to(split(k2, r2), s3), "y")
    r3 = fetch(s3, "c", 1)
    mid_grad, grad, ko, so = run_branch(tab, n_grad, mid, cot, gain, mixed_a, mixed_b, w)
    ro = fetch(so, "c", 1)
    g3 = grid.reduce(tail_to(split(k3, r3), so), "x")
    kb, sb, vgb = run_mixer_back(tab, True, after(grad, g1, r3), dq, dk, vals, b)
    rb = fetch(sb, "c", 1)
    g2 = grid.reduce(tail_to(g2, sb), "x")
    go = grid.reduce(tail_to(split(ko, ro), sb), "x")
    ka, sa, vga = run_mixer_back(tab, False, after(grad, g2[:-1], ro), dq, dk, vals, a)
    ra = fetch(sa, "c", 1)
    gb = grid.reduce(tail_to((kb, rb), sa), "z")
    g3 = grid.reduce(tail_to(g3, sa), "y")
    go = grid.reduce(tail_to(go, sa), "y")
    low = after(low, g3[:-1], rb, g2, go[:-1])
    grad_in, kv, sv = run_last(tab, layer_in, gain, low, vga, vgb, w, mid_grad)
    rv = fetch(sv, "c", 1)
    ga = grid.reduce(split(ka, ra), "y")
    gf = [jnp.stack(v, axis=1) for v in zip(g1, g2, g3)]
    gf = add_up(grid.reduce(tail_to(gf, gb), "z"))
    wide = []
    for v in gb:
        blocks = []
        for k in range(G):
            spot = (at["y"] - k // 2) % 2 * 2 + (at["x"] - k % 2) % 2 - start
            blk = lax.dynamic_index_in_dim(v, jnp.clip(spot, 0, WIN - 1), 0, False)
            ok = jnp.logical_and(spot >= 0, spot < WIN)
            blocks.append(jnp.where(ok, blk, jnp.zeros_like(blk)))
        wide.append(jnp.stack(blocks).reshape(2, 2, HR, KB))
    gv = grid.reduce(split(kv, rv), "x")
    gb = add_up(grid.reduce(grid.reduce(wide, "y"), "x"))
    ga = grid.reduce(ga, "x")
    gv = grid.reduce(gv, "y")
    gm = [jnp.concatenate(v, axis=1) for v in zip(ga, go, gv)]
    gm = add_up(grid.reduce(gm, "z"))

    go, gv = gm[HR : HR + DB], gm[HR + DB :]
    grad_mixing = jnp.concatenate([gm[:HR], gb], axis=0).reshape(H, QB, KB)
    grad_up = jnp.concatenate([gf[i, :DB] for i in range(FB // LN)], axis=1)
    grad_down = jnp.concatenate([gf[i, DB:] for i in range(FB // LN)], axis=1)
    return (
        layer_out, grad_in, gv[0, CB : CB + GN], gv[:, :CB], grad_mixing, go[:, :CB].T,
        go[0, CB : CB + GN], grad_up, grad_down.T,
    )


def compute(tab, x, docs, cot, a, b, w, ffn):
    dq, dk = docs.reshape(L, 1), docs
    low, vals, gain = run_values(tab, x, w)
    mixed_a = run_mixer(tab, 0, x, gain, dq, dk, vals, a)[0]
    mixed_b, mid, n_two = run_mixer(tab, 1, x, gain, dq, dk, vals, b, mixed_a, w)
    k1, s1, *acc = run_ffn(tab, tab_a, n_two, cot, ffn[0])
    k2, s2, *acc = run_ffn(tab, tab_a, n_two, cot, ffn[1], acc)
    k3, s3, _, n_grad, layer_out = run_ffn(tab, tab_a, n_two, cot, ffn[2], acc, mid)
    mid_grad, grad, *go = run_branch(tab, n_grad, mid, cot, gain, mixed_a, mixed_b, w)
    *gb, vgb = run_mixer_back(tab, True, grad, dq, dk, vals, b)
    *ga, vga = run_mixer_back(tab, False, grad, dq, dk, vals, a)
    grad_in, *gv = run_last(tab, x, gain, low, vga, vgb, w, mid_grad)
    return layer_out, grad_in, ((k1, s1), (k2, s2), (k3, s3)), ga, gb, go, gv


def cols_in(v, o, gains):
    def blocks(mat, gain):
        mat = mat.reshape(G, DB, Z, 2, CB).transpose(3, 0, 2, 1, 4)
        gain = gain.reshape(G, Z, 2, 1, GN).transpose(2, 0, 1, 3, 4)
        gain = jnp.pad(gain, ((0, 0),) * 3 + ((0, DB - 1), (0, LN - CB - GN)))
        return jnp.concatenate([mat, gain], axis=-1)

    return jnp.concatenate([blocks(v, gains[0]), blocks(o, gains[1])], axis=3)


def cols_out(keep, send):
    mat = jnp.stack([keep, send])
    dg = mat[:, :, :, 0, CB : CB + GN].transpose(1, 2, 0, 3).reshape(D)
    return mat[..., :CB].transpose(1, 3, 2, 0, 4).reshape(D, D), dg


def any_shards(layer_in, doc_ids, mix_gain, value_w, mixing, output_w, ffn_gain, up_w, down_w, cot):
    ax = ("gx", "gy")
    seqs = layer_in.shape[0] // L
    me = lax.axis_index("gy") * seqs

    def gather(arr, d0, d1):
        arr = lax.all_gather(arr, "gx", axis=d0, tiled=True)
        return lax.all_gather(arr, "gy", axis=d1, tiled=True)

    def scatter(arr, d0, d1):
        arr = lax.psum_scatter(arr, "gx", scatter_dimension=d0, tiled=True)
        return lax.psum_scatter(arr, "gy", scatter_dimension=d1, tiled=True).astype(F32)

    gains = lax.all_gather(jnp.stack([mix_gain, ffn_gain]), ax, axis=1, tiled=True)
    w = cols_in(gather(value_w, 0, 1), gather(output_w.T, 0, 1), gains)
    mix_full = gather(mixing, 2, 1).reshape(2, HA, Z, 2, QB, G, KB).transpose(0, 3, 5, 2, 1, 4, 6)
    a, b = mix_full.reshape((2, 2) + U_SHAPE)
    starts = [min(max(m - 1, 0), G - WIN) for m in range(Z)]
    b = jnp.stack([b[:, s : s + WIN, m] for m, s in enumerate(starts)], axis=1)
    ffn = jnp.stack([gather(up_w, 0, 1), gather(down_w.T, 0, 1)])
    ffn = ffn.reshape(2, G, DB, Z, 2, FB // LN, LN).transpose(5, 4, 1, 3, 0, 2, 6)
    ffn = ffn.reshape((FB // LN, 2) + U_SHAPE)
    tab = jnp.array([0] + [0, 1, 2, 3] * 3, jnp.int32)

    rows_out, grads = [], None
    for s in range(seqs):
        docs = lax.dynamic_slice_in_dim(doc_ids, me + s, 1, 0)
        part = slice(s * L, (s + 1) * L)
        out, g_in, *rest = compute(tab, layer_in[part], docs, cot[part], a, b, w, ffn)
        rows_out.append((out, g_in))
        rest = jax.tree.map(lambda v: v.astype(F32), rest) if seqs > 1 else rest
        grads = rest if grads is None else jax.tree.map(jnp.add, grads, rest)
    layer_out = jnp.concatenate([r[0] for r in rows_out], axis=0)
    grad_in = jnp.concatenate([r[1] for r in rows_out], axis=0)
    gf, ga, gb, go, gv = jax.tree.map(lambda v: v.astype(BF16), grads)
    value_full, dg_one = cols_out(*gv)
    output_full, dg_two = cols_out(*go)
    gb = jnp.stack(gb)
    gb = jnp.stack(
        [
            jnp.pad(gb[:, m], ((0, 0), (s, G - WIN - s), (0, 0), (0, 0)))
            for m, s in enumerate(starts)
        ],
        axis=2,
    )
    gm = jnp.stack([jnp.stack(ga), gb]).reshape(2, 2, G, Z, HA, QB, KB)
    gm = gm.transpose(0, 4, 3, 1, 5, 2, 6)
    gf = jnp.stack([jnp.stack(pair) for pair in gf]).reshape(FB // LN, 2, G, Z, 2, DB, LN)
    grad_up, grad_down = gf.transpose(4, 2, 5, 3, 1, 0, 6).reshape(2, D, FF)
    dgs = jnp.stack([dg_one, dg_two]).astype(F32)
    dgs = lax.psum_scatter(dgs, ax, scatter_dimension=1, tiled=True)
    return (
        layer_out, grad_in, dgs[0], scatter(value_full, 0, 1), scatter(gm.reshape(H, L, L), 2, 1),
        scatter(output_full, 0, 1).T, dgs[1], scatter(grad_up, 0, 1), scatter(grad_down, 0, 1).T,
    )


def solution(mesh):
    tok = P(("gx", "gy"), None)
    vec = P(("gx", "gy"))
    wgt = P("gx", "gy")
    twg = P("gy", "gx")
    mix = P(None, "gy", "gx")
    in_specs = (tok, P("gx", None), vec, wgt, mix, twg, vec, wgt, twg, tok)
    out_specs = (tok, tok, vec, wgt, mix, twg, vec, wgt, twg)

    def run(*args):
        small = (mesh.shape["gx"], mesh.shape["gy"], args[0].shape[0]) == (G, 2 * Z, L)
        return (small_shards if small else any_shards)(*args)

    return jax.shard_map(run, mesh=mesh, in_specs=in_specs, out_specs=out_specs, check_vma=False)
```

time: 377 us -> 405 us (1.074)
  starting transfers between devices: 54.2 us -> 76 us
  Pallas kernels: 81.8 us -> 94.5 us
  other arithmetic: 34.6 us -> 27.3 us
  local copies, waits for them, and re-layouts: 15.1 us -> 19.4 us
    ppermute x52 -> x60, starting transfers between devices: 54.2 us -> 76 us  [fetch(): return lax.ppermute(val, ('gx', 'gy'), pairs)]
    pallas_call x6 -> x10, Pallas kernels: 81.8 us -> 94.5 us  [the longest x3 39.4 us: run_ffn(): call(functools.partial(ffn_body, first, last, order), (Z,), in_specs, out...]
    another operation x16 -> x17, other arithmetic: 17.7 us -> 9.66 us  [spread(): jnp.stack([val] + [self.fetch(val, axis, k) for k in range(1, self.size[a...]
    unnamed x40 -> x84, local copies, waits for them, and re-layouts: 4.82 us -> 8.26 us
    convert_element_type x13 -> x15, other arithmetic: 11.7 us -> 8.89 us  [reduce(): add_up([t[k] for t in terms]).astype(BF16)]
    ppermute x52 -> x60, waiting for transfers between devices: 180 us -> 179 us  [fetch(): return lax.ppermute(val, ('gx', 'gy'), pairs)]
  transfers between devices with their start and end apart: 52 -> 60, of which waited for: 23 -> 26; matrix products, arithmetic and copies ran while one was open for 12% -> 9% of each run, Pallas kernels for 9% -> 23%
where the time goes in v3:
time: 405 us; the launch traced here: 404 us
  waiting for transfers between devices  179 us (44%)
  Pallas kernels  94.5 us (23%)
  starting transfers between devices  76 us (19%)
  other arithmetic  27.3 us (7%)
  local copies, waits for them, and re-layouts  19.4 us (5%)
  between operations  7.64 us (2%)
    ppermute x60, waiting for transfers between devices, fetch(): return lax.ppermute(val, ('gx', 'gy'), pairs)  179 us
    ppermute x60, starting transfers between devices, fetch(): return lax.ppermute(val, ('gx', 'gy'), pairs)  76 us
    pallas_call x3, Pallas kernels, run_ffn(): call(functools.partial(ffn_body, first, last, order), (Z,), in_specs, out...  39.4 us
    pallas_call x2, Pallas kernels, run_mixer_back(): call(functools.partial(mixer_back_body, banded), (L // TM,), [half_rows(i...  16.6 us
    pallas_call x2, Pallas kernels, run_mixer(): call(functools.partial(mixer_body, last), (L // TM,), in_specs, out_specs...  14.2 us
    another operation x17, other arithmetic, spread(): jnp.stack([val] + [self.fetch(val, axis, k) for k in range(1, self.size[a...  9.66 us
    pallas_call x1, Pallas kernels, run_branch(): call(branch_body, (L // TM,), [rows(D), rows(D), rows(D), whole((8, D)),...  9.34 us
    pallas_call x1, Pallas kernels, run_last(): call(last_body, (L // TM,), [rows(D), whole((8, D)), rows(D), H_ROWS, H_R...  9.2 us
  transfers between devices with their start and end apart: 60, of which 26 were waited for; matrix products, arithmetic and copies ran while one was open for 9% of the time, Pallas kernels for 23%

profile of v3, /device:TPU:0, one launch (start us, length us, event | category | flops | bytes accessed | tf_op | source)
XLA Modules:
  0.0 404.1 jit_solution(2094358785192935487)
XLA Ops:
  16.7 5.3 %collective-permute-done.1 = bf16[2,384,128]{2,1,0:T(8,128)(2,1)S(1)} collective-permute-done((bf16[2,384,128]{2,1,0:T(8,128)(2,1)S(1)}, bf16[2,384,128]{2,1,0:T(8,128)(2,1)S(1)}, u32[]{:S(2)}, u32[]{:S(2)}) %collective-permute-start.1) | collective-permute-done | bytes 196640 | tf_op jit(solution)/shard_map/ppermute | solution.py:558
  31.9 4.7 %collective-permute-start.8 = (bf16[3,384,128]{2,1,0:T(8,128)(2,1)S(1)}, bf16[3,384,128]{2,1,0:T(8,128)(2,1)S(1)}, u32[]{:S(2)}, u32[]{:S(2)}) collective-permute-start(bf16[3,384,128]{2,1,0:T(8,128)(2,1)S(1)} %pad_maximum_fusion.23), channel_id=1, source_target_pairs={{0,2},{1,3},{2,4},{3,5},{4,6},{5,7},{6,0},{7,1},{8,10},{9,11},{10,... | collective-permute-start | bytes 884744 | tf_op jit(solution)/shard_map/ppermute | solution.py:558
  42.5 3.3 collective-permute-done.8
  45.8 10.3 %collective-permute-done.9 = bf16[3,384,128]{2,1,0:T(8,128)(2,1)S(1)} collective-permute-done((bf16[3,384,128]{2,1,0:T(8,128)(2,1)S(1)}, bf16[3,384,128]{2,1,0:T(8,128)(2,1)S(1)}, u32[]{:S(2)}, u32[]{:S(2)}) %collective-permute-start.9) | collective-permute-done | bytes 294944 | tf_op jit(solution)/shard_map/ppermute | solution.py:558
  57.3 6.8 %collective-permute-start.15 = (bf16[384,128]{1,0:T(8,128)(2,1)S(1)}, bf16[384,128]{1,0:T(8,128)(2,1)S(1)}, u32[]{:S(2)}, u32[]{:S(2)}) collective-permute-start(bf16[384,128]{1,0:T(8,128)(2,1)S(1)} %pad_maximum_fusion.28), channel_id=1, source_target_pairs={{0,2},{1,3},{2,4},{3,5},{4,6},{5,7},{6,0},{7,1},{8,10},{9,11},{10,... | collective-permute-start | bytes 294920 | tf_op jit(solution)/shard_map/ppermute | solution.py:558
  74.9 10.7 %collective-permute-done.18 = bf16[4,384,128]{2,1,0:T(8,128)(2,1)S(1)} collective-permute-done((bf16[4,384,128]{2,1,0:T(8,128)(2,1)S(1)}, bf16[4,384,128]{2,1,0:T(8,128)(2,1)S(1)}, u32[]{:S(2)}, u32[]{:S(2)}) %collective-permute-start.18) | collective-permute-done | bytes 393248 | tf_op jit(solution)/shard_map/ppermute | solution.py:558
  88.1 16.6 %collective-permute-done.19 = bf16[2,4,384,128]{3,2,1,0:T(8,128)(2,1)} collective-permute-done((bf16[2,4,384,128]{3,2,1,0:T(8,128)(2,1)S(1)}, bf16[2,4,384,128]{3,2,1,0:T(8,128)(2,1)}, u32[]{:S(2)}, u32[]{:S(2)}) %collective-permute-start.19) | collective-permute-done | bytes 786464 | tf_op jit(solution)/shard_map/ppermute | solution.py:558
  107.3 5.7 %shard_map.169 = (bf16[512,768]{1,0:T(8,128)(2,1)S(1)}, bf16[4,512,256]{2,1,0:T(8,128)(2,1)}, f32[8,768]{1,0:T(8,128)S(1)}) custom-call(s32[13]{0:T(128)S(1)} %stack.304.t, bf16[512,768]{1,0:T(8,128)(2,1)S(1)} %copy-done.5, bf16[4,4,384,128]{3,2,1,0:T(8,128)(2,1)} %bitcast.292, bf16[4,4,384,128]{3,2,1,0:T(8,128)(2,1)} %collective-permute-done.5.oth_ref.refs_2_.w_oth), custom_call_target="tpu_custom_call" | custom-call | flops 68719476736 | bytes 6291456 | tf_op jit(solution)/shard_map/pallas_call | solution.py:424
  118.0 4.9 %shard_map.170.refs_0_.mixa_ref = bf16[2,512,256]{2,1,0:T(8,128)(2,1)S(1)} custom-call(s32[13]{0:T(128)S(1)} %stack.304.t, bf16[512,768]{1,0:T(8,128)(2,1)S(1)} %copy-done.5, f32[8,768]{1,0:T(8,128)S(1)} %get-tuple-element.82.gain_ref, s32[512,1]{1,0:T(8,128)S(1)} %copy.37.dq_ref, s32[1,512]{1,0:T(1,128)S(1)} %constant_dynamic-slice_fusion.3.dk_ref, ...), custom_call_target="tpu_custom_call" | custom-call | flops 68719476736 | bytes 9437184 | tf_op jit(solution)/shard_map/pallas_call | solution.py:448
  122.9 7.8 %collective-permute-done.23 = bf16[2,384,128]{2,1,0:T(8,128)(2,1)S(1)} collective-permute-done((bf16[2,384,128]{2,1,0:T(8,128)(2,1)S(1)}, bf16[2,384,128]{2,1,0:T(8,128)(2,1)S(1)}, u32[]{:S(2)}, u32[]{:S(2)}) %collective-permute-start.23) | collective-permute-done | bytes 196640 | tf_op jit(solution)/shard_map/ppermute | solution.py:558
  132.4 9.3 %shard_map.171 = (bf16[2,512,256]{2,1,0:T(8,128)(2,1)S(1)}, f32[512,768]{1,0:T(8,128)}, bf16[512,768]{1,0:T(8,128)(2,1)}) custom-call(s32[13]{0:T(128)S(1)} %stack.304.t, bf16[512,768]{1,0:T(8,128)(2,1)} %x_ref.7, f32[8,768]{1,0:T(8,128)S(1)} %get-tuple-element.82.gain_ref, s32[512,1]{1,0:T(8,128)S(1)} %copy.37.dq_ref, ...), custom_call_target="tpu_custom_call" | custom-call | flops 68719476736 | bytes 9437184 | tf_op jit(solution)/shard_map/pallas_call | solution.py:448
  143.1 12.0 %shard_map.172 = (bf16[4,4,384,128]{3,2,1,0:T(8,128)(2,1)}, bf16[4,4,384,128]{3,2,1,0:T(8,128)(2,1)}, f32[512,768]{1,0:T(8,128)}, f32[512,768]{1,0:T(8,128)}) custom-call(s32[13]{0:T(128)S(1)} %stack.304.t, bf16[512,768]{1,0:T(8,128)(2,1)S(1)} %copy-done.7, bf16[512,768]{1,0:T(8,128)(2,1)S(1)} %copy-done.4, bf16[4,4,384,128]{3,2,1,0:T(8,128)(2,1)} %bitcast.57.own, ...), custom_call_target="tpu_custom_call" | custom-call | flops 68719476736 | bytes 14680064 | tf_op jit(solution)/shard_map/pallas_call | solution.py:475
  155.2 5.9 %collective-permute-done.29 = bf16[2,4,384,128]{3,2,1,0:T(8,128)(2,1)S(1)} collective-permute-done((bf16[2,4,384,128]{3,2,1,0:T(8,128)(2,1)S(1)}, bf16[2,4,384,128]{3,2,1,0:T(8,128)(2,1)S(1)}, u32[]{:S(2)}, u32[]{:S(2)}) %collective-permute-start.29) | collective-permute-done | bytes 786464 | tf_op jit(solution)/shard_map/ppermute | solution.py:558
  163.0 11.0 %collective-permute-done.25 = bf16[4,384,128]{2,1,0:T(8,128)(2,1)S(1)} collective-permute-done((bf16[4,384,128]{2,1,0:T(8,128)(2,1)S(1)}, bf16[4,384,128]{2,1,0:T(8,128)(2,1)S(1)}, u32[]{:S(2)}, u32[]{:S(2)}) %collective-permute-start.25) | collective-permute-done | bytes 393248 | tf_op jit(solution)/shard_map/ppermute | solution.py:558
  176.4 18.0 %collective-permute-done.26 = bf16[2,4,384,128]{3,2,1,0:T(8,128)(2,1)} collective-permute-done((bf16[2,4,384,128]{3,2,1,0:T(8,128)(2,1)}, bf16[2,4,384,128]{3,2,1,0:T(8,128)(2,1)}, u32[]{:S(2)}, u32[]{:S(2)}) %collective-permute-start.26) | collective-permute-done | bytes 786464 | tf_op jit(solution)/shard_map/ppermute | solution.py:558
  195.8 13.5 %shard_map.173 = (bf16[4,4,384,128]{3,2,1,0:T(8,128)(2,1)}, bf16[4,4,384,128]{3,2,1,0:T(8,128)(2,1)}, f32[512,768]{1,0:T(8,128)}, f32[512,768]{1,0:T(8,128)}) custom-call(s32[13]{0:T(128)S(1)} %stack.304.t, bf16[512,768]{1,0:T(8,128)(2,1)S(1)} %copy-done.7, bf16[512,768]{1,0:T(8,128)(2,1)S(1)} %copy-done.4, bf16[4,4,384,128]{3,2,1,0:T(8,128)(2,1)} %bitcast.75.own, ...), custom_call_target="tpu_custom_call" | custom-call | flops 68719476736 | bytes 14680064 | tf_op jit(solution)/shard_map/pallas_call | solution.py:475
  213.5 14.0 %shard_map.174 = (bf16[4,4,384,128]{3,2,1,0:T(8,128)(2,1)}, bf16[4,4,384,128]{3,2,1,0:T(8,128)(2,1)}, f32[512,768]{1,0:T(8,128)}, f32[512,768]{1,0:T(8,128)}, bf16[512,768]{1,0:T(8,128)(2,1)}) custom-call(s32[13]{0:T(128)S(1)} %stack.304.t, bf16[512,768]{1,0:T(8,128)(2,1)S(1)} %copy-done.7, bf16[512,768]{1,0:T(8,128)(2,1)S(1)} %copy-done.4, ...), custom_call_target="tpu_custom_call" | custom-call | flops 68719476736 | bytes 14680064 | tf_op jit(solution)/shard_map/pallas_call | solution.py:475
  233.8 9.3 %shard_map.175 = (f32[512,768]{1,0:T(8,128)}, bf16[4,512,256]{2,1,0:T(8,128)(2,1)}, bf16[4,4,192,128]{3,2,1,0:T(8,128)(2,1)S(1)}, bf16[4,4,192,128]{3,2,1,0:T(8,128)(2,1)}) custom-call(s32[13]{0:T(128)S(1)} %stack.304.t, f32[512,768]{1,0:T(8,128)} %get-tuple-element.108.dn_ref, f32[512,768]{1,0:T(8,128)} %get-tuple-element.101.refs_2_.mid_ref, ...), custom_call_target="tpu_custom_call" | custom-call | flops 68719476736 | bytes 12582912 | tf_op jit(solution)/shard_map/pallas_call | solution.py:482
  250.1 8.1 %shard_map.176 = (bf16[4,3,384,128]{3,2,1,0:T(8,128)(2,1)}, bf16[4,3,384,128]{3,2,1,0:T(8,128)(2,1)}, bf16[2,512,256]{2,1,0:T(8,128)(2,1)S(1)}) custom-call(s32[13]{0:T(128)S(1)} %stack.304.t, bf16[4,512,256]{2,1,0:T(8,128)(2,1)S(1)} %copy-done.6, s32[512,1]{1,0:T(8,128)S(1)} %copy.37.dq_ref, s32[1,512]{1,0:T(1,128)S(1)} %copy-done.3, ...), custom_call_target="tpu_custom_call" | custom-call | flops 68719476736 | bytes 10485760 | tf_op jit(solution)/shard_map/pallas_call | solution.py:504
  258.2 10.1 %collective-permute-done.36 = bf16[2,4,384,128]{3,2,1,0:T(8,128)(2,1)S(1)} collective-permute-done((bf16[2,4,384,128]{3,2,1,0:T(8,128)(2,1)}, bf16[2,4,384,128]{3,2,1,0:T(8,128)(2,1)S(1)}, u32[]{:S(2)}, u32[]{:S(2)}) %collective-permute-start.36) | collective-permute-done | bytes 786464 | tf_op jit(solution)/shard_map/ppermute | solution.py:558
  269.3 8.5 %shard_map.177 = (bf16[4,4,384,128]{3,2,1,0:T(8,128)(2,1)}, bf16[4,4,384,128]{3,2,1,0:T(8,128)(2,1)}, bf16[2,512,256]{2,1,0:T(8,128)(2,1)S(1)}) custom-call(s32[13]{0:T(128)S(1)} %stack.304.t, bf16[4,512,256]{2,1,0:T(8,128)(2,1)S(1)} %copy-done.6, s32[512,1]{1,0:T(8,128)S(1)} %copy.37.dq_ref, s32[1,512]{1,0:T(1,128)S(1)} %copy-done.3, ...), custom_call_target="tpu_custom_call" | custom-call | flops 68719476736 | bytes 10485760 | tf_op jit(solution)/shard_map/pallas_call | solution.py:504
  289.9 5.3 %collective-permute-start.50 = (bf16[3,384,128]{2,1,0:T(8,128)(2,1)}, bf16[3,384,128]{2,1,0:T(8,128)(2,1)S(1)}, u32[]{:S(2)}, u32[]{:S(2)}) collective-permute-start(bf16[3,384,128]{2,1,0:T(8,128)(2,1)} %get-tuple-element.179), channel_id=1, source_target_pairs={{0,6},{1,7},{2,0},{3,1},{4,2},{5,3},{6,4},{7,5},{8,14},{9,15},{10,... | collective-permute-start | bytes 884744 | tf_op jit(solution)/shard_map/ppermute | solution.py:558
  296.6 5.7 %collective-permute-done.39 = bf16[2,4,192,128]{3,2,1,0:T(8,128)(2,1)S(1)} collective-permute-done((bf16[2,4,192,128]{3,2,1,0:T(8,128)(2,1)S(1)}, bf16[2,4,192,128]{3,2,1,0:T(8,128)(2,1)S(1)}, u32[]{:S(2)}, u32[]{:S(2)}) %collective-permute-start.39) | collective-permute-done | bytes 393248 | tf_op jit(solution)/shard_map/ppermute | solution.py:558
  302.2 3.8 collective-permute-start.51
  308.2 9.2 %shard_map.178 = (f32[512,768]{1,0:T(8,128)}, bf16[4,4,192,128]{3,2,1,0:T(8,128)(2,1)S(1)}, bf16[4,4,192,128]{3,2,1,0:T(8,128)(2,1)}) custom-call(s32[13]{0:T(128)S(1)} %stack.304.t, bf16[512,768]{1,0:T(8,128)(2,1)} %x_ref.7, f32[8,768]{1,0:T(8,128)S(1)} %copy-done.13, bf16[512,768]{1,0:T(8,128)(2,1)} %copy-done.8, ...), custom_call_target="tpu_custom_call" | custom-call | flops 68719476736 | bytes 12582912 | tf_op jit(solution)/shard_map/pallas_call | solution.py:517
  318.9 6.5 %collective-permute-done.51 = bf16[3,384,128]{2,1,0:T(8,128)(2,1)S(1)} collective-permute-done((bf16[3,384,128]{2,1,0:T(8,128)(2,1)}, bf16[3,384,128]{2,1,0:T(8,128)(2,1)S(1)}, u32[]{:S(2)}, u32[]{:S(2)}) %collective-permute-start.51) | collective-permute-done | bytes 294944 | tf_op jit(solution)/shard_map/ppermute | solution.py:558
  336.1 19.2 %collective-permute-done.58 = bf16[3,384,128]{2,1,0:T(8,128)(2,1)S(1)} collective-permute-done((bf16[3,384,128]{2,1,0:T(8,128)(2,1)S(1)}, bf16[3,384,128]{2,1,0:T(8,128)(2,1)S(1)}, u32[]{:S(2)}, u32[]{:S(2)}) %collective-permute-start.58) | collective-permute-done | bytes 294944 | tf_op jit(solution)/shard_map/ppermute | solution.py:558
  361.3 7.1 %collective-permute-done.43 = bf16[2,4,192,128]{3,2,1,0:T(8,128)(2,1)S(1)} collective-permute-done((bf16[2,4,192,128]{3,2,1,0:T(8,128)(2,1)S(1)}, bf16[2,4,192,128]{3,2,1,0:T(8,128)(2,1)S(1)}, u32[]{:S(2)}, u32[]{:S(2)}) %collective-permute-start.43) | collective-permute-done | bytes 393248 | tf_op jit(solution)/shard_map/ppermute | solution.py:558
  370.1 9.7 %collective-permute-done.42 = bf16[2,4,384,128]{3,2,1,0:T(8,128)(2,1)S(1)} collective-permute-done((bf16[2,4,384,128]{3,2,1,0:T(8,128)(2,1)S(1)}, bf16[2,4,384,128]{3,2,1,0:T(8,128)(2,1)S(1)}, u32[]{:S(2)}, u32[]{:S(2)}) %collective-permute-start.42) | collective-permute-done | bytes 786464 | tf_op jit(solution)/shard_map/ppermute | solution.py:558
  380.7 7.1 %collective-permute-done.44 = bf16[4,384,128]{2,1,0:T(8,128)(2,1)S(1)} collective-permute-done((bf16[4,384,128]{2,1,0:T(8,128)(2,1)S(1)}, bf16[4,384,128]{2,1,0:T(8,128)(2,1)S(1)}, u32[]{:S(2)}, u32[]{:S(2)}) %collective-permute-start.44) | collective-permute-done | bytes 393248 | tf_op jit(solution)/shard_map/ppermute | solution.py:558
  390.5 4.5 %collective-permute-done.47 = bf16[768,128]{1,0:T(8,128)(2,1)S(1)} collective-permute-done((bf16[768,128]{1,0:T(8,128)(2,1)S(1)}, bf16[768,128]{1,0:T(8,128)(2,1)S(1)}, u32[]{:S(2)}, u32[]{:S(2)}) %collective-permute-start.47) | collective-permute-done | bytes 196640 | tf_op jit(solution)/shard_map/ppermute | solution.py:558
  395.0 6.1 %collective-permute-done.48 = bf16[768,128]{1,0:T(8,128)(2,1)S(1)} collective-permute-done((bf16[768,128]{1,0:T(8,128)(2,1)S(1)}, bf16[768,128]{1,0:T(8,128)(2,1)S(1)}, u32[]{:S(2)}, u32[]{:S(2)}) %collective-permute-start.48) | collective-permute-done | bytes 196640 | tf_op jit(solution)/shard_map/ppermute | solution.py:558
  (284 shorter events, 116.5 us)
Async XLA Ops:
  36.7 19.4 %collective-permute-start.9 = (bf16[3,384,128]{2,1,0:T(8,128)(2,1)S(1)}, bf16[3,384,128]{2,1,0:T(8,128)(2,1)S(1)}, u32[]{:S(2)}, u32[]{:S(2)}) collective-permute-start(bf16[3,384,128]{2,1,0:T(8,128)(2,1)S(1)} %pad_maximum_fusion.23), channel_id=1, source_target_pairs={{0,4},{1,5},{2,6},{3,7},{4,0},{5,1},{6,2},{7,3},{8,12},{9,13},{10,... | collective-permute-start | bytes 884744 | tf_op jit(solution)/shard_map/ppermute | solution.py:558
  39.2 33.4 %collective-permute-start.4 = (bf16[2,4,384,128]{3,2,1,0:T(8,128)(2,1)S(1)}, bf16[2,4,384,128]{3,2,1,0:T(8,128)(2,1)S(1)}, u32[]{:S(2)}, u32[]{:S(2)}) collective-permute-start(bf16[2,4,384,128]{3,2,1,0:T(8,128)(2,1)S(1)} %get-tuple-element.197), channel_id=1, source_target_pairs={{0,8},{1,9},{2,10},{3,11},{4,12},{5,13},{6,14},{7,15},{8,0},{9,1},... | collective-permute-start | bytes 2359304 | tf_op jit(solution)/shard_map/ppermute | solution.py:558
  41.2 31.6 %collective-permute-start.13 = (bf16[2,4,384,128]{3,2,1,0:T(8,128)(2,1)S(1)}, bf16[2,4,384,128]{3,2,1,0:T(8,128)(2,1)S(1)}, u32[]{:S(2)}, u32[]{:S(2)}) collective-permute-start(bf16[2,4,384,128]{3,2,1,0:T(8,128)(2,1)S(1)} %get-tuple-element.195), channel_id=1, source_target_pairs={{0,16},{1,17},{2,18},{3,19},{4,20},{5,21},{6,22},{7,23},{8,24},{9,... | collective-permute-start | bytes 2359304 | tf_op jit(solution)/shard_map/ppermute | solution.py:558
  72.8 34.5 %collective-permute-start.5 = (bf16[4,4,384,128]{3,2,1,0:T(8,128)(2,1)S(1)}, bf16[4,4,384,128]{3,2,1,0:T(8,128)(2,1)}, u32[]{:S(2)}, u32[]{:S(2)}) collective-permute-start(bf16[4,4,384,128]{3,2,1,0:T(8,128)(2,1)S(1)} %bitcast.291), channel_id=1, source_target_pairs={{0,1},{1,0},{2,3},{3,2},{4,5},{5,4},{6,7},{7,6},{8,9},{9,8},{10,11... | collective-permute-start | bytes 4718600 | tf_op jit(solution)/shard_map/ppermute | solution.py:558
  85.7 19.0 %collective-permute-start.19 = (bf16[2,4,384,128]{3,2,1,0:T(8,128)(2,1)S(1)}, bf16[2,4,384,128]{3,2,1,0:T(8,128)(2,1)}, u32[]{:S(2)}, u32[]{:S(2)}) collective-permute-start(bf16[2,4,384,128]{3,2,1,0:T(8,128)(2,1)S(1)} %get-tuple-element.193), channel_id=1, source_target_pairs={{0,8},{1,9},{2,10},{3,11},{4,12},{5,13},{6,14},{7,15},{8,0},{9,1},... | collective-permute-start | bytes 2359304 | tf_op jit(solution)/shard_map/ppermute | solution.py:558
  87.5 43.9 %collective-permute-start.11 = (bf16[4,3,384,128]{3,2,1,0:T(8,128)(2,1)}, bf16[4,3,384,128]{3,2,1,0:T(8,128)(2,1)S(1)}, u32[]{:S(2)}, u32[]{:S(2)}) collective-permute-start(bf16[4,3,384,128]{3,2,1,0:T(8,128)(2,1)} %pad_maximum_fusion.5.own), channel_id=1, source_target_pairs={{0,1},{1,0},{2,3},{3,2},{4,5},{5,4},{6,7},{7,6},{8,9},{9,8},{10,11... | collective-permute-start | bytes 3538952 | tf_op jit(solution)/shard_map/ppermute | solution.py:558
  87.6 29.1 %collective-permute-start.14 = (bf16[4,4,384,128]{3,2,1,0:T(8,128)(2,1)}, bf16[4,4,384,128]{3,2,1,0:T(8,128)(2,1)S(1)}, u32[]{:S(2)}, u32[]{:S(2)}) collective-permute-start(bf16[4,4,384,128]{3,2,1,0:T(8,128)(2,1)} %bitcast.296), channel_id=1, source_target_pairs={{0,1},{1,0},{2,3},{3,2},{4,5},{5,4},{6,7},{7,6},{8,9},{9,8},{10,11... | collective-permute-start | bytes 4718600 | tf_op jit(solution)/shard_map/ppermute | solution.py:558
  107.3 35.3 %collective-permute-start.20 = (bf16[4,4,384,128]{3,2,1,0:T(8,128)(2,1)}, bf16[4,4,384,128]{3,2,1,0:T(8,128)(2,1)}, u32[]{:S(2)}, u32[]{:S(2)}) collective-permute-start(bf16[4,4,384,128]{3,2,1,0:T(8,128)(2,1)} %bitcast.57.own), channel_id=1, source_target_pairs={{0,1},{1,0},{2,3},{3,2},{4,5},{5,4},{6,7},{7,6},{8,9},{9,8},{10,11... | collective-permute-start | bytes 4718600 | tf_op jit(solution)/shard_map/ppermute | solution.py:558
  142.0 19.1 %collective-permute-start.29 = (bf16[2,4,384,128]{3,2,1,0:T(8,128)(2,1)S(1)}, bf16[2,4,384,128]{3,2,1,0:T(8,128)(2,1)S(1)}, u32[]{:S(2)}, u32[]{:S(2)}) collective-permute-start(bf16[2,4,384,128]{3,2,1,0:T(8,128)(2,1)S(1)} %get-tuple-element.187), channel_id=1, source_target_pairs={{0,16},{1,17},{2,18},{3,19},{4,20},{5,21},{6,22},{7,23},{8,24},{9,... | collective-permute-start | bytes 2359304 | tf_op jit(solution)/shard_map/ppermute | solution.py:558
  155.1 40.6 %collective-permute-start.21 = (bf16[4,4,384,128]{3,2,1,0:T(8,128)(2,1)}, bf16[4,4,384,128]{3,2,1,0:T(8,128)(2,1)}, u32[]{:S(2)}, u32[]{:S(2)}) collective-permute-start(bf16[4,4,384,128]{3,2,1,0:T(8,128)(2,1)} %get-tuple-element.89), channel_id=1, source_target_pairs={{0,1},{1,0},{2,3},{3,2},{4,5},{5,4},{6,7},{7,6},{8,9},{9,8},{10,11... | collective-permute-start | bytes 4718600 | tf_op jit(solution)/shard_map/ppermute | solution.py:558
  162.4 33.4 %collective-permute-start.30 = (bf16[4,4,384,128]{3,2,1,0:T(8,128)(2,1)}, bf16[4,4,384,128]{3,2,1,0:T(8,128)(2,1)}, u32[]{:S(2)}, u32[]{:S(2)}) collective-permute-start(bf16[4,4,384,128]{3,2,1,0:T(8,128)(2,1)} %bitcast.75.own), channel_id=1, source_target_pairs={{0,1},{1,0},{2,3},{3,2},{4,5},{5,4},{6,7},{7,6},{8,9},{9,8},{10,11... | collective-permute-start | bytes 4718600 | tf_op jit(solution)/shard_map/ppermute | solution.py:558
  174.9 19.5 %collective-permute-start.26 = (bf16[2,4,384,128]{3,2,1,0:T(8,128)(2,1)}, bf16[2,4,384,128]{3,2,1,0:T(8,128)(2,1)}, u32[]{:S(2)}, u32[]{:S(2)}) collective-permute-start(bf16[2,4,384,128]{3,2,1,0:T(8,128)(2,1)} %get-tuple-element.189), channel_id=1, source_target_pairs={{0,8},{1,9},{2,10},{3,11},{4,12},{5,13},{6,14},{7,15},{8,0},{9,1},... | collective-permute-start | bytes 2359304 | tf_op jit(solution)/shard_map/ppermute | solution.py:558
  209.3 24.6 %collective-permute-start.32 = (bf16[4,4,384,128]{3,2,1,0:T(8,128)(2,1)}, bf16[4,4,384,128]{3,2,1,0:T(8,128)(2,1)S(1)}, u32[]{:S(2)}, u32[]{:S(2)}) collective-permute-start(bf16[4,4,384,128]{3,2,1,0:T(8,128)(2,1)} %get-tuple-element.105), channel_id=1, source_target_pairs={{0,1},{1,0},{2,3},{3,2},{4,5},{5,4},{6,7},{7,6},{8,9},{9,8},{10,11... | collective-permute-start | bytes 4718600 | tf_op jit(solution)/shard_map/ppermute | solution.py:558
  210.8 19.9 %collective-permute-start.31 = (bf16[2,4,384,128]{3,2,1,0:T(8,128)(2,1)S(1)}, bf16[2,4,384,128]{3,2,1,0:T(8,128)(2,1)S(1)}, u32[]{:S(2)}, u32[]{:S(2)}) collective-permute-start(bf16[2,4,384,128]{3,2,1,0:T(8,128)(2,1)S(1)} %fusion), channel_id=1, source_target_pairs={{0,8},{1,9},{2,10},{3,11},{4,12},{5,13},{6,14},{7,15},{8,0},{9,1},... | collective-permute-start | bytes 2359304 | tf_op jit(solution)/shard_map/ppermute | solution.py:558
  230.9 19.2 %collective-permute-start.33 = (bf16[4,384,128]{2,1,0:T(8,128)(2,1)S(1)}, bf16[4,384,128]{2,1,0:T(8,128)(2,1)S(1)}, u32[]{:S(2)}, u32[]{:S(2)}) collective-permute-start(bf16[4,384,128]{2,1,0:T(8,128)(2,1)S(1)} %fusion.5), channel_id=1, source_target_pairs={{0,16},{1,17},{2,18},{3,19},{4,20},{5,21},{6,22},{7,23},{8,24},{9,... | collective-permute-start | bytes 1179656 | tf_op jit(solution)/shard_map/ppermute | solution.py:558
  245.8 23.5 %collective-permute-start.38 = (bf16[4,4,192,128]{3,2,1,0:T(8,128)(2,1)}, bf16[4,4,192,128]{3,2,1,0:T(8,128)(2,1)}, u32[]{:S(2)}, u32[]{:S(2)}) collective-permute-start(bf16[4,4,192,128]{3,2,1,0:T(8,128)(2,1)} %get-tuple-element.124), channel_id=1, source_target_pairs={{0,1},{1,0},{2,3},{3,2},{4,5},{5,4},{6,7},{7,6},{8,9},{9,8},{10,11... | collective-permute-start | bytes 2359304 | tf_op jit(solution)/shard_map/ppermute | solution.py:558
  245.8 32.2 %collective-permute-start.55 = (bf16[2,4,384,128]{3,2,1,0:T(8,128)(2,1)}, bf16[2,4,384,128]{3,2,1,0:T(8,128)(2,1)}, u32[]{:S(2)}, u32[]{:S(2)}) collective-permute-start(bf16[2,4,384,128]{3,2,1,0:T(8,128)(2,1)} %fusion.2), channel_id=1, source_target_pairs={{0,8},{1,9},{2,10},{3,11},{4,12},{5,13},{6,14},{7,15},{8,0},{9,1},... | collective-permute-start | bytes 2359304 | tf_op jit(solution)/shard_map/ppermute | solution.py:558
  248.5 19.8 %collective-permute-start.36 = (bf16[2,4,384,128]{3,2,1,0:T(8,128)(2,1)}, bf16[2,4,384,128]{3,2,1,0:T(8,128)(2,1)S(1)}, u32[]{:S(2)}, u32[]{:S(2)}) collective-permute-start(bf16[2,4,384,128]{3,2,1,0:T(8,128)(2,1)} %fusion.1), channel_id=1, source_target_pairs={{0,16},{1,17},{2,18},{3,19},{4,20},{5,21},{6,22},{7,23},{8,24},{9,... | collective-permute-start | bytes 2359304 | tf_op jit(solution)/shard_map/ppermute | solution.py:558
  258.2 30.3 %collective-permute-start.35 = (bf16[4,3,384,128]{3,2,1,0:T(8,128)(2,1)}, bf16[4,3,384,128]{3,2,1,0:T(8,128)(2,1)S(1)}, u32[]{:S(2)}, u32[]{:S(2)}) collective-permute-start(bf16[4,3,384,128]{3,2,1,0:T(8,128)(2,1)} %get-tuple-element.116), channel_id=1, source_target_pairs={{0,1},{1,0},{2,3},{3,2},{4,5},{5,4},{6,7},{7,6},{8,9},{9,8},{10,11... | collective-permute-start | bytes 3538952 | tf_op jit(solution)/shard_map/ppermute | solution.py:558
  277.8 81.5 %collective-permute-start.40 = (bf16[4,4,384,128]{3,2,1,0:T(8,128)(2,1)}, bf16[4,4,384,128]{3,2,1,0:T(8,128)(2,1)S(1)}, u32[]{:S(2)}, u32[]{:S(2)}) collective-permute-start(bf16[4,4,384,128]{3,2,1,0:T(8,128)(2,1)} %get-tuple-element.128), channel_id=1, source_target_pairs={{0,1},{1,0},{2,3},{3,2},{4,5},{5,4},{6,7},{7,6},{8,9},{9,8},{10,11... | collective-permute-start | bytes 4718600 | tf_op jit(solution)/shard_map/ppermute | solution.py:558
  281.1 36.4 %collective-permute-start.56 = (bf16[4,384,128]{2,1,0:T(8,128)(2,1)}, bf16[4,384,128]{2,1,0:T(8,128)(2,1)}, u32[]{:S(2)}, u32[]{:S(2)}) collective-permute-start(bf16[4,384,128]{2,1,0:T(8,128)(2,1)} %fusion.9), channel_id=1, source_target_pairs={{0,16},{1,17},{2,18},{3,19},{4,20},{5,21},{6,22},{7,23},{8,24},{9,... | collective-permute-start | bytes 1179656 | tf_op jit(solution)/shard_map/ppermute | solution.py:558
  282.6 23.5 %collective-permute-start.37 = (bf16[4,384,128]{2,1,0:T(8,128)(2,1)S(1)}, bf16[4,384,128]{2,1,0:T(8,128)(2,1)}, u32[]{:S(2)}, u32[]{:S(2)}) collective-permute-start(bf16[4,384,128]{2,1,0:T(8,128)(2,1)S(1)} %fusion.6), channel_id=1, source_target_pairs={{0,8},{1,9},{2,10},{3,11},{4,12},{5,13},{6,14},{7,15},{8,0},{9,1},... | collective-permute-start | bytes 1179656 | tf_op jit(solution)/shard_map/ppermute | solution.py:558
  289.9 29.0 %collective-permute-start.50 = (bf16[3,384,128]{2,1,0:T(8,128)(2,1)}, bf16[3,384,128]{2,1,0:T(8,128)(2,1)S(1)}, u32[]{:S(2)}, u32[]{:S(2)}) collective-permute-start(bf16[3,384,128]{2,1,0:T(8,128)(2,1)} %get-tuple-element.179), channel_id=1, source_target_pairs={{0,6},{1,7},{2,0},{3,1},{4,2},{5,3},{6,4},{7,5},{8,14},{9,15},{10,... | collective-permute-start | bytes 884744 | tf_op jit(solution)/shard_map/ppermute | solution.py:558
  302.2 23.2 %collective-permute-start.51 = (bf16[3,384,128]{2,1,0:T(8,128)(2,1)}, bf16[3,384,128]{2,1,0:T(8,128)(2,1)S(1)}, u32[]{:S(2)}, u32[]{:S(2)}) collective-permute-start(bf16[3,384,128]{2,1,0:T(8,128)(2,1)} %get-tuple-element.178), channel_id=1, source_target_pairs={{0,4},{1,5},{2,6},{3,7},{4,0},{5,1},{6,2},{7,3},{8,12},{9,13},{10,... | collective-permute-start | bytes 884744 | tf_op jit(solution)/shard_map/ppermute | solution.py:558
  306.1 19.3 %collective-permute-start.52 = (bf16[3,384,128]{2,1,0:T(8,128)(2,1)}, bf16[3,384,128]{2,1,0:T(8,128)(2,1)S(1)}, u32[]{:S(2)}, u32[]{:S(2)}) collective-permute-start(bf16[3,384,128]{2,1,0:T(8,128)(2,1)} %get-tuple-element.177), channel_id=1, source_target_pairs={{0,2},{1,3},{2,4},{3,5},{4,6},{5,7},{6,0},{7,1},{8,10},{9,11},{10,... | collective-permute-start | bytes 884744 | tf_op jit(solution)/shard_map/ppermute | solution.py:558
  326.8 28.5 %collective-permute-start.58 = (bf16[3,384,128]{2,1,0:T(8,128)(2,1)S(1)}, bf16[3,384,128]{2,1,0:T(8,128)(2,1)S(1)}, u32[]{:S(2)}, u32[]{:S(2)}) collective-permute-start(bf16[3,384,128]{2,1,0:T(8,128)(2,1)S(1)} %get-tuple-element.173), channel_id=1, source_target_pairs={{0,4},{1,5},{2,6},{3,7},{4,0},{5,1},{6,2},{7,3},{8,12},{9,13},{10,... | collective-permute-start | bytes 884744 | tf_op jit(solution)/shard_map/ppermute | solution.py:558
  329.6 26.4 %collective-permute-start.59 = (bf16[3,384,128]{2,1,0:T(8,128)(2,1)S(1)}, bf16[3,384,128]{2,1,0:T(8,128)(2,1)S(1)}, u32[]{:S(2)}, u32[]{:S(2)}) collective-permute-start(bf16[3,384,128]{2,1,0:T(8,128)(2,1)S(1)} %get-tuple-element.172), channel_id=1, source_target_pairs={{0,2},{1,3},{2,4},{3,5},{4,6},{5,7},{6,0},{7,1},{8,10},{9,11},{10,... | collective-permute-start | bytes 884744 | tf_op jit(solution)/shard_map/ppermute | solution.py:558
  331.6 26.2 %collective-permute-start.41 = (bf16[4,4,192,128]{3,2,1,0:T(8,128)(2,1)S(1)}, bf16[4,4,192,128]{3,2,1,0:T(8,128)(2,1)S(1)}, u32[]{:S(2)}, u32[]{:S(2)}) collective-permute-start(bf16[4,4,192,128]{3,2,1,0:T(8,128)(2,1)S(1)} %copy-done.39), channel_id=1, source_target_pairs={{0,1},{1,0},{2,3},{3,2},{4,5},{5,4},{6,7},{7,6},{8,9},{9,8},{10,11... | collective-permute-start | bytes 2359304 | tf_op jit(solution)/shard_map/ppermute | solution.py:558
  334.6 53.3 %collective-permute-start.45 = (bf16[4,192,128]{2,1,0:T(8,128)(2,1)S(1)}, bf16[4,192,128]{2,1,0:T(8,128)(2,1)S(1)}, u32[]{:S(2)}, u32[]{:S(2)}) collective-permute-start(bf16[4,192,128]{2,1,0:T(8,128)(2,1)S(1)} %fusion.18), channel_id=1, source_target_pairs={{0,16},{1,17},{2,18},{3,19},{4,20},{5,21},{6,22},{7,23},{8,24},{9,... | collective-permute-start | bytes 589832 | tf_op jit(solution)/shard_map/ppermute | solution.py:558
  355.4 35.0 %collective-permute-start.54 = (bf16[384,128]{1,0:T(8,128)(2,1)S(1)}, bf16[384,128]{1,0:T(8,128)(2,1)S(1)}, u32[]{:S(2)}, u32[]{:S(2)}) collective-permute-start(bf16[384,128]{1,0:T(8,128)(2,1)S(1)} %fusion.27), channel_id=1, source_target_pairs={{0,8},{1,9},{2,10},{3,11},{4,12},{5,13},{6,14},{7,15},{8,0},{9,1},... | collective-permute-start | bytes 294920 | tf_op jit(solution)/shard_map/ppermute | solution.py:558
  359.6 20.2 %collective-permute-start.42 = (bf16[2,4,384,128]{3,2,1,0:T(8,128)(2,1)S(1)}, bf16[2,4,384,128]{3,2,1,0:T(8,128)(2,1)S(1)}, u32[]{:S(2)}, u32[]{:S(2)}) collective-permute-start(bf16[2,4,384,128]{3,2,1,0:T(8,128)(2,1)S(1)} %add_convert_fusion.1), channel_id=1, source_target_pairs={{0,16},{1,17},{2,18},{3,19},{4,20},{5,21},{6,22},{7,23},{8,24},{9,... | collective-permute-start | bytes 2359304 | tf_op jit(solution)/shard_map/ppermute | solution.py:558
  368.5 19.4 %collective-permute-start.46 = (bf16[4,192,128]{2,1,0:T(8,128)(2,1)S(1)}, bf16[4,192,128]{2,1,0:T(8,128)(2,1)S(1)}, u32[]{:S(2)}, u32[]{:S(2)}) collective-permute-start(bf16[4,192,128]{2,1,0:T(8,128)(2,1)S(1)} %fusion.19), channel_id=1, source_target_pairs={{0,16},{1,17},{2,18},{3,19},{4,20},{5,21},{6,22},{7,23},{8,24},{9,... | collective-permute-start | bytes 589832 | tf_op jit(solution)/shard_map/ppermute | solution.py:558
  (68 other events, 673.3 us)

commit v4 on v2

--- a/solution.py
+++ b/solution.py
@@ -31,6 +31,7 @@
 GC = 0.7978845608
 GA = 0.044715
 VMEM_LIMIT = 52 * 1024 * 1024
+COST = 1 << 38
 
 F32 = jnp.float32
 BF16 = jnp.bfloat16
@@ -54,7 +55,7 @@
         compiler_params=pltpu.CompilerParams(
             dimension_semantics=("arbitrary",) * len(grid), vmem_limit_bytes=VMEM_LIMIT
         ),
-        cost_estimate=pl.CostEstimate(flops=flops, bytes_accessed=nbytes, transcendentals=0),
+        cost_estimate=pl.CostEstimate(flops=COST, bytes_accessed=nbytes, transcendentals=0),
     )
 
 
@@ -488,6 +489,10 @@
     return total
 
 
+def after(val, *deps):
+    return lax.optimization_barrier((val, deps))[0]
+
+
 class Grid:
     def __init__(self, gx, gy):
         self.gy = gy
@@ -514,12 +519,36 @@
     def spread(self, val, axis):
         return jnp.stack([val] + [self.fetch(val, axis, k) for k in range(1, self.size[axis])])
 
-    def reduce(self, terms, axis):
-        got = [
-            self.fetch(add_up([t[k] for t in terms]).astype(BF16), axis, -k)
-            for k in range(1, self.size[axis])
-        ]
-        return [t[0] for t in terms] + got
+    def reduce(self, terms, stage, axis, *deps):
+        if deps:
+            terms = terms[:-1] + [(after(terms[-1][0], *deps), terms[-1][1])]
+        got = []
+        for k in range(1, self.size[axis]):
+            part = add_up([v[(0,) * (stage - born) + (k,)] for v, born in terms]).astype(BF16)
+            got.append((self.fetch(part, axis, -k), stage + 1))
+        return terms + got
+
+    def total(self, terms, stage):
+        return add_up([v[(0,) * (stage - born)] for v, born in terms])
+
+    def reduce_joined(self, groups, axis, *deps):
+        groups = list(groups)
+        if deps:
+            groups[-1] = groups[-1][:-1] + [(after(groups[-1][-1][0], *deps), groups[-1][-1][1])]
+        got = []
+        for k in range(1, self.size[axis]):
+            parts = [
+                add_up([v[(0,) * (2 - born) + (k,)] for v, born in terms]).astype(BF16)
+                for terms in groups
+            ]
+            got.append(self.fetch(jnp.concatenate(parts, axis=0), axis, -k))
+        out, at_row = [], 0
+        for terms in groups:
+            n = terms[0][0].shape[-2]
+            own = [v[(0,) * (3 - born)] for v, born in terms]
+            out.append(add_up(own + [v[at_row : at_row + n] for v in got]))
+            at_row += n
+        return out
 
 
 def compute(tab, x, docs, cot, a, b, w, u, d):
@@ -549,60 +578,80 @@
     tab = jnp.stack([at["c"]] + order_a + order_b + order_z).astype(jnp.int32)
     docs = lax.dynamic_slice_in_dim(doc_ids, lax.axis_index("gy"), 1, 0)
 
+    dq, dk = docs.reshape(L, 1), docs
     mix = mixing.reshape(2, HR, KB)
+    fetch, spread = grid.fetch, grid.spread
     wts = jnp.concatenate([lane_pad(value_w, mix_gain), lane_pad(output_w.T, ffn_gain)], axis=0)
-    first = jnp.concatenate([mix[0], wts], axis=0)
-    first = grid.spread(first, "z")
-    a = grid.spread(grid.spread(first[:, :HR], "x"), "y").reshape(A_SHAPE)
-    w = grid.spread(grid.spread(first[:, HR:], "y"), "x").reshape(W_SHAPE)
-    b = grid.spread(grid.spread(mix[1], "x"), "y").reshape(G, HR, KB)
+
+    def both(val, *deps):
+        return val, fetch(after(val, *deps) if deps else val, "c", 1)
+
+    def along_z(val):
+        return [val] + [fetch(val, "z", k) for k in range(1, Z)]
+
+    c1 = along_z(jnp.concatenate([mix[0], wts], axis=0))
+    b = spread(spread(mix[1], "x"), "y").reshape(G, HR, KB)
     start = window(at["z"])
     order = jnp.stack(order_b)
     b = jnp.stack([lax.dynamic_index_in_dim(b, order[start + i], 0, False) for i in range(WIN)])
-    b = grid.spread(b, "z")
-    ffn = grid.spread(jnp.stack([up_w, down_w.T]), "z")
-    u = grid.spread(grid.spread(ffn[:, 0], "x"), "y").reshape(F_SHAPE)
-    d = grid.spread(grid.spread(ffn[:, 1], "y"), "x").reshape(F_SHAPE)
-    a, b, w, u, d = ((v, grid.fetch(v, "c", 1)) for v in (a, b, w, u, d))
-
-    layer_out, grad_in, gu, gd, ga, gb, go, gv = compute(
-        tab, layer_in, docs, cot, a, b, w, u, d
+    a, w = (jnp.stack([v[i * HR : (i + 1) * HR] for v in c1]) for i in range(2))
+    ffn = along_z(after(jnp.stack([up_w, down_w.T]), c1[1:]))
+    a, w = spread(a, "x"), spread(w, "y")
+    a, w = spread(a, "y").reshape(A_SHAPE), spread(w, "x").reshape(W_SHAPE)
+    b = spread(after(b, ffn[1:]), "z")
+    ffn[1:] = after(ffn[1:], a, w)
+    u, d = (jnp.stack([v[i] for v in ffn]) for i in range(2))
+    w, a = both(w), both(a)
+    low, vals, gain = run_values(tab, layer_in, w)
+    u, d = spread(u, "x"), spread(d, "y")
+    b = both(b)
+    u, d = after((u, d), low)
+    u, d = spread(u, "y").reshape(F_SHAPE), spread(d, "x").reshape(F_SHAPE)
+    mixed, mid, n_two = run_mixer(tab, layer_in, gain, dq, dk, vals, a, b, w)
+    u, d = both(u, n_two), both(d, n_two)
+
+    def begin(keep, send):
+        got = fetch(send, "c", 1)
+        return [(v.reshape((2, 2) + v.shape[1:]), 0) for v in (keep, got)]
+
+    def last(*groups):
+        return [terms[-1][0] for terms in groups]
+
+    su, sd, acc_b, acc_a = run_ffn(tab, n_two, cot, u[1], d[1])
+    ku, kd, n_grad, layer_out = run_ffn(tab, n_two, cot, u[0], d[0], (acc_a, acc_b), mid)
+    gu, gd = begin(ku, su), begin(kd, sd)
+    n_grad = after(n_grad, last(gu, gd))
+    gu, gd = grid.reduce(gu, 0, "y"), grid.reduce(gd, 0, "x")
+    mid_grad, ka, sa, kb, sb, ko, so, vg = run_mixer_back(
+        tab, n_grad, mid, cot, gain, dq, dk, mixed, vals, a, b, w
     )
-
-    def core_sum(pair):
-        return [pair[0], grid.fetch(pair[1], "c", 1)]
-
-    def split(vals, *lead):
-        return [v.reshape(lead + v.shape[-3:]) for v in vals]
-
-    up = grid.reduce(grid.reduce(split(core_sum(gu), 2, 2), "y"), "x")
-    dn = grid.reduce(grid.reduce(split(core_sum(gd), 2, 2), "x"), "y")
-    both = [jnp.stack([p, q], axis=1) for p, q in zip(up, dn)]
-    ffn = add_up(grid.reduce(both, "z"))
-    gb = core_sum(gb)
-    gb = grid.reduce(gb, "z")
-    wide = []
-    for v in gb:
-        blocks = []
-        for k in range(G):
-            y = (at["y"] - k // 2) % 2
-            x = (at["x"] - k % 2) % 2
-            spot = y * 2 + x - start
-            blk = lax.dynamic_index_in_dim(v, jnp.clip(spot, 0, WIN - 1), 0, False)
-            ok = jnp.logical_and(spot >= 0, spot < WIN)
-            blocks.append(jnp.where(ok, blk, jnp.zeros_like(blk)))
-        wide.append(jnp.stack(blocks).reshape(2, 2, HR, KB))
-    gb = add_up(grid.reduce(grid.reduce(wide, "y"), "x"))
-    ga = split(core_sum(ga), 2, 2)
-    ga = add_up(grid.reduce(grid.reduce(grid.reduce(ga, "y"), "x"), "z"))
-    go, gv = core_sum(go), core_sum(gv)
-    gw = split([jnp.concatenate([p, q], axis=2) for p, q in zip(gv, go)], 2, 2)
-    gw = add_up(grid.reduce(grid.reduce(grid.reduce(gw, "x"), "y"), "z"))
+    vg = after(vg, last(gu, gd))
+    ga, go, rb = begin(ka, sa), begin(ko, so), fetch(sb, "c", 1)
+    gu, gd = grid.reduce(gu, 1, "x", sa), grid.reduce(gd, 1, "y", sa)
+    gb = grid.reduce([(kb, 2), (rb, 2)], 2, "z")
+    grad_in, kv, sv = run_last(tab, layer_in, gain, low, vg, w, mid_grad)
+    gv = begin(kv, sv)
+    ga = grid.reduce(ga, 0, "y", sv)
+    go = grid.reduce(go, 0, "x", sv)
+    gu, gd = grid.reduce_joined((gu, gd), "z", last(gb))
+    gv = grid.reduce(gv, 0, "x")
+    wide = grid.total(gb, 3)
+    blocks = []
+    for k in range(G):
+        spot = (at["y"] - k // 2) % 2 * 2 + (at["x"] - k % 2) % 2 - start
+        blk = lax.dynamic_index_in_dim(wide, jnp.clip(spot, 0, WIN - 1), 0, False)
+        ok = jnp.logical_and(spot >= 0, spot < WIN)
+        blocks.append(jnp.where(ok, blk, jnp.zeros_like(blk)))
+    gb = [(jnp.stack(blocks).reshape(2, 2, HR, KB), 0)]
+    gb = grid.total(grid.reduce(grid.reduce(gb, 0, "y"), 1, "x"), 2)
+    ga, go = grid.reduce(ga, 1, "x"), grid.reduce(go, 1, "y")
+    gv = grid.reduce(gv, 1, "y")
+    ga, go, gv = grid.reduce_joined((ga, go, gv), "z")
 
     grad_mixing = jnp.concatenate([ga, gb], axis=0).reshape(H, QB, KB)
     return (
-        layer_out, grad_in, gw[0, CB : CB + GN], gw[:DB, :CB], grad_mixing, gw[DB:, :CB].T,
-        gw[DB, CB : CB + GN], ffn[0], ffn[1].T,
+        layer_out, grad_in, gv[0, CB : CB + GN], gv[:, :CB], grad_mixing, go[:, :CB].T,
+        go[0, CB : CB + GN], gu, gd.T,
     )
 
 

time: 377 us -> 335 us (0.89)
  waiting for transfers between devices: 180 us -> 124 us
  starting transfers between devices: 54.2 us -> 66 us
  other arithmetic: 34.6 us -> 46 us
  local copies, waits for them, and re-layouts: 15.1 us -> 7.1 us
    ppermute x52 -> x51, waiting for transfers between devices: 180 us -> 124 us  [fetch(): return lax.ppermute(val, ('gx', 'gy'), pairs)]
    ppermute x52 -> x51, starting transfers between devices: 54.2 us -> 66 us  [fetch(): return lax.ppermute(val, ('gx', 'gy'), pairs)]
    convert_element_type x13 -> x17, other arithmetic: 11.7 us -> 20.2 us  [the longest x12 15.1 us: reduce(): add_up([v[(0,) * (stage - born) + (k,)] for v, born in terms]).astype(BF16)]
    another operation x16 -> x15, other arithmetic: 17.7 us -> 17.4 us  [spread(): jnp.stack([val] + [self.fetch(val, axis, k) for k in range(1, self.size[a...]
  transfers between devices with their start and end apart: 52 -> 51, of which waited for: 23 -> 21; matrix products, arithmetic and copies ran while one was open for 12% -> 12% of each run, Pallas kernels for 9% -> 20%
where the time goes in v4:
time: 335 us; the launch traced here: 332 us
  waiting for transfers between devices  124 us (37%)
  Pallas kernels  81.8 us (24%)
  starting transfers between devices  66 us (20%)
  other arithmetic  46 us (14%)
  between operations  7.13 us (2%)
  local copies, waits for them, and re-layouts  7.1 us (2%)
    ppermute x51, waiting for transfers between devices, fetch(): return lax.ppermute(val, ('gx', 'gy'), pairs)  124 us
    ppermute x51, starting transfers between devices, fetch(): return lax.ppermute(val, ('gx', 'gy'), pairs)  66 us
    pallas_call x2, Pallas kernels, run_ffn(): call(body, (Z,), in_specs, out_specs, outs, scratch, flops=6 * L * D * FF...  33.7 us
    pallas_call x1, Pallas kernels, run_mixer_back(): call(mixer_back_body, (L // TM,), [rows(D), rows(D), rows(D), whole((8, D...  20.7 us
    another operation x15, other arithmetic, spread(): jnp.stack([val] + [self.fetch(val, axis, k) for k in range(1, self.size[a...  17.4 us
    convert_element_type x12, other arithmetic, reduce(): add_up([v[(0,) * (stage - born) + (k,)] for v, born in terms]).astype(BF16)  15.1 us
    pallas_call x1, Pallas kernels, run_mixer(): call(mixer_body, (L // TM,), [rows(D), whole((8, D)), rows(1), whole((1,...  12.6 us
    pallas_call x1, Pallas kernels, run_last(): call(last_body, (L // TM,), [rows(D), whole((8, D)), rows(D), Z_ROWS, who...  9.04 us
  transfers between devices with their start and end apart: 51, of which 21 were waited for; matrix products, arithmetic and copies ran while one was open for 12% of the time, Pallas kernels for 20%

profile of v4, /device:TPU:0, one launch (start us, length us, event | category | flops | bytes accessed | tf_op | source)
XLA Modules:
  0.0 332.2 jit_solution(15051735320864802853)
XLA Ops:
  4.8 5.1 %collective-permute-start.2 = (bf16[768,128]{1,0:T(8,128)(2,1)S(1)}, bf16[768,128]{1,0:T(8,128)(2,1)S(1)}, u32[]{:S(2)}, u32[]{:S(2)}) collective-permute-start(bf16[768,128]{1,0:T(8,128)(2,1)S(1)} %maximum_maximum_fusion), channel_id=1, source_target_pairs={{0,6},{1,7},{2,0},{3,1},{4,2},{5,3},{6,4},{7,5},{8,14},{9,15},{10,... | collective-permute-start | bytes 589832 | tf_op jit(solution)/shard_map/ppermute | solution.py:514
  11.8 3.4 %collective-permute-done.2 = bf16[768,128]{1,0:T(8,128)(2,1)S(1)} collective-permute-done((bf16[768,128]{1,0:T(8,128)(2,1)S(1)}, bf16[768,128]{1,0:T(8,128)(2,1)S(1)}, u32[]{:S(2)}, u32[]{:S(2)}) %collective-permute-start.2) | collective-permute-done | bytes 196640 | tf_op jit(solution)/shard_map/ppermute | solution.py:514
  15.2 11.3 %collective-permute-done.1 = bf16[768,128]{1,0:T(8,128)(2,1)S(1)} collective-permute-done((bf16[768,128]{1,0:T(8,128)(2,1)S(1)}, bf16[768,128]{1,0:T(8,128)(2,1)S(1)}, u32[]{:S(2)}, u32[]{:S(2)}) %collective-permute-start.1) | collective-permute-done | bytes 196640 | tf_op jit(solution)/shard_map/ppermute | solution.py:514
  45.6 15.0 %collective-permute-done.10 = bf16[2,384,128]{2,1,0:T(8,128)(2,1)S(1)} collective-permute-done((bf16[2,384,128]{2,1,0:T(8,128)(2,1)S(1)}, bf16[2,384,128]{2,1,0:T(8,128)(2,1)S(1)}, u32[]{:S(2)}, u32[]{:S(2)}) %collective-permute-start.10) | collective-permute-done | bytes 196640 | tf_op jit(solution)/shard_map/ppermute | solution.py:514
  62.2 5.9 %collective-permute-done.13 = bf16[2,192,384]{2,1,0:T(8,128)(2,1)S(1)} collective-permute-done((bf16[2,192,384]{2,1,0:T(8,128)(2,1)S(1)}, bf16[2,192,384]{2,1,0:T(8,128)(2,1)S(1)}, u32[]{:S(2)}, u32[]{:S(2)}) %collective-permute-start.13) | collective-permute-done | bytes 294944 | tf_op jit(solution)/shard_map/ppermute | solution.py:514
  68.2 3.8 %collective-permute-start.16 = (bf16[3,384,128]{2,1,0:T(8,128)(2,1)S(1)}, bf16[3,384,128]{2,1,0:T(8,128)(2,1)S(1)}, u32[]{:S(2)}, u32[]{:S(2)}) collective-permute-start(bf16[3,384,128]{2,1,0:T(8,128)(2,1)S(1)} %pad_maximum_fusion.16), channel_id=1, source_target_pairs={{0,6},{1,7},{2,0},{3,1},{4,2},{5,3},{6,4},{7,5},{8,14},{9,15},{10,... | collective-permute-start | bytes 884744 | tf_op jit(solution)/shard_map/ppermute | solution.py:514
  80.1 18.6 %collective-permute-done.15 = bf16[3,384,128]{2,1,0:T(8,128)(2,1)} collective-permute-done((bf16[3,384,128]{2,1,0:T(8,128)(2,1)S(1)}, bf16[3,384,128]{2,1,0:T(8,128)(2,1)}, u32[]{:S(2)}, u32[]{:S(2)}) %collective-permute-start.15) | collective-permute-done | bytes 294944 | tf_op jit(solution)/shard_map/ppermute | solution.py:514
  103.7 2.4 pad_maximum_fusion.6
  106.1 5.6 %shard_map.169 = (bf16[512,768]{1,0:T(8,128)(2,1)S(1)}, bf16[4,512,256]{2,1,0:T(8,128)(2,1)}, f32[8,768]{1,0:T(8,128)S(1)}) custom-call(s32[13]{0:T(128)S(1)} %stack.221.t, bf16[512,768]{1,0:T(8,128)(2,1)S(1)} %copy-done.5, bf16[4,4,384,128]{3,2,1,0:T(8,128)(2,1)} %bitcast.401, bf16[4,4,384,128]{3,2,1,0:T(8,128)(2,1)} %collective-permute-done.5.oth_ref.w_oth), custom_call_target="tpu_custom_call" | custom-call | flops 274877906944 | bytes 6291456 | tf_op jit(solution)/shard_map/pallas_call | solution.py:391
  115.0 12.6 %shard_map.170 = (bf16[4,512,256]{2,1,0:T(8,128)(2,1)}, f32[512,768]{1,0:T(8,128)}, bf16[512,768]{1,0:T(8,128)(2,1)S(1)}) custom-call(s32[13]{0:T(128)S(1)} %stack.221.t, bf16[512,768]{1,0:T(8,128)(2,1)S(1)} %copy-done.5, f32[8,768]{1,0:T(8,128)S(1)} %get-tuple-element.50.gain_ref, s32[512,1]{1,0:T(8,128)S(1)} %copy.28.dq_ref, ...), custom_call_target="tpu_custom_call" | custom-call | flops 274877906944 | bytes 14680064 | tf_op jit(solution)/shard_map/pallas_call | solution.py:403
  127.6 12.4 %collective-permute-done.20 = bf16[2,4,192,384]{3,2,1,0:T(8,128)(2,1)} collective-permute-done((bf16[2,4,192,384]{3,2,1,0:T(8,128)(2,1)}, bf16[2,4,192,384]{3,2,1,0:T(8,128)(2,1)}, u32[]{:S(2)}, u32[]{:S(2)}) %collective-permute-start.20) | collective-permute-done | bytes 1179680 | tf_op jit(solution)/shard_map/ppermute | solution.py:514
  140.0 3.3 pad_maximum_fusion
  143.3 3.4 %pad_maximum_fusion.1 = bf16[2,2,4,192,384]{4,3,2,1,0:T(8,128)(2,1)} fusion(bf16[1,2,4,192,384]{4,3,2,1,0:T(8,128)(2,1)} %bitcast.60, bf16[1,2,4,192,384]{4,3,2,1,0:T(8,128)(2,1)} %bitcast.59), kind=kLoop, calls=%fused_computation.1 | loop fusion | flops 1179648 | bytes 4718592 | tf_op jit(solution)/shard_map/stack | solution.py:520
  148.1 3.5 %collective-permute-done.23.refs_3_ = bf16[4,4,192,384]{3,2,1,0:T(8,128)(2,1)} collective-permute-done((bf16[4,4,192,384]{3,2,1,0:T(8,128)(2,1)}, bf16[4,4,192,384]{3,2,1,0:T(8,128)(2,1)}, u32[]{:S(2)}, u32[]{:S(2)}) %collective-permute-start.23) | collective-permute-done | bytes 2359328 | tf_op jit(solution)/shard_map/ppermute | solution.py:514
  151.6 16.1 %shard_map.171 = (bf16[4,4,192,384]{3,2,1,0:T(8,128)(2,1)}, bf16[4,4,192,384]{3,2,1,0:T(8,128)(2,1)}, f32[512,768]{1,0:T(8,128)}, f32[512,768]{1,0:T(8,128)}) custom-call(s32[13]{0:T(128)S(1)} %stack.221.t, bf16[512,768]{1,0:T(8,128)(2,1)S(1)} %get-tuple-element.54.refs_0_, bf16[512,768]{1,0:T(8,128)(2,1)S(1)} %copy-done.4, ...), custom_call_target="tpu_custom_call" | custom-call | flops 274877906944 | bytes 20971520 | tf_op jit(solution)/shard_map/pallas_call | solution.py:445
  168.4 17.6 %shard_map.172 = (bf16[4,4,192,384]{3,2,1,0:T(8,128)(2,1)}, bf16[4,4,192,384]{3,2,1,0:T(8,128)(2,1)}, f32[512,768]{1,0:T(8,128)}, bf16[512,768]{1,0:T(8,128)(2,1)}) custom-call(s32[13]{0:T(128)S(1)} %stack.221.t, bf16[512,768]{1,0:T(8,128)(2,1)S(1)} %get-tuple-element.54.refs_0_, bf16[512,768]{1,0:T(8,128)(2,1)S(1)} %copy-done.4, ...), custom_call_target="tpu_custom_call" | custom-call | flops 274877906944 | bytes 20971520 | tf_op jit(solution)/shard_map/pallas_call | solution.py:445
  186.0 3.1 add_convert_fusion.1
  190.5 2.6 add_convert_fusion
  194.9 20.7 %shard_map.173 = (f32[512,768]{1,0:T(8,128)}, bf16[4,4,384,128]{3,2,1,0:T(8,128)(2,1)}, bf16[4,4,384,128]{3,2,1,0:T(8,128)(2,1)}, bf16[4,3,384,128]{3,2,1,0:T(8,...) custom-call(s32[13]{0:T(128)S(1)} %stack.221.t, ...), custom_call_target="tpu_custom_call" | custom-call | flops 274877906944 | bytes 29360128 | tf_op jit(solution)/shard_map/pallas_call | solution.py:453
  217.6 3.8 %collective-permute-done.27 = bf16[2,4,192,384]{3,2,1,0:T(8,128)(2,1)} collective-permute-done((bf16[2,4,192,384]{3,2,1,0:T(8,128)(2,1)}, bf16[2,4,192,384]{3,2,1,0:T(8,128)(2,1)}, u32[]{:S(2)}, u32[]{:S(2)}) %collective-permute-start.27) | collective-permute-done | bytes 1179680 | tf_op jit(solution)/shard_map/ppermute | solution.py:514
  221.4 9.0 %shard_map.174 = (f32[512,768]{1,0:T(8,128)}, bf16[4,4,192,128]{3,2,1,0:T(8,128)(2,1)S(1)}, bf16[4,4,192,128]{3,2,1,0:T(8,128)(2,1)S(1)}) custom-call(s32[13]{0:T(128)S(1)} %stack.221.t, bf16[512,768]{1,0:T(8,128)(2,1)} %x_ref.5, f32[8,768]{1,0:T(8,128)S(1)} %copy-done.8, bf16[512,768]{1,0:T(8,128)(2,1)} %copy-done.6, ...), custom_call_target="tpu_custom_call" | custom-call | flops 274877906944 | bytes 12582912 | tf_op jit(solution)/shard_map/pallas_call | solution.py:473
  235.0 2.9 collective-permute-start.41
  240.5 3.3 %collective-permute-done.43 = bf16[3,384,128]{2,1,0:T(8,128)(2,1)S(1)} collective-permute-done((bf16[3,384,128]{2,1,0:T(8,128)(2,1)S(1)}, bf16[3,384,128]{2,1,0:T(8,128)(2,1)S(1)}, u32[]{:S(2)}, u32[]{:S(2)}) %collective-permute-start.43) | collective-permute-done | bytes 294944 | tf_op jit(solution)/shard_map/ppermute | solution.py:514
  245.6 10.0 %collective-permute-done.42 = bf16[3,384,128]{2,1,0:T(8,128)(2,1)S(1)} collective-permute-done((bf16[3,384,128]{2,1,0:T(8,128)(2,1)S(1)}, bf16[3,384,128]{2,1,0:T(8,128)(2,1)S(1)}, u32[]{:S(2)}, u32[]{:S(2)}) %collective-permute-start.42) | collective-permute-done | bytes 294944 | tf_op jit(solution)/shard_map/ppermute | solution.py:514
  262.2 13.9 %collective-permute-done.44 = bf16[2,384,128]{2,1,0:T(8,128)(2,1)S(1)} collective-permute-done((bf16[2,384,128]{2,1,0:T(8,128)(2,1)S(1)}, bf16[2,384,128]{2,1,0:T(8,128)(2,1)S(1)}, u32[]{:S(2)}, u32[]{:S(2)}) %collective-permute-start.44) | collective-permute-done | bytes 196640 | tf_op jit(solution)/shard_map/ppermute | solution.py:514
  286.4 3.8 %collective-permute-start.50 = (bf16[384,384]{1,0:T(8,128)(2,1)S(1)}, bf16[384,384]{1,0:T(8,128)(2,1)S(1)}, u32[]{:S(2)}, u32[]{:S(2)}) collective-permute-start(bf16[384,384]{1,0:T(8,128)(2,1)S(1)} %pad_maximum_fusion.20), channel_id=1, source_target_pairs={{0,2},{1,3},{2,4},{3,5},{4,6},{5,7},{6,0},{7,1},{8,10},{9,11},{10,... | collective-permute-start | bytes 884744 | tf_op jit(solution)/shard_map/ppermute | solution.py:514
  290.2 3.4 %collective-permute-start.49 = (bf16[384,384]{1,0:T(8,128)(2,1)S(1)}, bf16[384,384]{1,0:T(8,128)(2,1)S(1)}, u32[]{:S(2)}, u32[]{:S(2)}) collective-permute-start(bf16[384,384]{1,0:T(8,128)(2,1)S(1)} %pad_maximum_fusion.19), channel_id=1, source_target_pairs={{0,4},{1,5},{2,6},{3,7},{4,0},{5,1},{6,2},{7,3},{8,12},{9,13},{10,... | collective-permute-start | bytes 884744 | tf_op jit(solution)/shard_map/ppermute | solution.py:514
  293.7 3.9 %collective-permute-start.48 = (bf16[384,384]{1,0:T(8,128)(2,1)S(1)}, bf16[384,384]{1,0:T(8,128)(2,1)S(1)}, u32[]{:S(2)}, u32[]{:S(2)}) collective-permute-start(bf16[384,384]{1,0:T(8,128)(2,1)S(1)} %pad_maximum_fusion.18), channel_id=1, source_target_pairs={{0,6},{1,7},{2,0},{3,1},{4,2},{5,3},{6,4},{7,5},{8,14},{9,15},{10,... | collective-permute-start | bytes 884744 | tf_op jit(solution)/shard_map/ppermute | solution.py:514
  303.5 4.8 %collective-permute-done.33 = bf16[4,384,128]{2,1,0:T(8,128)(2,1)S(1)} collective-permute-done((bf16[4,384,128]{2,1,0:T(8,128)(2,1)S(1)}, bf16[4,384,128]{2,1,0:T(8,128)(2,1)S(1)}, u32[]{:S(2)}, u32[]{:S(2)}) %collective-permute-start.33) | collective-permute-done | bytes 393248 | tf_op jit(solution)/shard_map/ppermute | solution.py:514
  309.5 3.7 %collective-permute-start.39 = (bf16[768,128]{1,0:T(8,128)(2,1)S(1)}, bf16[768,128]{1,0:T(8,128)(2,1)S(1)}, u32[]{:S(2)}, u32[]{:S(2)}) collective-permute-start(bf16[768,128]{1,0:T(8,128)(2,1)S(1)} %pad_maximum_fusion.24), channel_id=1, source_target_pairs={{0,2},{1,3},{2,4},{3,5},{4,6},{5,7},{6,0},{7,1},{8,10},{9,11},{10,... | collective-permute-start | bytes 589832 | tf_op jit(solution)/shard_map/ppermute | solution.py:514
  313.2 3.4 %collective-permute-start.38 = (bf16[768,128]{1,0:T(8,128)(2,1)S(1)}, bf16[768,128]{1,0:T(8,128)(2,1)S(1)}, u32[]{:S(2)}, u32[]{:S(2)}) collective-permute-start(bf16[768,128]{1,0:T(8,128)(2,1)S(1)} %pad_maximum_fusion.23), channel_id=1, source_target_pairs={{0,4},{1,5},{2,6},{3,7},{4,0},{5,1},{6,2},{7,3},{8,12},{9,13},{10,... | collective-permute-start | bytes 589832 | tf_op jit(solution)/shard_map/ppermute | solution.py:514
  319.8 7.8 %collective-permute-done.38 = bf16[768,128]{1,0:T(8,128)(2,1)S(1)} collective-permute-done((bf16[768,128]{1,0:T(8,128)(2,1)S(1)}, bf16[768,128]{1,0:T(8,128)(2,1)S(1)}, u32[]{:S(2)}, u32[]{:S(2)}) %collective-permute-start.38) | collective-permute-done | bytes 196640 | tf_op jit(solution)/shard_map/ppermute | solution.py:514
  (188 shorter events, 84.7 us)
Async XLA Ops:
  9.9 16.7 %collective-permute-start.1 = (bf16[768,128]{1,0:T(8,128)(2,1)S(1)}, bf16[768,128]{1,0:T(8,128)(2,1)S(1)}, u32[]{:S(2)}, u32[]{:S(2)}) collective-permute-start(bf16[768,128]{1,0:T(8,128)(2,1)S(1)} %maximum_maximum_fusion), channel_id=1, source_target_pairs={{0,4},{1,5},{2,6},{3,7},{4,0},{5,1},{6,2},{7,3},{8,12},{9,13},{10,... | collective-permute-start | bytes 589832 | tf_op jit(solution)/shard_map/ppermute | solution.py:514
  9.9 16.7 %collective-permute-start = (bf16[768,128]{1,0:T(8,128)(2,1)S(1)}, bf16[768,128]{1,0:T(8,128)(2,1)S(1)}, u32[]{:S(2)}, u32[]{:S(2)}) collective-permute-start(bf16[768,128]{1,0:T(8,128)(2,1)S(1)} %maximum_maximum_fusion), channel_id=1, source_target_pairs={{0,2},{1,3},{2,4},{3,5},{4,6},{5,7},{6,0},{7,1},{8,10},{9,11},{10,... | collective-permute-start | bytes 589832 | tf_op jit(solution)/shard_map/ppermute | solution.py:514
  37.2 34.8 %collective-permute-start.4 = (bf16[2,4,384,128]{3,2,1,0:T(8,128)(2,1)S(1)}, bf16[2,4,384,128]{3,2,1,0:T(8,128)(2,1)S(1)}, u32[]{:S(2)}, u32[]{:S(2)}) collective-permute-start(bf16[2,4,384,128]{3,2,1,0:T(8,128)(2,1)S(1)} %get-tuple-element.136), channel_id=1, source_target_pairs={{0,8},{1,9},{2,10},{3,11},{4,12},{5,13},{6,14},{7,15},{8,0},{9,1},... | collective-permute-start | bytes 2359304 | tf_op jit(solution)/shard_map/ppermute | solution.py:514
  40.6 31.6 %collective-permute-start.7 = (bf16[2,4,384,128]{3,2,1,0:T(8,128)(2,1)S(1)}, bf16[2,4,384,128]{3,2,1,0:T(8,128)(2,1)S(1)}, u32[]{:S(2)}, u32[]{:S(2)}) collective-permute-start(bf16[2,4,384,128]{3,2,1,0:T(8,128)(2,1)S(1)} %get-tuple-element.134), channel_id=1, source_target_pairs={{0,16},{1,17},{2,18},{3,19},{4,20},{5,21},{6,22},{7,23},{8,24},{9,... | collective-permute-start | bytes 2359304 | tf_op jit(solution)/shard_map/ppermute | solution.py:514
  42.6 18.0 %collective-permute-start.10 = (bf16[2,384,128]{2,1,0:T(8,128)(2,1)S(1)}, bf16[2,384,128]{2,1,0:T(8,128)(2,1)S(1)}, u32[]{:S(2)}, u32[]{:S(2)}) collective-permute-start(bf16[2,384,128]{2,1,0:T(8,128)(2,1)S(1)} %get-tuple-element.165), channel_id=1, source_target_pairs={{0,16},{1,17},{2,18},{3,19},{4,20},{5,21},{6,22},{7,23},{8,24},{9,... | collective-permute-start | bytes 589832 | tf_op jit(solution)/shard_map/ppermute | solution.py:514
  42.8 17.9 %collective-permute-start.11 = (bf16[2,192,384]{2,1,0:T(8,128)(2,1)S(1)}, bf16[2,192,384]{2,1,0:T(8,128)(2,1)S(1)}, u32[]{:S(2)}, u32[]{:S(2)}) collective-permute-start(bf16[2,192,384]{2,1,0:T(8,128)(2,1)S(1)} %pad_maximum_fusion.17), channel_id=1, source_target_pairs={{0,2},{1,3},{2,4},{3,5},{4,6},{5,7},{6,0},{7,1},{8,10},{9,11},{10,... | collective-permute-start | bytes 884744 | tf_op jit(solution)/shard_map/ppermute | solution.py:514
  43.6 18.6 %collective-permute-start.12 = (bf16[2,192,384]{2,1,0:T(8,128)(2,1)S(1)}, bf16[2,192,384]{2,1,0:T(8,128)(2,1)S(1)}, u32[]{:S(2)}, u32[]{:S(2)}) collective-permute-start(bf16[2,192,384]{2,1,0:T(8,128)(2,1)S(1)} %pad_maximum_fusion.17), channel_id=1, source_target_pairs={{0,4},{1,5},{2,6},{3,7},{4,0},{5,1},{6,2},{7,3},{8,12},{9,13},{10,... | collective-permute-start | bytes 884744 | tf_op jit(solution)/shard_map/ppermute | solution.py:514
  72.1 34.0 %collective-permute-start.5 = (bf16[4,4,384,128]{3,2,1,0:T(8,128)(2,1)S(1)}, bf16[4,4,384,128]{3,2,1,0:T(8,128)(2,1)}, u32[]{:S(2)}, u32[]{:S(2)}) collective-permute-start(bf16[4,4,384,128]{3,2,1,0:T(8,128)(2,1)S(1)} %bitcast.400), channel_id=1, source_target_pairs={{0,1},{1,0},{2,3},{3,2},{4,5},{5,4},{6,7},{7,6},{8,9},{9,8},{10,11... | collective-permute-start | bytes 4718600 | tf_op jit(solution)/shard_map/ppermute | solution.py:514
  74.8 26.7 %collective-permute-start.18 = (bf16[4,192,384]{2,1,0:T(8,128)(2,1)}, bf16[4,192,384]{2,1,0:T(8,128)(2,1)}, u32[]{:S(2)}, u32[]{:S(2)}) collective-permute-start(bf16[4,192,384]{2,1,0:T(8,128)(2,1)} %get-tuple-element.148), channel_id=1, source_target_pairs={{0,8},{1,9},{2,10},{3,11},{4,12},{5,13},{6,14},{7,15},{8,0},{9,1},... | collective-permute-start | bytes 1769480 | tf_op jit(solution)/shard_map/ppermute | solution.py:514
  76.0 27.7 %collective-permute-start.19 = (bf16[4,192,384]{2,1,0:T(8,128)(2,1)}, bf16[4,192,384]{2,1,0:T(8,128)(2,1)}, u32[]{:S(2)}, u32[]{:S(2)}) collective-permute-start(bf16[4,192,384]{2,1,0:T(8,128)(2,1)} %get-tuple-element.146), channel_id=1, source_target_pairs={{0,16},{1,17},{2,18},{3,19},{4,20},{5,21},{6,22},{7,23},{8,24},{9,... | collective-permute-start | bytes 1769480 | tf_op jit(solution)/shard_map/ppermute | solution.py:514
  77.3 21.4 %collective-permute-start.15 = (bf16[3,384,128]{2,1,0:T(8,128)(2,1)S(1)}, bf16[3,384,128]{2,1,0:T(8,128)(2,1)}, u32[]{:S(2)}, u32[]{:S(2)}) collective-permute-start(bf16[3,384,128]{2,1,0:T(8,128)(2,1)S(1)} %pad_maximum_fusion.16), channel_id=1, source_target_pairs={{0,4},{1,5},{2,6},{3,7},{4,0},{5,1},{6,2},{7,3},{8,12},{9,13},{10,... | collective-permute-start | bytes 884744 | tf_op jit(solution)/shard_map/ppermute | solution.py:514
  78.0 20.7 %collective-permute-start.14 = (bf16[3,384,128]{2,1,0:T(8,128)(2,1)S(1)}, bf16[3,384,128]{2,1,0:T(8,128)(2,1)}, u32[]{:S(2)}, u32[]{:S(2)}) collective-permute-start(bf16[3,384,128]{2,1,0:T(8,128)(2,1)S(1)} %pad_maximum_fusion.16), channel_id=1, source_target_pairs={{0,2},{1,3},{2,4},{3,5},{4,6},{5,7},{6,0},{7,1},{8,10},{9,11},{10,... | collective-permute-start | bytes 884744 | tf_op jit(solution)/shard_map/ppermute | solution.py:514
  111.8 28.2 %collective-permute-start.20 = (bf16[2,4,192,384]{3,2,1,0:T(8,128)(2,1)}, bf16[2,4,192,384]{3,2,1,0:T(8,128)(2,1)}, u32[]{:S(2)}, u32[]{:S(2)}) collective-permute-start(bf16[2,4,192,384]{3,2,1,0:T(8,128)(2,1)} %pad_maximum_fusion.5), channel_id=1, source_target_pairs={{0,16},{1,17},{2,18},{3,19},{4,20},{5,21},{6,22},{7,23},{8,24},{9,... | collective-permute-start | bytes 3538952 | tf_op jit(solution)/shard_map/ppermute | solution.py:514
  113.2 30.1 %collective-permute-start.21 = (bf16[2,4,192,384]{3,2,1,0:T(8,128)(2,1)}, bf16[2,4,192,384]{3,2,1,0:T(8,128)(2,1)}, u32[]{:S(2)}, u32[]{:S(2)}) collective-permute-start(bf16[2,4,192,384]{3,2,1,0:T(8,128)(2,1)} %pad_maximum_fusion.6), channel_id=1, source_target_pairs={{0,8},{1,9},{2,10},{3,11},{4,12},{5,13},{6,14},{7,15},{8,0},{9,1},... | collective-permute-start | bytes 3538952 | tf_op jit(solution)/shard_map/ppermute | solution.py:514
  167.8 18.2 %collective-permute-start.24 = (bf16[4,4,192,384]{3,2,1,0:T(8,128)(2,1)}, bf16[4,4,192,384]{3,2,1,0:T(8,128)(2,1)}, u32[]{:S(2)}, u32[]{:S(2)}) collective-permute-start(bf16[4,4,192,384]{3,2,1,0:T(8,128)(2,1)} %get-tuple-element.68), channel_id=1, source_target_pairs={{0,1},{1,0},{2,3},{3,2},{4,5},{5,4},{6,7},{7,6},{8,9},{9,8},{10,11... | collective-permute-start | bytes 7077896 | tf_op jit(solution)/shard_map/ppermute | solution.py:514
  168.2 17.7 %collective-permute-start.25 = (bf16[4,4,192,384]{3,2,1,0:T(8,128)(2,1)}, bf16[4,4,192,384]{3,2,1,0:T(8,128)(2,1)}, u32[]{:S(2)}, u32[]{:S(2)}) collective-permute-start(bf16[4,4,192,384]{3,2,1,0:T(8,128)(2,1)} %get-tuple-element.69), channel_id=1, source_target_pairs={{0,1},{1,0},{2,3},{3,2},{4,5},{5,4},{6,7},{7,6},{8,9},{9,8},{10,11... | collective-permute-start | bytes 7077896 | tf_op jit(solution)/shard_map/ppermute | solution.py:514
  189.1 28.6 %collective-permute-start.26 = (bf16[2,4,192,384]{3,2,1,0:T(8,128)(2,1)}, bf16[2,4,192,384]{3,2,1,0:T(8,128)(2,1)}, u32[]{:S(2)}, u32[]{:S(2)}) collective-permute-start(bf16[2,4,192,384]{3,2,1,0:T(8,128)(2,1)} %add_convert_fusion.1), channel_id=1, source_target_pairs={{0,16},{1,17},{2,18},{3,19},{4,20},{5,21},{6,22},{7,23},{8,24},{9,... | collective-permute-start | bytes 3538952 | tf_op jit(solution)/shard_map/ppermute | solution.py:514
  193.2 28.3 %collective-permute-start.27 = (bf16[2,4,192,384]{3,2,1,0:T(8,128)(2,1)}, bf16[2,4,192,384]{3,2,1,0:T(8,128)(2,1)}, u32[]{:S(2)}, u32[]{:S(2)}) collective-permute-start(bf16[2,4,192,384]{3,2,1,0:T(8,128)(2,1)} %add_convert_fusion), channel_id=1, source_target_pairs={{0,8},{1,9},{2,10},{3,11},{4,12},{5,13},{6,14},{7,15},{8,0},{9,1},... | collective-permute-start | bytes 3538952 | tf_op jit(solution)/shard_map/ppermute | solution.py:514
  215.7 19.4 %collective-permute-start.34 = (bf16[4,4,192,128]{3,2,1,0:T(8,128)(2,1)}, bf16[4,4,192,128]{3,2,1,0:T(8,128)(2,1)}, u32[]{:S(2)}, u32[]{:S(2)}) collective-permute-start(bf16[4,4,192,128]{3,2,1,0:T(8,128)(2,1)} %get-tuple-element.84), channel_id=1, source_target_pairs={{0,1},{1,0},{2,3},{3,2},{4,5},{5,4},{6,7},{7,6},{8,9},{9,8},{10,11... | collective-permute-start | bytes 2359304 | tf_op jit(solution)/shard_map/ppermute | solution.py:514
  215.7 46.0 %collective-permute-start.31 = (bf16[4,4,384,128]{3,2,1,0:T(8,128)(2,1)}, bf16[4,4,384,128]{3,2,1,0:T(8,128)(2,1)}, u32[]{:S(2)}, u32[]{:S(2)}) collective-permute-start(bf16[4,4,384,128]{3,2,1,0:T(8,128)(2,1)} %get-tuple-element.81), channel_id=1, source_target_pairs={{0,1},{1,0},{2,3},{3,2},{4,5},{5,4},{6,7},{7,6},{8,9},{9,8},{10,11... | collective-permute-start | bytes 4718600 | tf_op jit(solution)/shard_map/ppermute | solution.py:514
  230.5 52.4 %collective-permute-start.28 = (bf16[4,4,192,128]{3,2,1,0:T(8,128)(2,1)S(1)}, bf16[4,4,192,128]{3,2,1,0:T(8,128)(2,1)S(1)}, u32[]{:S(2)}, u32[]{:S(2)}) collective-permute-start(bf16[4,4,192,128]{3,2,1,0:T(8,128)(2,1)S(1)} %get-tuple-element.79), channel_id=1, source_target_pairs={{0,1},{1,0},{2,3},{3,2},{4,5},{5,4},{6,7},{7,6},{8,9},{9,8},{10,11... | collective-permute-start | bytes 2359304 | tf_op jit(solution)/shard_map/ppermute | solution.py:514
  232.1 23.5 %collective-permute-start.42 = (bf16[3,384,128]{2,1,0:T(8,128)(2,1)S(1)}, bf16[3,384,128]{2,1,0:T(8,128)(2,1)S(1)}, u32[]{:S(2)}, u32[]{:S(2)}) collective-permute-start(bf16[3,384,128]{2,1,0:T(8,128)(2,1)S(1)} %get-tuple-element.124), channel_id=1, source_target_pairs={{0,4},{1,5},{2,6},{3,7},{4,0},{5,1},{6,2},{7,3},{8,12},{9,13},{10,... | collective-permute-start | bytes 884744 | tf_op jit(solution)/shard_map/ppermute | solution.py:514
  235.0 21.1 %collective-permute-start.41 = (bf16[3,384,128]{2,1,0:T(8,128)(2,1)S(1)}, bf16[3,384,128]{2,1,0:T(8,128)(2,1)S(1)}, u32[]{:S(2)}, u32[]{:S(2)}) collective-permute-start(bf16[3,384,128]{2,1,0:T(8,128)(2,1)S(1)} %get-tuple-element.122), channel_id=1, source_target_pairs={{0,6},{1,7},{2,0},{3,1},{4,2},{5,3},{6,4},{7,5},{8,14},{9,15},{10,... | collective-permute-start | bytes 884744 | tf_op jit(solution)/shard_map/ppermute | solution.py:514
  243.9 15.1 %collective-permute-start.35 = (bf16[2,4,192,128]{3,2,1,0:T(8,128)(2,1)S(1)}, bf16[2,4,192,128]{3,2,1,0:T(8,128)(2,1)S(1)}, u32[]{:S(2)}, u32[]{:S(2)}) collective-permute-start(bf16[2,4,192,128]{3,2,1,0:T(8,128)(2,1)S(1)} %fusion.3), channel_id=1, source_target_pairs={{0,8},{1,9},{2,10},{3,11},{4,12},{5,13},{6,14},{7,15},{8,0},{9,1},... | collective-permute-start | bytes 1179656 | tf_op jit(solution)/shard_map/ppermute | solution.py:514
  255.6 25.8 %collective-permute-start.47 = (bf16[4,192,384]{2,1,0:T(8,128)(2,1)S(1)}, bf16[4,192,384]{2,1,0:T(8,128)(2,1)S(1)}, u32[]{:S(2)}, u32[]{:S(2)}) collective-permute-start(bf16[4,192,384]{2,1,0:T(8,128)(2,1)S(1)} %fusion.1), channel_id=1, source_target_pairs={{0,16},{1,17},{2,18},{3,19},{4,20},{5,21},{6,22},{7,23},{8,24},{9,... | collective-permute-start | bytes 1769480 | tf_op jit(solution)/shard_map/ppermute | solution.py:514
  256.2 28.7 %collective-permute-start.46 = (bf16[4,192,384]{2,1,0:T(8,128)(2,1)S(1)}, bf16[4,192,384]{2,1,0:T(8,128)(2,1)S(1)}, u32[]{:S(2)}, u32[]{:S(2)}) collective-permute-start(bf16[4,192,384]{2,1,0:T(8,128)(2,1)S(1)} %fusion.2), channel_id=1, source_target_pairs={{0,8},{1,9},{2,10},{3,11},{4,12},{5,13},{6,14},{7,15},{8,0},{9,1},... | collective-permute-start | bytes 1769480 | tf_op jit(solution)/shard_map/ppermute | solution.py:514
  259.0 17.1 %collective-permute-start.44 = (bf16[2,384,128]{2,1,0:T(8,128)(2,1)S(1)}, bf16[2,384,128]{2,1,0:T(8,128)(2,1)S(1)}, u32[]{:S(2)}, u32[]{:S(2)}) collective-permute-start(bf16[2,384,128]{2,1,0:T(8,128)(2,1)S(1)} %pad_maximum_fusion.25), channel_id=1, source_target_pairs={{0,16},{1,17},{2,18},{3,19},{4,20},{5,21},{6,22},{7,23},{8,24},{9,... | collective-permute-start | bytes 589832 | tf_op jit(solution)/shard_map/ppermute | solution.py:514
  261.8 38.7 %collective-permute-start.36 = (bf16[4,192,128]{2,1,0:T(8,128)(2,1)S(1)}, bf16[4,192,128]{2,1,0:T(8,128)(2,1)S(1)}, u32[]{:S(2)}, u32[]{:S(2)}) collective-permute-start(bf16[4,192,128]{2,1,0:T(8,128)(2,1)S(1)} %fusion.7), channel_id=1, source_target_pairs={{0,16},{1,17},{2,18},{3,19},{4,20},{5,21},{6,22},{7,23},{8,24},{9,... | collective-permute-start | bytes 589832 | tf_op jit(solution)/shard_map/ppermute | solution.py:514
  281.1 16.6 %collective-permute-start.32 = (bf16[2,4,384,128]{3,2,1,0:T(8,128)(2,1)S(1)}, bf16[2,4,384,128]{3,2,1,0:T(8,128)(2,1)S(1)}, u32[]{:S(2)}, u32[]{:S(2)}) collective-permute-start(bf16[2,4,384,128]{3,2,1,0:T(8,128)(2,1)S(1)} %fusion), channel_id=1, source_target_pairs={{0,16},{1,17},{2,18},{3,19},{4,20},{5,21},{6,22},{7,23},{8,24},{9,... | collective-permute-start | bytes 2359304 | tf_op jit(solution)/shard_map/ppermute | solution.py:514
  286.4 30.3 %collective-permute-start.50 = (bf16[384,384]{1,0:T(8,128)(2,1)S(1)}, bf16[384,384]{1,0:T(8,128)(2,1)S(1)}, u32[]{:S(2)}, u32[]{:S(2)}) collective-permute-start(bf16[384,384]{1,0:T(8,128)(2,1)S(1)} %pad_maximum_fusion.20), channel_id=1, source_target_pairs={{0,2},{1,3},{2,4},{3,5},{4,6},{5,7},{6,0},{7,1},{8,10},{9,11},{10,... | collective-permute-start | bytes 884744 | tf_op jit(solution)/shard_map/ppermute | solution.py:514
  290.2 26.6 %collective-permute-start.49 = (bf16[384,384]{1,0:T(8,128)(2,1)S(1)}, bf16[384,384]{1,0:T(8,128)(2,1)S(1)}, u32[]{:S(2)}, u32[]{:S(2)}) collective-permute-start(bf16[384,384]{1,0:T(8,128)(2,1)S(1)} %pad_maximum_fusion.19), channel_id=1, source_target_pairs={{0,4},{1,5},{2,6},{3,7},{4,0},{5,1},{6,2},{7,3},{8,12},{9,13},{10,... | collective-permute-start | bytes 884744 | tf_op jit(solution)/shard_map/ppermute | solution.py:514
  293.7 23.1 %collective-permute-start.48 = (bf16[384,384]{1,0:T(8,128)(2,1)S(1)}, bf16[384,384]{1,0:T(8,128)(2,1)S(1)}, u32[]{:S(2)}, u32[]{:S(2)}) collective-permute-start(bf16[384,384]{1,0:T(8,128)(2,1)S(1)} %pad_maximum_fusion.18), channel_id=1, source_target_pairs={{0,6},{1,7},{2,0},{3,1},{4,2},{5,3},{6,4},{7,5},{8,14},{9,15},{10,... | collective-permute-start | bytes 884744 | tf_op jit(solution)/shard_map/ppermute | solution.py:514
  (39 other events, 441.0 us)

commit v5 on v4

--- a/solution.py
+++ b/solution.py
@@ -24,13 +24,14 @@
 GW = 2 * LN
 GN = CB // 4
 HA = H // 2
+ZS = 2
 HR = HA * QB
 TM = 128
 WIN = 3
 HZ = H // Z
 GC = 0.7978845608
 GA = 0.044715
-VMEM_LIMIT = 52 * 1024 * 1024
+VMEM_LIMIT = 32 * 1024 * 1024
 COST = 1 << 38
 
 F32 = jnp.float32
@@ -60,8 +61,7 @@
 
 
 def whole(shape):
-    zeros = (0,) * len(shape)
-    return pl.BlockSpec(shape, lambda i, t: zeros, pipeline_mode=pl.Buffered(1))
+    return pl.BlockSpec(memory_space=pltpu.VMEM)
 
 
 def rows(width):
@@ -69,8 +69,7 @@
 
 
 def out_whole(shape):
-    zeros = (0,) * len(shape)
-    return pl.BlockSpec(shape, lambda i, t: zeros)
+    return pl.BlockSpec(memory_space=pltpu.VMEM)
 
 
 def tab_a(t, g):
@@ -111,17 +110,17 @@
     return [jnp.logical_and(col >= HS * i, col < HS * (i + 1)) for i in range(HZ)]
 
 
-def halves(ref, core, lead=None):
-    lo = pl.multiple_of(core * QB, QB)
-    hi = pl.multiple_of((1 - core) * QB, QB)
+def halves(ref, core, lead=None, base=0):
+    lo = pl.multiple_of(base + core * QB, QB)
+    hi = pl.multiple_of(base + (1 - core) * QB, QB)
     if lead is None:
         return jnp.concatenate([ref[pl.ds(lo, QB), :], ref[pl.ds(hi, QB), :]], axis=0)
     return jnp.concatenate([ref[lead, pl.ds(lo, QB), :], ref[lead, pl.ds(hi, QB), :]], axis=0)
 
 
-def put_halves(ref, core, val, lead=None):
-    lo = pl.multiple_of(core * QB, QB)
-    hi = pl.multiple_of((1 - core) * QB, QB)
+def put_halves(ref, core, val, lead=None, base=0):
+    lo = pl.multiple_of(base + core * QB, QB)
+    hi = pl.multiple_of(base + (1 - core) * QB, QB)
     if lead is None:
         ref[pl.ds(lo, QB), :] = val[:QB]
         ref[pl.ds(hi, QB), :] = val[QB:]
@@ -185,26 +184,44 @@
         if off + GN > LN:
             row = jnp.where(lane < off, dg[:, (tile + 1) * LN : (tile + 2) * LN], row)
         rows_of[g, z, c] = pltpu.roll(row, (CB - off) % LN, 1)
-    for g in range(G):
-        for z in range(Z):
+    for z in range(Z):
+        full = acc(z)
+        for g in range(G):
             for p, ref in ((0, keep), (1, send)):
-                blk = acc[z, g * DB : (g + 1) * DB, p * LN : (p + 1) * LN]
+                blk = full[g * DB : (g + 1) * DB, p * LN : (p + 1) * LN]
                 row = pick(t[0], p, rows_of[g, z, 0], rows_of[g, z, 1])
                 ref[tab_a(t, g), tab_z(t, z)] = blk.astype(BF16)
                 ref[tab_a(t, g), tab_z(t, z), 0:16, :] = jnp.where(spot, row, blk[:16]).astype(BF16)
 
 
+def by_rows(body):
+    def step(i, carry):
+        body(pl.ds(pl.multiple_of(i * TM, TM), TM))
+        return carry
+
+    lax.fori_loop(0, L // TM, step, 0)
+
+
 def values_body(t, x_ref, own_ref, oth_ref, n_ref, val_ref, gain_ref):
-    @pl.when(pl.program_id(0) == 0)
-    def _():
-        gain_ref[0:1, :] = gains_row(own_ref, oth_ref, t, 0)
-        gain_ref[1:2, :] = gains_row(own_ref, oth_ref, t, DB)
-
-    cen, rstd = norm_stats(x_ref[...].astype(F32))
-    low = (cen * rstd * gain_ref[0:1, :]).astype(BF16)
-    n_ref[...] = low
+    gain_ref[0:1, :] = gains_row(own_ref, oth_ref, t, 0)
+    gain_ref[1:2, :] = gains_row(own_ref, oth_ref, t, DB)
+
+    def norm(at):
+        cen, rstd = norm_stats(x_ref[at, :].astype(F32))
+        n_ref[at, :] = (cen * rstd * gain_ref[0:1, :]).astype(BF16)
+
+    by_rows(norm)
     for z in range(Z):
-        val_ref[z] = dot(low, weight_z(own_ref, oth_ref, t, z, 0), 1, 0).astype(BF16)
+        val_ref[z] = dot(n_ref[...], weight_z(own_ref, oth_ref, t, z, 0), 1, 0).astype(BF16)
+
+
+def probs_of(units, t, m, z, mask):
+    parts = []
+    for i in range(HZ):
+        e = exp_scores(*units, t, m, HZ * z + i, mask)
+        inv = 1.0 / jnp.sum(e, axis=-1, keepdims=True)
+        parts.append(e * inv)
+    return parts
 
 
 def mixer_body(
@@ -213,24 +230,33 @@
 ):
     m = pl.program_id(0)
     core = t[0]
+    base = m * TM
     k0 = pl.multiple_of(window(m) * KB, KB)
     mask = halves(dq_ref, core) == dk_ref[:, pl.ds(k0, WIN * KB)]
     heads = head_masks(core, TM)
-    acc = halves(x_ref, core).astype(F32)
     for z in range(Z):
         win = val_ref[z, pl.ds(k0, WIN * KB), :]
+        prob = probs_of((a_own, a_oth, b_own, b_oth), t, m, z, mask)
+        part = dot(jnp.concatenate([p.astype(BF16) for p in prob], axis=0), win, 1, 0)
         out = jnp.zeros((TM, GW), F32)
         for i in range(HZ):
-            e = exp_scores(a_own, a_oth, b_own, b_oth, t, m, HZ * z + i, mask)
-            inv = 1.0 / jnp.sum(e, axis=-1, keepdims=True)
-            part = dot((e * inv).astype(BF16), win, 1, 0)
-            out = jnp.where(heads[i], part, out)
-        low = out.astype(BF16)
-        put_halves(mix_ref, core, low, z)
-        acc = acc + dot(low, weight_z(w_own, w_oth, t, z, DB), 1, 1)
-    put_halves(mid_ref, core, acc)
-    cen, rstd = norm_stats(acc)
-    put_halves(n_ref, core, (cen * rstd * gain_ref[1:2, :]).astype(BF16))
+            out = jnp.where(heads[i], part[i * TM : (i + 1) * TM], out)
+        put_halves(mix_ref, core, out.astype(BF16), z, base)
+
+    @pl.when(m == Z - 1)
+    def _():
+        acc = dot(mix_ref[0], weight_z(w_own, w_oth, t, 0, DB), 1, 1)
+        for z in range(1, Z):
+            acc = acc + dot(mix_ref[z], weight_z(w_own, w_oth, t, z, DB), 1, 1)
+        mid_ref[...] = acc
+
+        def norm(at):
+            mid = x_ref[at, :].astype(F32) + mid_ref[at, :]
+            mid_ref[at, :] = mid
+            cen, rstd = norm_stats(mid)
+            n_ref[at, :] = (cen * rstd * gain_ref[1:2, :]).astype(BF16)
+
+        by_rows(norm)
 
 
 def ffn_body(first, last, t, n_ref, c_ref, u_ref, d_ref, *refs):
@@ -245,8 +271,12 @@
     j = pl.program_id(0)
     n = n_ref[...]
     cot = c_ref[...]
-    up_w = jnp.concatenate([u_ref[tab_b(t, g), 0] for g in range(G)], axis=0)
-    dn_w = jnp.concatenate([d_ref[tab_a(t, g), 0] for g in range(G)], axis=0)
+    up_w = jnp.concatenate(
+        [jnp.concatenate([u_ref[tab_b(t, g), i] for g in range(G)], axis=0) for i in range(ZS)], axis=1
+    )
+    dn_w = jnp.concatenate(
+        [jnp.concatenate([d_ref[tab_a(t, g), i] for g in range(G)], axis=0) for i in range(ZS)], axis=1
+    )
 
     @pl.when(j == 0)
     def _():
@@ -269,12 +299,14 @@
     gu = dot(n, up_g, 0, 0).astype(BF16)
     b_ref[...] += dot(up_g, up_w, 1, 1)
     for g in range(G):
-        gu_ref[tab_b(t, g), 0] = gu[g * DB : (g + 1) * DB]
-        gd_ref[tab_a(t, g), 0] = gd[g * DB : (g + 1) * DB]
+        for i in range(ZS):
+            part = slice(g * DB, (g + 1) * DB), slice(i * FB, (i + 1) * FB)
+            gu_ref[tab_b(t, g), i] = gu[part]
+            gd_ref[tab_a(t, g), i] = gd[part]
     if last:
         lo_ref = refs[4]
 
-        @pl.when(j == Z - 1)
+        @pl.when(j == Z // ZS - 1)
         def _():
             lo_ref[...] = (mid_ref[...] + a_ref[...]).astype(BF16)
 
@@ -293,46 +325,54 @@
 def mixer_back_body(
     t, dn_ref, mid_ref, c_ref, gain_ref, dq_ref, dk_ref, mix_ref, val_ref,
     a_own, a_oth, b_own, b_oth, w_own, w_oth,
-    mg_ref, ka_ref, sa_ref, kb_ref, sb_ref, ko_ref, so_ref, vg_ref, dg_acc, go_acc, vg_acc,
+    mg_ref, ka_ref, sa_ref, kb_ref, sb_ref, ko_ref, so_ref, vg_ref, dg_acc, br_ref, grad_ref, vg_acc,
 ):
     m = pl.program_id(0)
     core = t[0]
+    base = m * TM
     start = window(m)
     k0 = pl.multiple_of(start * KB, KB)
 
     @pl.when(m == 0)
     def _():
-        go_acc[...] = jnp.zeros_like(go_acc)
         vg_acc[...] = jnp.zeros_like(vg_acc)
         dg_acc[...] = jnp.zeros_like(dg_acc)
 
-    cen, rstd = norm_stats(halves(mid_ref, core))
-    dv, dg = norm_back(cen, rstd, gain_ref[1:2, :], halves(dn_ref, core))
-    dg_acc[0:1, :] += dg
-    mid_grad = halves(c_ref, core).astype(F32) + dv
-    put_halves(mg_ref, core, mid_grad)
-    branch = mid_grad.astype(BF16)
+        def norm(at):
+            cen, rstd = norm_stats(mid_ref[at, :])
+            dv, dg = norm_back(cen, rstd, gain_ref[1:2, :], dn_ref[at, :])
+            dg_acc[0:1, :] += dg
+            mid_grad = c_ref[at, :].astype(F32) + dv
+            mg_ref[at, :] = mid_grad
+            br_ref[at, :] = mid_grad.astype(BF16)
+
+        by_rows(norm)
+        branch = br_ref[...]
+        for z in range(Z):
+            grad_ref[z] = dot(branch, weight_z(w_own, w_oth, t, z, DB), 1, 0).astype(BF16)
+        put_weight_grads(
+            lambda z: dot(branch, mix_ref[z], 0, 0), dg_acc[0:1, :], t, ko_ref, so_ref
+        )
+
     mask = halves(dq_ref, core) == dk_ref[:, pl.ds(k0, WIN * KB)]
     heads = head_masks(core, TM)
     rest = tab_b(t, jnp.where(start == 0, G - 1, 0))
     ka_ref[rest, 0] = jnp.zeros((HR, KB), BF16)
     sa_ref[rest, 0] = jnp.zeros((HR, KB), BF16)
     for z in range(Z):
-        go_acc[z] += dot(branch, halves(mix_ref, core, z), 0, 0)
-        grad = dot(branch, weight_z(w_own, w_oth, t, z, DB), 1, 0)
-        grad = grad.astype(BF16).astype(F32)
+        grad = halves(grad_ref, core, z, base)
+        mine = jnp.concatenate(
+            [jnp.where(heads[i], grad, jnp.zeros_like(grad)) for i in range(HZ)], axis=0
+        )
         win = val_ref[z, pl.ds(k0, WIN * KB), :]
-        total = jnp.zeros((WIN * KB, GW), F32)
+        prob = probs_of((a_own, a_oth, b_own, b_oth), t, m, z, mask)
+        dp = dot(mine, win, 1, 1)
+        low = jnp.concatenate([p.astype(BF16) for p in prob], axis=0)
+        vg_acc[z, pl.ds(k0, WIN * KB), :] += dot(low, mine, 0, 0)
         for i in range(HZ):
             head = HZ * z + i
-            e = exp_scores(a_own, a_oth, b_own, b_oth, t, m, head, mask)
-            inv = 1.0 / jnp.sum(e, axis=-1, keepdims=True)
-            prob = e * inv
-            mine = jnp.where(heads[i], grad, 0.0).astype(BF16)
-            total = total + dot(prob.astype(BF16), mine, 0, 0)
-            dp = dot(mine, win, 1, 1)
-            pd = prob * dp
-            ds = (pd - prob * jnp.sum(pd, axis=-1, keepdims=True)).astype(BF16)
+            pd = prob[i] * dp[i * TM : (i + 1) * TM]
+            ds = (pd - prob[i] * jnp.sum(pd, axis=-1, keepdims=True)).astype(BF16)
             for k in range(WIN):
                 for p, (ra, rb) in enumerate(((ka_ref, kb_ref), (sa_ref, sb_ref))):
                     blk = ds[p * QB : (p + 1) * QB, k * KB : (k + 1) * KB]
@@ -341,38 +381,30 @@
                     else:
                         h = head - HA
                         rb[0, k, h * QB : (h + 1) * QB, :] = blk
-        vg_acc[z, pl.ds(k0, WIN * KB), :] += total
 
     @pl.when(m == Z - 1)
     def _():
         vg_ref[...] = vg_acc[...].astype(BF16)
-        put_weight_grads(go_acc, dg_acc[0:1, :], t, ko_ref, so_ref)
 
 
 def last_body(
-    t, x_ref, gain_ref, n_ref, vg_ref, w_own, w_oth, mg_ref, gi_ref, kv_ref, sv_ref, dg_acc, gv_acc
+    t, x_ref, gain_ref, n_ref, vg_ref, w_own, w_oth, mg_ref, gi_ref, kv_ref, sv_ref, dg_acc, dn_ref
 ):
-    m = pl.program_id(0)
-
-    @pl.when(m == 0)
-    def _():
-        gv_acc[...] = jnp.zeros_like(gv_acc)
-        dg_acc[...] = jnp.zeros_like(dg_acc)
-
+    dg_acc[...] = jnp.zeros_like(dg_acc)
+    acc = dot(vg_ref[0], weight_z(w_own, w_oth, t, 0, 0), 1, 1)
+    for z in range(1, Z):
+        acc = acc + dot(vg_ref[z], weight_z(w_own, w_oth, t, z, 0), 1, 1)
+    dn_ref[...] = acc
+
+    def norm(at):
+        cen, rstd = norm_stats(x_ref[at, :].astype(F32))
+        dv, dg = norm_back(cen, rstd, gain_ref[0:1, :], dn_ref[at, :])
+        dg_acc[0:1, :] += dg
+        gi_ref[at, :] = mg_ref[at, :] + dv
+
+    by_rows(norm)
     low = n_ref[...]
-    dn = jnp.zeros((TM, D), F32)
-    for z in range(Z):
-        vg = vg_ref[z]
-        gv_acc[z] += dot(low, vg, 0, 0)
-        dn = dn + dot(vg, weight_z(w_own, w_oth, t, z, 0), 1, 1)
-    cen, rstd = norm_stats(x_ref[...].astype(F32))
-    dv, dg = norm_back(cen, rstd, gain_ref[0:1, :], dn)
-    dg_acc[0:1, :] += dg
-    gi_ref[...] = mg_ref[...] + dv
-
-    @pl.when(m == Z - 1)
-    def _():
-        put_weight_grads(gv_acc, dg_acc[0:1, :], t, kv_ref, sv_ref)
+    put_weight_grads(lambda z: dot(low, vg_ref[z], 0, 0), dg_acc[0:1, :], t, kv_ref, sv_ref)
 
 
 def sds(shape, dtype):
@@ -390,9 +422,9 @@
 def run_values(tab, x, w):
     return call(
         values_body,
-        (L // TM,),
-        [rows(D), whole(W_SHAPE), whole(W_SHAPE)],
-        [rows(D), Z_ROWS, out_whole((8, D))],
+        (1,),
+        [whole((L, D)), whole(W_SHAPE), whole(W_SHAPE)],
+        [out_whole((L, D)), out_whole((Z, L, GW)), out_whole((8, D))],
         [sds((L, D), BF16), sds((Z, L, GW), BF16), sds((8, D), F32)],
         flops=2 * L * D * Z * GW,
         nbytes=6 << 20,
@@ -404,19 +436,20 @@
         mixer_body,
         (L // TM,),
         [
-            rows(D), whole((8, D)), rows(1), whole((1, L)), whole((Z, L, GW)),
+            whole((L, D)), whole((8, D)), rows(1), whole((1, L)), whole((Z, L, GW)),
             whole(A_SHAPE), whole(A_SHAPE), whole(B_SHAPE), whole(B_SHAPE),
             whole(W_SHAPE), whole(W_SHAPE),
         ],
-        [Z_ROWS, rows(D), rows(D)],
+        [out_whole((Z, L, GW)), out_whole((L, D)), out_whole((L, D))],
         [sds((Z, L, GW), BF16), sds((L, D), F32), sds((L, D), BF16)],
         flops=2 * L * D * Z * GW + 2 * H * L * WIN * KB * GW,
         nbytes=14 << 20,
     )(tab, x, gain, dq, dk, vals, *a, *b, *w)
 
+
 def run_ffn(tab, n, cot, u_w, d_w, acc=None, mid=None):
     first, last = acc is None, mid is not None
-    blk = pl.BlockSpec((G, 1, DB, FB), lambda i, t: (0, i, 0, 0))
+    blk = pl.BlockSpec((G, ZS, DB, FB), lambda i, t: (0, i, 0, 0))
     in_specs = [whole((L, D)), whole((L, D)), blk, blk]
     args = [tab, n, cot, u_w, d_w]
     if not first:
@@ -443,7 +476,7 @@
         ffn_body(first, last, t, *refs)
 
     return call(
-        body, (Z,), in_specs, out_specs, outs, scratch, flops=6 * L * D * FF, nbytes=20 << 20
+        body, (Z // ZS,), in_specs, out_specs, outs, scratch, flops=6 * L * D * FF, nbytes=20 << 20
     )(*args)
 
 
@@ -454,16 +487,19 @@
         mixer_back_body,
         (L // TM,),
         [
-            rows(D), rows(D), rows(D), whole((8, D)), rows(1), whole((1, L)), Z_ROWS,
-            whole((Z, L, GW)), whole(A_SHAPE), whole(A_SHAPE), whole(B_SHAPE), whole(B_SHAPE),
+            whole((L, D)), whole((L, D)), whole((L, D)), whole((8, D)), rows(1), whole((1, L)),
+            whole((Z, L, GW)), whole((Z, L, GW)), whole(A_SHAPE), whole(A_SHAPE), whole(B_SHAPE), whole(B_SHAPE),
             whole(W_SHAPE), whole(W_SHAPE),
         ],
-        [rows(D), blk_a, blk_a, blk_b, blk_b, out_whole(V_SHAPE), out_whole(V_SHAPE), out_whole((Z, L, GW))],
+        [out_whole((L, D)), blk_a, blk_a, blk_b, blk_b, out_whole(V_SHAPE), out_whole(V_SHAPE), out_whole((Z, L, GW))],
         [
             sds((L, D), F32), sds(A_SHAPE, BF16), sds(A_SHAPE, BF16), sds(B_SHAPE, BF16),
             sds(B_SHAPE, BF16), sds(V_SHAPE, BF16), sds(V_SHAPE, BF16), sds((Z, L, GW), BF16),
         ],
-        scratch=(pltpu.VMEM((8, D), F32), pltpu.VMEM((Z, D, GW), F32), pltpu.VMEM((Z, L, GW), F32)),
+        scratch=(
+            pltpu.VMEM((8, D), F32), pltpu.VMEM((L, D), BF16), pltpu.VMEM((Z, L, GW), BF16),
+            pltpu.VMEM((Z, L, GW), F32),
+        ),
         flops=4 * L * D * Z * GW + 6 * H * L * WIN * KB * GW,
         nbytes=28 << 20,
     )(tab, dn, mid, cot, gain, dq, dk, mixed, vals, *a, *b, *w)
@@ -472,11 +508,14 @@
 def run_last(tab, x, gain, low, vg, w, mid_grad):
     return call(
         last_body,
-        (L // TM,),
-        [rows(D), whole((8, D)), rows(D), Z_ROWS, whole(W_SHAPE), whole(W_SHAPE), rows(D)],
-        [rows(D), out_whole(V_SHAPE), out_whole(V_SHAPE)],
+        (1,),
+        [
+            whole((L, D)), whole((8, D)), whole((L, D)), whole((Z, L, GW)), whole(W_SHAPE),
+            whole(W_SHAPE), whole((L, D)),
+        ],
+        [out_whole((L, D)), out_whole(V_SHAPE), out_whole(V_SHAPE)],
         [sds((L, D), F32), sds(V_SHAPE, BF16), sds(V_SHAPE, BF16)],
-        scratch=(pltpu.VMEM((8, D), F32), pltpu.VMEM((Z, D, GW), F32)),
+        scratch=(pltpu.VMEM((8, D), F32), pltpu.VMEM((L, D), F32)),
         flops=4 * L * D * Z * GW,
         nbytes=12 << 20,
     )(tab, x, gain, low, vg, *w, mid_grad)
@@ -509,12 +548,12 @@
                     for c in range(sizes["c"]):
                         src = {"y": y, "x": x, "z": z, "c": c}
                         dst = dict(src)
-                        dst[axis] = (src[axis] + k) % sizes[axis]
+                        dst[axis] = src[axis] ^ k
                         pairs.append(tuple((p["y"] * 2 + p["x"]) * self.gy + p["z"] * 2 + p["c"] for p in (src, dst)))
         return lax.ppermute(val, ("gx", "gy"), pairs)
 
     def rel(self, axis, v):
-        return (self.at[axis] - v) % self.size[axis]
+        return self.at[axis] ^ v
 
     def spread(self, val, axis):
         return jnp.stack([val] + [self.fetch(val, axis, k) for k in range(1, self.size[axis])])
@@ -525,7 +564,7 @@
         got = []
         for k in range(1, self.size[axis]):
             part = add_up([v[(0,) * (stage - born) + (k,)] for v, born in terms]).astype(BF16)
-            got.append((self.fetch(part, axis, -k), stage + 1))
+            got.append((self.fetch(part, axis, k), stage + 1))
         return terms + got
 
     def total(self, terms, stage):
@@ -541,7 +580,7 @@
                 add_up([v[(0,) * (2 - born) + (k,)] for v, born in terms]).astype(BF16)
                 for terms in groups
             ]
-            got.append(self.fetch(jnp.concatenate(parts, axis=0), axis, -k))
+            got.append(self.fetch(jnp.concatenate(parts, axis=0), axis, k))
         out, at_row = [], 0
         for terms in groups:
             n = terms[0][0].shape[-2]
@@ -596,19 +635,20 @@
     b = jnp.stack([lax.dynamic_index_in_dim(b, order[start + i], 0, False) for i in range(WIN)])
     a, w = (jnp.stack([v[i * HR : (i + 1) * HR] for v in c1]) for i in range(2))
     ffn = along_z(after(jnp.stack([up_w, down_w.T]), c1[1:]))
+    a, w = after((a, w), b)
     a, w = spread(a, "x"), spread(w, "y")
+    a, w = after((a, w), ffn[1])
     a, w = spread(a, "y").reshape(A_SHAPE), spread(w, "x").reshape(W_SHAPE)
+    a, w = after((a, w), ffn[2:])
     b = spread(after(b, ffn[1:]), "z")
-    ffn[1:] = after(ffn[1:], a, w)
     u, d = (jnp.stack([v[i] for v in ffn]) for i in range(2))
     w, a = both(w), both(a)
     low, vals, gain = run_values(tab, layer_in, w)
     u, d = spread(u, "x"), spread(d, "y")
-    b = both(b)
-    u, d = after((u, d), low)
+    b = both(b, u, d)
     u, d = spread(u, "y").reshape(F_SHAPE), spread(d, "x").reshape(F_SHAPE)
-    mixed, mid, n_two = run_mixer(tab, layer_in, gain, dq, dk, vals, a, b, w)
-    u, d = both(u, n_two), both(d, n_two)
+    mixed, mid, n_two = run_mixer(tab, layer_in, after(gain, u, d), dq, dk, vals, a, b, w)
+    u, d = both(u), both(d)
 
     def begin(keep, send):
         got = fetch(send, "c", 1)
@@ -626,13 +666,13 @@
         tab, n_grad, mid, cot, gain, dq, dk, mixed, vals, a, b, w
     )
     vg = after(vg, last(gu, gd))
-    ga, go, rb = begin(ka, sa), begin(ko, so), fetch(sb, "c", 1)
     gu, gd = grid.reduce(gu, 1, "x", sa), grid.reduce(gd, 1, "y", sa)
+    grad_in, kv, sv = run_last(tab, layer_in, gain, low, vg, w, mid_grad)
+    sa, sb, so = after((sa, sb, so), sv)
+    gv, ga, go, rb = begin(kv, sv), begin(ka, sa), begin(ko, so), fetch(sb, "c", 1)
     gb = grid.reduce([(kb, 2), (rb, 2)], 2, "z")
-    grad_in, kv, sv = run_last(tab, layer_in, gain, low, vg, w, mid_grad)
-    gv = begin(kv, sv)
-    ga = grid.reduce(ga, 0, "y", sv)
-    go = grid.reduce(go, 0, "x", sv)
+    ga = grid.reduce(ga, 0, "y")
+    go = grid.reduce(go, 0, "x")
     gu, gd = grid.reduce_joined((gu, gd), "z", last(gb))
     gv = grid.reduce(gv, 0, "x")
     wide = grid.total(gb, 3)

time: 335 us -> 313 us (0.934)
  Pallas kernels: 81.8 us -> 59.4 us
  starting transfers between devices: 66 us -> 72.3 us
  other arithmetic: 46 us -> 41.9 us
    pallas_call x6, Pallas kernels: 81.8 us -> 59.4 us  [the longest x2 25.5 us: run_ffn(): call(body, (Z // ZS,), in_specs, out_specs, outs, scratch, flops=6 * L *...]
    ppermute x51, starting transfers between devices: 66 us -> 72.3 us  [fetch(): return lax.ppermute(val, ('gx', 'gy'), pairs)]
    another operation x15 -> x13, other arithmetic: 17.4 us -> 13.6 us  [spread(): jnp.stack([val] + [self.fetch(val, axis, k) for k in range(1, self.size[a...]
  transfers between devices with their start and end apart: 51 -> 51, of which waited for: 21 -> 25; matrix products, arithmetic and copies ran while one was open for 12% -> 11% of each run, Pallas kernels for 20% -> 15%
where the time goes in v5:
time: 313 us; the launch traced here: 312 us
  waiting for transfers between devices  122 us (39%)
  starting transfers between devices  72.3 us (23%)
  Pallas kernels  59.4 us (19%)
  other arithmetic  41.9 us (13%)
  local copies, waits for them, and re-layouts  8.68 us (3%)
  between operations  7.15 us (2%)
    ppermute x51, waiting for transfers between devices, fetch(): return lax.ppermute(val, ('gx', 'gy'), pairs)  122 us
    ppermute x51, starting transfers between devices, fetch(): return lax.ppermute(val, ('gx', 'gy'), pairs)  72.3 us
    pallas_call x2, Pallas kernels, run_ffn(): call(body, (Z // ZS,), in_specs, out_specs, outs, scratch, flops=6 * L *...  25.5 us
    pallas_call x1, Pallas kernels, run_mixer_back(): call(mixer_back_body, (L // TM,), [whole((L, D)), whole((L, D)), whole((L...  16.1 us
    convert_element_type x12, other arithmetic, reduce(): add_up([v[(0,) * (stage - born) + (k,)] for v, born in terms]).astype(BF16)  14.4 us
    another operation x13, other arithmetic, spread(): jnp.stack([val] + [self.fetch(val, axis, k) for k in range(1, self.size[a...  13.6 us
    pallas_call x1, Pallas kernels, run_mixer(): call(mixer_body, (L // TM,), [whole((L, D)), whole((8, D)), rows(1), whol...  8.7 us
    pallas_call x1, Pallas kernels, run_last(): call(last_body, (1,), [whole((L, D)), whole((8, D)), whole((L, D)), whole...  6.37 us
  transfers between devices with their start and end apart: 51, of which 25 were waited for; matrix products, arithmetic and copies ran while one was open for 11% of the time, Pallas kernels for 15%

profile of v5, /device:TPU:0, one launch (start us, length us, event | category | flops | bytes accessed | tf_op | source)
XLA Modules:
  0.0 311.6 jit_solution(12193402539360235809)
XLA Ops:
  4.8 5.1 %collective-permute-start.2 = (bf16[768,128]{1,0:T(8,128)(2,1)S(1)}, bf16[768,128]{1,0:T(8,128)(2,1)S(1)}, u32[]{:S(2)}, u32[]{:S(2)}) collective-permute-start(bf16[768,128]{1,0:T(8,128)(2,1)S(1)} %maximum_maximum_fusion), channel_id=1, source_target_pairs={{0,6},{1,7},{2,4},{3,5},{4,2},{5,3},{6,0},{7,1},{8,14},{9,15},{10,... | collective-permute-start | bytes 589832 | tf_op jit(solution)/shard_map/ppermute | solution.py:553
  21.5 5.1 %collective-permute-done.1 = bf16[768,128]{1,0:T(8,128)(2,1)S(1)} collective-permute-done((bf16[768,128]{1,0:T(8,128)(2,1)S(1)}, bf16[768,128]{1,0:T(8,128)(2,1)S(1)}, u32[]{:S(2)}, u32[]{:S(2)}) %collective-permute-start.1) | collective-permute-done | bytes 196640 | tf_op jit(solution)/shard_map/ppermute | solution.py:553
  26.6 3.0 collective-permute-start.10
  35.1 4.8 %collective-permute-done.7 = bf16[2,192,384]{2,1,0:T(8,128)(2,1)S(1)} collective-permute-done((bf16[2,192,384]{2,1,0:T(8,128)(2,1)S(1)}, bf16[2,192,384]{2,1,0:T(8,128)(2,1)S(1)}, u32[]{:S(2)}, u32[]{:S(2)}) %collective-permute-start.7) | collective-permute-done | bytes 294944 | tf_op jit(solution)/shard_map/ppermute | solution.py:553
  44.3 3.6 %collective-permute-done.11 = bf16[2,192,384]{2,1,0:T(8,128)(2,1)S(1)} collective-permute-done((bf16[2,192,384]{2,1,0:T(8,128)(2,1)S(1)}, bf16[2,192,384]{2,1,0:T(8,128)(2,1)S(1)}, u32[]{:S(2)}, u32[]{:S(2)}) %collective-permute-start.11) | collective-permute-done | bytes 294944 | tf_op jit(solution)/shard_map/ppermute | solution.py:553
  53.7 9.6 %collective-permute-done.8 = bf16[2,4,384,128]{3,2,1,0:T(8,128)(2,1)S(1)} collective-permute-done((bf16[2,4,384,128]{3,2,1,0:T(8,128)(2,1)S(1)}, bf16[2,4,384,128]{3,2,1,0:T(8,128)(2,1)S(1)}, u32[]{:S(2)}, u32[]{:S(2)}) %collective-permute-start.8) | collective-permute-done | bytes 786464 | tf_op jit(solution)/shard_map/ppermute | solution.py:553
  64.5 4.0 %collective-permute-done.9 = bf16[2,4,384,128]{3,2,1,0:T(8,128)(2,1)S(1)} collective-permute-done((bf16[2,4,384,128]{3,2,1,0:T(8,128)(2,1)S(1)}, bf16[2,4,384,128]{3,2,1,0:T(8,128)(2,1)S(1)}, u32[]{:S(2)}, u32[]{:S(2)}) %collective-permute-start.9) | collective-permute-done | bytes 786464 | tf_op jit(solution)/shard_map/ppermute | solution.py:553
  68.8 9.6 %collective-permute-done.13 = bf16[4,192,384]{2,1,0:T(8,128)(2,1)S(1)} collective-permute-done((bf16[4,192,384]{2,1,0:T(8,128)(2,1)S(1)}, bf16[4,192,384]{2,1,0:T(8,128)(2,1)S(1)}, u32[]{:S(2)}, u32[]{:S(2)}) %collective-permute-start.13) | collective-permute-done | bytes 589856 | tf_op jit(solution)/shard_map/ppermute | solution.py:553
  86.3 6.8 %collective-permute-start.19 = (bf16[3,384,128]{2,1,0:T(8,128)(2,1)}, bf16[3,384,128]{2,1,0:T(8,128)(2,1)}, u32[]{:S(2)}, u32[]{:S(2)}) collective-permute-start(bf16[3,384,128]{2,1,0:T(8,128)(2,1)} %pad_maximum_fusion.16), channel_id=1, source_target_pairs={{0,4},{1,5},{2,6},{3,7},{4,0},{5,1},{6,2},{7,3},{8,12},{9,13},{10,... | collective-permute-start | bytes 884744 | tf_op jit(solution)/shard_map/ppermute | solution.py:553
  94.4 12.4 %collective-permute-start.18 = (bf16[3,384,128]{2,1,0:T(8,128)(2,1)}, bf16[3,384,128]{2,1,0:T(8,128)(2,1)}, u32[]{:S(2)}, u32[]{:S(2)}) collective-permute-start(bf16[3,384,128]{2,1,0:T(8,128)(2,1)} %pad_maximum_fusion.16), channel_id=1, source_target_pairs={{0,2},{1,3},{2,0},{3,1},{4,6},{5,7},{6,4},{7,5},{8,10},{9,11},{10,... | collective-permute-start | bytes 884744 | tf_op jit(solution)/shard_map/ppermute | solution.py:553
  107.1 5.5 %collective-permute-done.19 = bf16[3,384,128]{2,1,0:T(8,128)(2,1)} collective-permute-done((bf16[3,384,128]{2,1,0:T(8,128)(2,1)}, bf16[3,384,128]{2,1,0:T(8,128)(2,1)}, u32[]{:S(2)}, u32[]{:S(2)}) %collective-permute-start.19) | collective-permute-done | bytes 294944 | tf_op jit(solution)/shard_map/ppermute | solution.py:553
  112.5 6.2 %collective-permute-done.18 = bf16[3,384,128]{2,1,0:T(8,128)(2,1)} collective-permute-done((bf16[3,384,128]{2,1,0:T(8,128)(2,1)}, bf16[3,384,128]{2,1,0:T(8,128)(2,1)}, u32[]{:S(2)}, u32[]{:S(2)}) %collective-permute-start.18) | collective-permute-done | bytes 294944 | tf_op jit(solution)/shard_map/ppermute | solution.py:553
  121.7 3.1 pad_maximum_fusion
  124.8 3.1 pad_maximum_fusion.1
  131.2 8.7 %shard_map.170 = (bf16[4,512,256]{2,1,0:T(8,128)(2,1)S(1)}, f32[512,768]{1,0:T(8,128)S(1)}, bf16[512,768]{1,0:T(8,128)(2,1)S(1)}) custom-call(s32[13]{0:T(128)S(1)} %stack.221.t, bf16[512,768]{1,0:T(8,128)(2,1)S(1)} %copy-done.19, f32[8,768]{1,0:T(8,128)S(1)} %get-tuple-element.59.gain_ref, s32[512,1]{1,0:T(8,128)S(1)} %copy.28.dq_ref, ...), custom_call_target="tpu_custom_call" | custom-call | flops 274877906944 | bytes 14680064 | tf_op jit(solution)/shard_map/pallas_call | solution.py:435
  139.9 12.7 %shard_map.171 = (bf16[4,4,192,384]{3,2,1,0:T(8,128)(2,1)}, bf16[4,4,192,384]{3,2,1,0:T(8,128)(2,1)}, f32[512,768]{1,0:T(8,128)S(1)}, f32[512,768]{1,0:T(8,128)S(1)}) custom-call(s32[13]{0:T(128)S(1)} %stack.221.t, bf16[512,768]{1,0:T(8,128)(2,1)S(1)} %get-tuple-element.64.refs_0_, bf16[512,768]{1,0:T(8,128)(2,1)S(1)} %copy-done.18, ...), custom_call_target="tpu_custom_call" | custom-call | flops 274877906944 | bytes 20971520 | tf_op jit(solution)/shard_map/pallas_call | solution.py:478
  153.2 12.8 %shard_map.172 = (bf16[4,4,192,384]{3,2,1,0:T(8,128)(2,1)S(1)}, bf16[4,4,192,384]{3,2,1,0:T(8,128)(2,1)S(1)}, f32[512,768]{1,0:T(8,128)S(1)}, bf16[512,768]{1,0:T(8,128)(2,1)}) custom-call(s32[13]{0:T(128)S(1)} %stack.221.t, bf16[512,768]{1,0:T(8,128)(2,1)S(1)} %get-tuple-element.64.refs_0_, bf16[512,768]{1,0:T(8,128)(2,1)S(1)} %copy-done.18, ...), custom_call_target="tpu_custom_call" | custom-call | flops 274877906944 | bytes 20971520 | tf_op jit(solution)/shard_map/pallas_call | solution.py:478
  166.0 3.6 %add_convert_fusion.1 = bf16[2,4,192,384]{3,2,1,0:T(8,128)(2,1)} fusion(bf16[4,4,192,384]{3,2,1,0:T(8,128)(2,1)} %collective-permute-done.24, bf16[4,4,192,384]{3,2,1,0:T(8,128)(2,1)S(1)} %get-tuple-element.76), kind=kLoop, calls=%fused_computation.3 | loop fusion | flops 2359296 | bytes 3538944 | tf_op jit(solution)/shard_map/convert_element_type | solution.py:566
  170.0 2.8 add_convert_fusion
  173.4 16.1 %shard_map.173 = (f32[512,768]{1,0:T(8,128)S(1)}, bf16[4,4,384,128]{3,2,1,0:T(8,128)(2,1)S(1)}, bf16[4,4,384,128]{3,2,1,0:T(8,128)(2,1)S(1)}, bf16[4,3,384,128]{...) custom-call(s32[13]{0:T(128)S(1)} %stack.221.t, ...), custom_call_target="tpu_custom_call" | custom-call | flops 274877906944 | bytes 29360128 | tf_op jit(solution)/shard_map/pallas_call | solution.py:486
  189.5 8.3 %collective-permute-done.26 = bf16[2,4,192,384]{3,2,1,0:T(8,128)(2,1)} collective-permute-done((bf16[2,4,192,384]{3,2,1,0:T(8,128)(2,1)}, bf16[2,4,192,384]{3,2,1,0:T(8,128)(2,1)}, u32[]{:S(2)}, u32[]{:S(2)}) %collective-permute-start.26) | collective-permute-done | bytes 1179680 | tf_op jit(solution)/shard_map/ppermute | solution.py:553
  197.8 3.0 collective-permute-done.27
  205.3 6.4 %shard_map.174 = (f32[512,768]{1,0:T(8,128)}, bf16[4,4,192,128]{3,2,1,0:T(8,128)(2,1)S(1)}, bf16[4,4,192,128]{3,2,1,0:T(8,128)(2,1)}) custom-call(s32[13]{0:T(128)S(1)} %stack.221.t, bf16[512,768]{1,0:T(8,128)(2,1)S(1)} %copy-done.20, f32[8,768]{1,0:T(8,128)S(1)} %copy-done.25, bf16[512,768]{1,0:T(8,128)(2,1)S(1)} %get-tuple-element.69.n_ref, ...), custom_call_target="tpu_custom_call" | custom-call | flops 274877906944 | bytes 12582912 | tf_op jit(solution)/shard_map/pallas_call | solution.py:509
  226.1 6.7 %collective-permute-done.29 = bf16[2,4,192,128]{3,2,1,0:T(8,128)(2,1)S(1)} collective-permute-done((bf16[2,4,192,128]{3,2,1,0:T(8,128)(2,1)S(1)}, bf16[2,4,192,128]{3,2,1,0:T(8,128)(2,1)S(1)}, u32[]{:S(2)}, u32[]{:S(2)}) %collective-permute-start.29) | collective-permute-done | bytes 393248 | tf_op jit(solution)/shard_map/ppermute | solution.py:553
  233.7 4.3 %collective-permute-done.35 = bf16[2,4,192,128]{3,2,1,0:T(8,128)(2,1)S(1)} collective-permute-done((bf16[2,4,192,128]{3,2,1,0:T(8,128)(2,1)S(1)}, bf16[2,4,192,128]{3,2,1,0:T(8,128)(2,1)S(1)}, u32[]{:S(2)}, u32[]{:S(2)}) %collective-permute-start.35) | collective-permute-done | bytes 393248 | tf_op jit(solution)/shard_map/ppermute | solution.py:553
  239.7 5.3 %collective-permute-done.30 = bf16[4,192,128]{2,1,0:T(8,128)(2,1)S(1)} collective-permute-done((bf16[4,192,128]{2,1,0:T(8,128)(2,1)S(1)}, bf16[4,192,128]{2,1,0:T(8,128)(2,1)S(1)}, u32[]{:S(2)}, u32[]{:S(2)}) %collective-permute-start.30) | collective-permute-done | bytes 196640 | tf_op jit(solution)/shard_map/ppermute | solution.py:553
  247.4 5.3 %collective-permute-done.36 = bf16[4,192,128]{2,1,0:T(8,128)(2,1)S(1)} collective-permute-done((bf16[4,192,128]{2,1,0:T(8,128)(2,1)S(1)}, bf16[4,192,128]{2,1,0:T(8,128)(2,1)S(1)}, u32[]{:S(2)}, u32[]{:S(2)}) %collective-permute-start.36) | collective-permute-done | bytes 196640 | tf_op jit(solution)/shard_map/ppermute | solution.py:553
  258.2 10.8 %collective-permute-done.47 = bf16[4,192,384]{2,1,0:T(8,128)(2,1)S(1)} collective-permute-done((bf16[4,192,384]{2,1,0:T(8,128)(2,1)S(1)}, bf16[4,192,384]{2,1,0:T(8,128)(2,1)S(1)}, u32[]{:S(2)}, u32[]{:S(2)}) %collective-permute-start.47) | collective-permute-done | bytes 589856 | tf_op jit(solution)/shard_map/ppermute | solution.py:553
  275.2 7.0 %collective-permute-done.32 = bf16[2,4,384,128]{3,2,1,0:T(8,128)(2,1)S(1)} collective-permute-done((bf16[2,4,384,128]{3,2,1,0:T(8,128)(2,1)S(1)}, bf16[2,4,384,128]{3,2,1,0:T(8,128)(2,1)S(1)}, u32[]{:S(2)}, u32[]{:S(2)}) %collective-permute-start.32) | collective-permute-done | bytes 786464 | tf_op jit(solution)/shard_map/ppermute | solution.py:553
  285.3 7.5 %collective-permute-done.49 = bf16[384,384]{1,0:T(8,128)(2,1)S(1)} collective-permute-done((bf16[384,384]{1,0:T(8,128)(2,1)S(1)}, bf16[384,384]{1,0:T(8,128)(2,1)S(1)}, u32[]{:S(2)}, u32[]{:S(2)}) %collective-permute-start.49) | collective-permute-done | bytes 294944 | tf_op jit(solution)/shard_map/ppermute | solution.py:553
  299.9 3.1 collective-permute-done.39
  303.0 4.0 %collective-permute-done.38 = bf16[768,128]{1,0:T(8,128)(2,1)S(1)} collective-permute-done((bf16[768,128]{1,0:T(8,128)(2,1)S(1)}, bf16[768,128]{1,0:T(8,128)(2,1)S(1)}, u32[]{:S(2)}, u32[]{:S(2)}) %collective-permute-start.38) | collective-permute-done | bytes 196640 | tf_op jit(solution)/shard_map/ppermute | solution.py:553
  (210 shorter events, 94.2 us)
Async XLA Ops:
  4.8 16.7 %collective-permute-start.2 = (bf16[768,128]{1,0:T(8,128)(2,1)S(1)}, bf16[768,128]{1,0:T(8,128)(2,1)S(1)}, u32[]{:S(2)}, u32[]{:S(2)}) collective-permute-start(bf16[768,128]{1,0:T(8,128)(2,1)S(1)} %maximum_maximum_fusion), channel_id=1, source_target_pairs={{0,6},{1,7},{2,4},{3,5},{4,2},{5,3},{6,0},{7,1},{8,14},{9,15},{10,... | collective-permute-start | bytes 589832 | tf_op jit(solution)/shard_map/ppermute | solution.py:553
  9.9 16.7 %collective-permute-start.1 = (bf16[768,128]{1,0:T(8,128)(2,1)S(1)}, bf16[768,128]{1,0:T(8,128)(2,1)S(1)}, u32[]{:S(2)}, u32[]{:S(2)}) collective-permute-start(bf16[768,128]{1,0:T(8,128)(2,1)S(1)} %maximum_maximum_fusion), channel_id=1, source_target_pairs={{0,4},{1,5},{2,6},{3,7},{4,0},{5,1},{6,2},{7,3},{8,12},{9,13},{10,... | collective-permute-start | bytes 589832 | tf_op jit(solution)/shard_map/ppermute | solution.py:553
  9.9 16.7 %collective-permute-start = (bf16[768,128]{1,0:T(8,128)(2,1)S(1)}, bf16[768,128]{1,0:T(8,128)(2,1)S(1)}, u32[]{:S(2)}, u32[]{:S(2)}) collective-permute-start(bf16[768,128]{1,0:T(8,128)(2,1)S(1)} %maximum_maximum_fusion), channel_id=1, source_target_pairs={{0,2},{1,3},{2,0},{3,1},{4,6},{5,7},{6,4},{7,5},{8,10},{9,11},{10,... | collective-permute-start | bytes 589832 | tf_op jit(solution)/shard_map/ppermute | solution.py:553
  26.6 13.3 %collective-permute-start.7 = (bf16[2,192,384]{2,1,0:T(8,128)(2,1)S(1)}, bf16[2,192,384]{2,1,0:T(8,128)(2,1)S(1)}, u32[]{:S(2)}, u32[]{:S(2)}) collective-permute-start(bf16[2,192,384]{2,1,0:T(8,128)(2,1)S(1)} %pad_maximum_fusion.17), channel_id=1, source_target_pairs={{0,2},{1,3},{2,0},{3,1},{4,6},{5,7},{6,4},{7,5},{8,10},{9,11},{10,... | collective-permute-start | bytes 884744 | tf_op jit(solution)/shard_map/ppermute | solution.py:553
  26.6 23.6 %collective-permute-start.10 = (bf16[2,192,384]{2,1,0:T(8,128)(2,1)S(1)}, bf16[2,192,384]{2,1,0:T(8,128)(2,1)S(1)}, u32[]{:S(2)}, u32[]{:S(2)}) collective-permute-start(bf16[2,192,384]{2,1,0:T(8,128)(2,1)S(1)} %pad_maximum_fusion.17), channel_id=1, source_target_pairs={{0,4},{1,5},{2,6},{3,7},{4,0},{5,1},{6,2},{7,3},{8,12},{9,13},{10,... | collective-permute-start | bytes 884744 | tf_op jit(solution)/shard_map/ppermute | solution.py:553
  29.6 18.3 %collective-permute-start.11 = (bf16[2,192,384]{2,1,0:T(8,128)(2,1)S(1)}, bf16[2,192,384]{2,1,0:T(8,128)(2,1)S(1)}, u32[]{:S(2)}, u32[]{:S(2)}) collective-permute-start(bf16[2,192,384]{2,1,0:T(8,128)(2,1)S(1)} %pad_maximum_fusion.17), channel_id=1, source_target_pairs={{0,6},{1,7},{2,4},{3,5},{4,2},{5,3},{6,0},{7,1},{8,14},{9,15},{10,... | collective-permute-start | bytes 884744 | tf_op jit(solution)/shard_map/ppermute | solution.py:553
  42.7 20.5 %collective-permute-start.8 = (bf16[2,4,384,128]{3,2,1,0:T(8,128)(2,1)S(1)}, bf16[2,4,384,128]{3,2,1,0:T(8,128)(2,1)S(1)}, u32[]{:S(2)}, u32[]{:S(2)}) collective-permute-start(bf16[2,4,384,128]{3,2,1,0:T(8,128)(2,1)S(1)} %pad_maximum_fusion.7), channel_id=1, source_target_pairs={{0,16},{1,17},{2,18},{3,19},{4,20},{5,21},{6,22},{7,23},{8,24},{9,... | collective-permute-start | bytes 2359304 | tf_op jit(solution)/shard_map/ppermute | solution.py:553
  48.0 20.5 %collective-permute-start.9 = (bf16[2,4,384,128]{3,2,1,0:T(8,128)(2,1)S(1)}, bf16[2,4,384,128]{3,2,1,0:T(8,128)(2,1)S(1)}, u32[]{:S(2)}, u32[]{:S(2)}) collective-permute-start(bf16[2,4,384,128]{3,2,1,0:T(8,128)(2,1)S(1)} %pad_maximum_fusion.8), channel_id=1, source_target_pairs={{0,8},{1,9},{2,10},{3,11},{4,12},{5,13},{6,14},{7,15},{8,0},{9,1},... | collective-permute-start | bytes 2359304 | tf_op jit(solution)/shard_map/ppermute | solution.py:553
  50.4 28.0 %collective-permute-start.13 = (bf16[4,192,384]{2,1,0:T(8,128)(2,1)S(1)}, bf16[4,192,384]{2,1,0:T(8,128)(2,1)S(1)}, u32[]{:S(2)}, u32[]{:S(2)}) collective-permute-start(bf16[4,192,384]{2,1,0:T(8,128)(2,1)S(1)} %get-tuple-element.152), channel_id=1, source_target_pairs={{0,8},{1,9},{2,10},{3,11},{4,12},{5,13},{6,14},{7,15},{8,0},{9,1},... | collective-permute-start | bytes 1769480 | tf_op jit(solution)/shard_map/ppermute | solution.py:553
  52.1 29.5 %collective-permute-start.15 = (bf16[4,192,384]{2,1,0:T(8,128)(2,1)S(1)}, bf16[4,192,384]{2,1,0:T(8,128)(2,1)S(1)}, u32[]{:S(2)}, u32[]{:S(2)}) collective-permute-start(bf16[4,192,384]{2,1,0:T(8,128)(2,1)S(1)} %get-tuple-element.150), channel_id=1, source_target_pairs={{0,16},{1,17},{2,18},{3,19},{4,20},{5,21},{6,22},{7,23},{8,24},{9,... | collective-permute-start | bytes 1769480 | tf_op jit(solution)/shard_map/ppermute | solution.py:553
  68.7 59.6 %collective-permute-start.12 = (bf16[4,4,384,128]{3,2,1,0:T(8,128)(2,1)S(1)}, bf16[4,4,384,128]{3,2,1,0:T(8,128)(2,1)S(1)}, u32[]{:S(2)}, u32[]{:S(2)}) collective-permute-start(bf16[4,4,384,128]{3,2,1,0:T(8,128)(2,1)S(1)} %bitcast.384), channel_id=1, source_target_pairs={{0,1},{1,0},{2,3},{3,2},{4,5},{5,4},{6,7},{7,6},{8,9},{9,8},{10,11... | collective-permute-start | bytes 4718600 | tf_op jit(solution)/shard_map/ppermute | solution.py:553
  80.0 41.7 %collective-permute-start.14 = (bf16[2,4,192,384]{3,2,1,0:T(8,128)(2,1)}, bf16[2,4,192,384]{3,2,1,0:T(8,128)(2,1)}, u32[]{:S(2)}, u32[]{:S(2)}) collective-permute-start(bf16[2,4,192,384]{3,2,1,0:T(8,128)(2,1)} %get-tuple-element.138), channel_id=1, source_target_pairs={{0,16},{1,17},{2,18},{3,19},{4,20},{5,21},{6,22},{7,23},{8,24},{9,... | collective-permute-start | bytes 3538952 | tf_op jit(solution)/shard_map/ppermute | solution.py:553
  83.1 41.7 %collective-permute-start.16 = (bf16[2,4,192,384]{3,2,1,0:T(8,128)(2,1)}, bf16[2,4,192,384]{3,2,1,0:T(8,128)(2,1)}, u32[]{:S(2)}, u32[]{:S(2)}) collective-permute-start(bf16[2,4,192,384]{3,2,1,0:T(8,128)(2,1)} %get-tuple-element.136), channel_id=1, source_target_pairs={{0,8},{1,9},{2,10},{3,11},{4,12},{5,13},{6,14},{7,15},{8,0},{9,1},... | collective-permute-start | bytes 3538952 | tf_op jit(solution)/shard_map/ppermute | solution.py:553
  86.3 26.2 %collective-permute-start.19 = (bf16[3,384,128]{2,1,0:T(8,128)(2,1)}, bf16[3,384,128]{2,1,0:T(8,128)(2,1)}, u32[]{:S(2)}, u32[]{:S(2)}) collective-permute-start(bf16[3,384,128]{2,1,0:T(8,128)(2,1)} %pad_maximum_fusion.16), channel_id=1, source_target_pairs={{0,4},{1,5},{2,6},{3,7},{4,0},{5,1},{6,2},{7,3},{8,12},{9,13},{10,... | collective-permute-start | bytes 884744 | tf_op jit(solution)/shard_map/ppermute | solution.py:553
  94.4 24.3 %collective-permute-start.18 = (bf16[3,384,128]{2,1,0:T(8,128)(2,1)}, bf16[3,384,128]{2,1,0:T(8,128)(2,1)}, u32[]{:S(2)}, u32[]{:S(2)}) collective-permute-start(bf16[3,384,128]{2,1,0:T(8,128)(2,1)} %pad_maximum_fusion.16), channel_id=1, source_target_pairs={{0,2},{1,3},{2,0},{3,1},{4,6},{5,7},{6,4},{7,5},{8,10},{9,11},{10,... | collective-permute-start | bytes 884744 | tf_op jit(solution)/shard_map/ppermute | solution.py:553
  124.8 15.1 %collective-permute-start.22 = (bf16[4,4,192,384]{3,2,1,0:T(8,128)(2,1)}, bf16[4,4,192,384]{3,2,1,0:T(8,128)(2,1)}, u32[]{:S(2)}, u32[]{:S(2)}) collective-permute-start(bf16[4,4,192,384]{3,2,1,0:T(8,128)(2,1)} %bitcast.51.refs_2_), channel_id=1, source_target_pairs={{0,1},{1,0},{2,3},{3,2},{4,5},{5,4},{6,7},{7,6},{8,9},{9,8},{10,11... | collective-permute-start | bytes 7077896 | tf_op jit(solution)/shard_map/ppermute | solution.py:553
  152.7 13.3 %collective-permute-start.24 = (bf16[4,4,192,384]{3,2,1,0:T(8,128)(2,1)}, bf16[4,4,192,384]{3,2,1,0:T(8,128)(2,1)}, u32[]{:S(2)}, u32[]{:S(2)}) collective-permute-start(bf16[4,4,192,384]{3,2,1,0:T(8,128)(2,1)} %get-tuple-element.71), channel_id=1, source_target_pairs={{0,1},{1,0},{2,3},{3,2},{4,5},{5,4},{6,7},{7,6},{8,9},{9,8},{10,11... | collective-permute-start | bytes 7077896 | tf_op jit(solution)/shard_map/ppermute | solution.py:553
  169.5 28.2 %collective-permute-start.26 = (bf16[2,4,192,384]{3,2,1,0:T(8,128)(2,1)}, bf16[2,4,192,384]{3,2,1,0:T(8,128)(2,1)}, u32[]{:S(2)}, u32[]{:S(2)}) collective-permute-start(bf16[2,4,192,384]{3,2,1,0:T(8,128)(2,1)} %add_convert_fusion.1), channel_id=1, source_target_pairs={{0,16},{1,17},{2,18},{3,19},{4,20},{5,21},{6,22},{7,23},{8,24},{9,... | collective-permute-start | bytes 3538952 | tf_op jit(solution)/shard_map/ppermute | solution.py:553
  172.8 28.0 %collective-permute-start.27 = (bf16[2,4,192,384]{3,2,1,0:T(8,128)(2,1)}, bf16[2,4,192,384]{3,2,1,0:T(8,128)(2,1)}, u32[]{:S(2)}, u32[]{:S(2)}) collective-permute-start(bf16[2,4,192,384]{3,2,1,0:T(8,128)(2,1)} %add_convert_fusion), channel_id=1, source_target_pairs={{0,8},{1,9},{2,10},{3,11},{4,12},{5,13},{6,14},{7,15},{8,0},{9,1},... | collective-permute-start | bytes 3538952 | tf_op jit(solution)/shard_map/ppermute | solution.py:553
  203.3 14.4 %collective-permute-start.46 = (bf16[4,192,384]{2,1,0:T(8,128)(2,1)}, bf16[4,192,384]{2,1,0:T(8,128)(2,1)}, u32[]{:S(2)}, u32[]{:S(2)}) collective-permute-start(bf16[4,192,384]{2,1,0:T(8,128)(2,1)} %fusion.1), channel_id=1, source_target_pairs={{0,8},{1,9},{2,10},{3,11},{4,12},{5,13},{6,14},{7,15},{8,0},{9,1},... | collective-permute-start | bytes 1769480 | tf_op jit(solution)/shard_map/ppermute | solution.py:553
  213.1 42.7 %collective-permute-start.31 = (bf16[4,4,384,128]{3,2,1,0:T(8,128)(2,1)}, bf16[4,4,384,128]{3,2,1,0:T(8,128)(2,1)S(1)}, u32[]{:S(2)}, u32[]{:S(2)}) collective-permute-start(bf16[4,4,384,128]{3,2,1,0:T(8,128)(2,1)} %copy-done.15), channel_id=1, source_target_pairs={{0,1},{1,0},{2,3},{3,2},{4,5},{5,4},{6,7},{7,6},{8,9},{9,8},{10,11... | collective-permute-start | bytes 4718600 | tf_op jit(solution)/shard_map/ppermute | solution.py:553
  221.3 16.8 %collective-permute-start.35 = (bf16[2,4,192,128]{3,2,1,0:T(8,128)(2,1)S(1)}, bf16[2,4,192,128]{3,2,1,0:T(8,128)(2,1)S(1)}, u32[]{:S(2)}, u32[]{:S(2)}) collective-permute-start(bf16[2,4,192,128]{3,2,1,0:T(8,128)(2,1)S(1)} %add_convert_fusion.3), channel_id=1, source_target_pairs={{0,8},{1,9},{2,10},{3,11},{4,12},{5,13},{6,14},{7,15},{8,0},{9,1},... | collective-permute-start | bytes 1179656 | tf_op jit(solution)/shard_map/ppermute | solution.py:553
  224.3 30.1 %collective-permute-start.43 = (bf16[3,384,128]{2,1,0:T(8,128)(2,1)S(1)}, bf16[3,384,128]{2,1,0:T(8,128)(2,1)S(1)}, u32[]{:S(2)}, u32[]{:S(2)}) collective-permute-start(bf16[3,384,128]{2,1,0:T(8,128)(2,1)S(1)} %get-tuple-element.127), channel_id=1, source_target_pairs={{0,6},{1,7},{2,4},{3,5},{4,2},{5,3},{6,0},{7,1},{8,14},{9,15},{10,... | collective-permute-start | bytes 884744 | tf_op jit(solution)/shard_map/ppermute | solution.py:553
  226.1 28.3 %collective-permute-start.42 = (bf16[3,384,128]{2,1,0:T(8,128)(2,1)S(1)}, bf16[3,384,128]{2,1,0:T(8,128)(2,1)S(1)}, u32[]{:S(2)}, u32[]{:S(2)}) collective-permute-start(bf16[3,384,128]{2,1,0:T(8,128)(2,1)S(1)} %get-tuple-element.128), channel_id=1, source_target_pairs={{0,4},{1,5},{2,6},{3,7},{4,0},{5,1},{6,2},{7,3},{8,12},{9,13},{10,... | collective-permute-start | bytes 884744 | tf_op jit(solution)/shard_map/ppermute | solution.py:553
  232.7 21.7 %collective-permute-start.41 = (bf16[3,384,128]{2,1,0:T(8,128)(2,1)S(1)}, bf16[3,384,128]{2,1,0:T(8,128)(2,1)S(1)}, u32[]{:S(2)}, u32[]{:S(2)}) collective-permute-start(bf16[3,384,128]{2,1,0:T(8,128)(2,1)S(1)} %get-tuple-element.126), channel_id=1, source_target_pairs={{0,2},{1,3},{2,0},{3,1},{4,6},{5,7},{6,4},{7,5},{8,10},{9,11},{10,... | collective-permute-start | bytes 884744 | tf_op jit(solution)/shard_map/ppermute | solution.py:553
  252.7 16.3 %collective-permute-start.47 = (bf16[4,192,384]{2,1,0:T(8,128)(2,1)S(1)}, bf16[4,192,384]{2,1,0:T(8,128)(2,1)S(1)}, u32[]{:S(2)}, u32[]{:S(2)}) collective-permute-start(bf16[4,192,384]{2,1,0:T(8,128)(2,1)S(1)} %fusion), channel_id=1, source_target_pairs={{0,16},{1,17},{2,18},{3,19},{4,20},{5,21},{6,22},{7,23},{8,24},{9,... | collective-permute-start | bytes 1769480 | tf_op jit(solution)/shard_map/ppermute | solution.py:553
  256.1 26.2 %collective-permute-start.32 = (bf16[2,4,384,128]{3,2,1,0:T(8,128)(2,1)S(1)}, bf16[2,4,384,128]{3,2,1,0:T(8,128)(2,1)S(1)}, u32[]{:S(2)}, u32[]{:S(2)}) collective-permute-start(bf16[2,4,384,128]{3,2,1,0:T(8,128)(2,1)S(1)} %add_convert_fusion.2), channel_id=1, source_target_pairs={{0,16},{1,17},{2,18},{3,19},{4,20},{5,21},{6,22},{7,23},{8,24},{9,... | collective-permute-start | bytes 2359304 | tf_op jit(solution)/shard_map/ppermute | solution.py:553
  256.6 27.7 %collective-permute-start.44 = (bf16[2,384,128]{2,1,0:T(8,128)(2,1)S(1)}, bf16[2,384,128]{2,1,0:T(8,128)(2,1)S(1)}, u32[]{:S(2)}, u32[]{:S(2)}) collective-permute-start(bf16[2,384,128]{2,1,0:T(8,128)(2,1)S(1)} %pad_maximum_fusion.25), channel_id=1, source_target_pairs={{0,16},{1,17},{2,18},{3,19},{4,20},{5,21},{6,22},{7,23},{8,24},{9,... | collective-permute-start | bytes 589832 | tf_op jit(solution)/shard_map/ppermute | solution.py:553
  270.5 14.7 %collective-permute-start.50 = (bf16[384,384]{1,0:T(8,128)(2,1)S(1)}, bf16[384,384]{1,0:T(8,128)(2,1)S(1)}, u32[]{:S(2)}, u32[]{:S(2)}) collective-permute-start(bf16[384,384]{1,0:T(8,128)(2,1)S(1)} %pad_maximum_fusion.20), channel_id=1, source_target_pairs={{0,6},{1,7},{2,4},{3,5},{4,2},{5,3},{6,0},{7,1},{8,14},{9,15},{10,... | collective-permute-start | bytes 884744 | tf_op jit(solution)/shard_map/ppermute | solution.py:553
  272.3 20.4 %collective-permute-start.49 = (bf16[384,384]{1,0:T(8,128)(2,1)S(1)}, bf16[384,384]{1,0:T(8,128)(2,1)S(1)}, u32[]{:S(2)}, u32[]{:S(2)}) collective-permute-start(bf16[384,384]{1,0:T(8,128)(2,1)S(1)} %pad_maximum_fusion.19), channel_id=1, source_target_pairs={{0,4},{1,5},{2,6},{3,7},{4,0},{5,1},{6,2},{7,3},{8,12},{9,13},{10,... | collective-permute-start | bytes 884744 | tf_op jit(solution)/shard_map/ppermute | solution.py:553
  272.5 20.3 %collective-permute-start.48 = (bf16[384,384]{1,0:T(8,128)(2,1)S(1)}, bf16[384,384]{1,0:T(8,128)(2,1)S(1)}, u32[]{:S(2)}, u32[]{:S(2)}) collective-permute-start(bf16[384,384]{1,0:T(8,128)(2,1)S(1)} %pad_maximum_fusion.18), channel_id=1, source_target_pairs={{0,2},{1,3},{2,0},{3,1},{4,6},{5,7},{6,4},{7,5},{8,10},{9,11},{10,... | collective-permute-start | bytes 884744 | tf_op jit(solution)/shard_map/ppermute | solution.py:553
  284.4 15.5 %collective-permute-start.45 = (bf16[384,128]{1,0:T(8,128)(2,1)S(1)}, bf16[384,128]{1,0:T(8,128)(2,1)S(1)}, u32[]{:S(2)}, u32[]{:S(2)}) collective-permute-start(bf16[384,128]{1,0:T(8,128)(2,1)S(1)} %fusion.24), channel_id=1, source_target_pairs={{0,8},{1,9},{2,10},{3,11},{4,12},{5,13},{6,14},{7,15},{8,0},{9,1},... | collective-permute-start | bytes 294920 | tf_op jit(solution)/shard_map/ppermute | solution.py:553
  (50 other events, 661.2 us)

commit v6 on v5

--- a/solution.py
+++ b/solution.py
@@ -31,7 +31,7 @@
 HZ = H // Z
 GC = 0.7978845608
 GA = 0.044715
-VMEM_LIMIT = 32 * 1024 * 1024
+VMEM_LIMIT = 40 * 1024 * 1024
 COST = 1 << 38
 
 F32 = jnp.float32
@@ -42,7 +42,7 @@
     return lax.dot_general(a, b, (((ca,), (cb,)), ((), ())), preferred_element_type=F32)
 
 
-def call(body, grid, in_specs, out_specs, out_shape, scratch=(), flops=0, nbytes=0):
+def call(body, grid, in_specs, out_specs, out_shape, scratch=(), flops=0, nbytes=0, vmem=VMEM_LIMIT):
     return pl.pallas_call(
         body,
         grid_spec=pltpu.PrefetchScalarGridSpec(
@@ -54,7 +54,7 @@
         ),
         out_shape=out_shape,
         compiler_params=pltpu.CompilerParams(
-            dimension_semantics=("arbitrary",) * len(grid), vmem_limit_bytes=VMEM_LIMIT
+            dimension_semantics=("arbitrary",) * len(grid), vmem_limit_bytes=vmem
         ),
         cost_estimate=pl.CostEstimate(flops=COST, bytes_accessed=nbytes, transcendentals=0),
     )
@@ -82,6 +82,10 @@
 
 def tab_z(t, z):
     return t[1 + 2 * G + z]
+
+
+def g_of(t, r, order_b):
+    return t[1 + 2 * G + Z] ^ (r if order_b else (r % 2) * 2 + r // 2)
 
 
 def norm_stats(x):
@@ -173,7 +177,7 @@
     return jnp.concatenate(tiles, axis=1)
 
 
-def put_weight_grads(acc, dg, t, keep, send):
+def with_gains(full, dg, t):
     lane = lax.broadcasted_iota(jnp.int32, (1, LN), 1)
     top = lax.broadcasted_iota(jnp.int32, (16, LN), 0) == 0
     spot = jnp.logical_and(top, jnp.logical_and(lane >= CB, lane < CB + GN))
@@ -185,13 +189,11 @@
             row = jnp.where(lane < off, dg[:, (tile + 1) * LN : (tile + 2) * LN], row)
         rows_of[g, z, c] = pltpu.roll(row, (CB - off) % LN, 1)
     for z in range(Z):
-        full = acc(z)
         for g in range(G):
-            for p, ref in ((0, keep), (1, send)):
-                blk = full[g * DB : (g + 1) * DB, p * LN : (p + 1) * LN]
+            for p in range(2):
                 row = pick(t[0], p, rows_of[g, z, 0], rows_of[g, z, 1])
-                ref[tab_a(t, g), tab_z(t, z)] = blk.astype(BF16)
-                ref[tab_a(t, g), tab_z(t, z), 0:16, :] = jnp.where(spot, row, blk[:16]).astype(BF16)
+                at = z, slice(g * DB, g * DB + 16), slice(p * LN, (p + 1) * LN)
+                full[at] = jnp.where(spot, row, full[at].astype(F32)).astype(BF16)
 
 
 def by_rows(body):
@@ -259,56 +261,61 @@
         by_rows(norm)
 
 
-def ffn_body(first, last, t, n_ref, c_ref, u_ref, d_ref, *refs):
+def ffn_body(pair, t, *refs):
     refs = list(refs)
-    if not first:
-        ia_ref, ib_ref = refs[:2]
-        refs = refs[2:]
-    if last:
-        mid_ref = refs[0]
-        refs = refs[1:]
-    gu_ref, gd_ref, b_ref, a_ref = refs[:4]
+    n_refs, refs = refs[: 1 + pair], refs[1 + pair :]
+    c_refs, refs = refs[: 1 + pair], refs[1 + pair :]
+    u_refs, d_refs = refs[:2], refs[2:4]
+    ku, su, kd, sd = refs[4:8]
+    out_refs = refs[8:]
+    n_all, c_all, a_acc, b_acc, gu_all, gd_all = out_refs[2 + 2 * pair :]
+    out_refs = out_refs[: 2 + 2 * pair]
     j = pl.program_id(0)
-    n = n_ref[...]
-    cot = c_ref[...]
-    up_w = jnp.concatenate(
-        [jnp.concatenate([u_ref[tab_b(t, g), i] for g in range(G)], axis=0) for i in range(ZS)], axis=1
-    )
-    dn_w = jnp.concatenate(
-        [jnp.concatenate([d_ref[tab_a(t, g), i] for g in range(G)], axis=0) for i in range(ZS)], axis=1
-    )
 
     @pl.when(j == 0)
     def _():
-        if first:
-            a_ref[...] = jnp.zeros_like(a_ref)
-            b_ref[...] = jnp.zeros_like(b_ref)
-        else:
-            a_ref[...] = ia_ref[...]
-            b_ref[...] = ib_ref[...]
-
+        for i in range(1 + pair):
+            n_all[i * L : (i + 1) * L] = n_refs[i][...]
+            c_all[i * L : (i + 1) * L] = c_refs[i][...]
+        a_acc[...] = jnp.zeros_like(a_acc)
+        b_acc[...] = jnp.zeros_like(b_acc)
+
+    n, cot = n_all[...], c_all[...]
+    def weights(parts, tab):
+        cols = []
+        for i in range(ZS):
+            blocks = []
+            for g in range(G):
+                at = tab(t, g)
+                one, two = (r[at % 2, i] for r in parts)
+                blocks.append(jnp.where(at < 2, one, two))
+            cols.append(jnp.concatenate(blocks, axis=0))
+        return jnp.concatenate(cols, axis=1)
+
+    up_w, dn_w = weights(u_refs, tab_b), weights(d_refs, tab_a)
     up = dot(n, up_w, 1, 0)
     sq = up * up
     th = jnp.tanh(GC * up * (1.0 + GA * sq))
     half = 0.5 + 0.5 * th
     act = (up * half).astype(BF16)
     slope = half + (0.5 * GC) * up * (1.0 - th * th) * (1.0 + (3.0 * GA) * sq)
-    a_ref[...] += dot(act, dn_w, 1, 1)
-    gd = dot(cot, act, 0, 0).astype(BF16)
+    a_acc[...] += dot(act, dn_w, 1, 1)
+    gd_all[...] = dot(cot, act, 0, 0).astype(BF16)
     up_g = (dot(cot, dn_w, 1, 0) * slope).astype(BF16)
-    gu = dot(n, up_g, 0, 0).astype(BF16)
-    b_ref[...] += dot(up_g, up_w, 1, 1)
-    for g in range(G):
-        for i in range(ZS):
-            part = slice(g * DB, (g + 1) * DB), slice(i * FB, (i + 1) * FB)
-            gu_ref[tab_b(t, g), i] = gu[part]
-            gd_ref[tab_a(t, g), i] = gd[part]
-    if last:
-        lo_ref = refs[4]
-
-        @pl.when(j == Z // ZS - 1)
-        def _():
-            lo_ref[...] = (mid_ref[...] + a_ref[...]).astype(BF16)
+    gu_all[...] = dot(n, up_g, 0, 0).astype(BF16)
+    b_acc[...] += dot(up_g, up_w, 1, 1)
+    for src, order_b, keep, send in ((gu_all, True, ku, su), (gd_all, False, kd, sd)):
+        for r in range(G):
+            at = pl.ds(pl.multiple_of(g_of(t, r, order_b) * DB, DB), DB)
+            for i in range(ZS):
+                (keep, send)[r // 2][r % 2, i] = src[at, i * FB : (i + 1) * FB]
+
+    @pl.when(j == Z // ZS - 1)
+    def _():
+        for i in range(1 + pair):
+            part = slice(i * L, (i + 1) * L)
+            out_refs[i][...] = a_acc[part].astype(out_refs[i].dtype)
+            out_refs[1 + pair + i][...] = b_acc[part].astype(out_refs[1 + pair + i].dtype)
 
 
 def norm_back(cen, rstd, gain, dn):
@@ -323,9 +330,9 @@
 
 
 def mixer_back_body(
-    t, dn_ref, mid_ref, c_ref, gain_ref, dq_ref, dk_ref, mix_ref, val_ref,
+    t, dna_ref, dnb_ref, mid_ref, c_ref, gain_ref, dq_ref, dk_ref, mix_ref, val_ref,
     a_own, a_oth, b_own, b_oth, w_own, w_oth,
-    mg_ref, ka_ref, sa_ref, kb_ref, sb_ref, ko_ref, so_ref, vg_ref, dg_acc, br_ref, grad_ref, vg_acc,
+    mg_ref, ka_ref, sa_ref, kb_ref, sb_ref, vg_ref, dg_acc, br_ref, grad_ref, vg_acc, go_ref,
 ):
     m = pl.program_id(0)
     core = t[0]
@@ -340,7 +347,8 @@
 
         def norm(at):
             cen, rstd = norm_stats(mid_ref[at, :])
-            dv, dg = norm_back(cen, rstd, gain_ref[1:2, :], dn_ref[at, :])
+            dn = dna_ref[at, :] + dnb_ref[at, :].astype(F32)
+            dv, dg = norm_back(cen, rstd, gain_ref[1:2, :], dn)
             dg_acc[0:1, :] += dg
             mid_grad = c_ref[at, :].astype(F32) + dv
             mg_ref[at, :] = mid_grad
@@ -350,15 +358,17 @@
         branch = br_ref[...]
         for z in range(Z):
             grad_ref[z] = dot(branch, weight_z(w_own, w_oth, t, z, DB), 1, 0).astype(BF16)
-        put_weight_grads(
-            lambda z: dot(branch, mix_ref[z], 0, 0), dg_acc[0:1, :], t, ko_ref, so_ref
-        )
+            go_ref[z] = dot(branch, mix_ref[z], 0, 0).astype(BF16)
+        with_gains(go_ref, dg_acc[0:1, :], t)
 
     mask = halves(dq_ref, core) == dk_ref[:, pl.ds(k0, WIN * KB)]
     heads = head_masks(core, TM)
-    rest = tab_b(t, jnp.where(start == 0, G - 1, 0))
-    ka_ref[rest, 0] = jnp.zeros((HR, KB), BF16)
-    sa_ref[rest, 0] = jnp.zeros((HR, KB), BF16)
+    for g in range(G):
+        for p, ref in ((0, ka_ref), (1, sa_ref)):
+            ref[tab_b(t, g), 0, HR:, :] = go_ref[m, g * DB : (g + 1) * DB, p * LN : (p + 1) * LN]
+    rest = jnp.where(start == 0, G - 1, 0)
+    for ref, tab in ((ka_ref, tab_b), (sa_ref, tab_b), (kb_ref, tab_a), (sb_ref, tab_a)):
+        ref[tab(t, rest), 0, 0:HR, :] = jnp.zeros((HR, KB), BF16)
     for z in range(Z):
         grad = halves(grad_ref, core, z, base)
         mine = jnp.concatenate(
@@ -373,14 +383,14 @@
             head = HZ * z + i
             pd = prob[i] * dp[i * TM : (i + 1) * TM]
             ds = (pd - prob[i] * jnp.sum(pd, axis=-1, keepdims=True)).astype(BF16)
+            low_half = head < HA
+            row = (head if low_half else head - HA) * QB
+            tab = tab_b if low_half else tab_a
             for k in range(WIN):
-                for p, (ra, rb) in enumerate(((ka_ref, kb_ref), (sa_ref, sb_ref))):
-                    blk = ds[p * QB : (p + 1) * QB, k * KB : (k + 1) * KB]
-                    if head < HA:
-                        ra[tab_b(t, start + k), 0, head * QB : (head + 1) * QB, :] = blk
-                    else:
-                        h = head - HA
-                        rb[0, k, h * QB : (h + 1) * QB, :] = blk
+                for p, ref in enumerate((ka_ref, sa_ref) if low_half else (kb_ref, sb_ref)):
+                    ref[tab(t, start + k), 0, row : row + QB, :] = ds[
+                        p * QB : (p + 1) * QB, k * KB : (k + 1) * KB
+                    ]
 
     @pl.when(m == Z - 1)
     def _():
@@ -388,7 +398,8 @@
 
 
 def last_body(
-    t, x_ref, gain_ref, n_ref, vg_ref, w_own, w_oth, mg_ref, gi_ref, kv_ref, sv_ref, dg_acc, dn_ref
+    t, x_ref, gain_ref, n_ref, vg_ref, w_own, w_oth, mg_ref, gi_ref, kv_ref, sv_ref, dg_acc, dn_ref,
+    gv_ref,
 ):
     dg_acc[...] = jnp.zeros_like(dg_acc)
     acc = dot(vg_ref[0], weight_z(w_own, w_oth, t, 0, 0), 1, 1)
@@ -404,7 +415,14 @@
 
     by_rows(norm)
     low = n_ref[...]
-    put_weight_grads(lambda z: dot(low, vg_ref[z], 0, 0), dg_acc[0:1, :], t, kv_ref, sv_ref)
+    for z in range(Z):
+        gv_ref[z] = dot(low, vg_ref[z], 0, 0).astype(BF16)
+    with_gains(gv_ref, dg_acc[0:1, :], t)
+    for z in range(Z):
+        for g in range(G):
+            for p, ref in ((0, kv_ref), (1, sv_ref)):
+                blk = gv_ref[z, g * DB : (g + 1) * DB, p * LN : (p + 1) * LN]
+                ref[tab_a(t, g), tab_z(t, z)] = blk
 
 
 def sds(shape, dtype):
@@ -414,6 +432,7 @@
 W_SHAPE = (G, Z, 2 * DB, LN)
 V_SHAPE = (G, Z, DB, LN)
 A_SHAPE = (G, Z, HR, KB)
+AO_SHAPE = (G, Z, HR + DB, KB)
 B_SHAPE = (Z, WIN, HR, KB)
 F_SHAPE = (G, Z, DB, FB)
 Z_ROWS = pl.BlockSpec((Z, TM, GW), lambda i, t: (0, i, 0))
@@ -447,62 +466,50 @@
     )(tab, x, gain, dq, dk, vals, *a, *b, *w)
 
 
-def run_ffn(tab, n, cot, u_w, d_w, acc=None, mid=None):
-    first, last = acc is None, mid is not None
-    blk = pl.BlockSpec((G, ZS, DB, FB), lambda i, t: (0, i, 0, 0))
-    in_specs = [whole((L, D)), whole((L, D)), blk, blk]
-    args = [tab, n, cot, u_w, d_w]
-    if not first:
-        in_specs += [whole((L, D)), whole((L, D))]
-        args += list(acc)
-    if last:
-        in_specs += [whole((L, D))]
-        args += [mid]
-    out_specs = [blk, blk, out_whole((L, D))]
-    outs = [sds(F_SHAPE, BF16), sds(F_SHAPE, BF16), sds((L, D), F32)]
-    scratch = ()
-    if last:
-        scratch = (pltpu.VMEM((L, D), F32),)
-        out_specs += [out_whole((L, D))]
-        outs += [sds((L, D), BF16)]
-    else:
-        out_specs += [out_whole((L, D))]
-        outs += [sds((L, D), F32)]
-
-    def body(t, *refs):
-        if last:
-            refs = list(refs)
-            refs = refs[:-2] + [refs[-1], refs[-2]]
-        ffn_body(first, last, t, *refs)
-
+def run_ffn(tab, ns, cots, u_w, d_w):
+    n = len(ns)
+    out = pl.BlockSpec((2, ZS, DB, FB), lambda i, t: (0, i, 0, 0))
+    types = [F32, BF16][:n] * 2
     return call(
-        body, (Z // ZS,), in_specs, out_specs, outs, scratch, flops=6 * L * D * FF, nbytes=20 << 20
-    )(*args)
+        functools.partial(ffn_body, n - 1),
+        (Z // ZS,),
+        [whole((L, D))] * (2 * n) + [out] * 4,
+        [out] * 4 + [out_whole((L, D))] * (2 * n),
+        [sds((2, Z, DB, FB), BF16)] * 4 + [sds((L, D), k) for k in types],
+        scratch=(
+            pltpu.VMEM((n * L, D), BF16), pltpu.VMEM((n * L, D), BF16), pltpu.VMEM((n * L, D), F32),
+            pltpu.VMEM((n * L, D), F32), pltpu.VMEM((D, ZS * FB), BF16), pltpu.VMEM((D, ZS * FB), BF16),
+        ),
+        flops=6 * L * D * FF,
+        nbytes=20 << 20,
+        vmem=54 << 20,
+    )(tab, *ns, *cots, *u_w, *d_w)
 
 
 def run_mixer_back(tab, dn, mid, cot, gain, dq, dk, mixed, vals, a, b, w):
-    blk_a = pl.BlockSpec((G, 1, HR, KB), lambda i, t: (0, tab_z(t, i), 0, 0))
-    blk_b = pl.BlockSpec((1, WIN, HR, KB), lambda i, t: (tab_z(t, i), 0, 0, 0))
+    blk_a = pl.BlockSpec((G, 1, HR + DB, KB), lambda i, t: (0, tab_z(t, i), 0, 0))
+    blk_b = pl.BlockSpec((G, 1, HR, KB), lambda i, t: (0, tab_z(t, i), 0, 0))
     return call(
         mixer_back_body,
         (L // TM,),
         [
-            whole((L, D)), whole((L, D)), whole((L, D)), whole((8, D)), rows(1), whole((1, L)),
-            whole((Z, L, GW)), whole((Z, L, GW)), whole(A_SHAPE), whole(A_SHAPE), whole(B_SHAPE), whole(B_SHAPE),
+            whole((L, D)), whole((L, D)), whole((L, D)), whole((L, D)), whole((8, D)), rows(1),
+            whole((1, L)), whole((Z, L, GW)), whole((Z, L, GW)),
+            whole(A_SHAPE), whole(A_SHAPE), whole(B_SHAPE), whole(B_SHAPE),
             whole(W_SHAPE), whole(W_SHAPE),
         ],
-        [out_whole((L, D)), blk_a, blk_a, blk_b, blk_b, out_whole(V_SHAPE), out_whole(V_SHAPE), out_whole((Z, L, GW))],
+        [out_whole((L, D)), blk_a, blk_a, blk_b, blk_b, out_whole((Z, L, GW))],
         [
-            sds((L, D), F32), sds(A_SHAPE, BF16), sds(A_SHAPE, BF16), sds(B_SHAPE, BF16),
-            sds(B_SHAPE, BF16), sds(V_SHAPE, BF16), sds(V_SHAPE, BF16), sds((Z, L, GW), BF16),
+            sds((L, D), F32), sds(AO_SHAPE, BF16), sds(AO_SHAPE, BF16), sds(A_SHAPE, BF16),
+            sds(A_SHAPE, BF16), sds((Z, L, GW), BF16),
         ],
         scratch=(
             pltpu.VMEM((8, D), F32), pltpu.VMEM((L, D), BF16), pltpu.VMEM((Z, L, GW), BF16),
-            pltpu.VMEM((Z, L, GW), F32),
+            pltpu.VMEM((Z, L, GW), F32), pltpu.VMEM((Z, D, GW), BF16),
         ),
         flops=4 * L * D * Z * GW + 6 * H * L * WIN * KB * GW,
         nbytes=28 << 20,
-    )(tab, dn, mid, cot, gain, dq, dk, mixed, vals, *a, *b, *w)
+    )(tab, *dn, mid, cot, gain, dq, dk, mixed, vals, *a, *b, *w)
 
 
 def run_last(tab, x, gain, low, vg, w, mid_grad):
@@ -515,7 +522,7 @@
         ],
         [out_whole((L, D)), out_whole(V_SHAPE), out_whole(V_SHAPE)],
         [sds((L, D), F32), sds(V_SHAPE, BF16), sds(V_SHAPE, BF16)],
-        scratch=(pltpu.VMEM((8, D), F32), pltpu.VMEM((L, D), F32)),
+        scratch=(pltpu.VMEM((8, D), F32), pltpu.VMEM((L, D), F32), pltpu.VMEM((Z, D, GW), BF16)),
         flops=4 * L * D * Z * GW,
         nbytes=12 << 20,
     )(tab, x, gain, low, vg, *w, mid_grad)
@@ -569,6 +576,16 @@
 
     def total(self, terms, stage):
         return add_up([v[(0,) * (stage - born)] for v, born in terms])
+
+    def reduce_pair(self, p, q, stage, axis, *deps):
+        if deps:
+            p = p[:-1] + [(after(p[-1][0], *deps), p[-1][1])]
+        parts = [
+            add_up([v[(0,) * (stage - born) + (1,)] for v, born in terms]).astype(BF16) for terms in (p, q)
+        ]
+        rows_p = parts[0].shape[-2]
+        got = self.fetch(jnp.concatenate(parts, axis=-2), axis, 1)
+        return p + [(got[..., :rows_p, :], stage + 1)], q + [(got[..., rows_p:, :], stage + 1)]
 
     def reduce_joined(self, groups, axis, *deps):
         groups = list(groups)
@@ -594,13 +611,16 @@
     dq, dk = docs.reshape(L, 1), docs
     low, vals, gain = run_values(tab, x, w)
     mixed, mid, n_two = run_mixer(tab, x, gain, dq, dk, vals, a, b, w)
-    gu0, gd0, acc_b, acc_a = run_ffn(tab, n_two, cot, u[0], d[0])
-    gu1, gd1, n_grad, layer_out = run_ffn(tab, n_two, cot, u[1], d[1], (acc_a, acc_b), mid)
-    mid_grad, ka, sa, kb, sb, ko, so, vg = run_mixer_back(
-        tab, n_grad, mid, cot, gain, dq, dk, mixed, vals, a, b, w
+    sides = [
+        run_ffn(tab, [n_two], [cot], (u[p, :2], u[p, 2:]), (d[p, :2], d[p, 2:])) for p in range(2)
+    ]
+    gu, gd = ([jnp.concatenate(v[i : i + 2], axis=0) for v in sides] for i in (0, 2))
+    layer_out = (mid + sides[0][4] + sides[1][4]).astype(BF16)
+    mid_grad, *ga, vg = run_mixer_back(
+        tab, (sides[0][5], sides[1][5]), mid, cot, gain, dq, dk, mixed, vals, a, b, w
     )
-    grad_in, kv, sv = run_last(tab, x, gain, low, vg, w, mid_grad)
-    return layer_out, grad_in, (gu0, gu1), (gd0, gd1), (ka, sa), (kb, sb), (ko, so), (kv, sv)
+    grad_in, *gv = run_last(tab, x, gain, low, vg, w, mid_grad)
+    return layer_out, grad_in, gu, gd, ga[:2], ga[2:], gv
 
 
 def lane_pad(mat, gains):
@@ -614,7 +634,8 @@
     order_a = [grid.rel("x", g % 2) * 2 + grid.rel("y", g // 2) for g in range(G)]
     order_b = [grid.rel("y", g // 2) * 2 + grid.rel("x", g % 2) for g in range(G)]
     order_z = [grid.rel("z", z) for z in range(Z)]
-    tab = jnp.stack([at["c"]] + order_a + order_b + order_z).astype(jnp.int32)
+    own = [at["y"] * 2 + at["x"]]
+    tab = jnp.stack([at["c"]] + order_a + order_b + order_z + own).astype(jnp.int32)
     docs = lax.dynamic_slice_in_dim(doc_ids, lax.axis_index("gy"), 1, 0)
 
     dq, dk = docs.reshape(L, 1), docs
@@ -629,6 +650,7 @@
         return [val] + [fetch(val, "z", k) for k in range(1, Z)]
 
     c1 = along_z(jnp.concatenate([mix[0], wts], axis=0))
+    cots = [cot, fetch(cot, "c", 1)]
     b = spread(spread(mix[1], "x"), "y").reshape(G, HR, KB)
     start = window(at["z"])
     order = jnp.stack(order_b)
@@ -639,16 +661,15 @@
     a, w = spread(a, "x"), spread(w, "y")
     a, w = after((a, w), ffn[1])
     a, w = spread(a, "y").reshape(A_SHAPE), spread(w, "x").reshape(W_SHAPE)
-    a, w = after((a, w), ffn[2:])
-    b = spread(after(b, ffn[1:]), "z")
+    b = along_z(after(b, ffn[1:]))
     u, d = (jnp.stack([v[i] for v in ffn]) for i in range(2))
-    w, a = both(w), both(a)
-    low, vals, gain = run_values(tab, layer_in, w)
     u, d = spread(u, "x"), spread(d, "y")
-    b = both(b, u, d)
-    u, d = spread(u, "y").reshape(F_SHAPE), spread(d, "x").reshape(F_SHAPE)
-    mixed, mid, n_two = run_mixer(tab, layer_in, after(gain, u, d), dq, dk, vals, a, b, w)
-    u, d = both(u), both(d)
+    w, a = both(w, b[1:], u, d), both(a, b[1:], u, d)
+    u, d = after((u, d), a[0], w[0])
+    u, d = [u, fetch(u, "y", 1)], [d, fetch(d, "x", 1)]
+    b = both(jnp.stack(b))
+    low, vals, gain = run_values(tab, after(layer_in, a[1], b[1]), w)
+    mixed, mid, n_two = run_mixer(tab, layer_in, gain, dq, dk, vals, a, b, w)
 
     def begin(keep, send):
         got = fetch(send, "c", 1)
@@ -657,38 +678,31 @@
     def last(*groups):
         return [terms[-1][0] for terms in groups]
 
-    su, sd, acc_b, acc_a = run_ffn(tab, n_two, cot, u[1], d[1])
-    ku, kd, n_grad, layer_out = run_ffn(tab, n_two, cot, u[0], d[0], (acc_a, acc_b), mid)
-    gu, gd = begin(ku, su), begin(kd, sd)
-    n_grad = after(n_grad, last(gu, gd))
-    gu, gd = grid.reduce(gu, 0, "y"), grid.reduce(gd, 0, "x")
-    mid_grad, ka, sa, kb, sb, ko, so, vg = run_mixer_back(
-        tab, n_grad, mid, cot, gain, dq, dk, mixed, vals, a, b, w
+    ku, su, kd, sd, out_a, out_b, ng_a, ng_b = run_ffn(
+        tab, [n_two, fetch(n_two, "c", 1)], cots, u, d
+    )
+    ng_b = fetch(ng_b, "c", 1)
+    gu = [(ku, 1), (fetch(su, "y", 1), 1)]
+    gd = [(kd, 1), (fetch(sd, "x", 1), 1)]
+    out_b = fetch(out_b, "c", 1)
+    layer_out = (mid + out_a + out_b.astype(F32)).astype(BF16)
+    mid_grad, ka, sa, kb, sb, vg = run_mixer_back(
+        tab, (ng_a, ng_b), mid, cot, gain, dq, dk, mixed, vals, a, b, w
     )
     vg = after(vg, last(gu, gd))
     gu, gd = grid.reduce(gu, 1, "x", sa), grid.reduce(gd, 1, "y", sa)
     grad_in, kv, sv = run_last(tab, layer_in, gain, low, vg, w, mid_grad)
-    sa, sb, so = after((sa, sb, so), sv)
-    gv, ga, go, rb = begin(kv, sv), begin(ka, sa), begin(ko, so), fetch(sb, "c", 1)
-    gb = grid.reduce([(kb, 2), (rb, 2)], 2, "z")
+    ga, gb = begin(ka, sa), begin(kb, sb)
+    gv = begin(kv, after(sv, last(gu, gd, ga, gb)))
     ga = grid.reduce(ga, 0, "y")
-    go = grid.reduce(go, 0, "x")
-    gu, gd = grid.reduce_joined((gu, gd), "z", last(gb))
-    gv = grid.reduce(gv, 0, "x")
-    wide = grid.total(gb, 3)
-    blocks = []
-    for k in range(G):
-        spot = (at["y"] - k // 2) % 2 * 2 + (at["x"] - k % 2) % 2 - start
-        blk = lax.dynamic_index_in_dim(wide, jnp.clip(spot, 0, WIN - 1), 0, False)
-        ok = jnp.logical_and(spot >= 0, spot < WIN)
-        blocks.append(jnp.where(ok, blk, jnp.zeros_like(blk)))
-    gb = [(jnp.stack(blocks).reshape(2, 2, HR, KB), 0)]
-    gb = grid.total(grid.reduce(grid.reduce(gb, 0, "y"), 1, "x"), 2)
-    ga, go = grid.reduce(ga, 1, "x"), grid.reduce(go, 1, "y")
-    gv = grid.reduce(gv, 1, "y")
-    ga, go, gv = grid.reduce_joined((ga, go, gv), "z")
-
-    grad_mixing = jnp.concatenate([ga, gb], axis=0).reshape(H, QB, KB)
+    bv = grid.reduce_pair(gb, gv, 0, "x")
+    gu, gd = grid.reduce_joined((gu, gd), "z")
+    ga = grid.reduce(ga, 1, "x")
+    bv = grid.reduce_pair(*bv, 1, "y")
+    ga, gb, gv = grid.reduce_joined((ga, *bv), "z")
+
+    go = ga[HR:]
+    grad_mixing = jnp.concatenate([ga[:HR], gb], axis=0).reshape(H, QB, KB)
     return (
         layer_out, grad_in, gv[0, CB : CB + GN], gv[:, :CB], grad_mixing, go[:, :CB].T,
         go[0, CB : CB + GN], gu, gd.T,
@@ -733,7 +747,9 @@
     b = jnp.stack([mix_full[1][:, s : s + WIN, m] for m, s in enumerate(starts)], axis=1)
     u = gather(up_w, 0, 1).reshape(G, DB, Z, 2, FB).transpose(3, 0, 2, 1, 4)
     d = gather(down_w.T, 0, 1).reshape(G, DB, Z, 2, FB).transpose(3, 0, 2, 1, 4)
-    tab = jnp.array([0] + [0, 1, 2, 3] * 3, jnp.int32)
+    w = w.reshape((2, 2, 2) + w.shape[2:]).swapaxes(1, 2).reshape(w.shape)
+    d = d.reshape((2, 2, 2) + d.shape[2:]).swapaxes(1, 2).reshape(d.shape)
+    tab = jnp.array([0, 0, 2, 1, 3] + [0, 1, 2, 3] * 2 + [0], jnp.int32)
 
     rows_out, grads = [], None
     for s in range(seqs):
@@ -745,22 +761,19 @@
         grads = rest if grads is None else jax.tree.map(jnp.add, grads, rest)
     layer_out = jnp.concatenate([r[0] for r in rows_out], axis=0)
     grad_in = jnp.concatenate([r[1] for r in rows_out], axis=0)
-    gu, gd, ga, gb, go, gv = jax.tree.map(lambda v: v.astype(BF16), grads)
+    gu, gd, ga, gb, gv = jax.tree.map(lambda v: v.astype(BF16), grads)
+
+    def by_a(v):
+        return v.reshape((2, 2) + v.shape[1:]).swapaxes(0, 1).reshape(v.shape)
 
     def ffn_out(pair):
         return jnp.stack(pair).transpose(1, 3, 2, 0, 4).reshape(D, FF)
 
-    value_full, dg_one = cols_out(*gv)
-    output_full, dg_two = cols_out(*go)
-    ga, gb = jnp.stack(ga), jnp.stack(gb)
-    gb = jnp.stack(
-        [
-            jnp.pad(gb[:, m], ((0, 0), (s, G - WIN - s), (0, 0), (0, 0)))
-            for m, s in enumerate(starts)
-        ],
-        axis=2,
-    )
-    gm = jnp.stack([ga, gb]).reshape(2, 2, G, Z, HA, QB, KB).transpose(0, 4, 3, 1, 5, 2, 6)
+    value_full, dg_one = cols_out(*[by_a(v) for v in gv])
+    output_full, dg_two = cols_out(*[v[:, :, HR:] for v in ga])
+    gm = jnp.stack([jnp.stack([v[:, :, :HR] for v in ga]), jnp.stack([by_a(v) for v in gb])])
+    gm = gm.reshape(2, 2, G, Z, HA, QB, KB).transpose(0, 4, 3, 1, 5, 2, 6)
+    gd = [by_a(v) for v in gd]
     dgs = jnp.stack([dg_one, dg_two]).astype(F32)
     dgs = lax.psum_scatter(dgs, ax, scatter_dimension=1, tiled=True)
     return (

time: 313 us -> 289 us (0.923); the launches traced: 312 us -> 284 us
  starting transfers between devices: 72.3 us -> 42.2 us
  other arithmetic: 41.9 us -> 27.8 us
  waiting for transfers between devices: 122 us -> 131 us
  local copies, waits for them, and re-layouts: 8.68 us -> 13.9 us
    ppermute x51 -> x43, starting transfers between devices: 72.3 us -> 42.2 us  [fetch(): return lax.ppermute(val, ('gx', 'gy'), pairs)]
    another operation x13 -> x10, other arithmetic: 13.6 us -> 3.12 us  [spread(): jnp.stack([val] + [self.fetch(val, axis, k) for k in range(1, self.size[a...]
    ppermute x51 -> x43, waiting for transfers between devices: 122 us -> 131 us  [fetch(): return lax.ppermute(val, ('gx', 'gy'), pairs)]
    convert_element_type x12 -> x4, other arithmetic: 14.4 us -> 7.01 us  [reduce(): add_up([v[(0,) * (stage - born) + (k,)] for v, born in terms]).astype(BF16)]
    unnamed x64 -> x70, local copies, waits for them, and re-layouts: 4.17 us -> 8.69 us
    convert_element_type x0 -> x5, other arithmetic: none -> 3.97 us  [the longest x4 2.83 us: reduce_pair(): add_up([v[(0,) * (stage - born) + (1,)] for v, born in terms]).astype(BF16)]
    pallas_call x2 -> x1, Pallas kernels: 25.5 us -> 24.1 us  [run_ffn(): call(functools.partial(ffn_body, n - 1), (Z // ZS,), [whole((L, D))] * (2...]
  transfers between devices with their start and end apart: 51 -> 43, of which waited for: 25 -> 19; matrix products, arithmetic and copies ran while one was open for 11% -> 9% of each run, Pallas kernels for 15% -> 13%
where the time goes in v6:
time: 289 us; the launch traced here: 284 us
  waiting for transfers between devices  131 us (45%)
  Pallas kernels  62.3 us (22%)
  starting transfers between devices  42.2 us (15%)
  other arithmetic  27.8 us (10%)
  local copies, waits for them, and re-layouts  13.9 us (5%)
  between operations  7.22 us (2%)
    ppermute x43, waiting for transfers between devices, fetch(): return lax.ppermute(val, ('gx', 'gy'), pairs)  131 us
    ppermute x43, starting transfers between devices, fetch(): return lax.ppermute(val, ('gx', 'gy'), pairs)  42.2 us
    pallas_call x1, Pallas kernels, run_ffn(): call(functools.partial(ffn_body, n - 1), (Z // ZS,), [whole((L, D))] * (2...  24.1 us
    pallas_call x1, Pallas kernels, run_mixer_back(): call(mixer_back_body, (L // TM,), [whole((L, D)), whole((L, D)), whole((L...  17.8 us
    pallas_call x1, Pallas kernels, run_mixer(): call(mixer_body, (L // TM,), [whole((L, D)), whole((8, D)), rows(1), whol...  8.79 us
    unnamed x70, local copies, waits for them, and re-layouts  8.69 us
    pallas_call x1, Pallas kernels, run_last(): call(last_body, (1,), [whole((L, D)), whole((8, D)), whole((L, D)), whole...  7.45 us
    convert_element_type x4, other arithmetic, reduce(): add_up([v[(0,) * (stage - born) + (k,)] for v, born in terms]).astype(BF16)  7.01 us
  transfers between devices with their start and end apart: 43, of which 19 were waited for; matrix products, arithmetic and copies ran while one was open for 9% of the time, Pallas kernels for 13%

profile of v6, /device:TPU:0, one launch (start us, length us, event | category | flops | bytes accessed | tf_op | source)
XLA Modules:
  0.0 284.0 jit_solution(6110952357359706491)
XLA Ops:
  4.8 5.1 %collective-permute-start.2 = (bf16[768,128]{1,0:T(8,128)(2,1)S(1)}, bf16[768,128]{1,0:T(8,128)(2,1)S(1)}, u32[]{:S(2)}, u32[]{:S(2)}) collective-permute-start(bf16[768,128]{1,0:T(8,128)(2,1)S(1)} %maximum_maximum_fusion), channel_id=1, source_target_pairs={{0,6},{1,7},{2,4},{3,5},{4,2},{5,3},{6,0},{7,1},{8,14},{9,15},{10,... | collective-permute-start | bytes 589832 | tf_op jit(solution)/shard_map/ppermute | solution.py:560
  10.6 1.6 collective-permute-start.3
  20.6 6.1 %collective-permute-done.1 = bf16[768,128]{1,0:T(8,128)(2,1)S(1)} collective-permute-done((bf16[768,128]{1,0:T(8,128)(2,1)S(1)}, bf16[768,128]{1,0:T(8,128)(2,1)S(1)}, u32[]{:S(2)}, u32[]{:S(2)}) %collective-permute-start.1) | collective-permute-done | bytes 196640 | tf_op jit(solution)/shard_map/ppermute | solution.py:560
  26.7 2.7 collective-permute-start.10
  29.4 1.7 collective-permute-start.7
  34.5 4.0 %collective-permute-done.10 = bf16[2,192,384]{2,1,0:T(8,128)(2,1)S(1)} collective-permute-done((bf16[2,192,384]{2,1,0:T(8,128)(2,1)S(1)}, bf16[2,192,384]{2,1,0:T(8,128)(2,1)S(1)}, u32[]{:S(2)}, u32[]{:S(2)}) %collective-permute-start.10) | collective-permute-done | bytes 294944 | tf_op jit(solution)/shard_map/ppermute | solution.py:560
  38.5 14.1 %collective-permute-done.9 = bf16[2,192,384]{2,1,0:T(8,128)(2,1)S(1)} collective-permute-done((bf16[2,192,384]{2,1,0:T(8,128)(2,1)S(1)}, bf16[2,192,384]{2,1,0:T(8,128)(2,1)S(1)}, u32[]{:S(2)}, u32[]{:S(2)}) %collective-permute-start.9) | collective-permute-done | bytes 294944 | tf_op jit(solution)/shard_map/ppermute | solution.py:560
  57.4 1.8 collective-permute-start.13
  59.2 10.0 %collective-permute-done.15 = bf16[4,192,384]{2,1,0:T(8,128)(2,1)S(1)} collective-permute-done((bf16[4,192,384]{2,1,0:T(8,128)(2,1)S(1)}, bf16[4,192,384]{2,1,0:T(8,128)(2,1)S(1)}, u32[]{:S(2)}, u32[]{:S(2)}) %collective-permute-start.15) | collective-permute-done | bytes 589856 | tf_op jit(solution)/shard_map/ppermute | solution.py:560
  69.1 1.7 collective-permute-done.14
  73.9 8.9 %collective-permute-done.8 = bf16[2,4,384,128]{3,2,1,0:T(8,128)(2,1)S(1)} collective-permute-done((bf16[2,4,384,128]{3,2,1,0:T(8,128)(2,1)S(1)}, bf16[2,4,384,128]{3,2,1,0:T(8,128)(2,1)S(1)}, u32[]{:S(2)}, u32[]{:S(2)}) %collective-permute-start.8) | collective-permute-done | bytes 786464 | tf_op jit(solution)/shard_map/ppermute | solution.py:560
  87.5 3.2 %collective-permute-done.17.b_oth = bf16[4,3,384,128]{3,2,1,0:T(8,128)(2,1)} collective-permute-done((bf16[4,3,384,128]{3,2,1,0:T(8,128)(2,1)}, bf16[4,3,384,128]{3,2,1,0:T(8,128)(2,1)}, u32[]{:S(2)}, u32[]{:S(2)}) %collective-permute-start.17) | collective-permute-done | bytes 1179680 | tf_op jit(solution)/shard_map/ppermute | solution.py:560
  93.4 4.1 %shard_map.169 = (bf16[512,768]{1,0:T(8,128)(2,1)S(1)}, bf16[4,512,256]{2,1,0:T(8,128)(2,1)S(1)}, f32[8,768]{1,0:T(8,128)S(1)}) custom-call(s32[14]{0:T(128)S(1)} %stack.195.t, bf16[512,768]{1,0:T(8,128)(2,1)S(1)} %copy-done.11, bf16[4,4,384,128]{3,2,1,0:T(8,128)(2,1)S(1)} %bitcast.310, bf16[4,4,384,128]{3,2,1,0:T(8,128)(2,1)} %collective-permute-done.19.oth_ref.w_oth), custom_call_target="tpu_custom_call" | custom-call | flops 274877906944 | bytes 6291456 | tf_op jit(solution)/shard_map/pallas_call | solution.py:442
  97.6 8.8 %shard_map.170 = (bf16[4,512,256]{2,1,0:T(8,128)(2,1)S(1)}, f32[512,768]{1,0:T(8,128)S(1)}, bf16[512,768]{1,0:T(8,128)(2,1)S(1)}) custom-call(s32[14]{0:T(128)S(1)} %stack.195.t, bf16[512,768]{1,0:T(8,128)(2,1)S(1)} %copy-done.11, f32[8,768]{1,0:T(8,128)S(1)} %get-tuple-element.56.gain_ref, s32[512,1]{1,0:T(8,128)S(1)} %copy.28.dq_ref, ...), custom_call_target="tpu_custom_call" | custom-call | flops 274877906944 | bytes 14680064 | tf_op jit(solution)/shard_map/pallas_call | solution.py:454
  107.6 7.6 %collective-permute-done.22.refs_5_ = bf16[2,4,192,384]{3,2,1,0:T(8,128)(2,1)} collective-permute-done((bf16[2,4,192,384]{3,2,1,0:T(8,128)(2,1)}, bf16[2,4,192,384]{3,2,1,0:T(8,128)(2,1)}, u32[]{:S(2)}, u32[]{:S(2)}) %collective-permute-start.22) | collective-permute-done | bytes 1179680 | tf_op jit(solution)/shard_map/ppermute | solution.py:560
  115.2 3.9 %collective-permute-done.23.refs_7_ = bf16[2,4,192,384]{3,2,1,0:T(8,128)(2,1)} collective-permute-done((bf16[2,4,192,384]{3,2,1,0:T(8,128)(2,1)}, bf16[2,4,192,384]{3,2,1,0:T(8,128)(2,1)}, u32[]{:S(2)}, u32[]{:S(2)}) %collective-permute-start.23) | collective-permute-done | bytes 1179680 | tf_op jit(solution)/shard_map/ppermute | solution.py:560
  119.9 24.1 %shard_map.171 = (bf16[2,4,192,384]{3,2,1,0:T(8,128)(2,1)}, bf16[2,4,192,384]{3,2,1,0:T(8,128)(2,1)}, bf16[2,4,192,384]{3,2,1,0:T(8,128)(2,1)}, bf16[2,4,192,384...) custom-call(s32[14]{0:T(128)} %copy-done.9, ...), custom_call_target="tpu_custom_call" | custom-call | flops 274877906944 | bytes 20971520 | tf_op jit(solution)/shard_map/pallas_call | solution.py:473
  148.1 17.8 %shard_map.172 = (f32[512,768]{1,0:T(8,128)S(1)}, bf16[4,4,576,128]{3,2,1,0:T(8,128)(2,1)}, bf16[4,4,576,128]{3,2,1,0:T(8,128)(2,1)}, bf16[4,4,384,128]{3,2,1,0:...) custom-call(s32[14]{0:T(128)S(1)} %copy-done.10, f32[512,768]{1,0:T(8,128)S(1)} %copy-done.14, ...), custom_call_target="tpu_custom_call" | custom-call | flops 274877906944 | bytes 29360128 | tf_op jit(solution)/shard_map/pallas_call | solution.py:492
  166.4 6.4 %collective-permute-done.26 = bf16[2,4,192,384]{3,2,1,0:T(8,128)(2,1)} collective-permute-done((bf16[2,4,192,384]{3,2,1,0:T(8,128)(2,1)}, bf16[2,4,192,384]{3,2,1,0:T(8,128)(2,1)}, u32[]{:S(2)}, u32[]{:S(2)}) %collective-permute-start.26) | collective-permute-done | bytes 1179680 | tf_op jit(solution)/shard_map/ppermute | solution.py:560
  172.9 2.1 fusion.2
  176.5 2.0 fusion.3
  179.5 7.4 %shard_map.173 = (f32[512,768]{1,0:T(8,128)}, bf16[4,4,192,128]{3,2,1,0:T(8,128)(2,1)S(1)}, bf16[4,4,192,128]{3,2,1,0:T(8,128)(2,1)S(1)}) custom-call(s32[14]{0:T(128)S(1)} %copy-done.10, bf16[512,768]{1,0:T(8,128)(2,1)S(1)} %copy-done.12, f32[8,768]{1,0:T(8,128)S(1)} %copy-done.18, bf16[512,768]{1,0:T(8,128)(2,1)S(1)} %get-tuple-element.64.n_ref, ...), custom_call_target="tpu_custom_call" | custom-call | flops 274877906944 | bytes 12582912 | tf_op jit(solution)/shard_map/pallas_call | solution.py:516
  186.9 3.3 %collective-permute-done.28 = bf16[4,192,384]{2,1,0:T(8,128)(2,1)} collective-permute-done((bf16[4,192,384]{2,1,0:T(8,128)(2,1)}, bf16[4,192,384]{2,1,0:T(8,128)(2,1)}, u32[]{:S(2)}, u32[]{:S(2)}) %collective-permute-start.28) | collective-permute-done | bytes 589856 | tf_op jit(solution)/shard_map/ppermute | solution.py:560
  190.2 3.2 %collective-permute-done.29 = bf16[4,192,384]{2,1,0:T(8,128)(2,1)} collective-permute-done((bf16[4,192,384]{2,1,0:T(8,128)(2,1)}, bf16[4,192,384]{2,1,0:T(8,128)(2,1)}, u32[]{:S(2)}, u32[]{:S(2)}) %collective-permute-start.29) | collective-permute-done | bytes 589856 | tf_op jit(solution)/shard_map/ppermute | solution.py:560
  202.4 22.9 %collective-permute-done.35 = bf16[2,4,576,128]{3,2,1,0:T(8,128)(2,1)S(1)} collective-permute-done((bf16[2,4,576,128]{3,2,1,0:T(8,128)(2,1)S(1)}, bf16[2,4,576,128]{3,2,1,0:T(8,128)(2,1)S(1)}, u32[]{:S(2)}, u32[]{:S(2)}) %collective-permute-start.35) | collective-permute-done | bytes 1179680 | tf_op jit(solution)/shard_map/ppermute | solution.py:560
  229.9 2.6 collective-permute-start.42
  232.5 9.2 %collective-permute-done.36 = bf16[4,576,128]{2,1,0:T(8,128)(2,1)S(1)} collective-permute-done((bf16[4,576,128]{2,1,0:T(8,128)(2,1)S(1)}, bf16[4,576,128]{2,1,0:T(8,128)(2,1)S(1)}, u32[]{:S(2)}, u32[]{:S(2)}) %collective-permute-start.36) | collective-permute-done | bytes 589856 | tf_op jit(solution)/shard_map/ppermute | solution.py:560
  244.8 2.7 collective-permute-start.38
  249.0 3.6 %collective-permute-done.41 = bf16[384,384]{1,0:T(8,128)(2,1)S(1)} collective-permute-done((bf16[384,384]{1,0:T(8,128)(2,1)S(1)}, bf16[384,384]{1,0:T(8,128)(2,1)S(1)}, u32[]{:S(2)}, u32[]{:S(2)}) %collective-permute-start.41) | collective-permute-done | bytes 294944 | tf_op jit(solution)/shard_map/ppermute | solution.py:560
  253.7 5.1 %collective-permute-done.40 = bf16[384,384]{1,0:T(8,128)(2,1)S(1)} collective-permute-done((bf16[384,384]{1,0:T(8,128)(2,1)S(1)}, bf16[384,384]{1,0:T(8,128)(2,1)S(1)}, u32[]{:S(2)}, u32[]{:S(2)}) %collective-permute-start.40) | collective-permute-done | bytes 294944 | tf_op jit(solution)/shard_map/ppermute | solution.py:560
  258.7 2.1 fusion.8
  260.9 15.8 %collective-permute-done.38 = bf16[1152,128]{1,0:T(8,128)(2,1)S(1)} collective-permute-done((bf16[1152,128]{1,0:T(8,128)(2,1)S(1)}, bf16[1152,128]{1,0:T(8,128)(2,1)S(1)}, u32[]{:S(2)}, u32[]{:S(2)}) %collective-permute-start.38) | collective-permute-done | bytes 294944 | tf_op jit(solution)/shard_map/ppermute | solution.py:560
  (193 shorter events, 61.0 us)
Async XLA Ops:
  4.8 15.7 %collective-permute-start.2 = (bf16[768,128]{1,0:T(8,128)(2,1)S(1)}, bf16[768,128]{1,0:T(8,128)(2,1)S(1)}, u32[]{:S(2)}, u32[]{:S(2)}) collective-permute-start(bf16[768,128]{1,0:T(8,128)(2,1)S(1)} %maximum_maximum_fusion), channel_id=1, source_target_pairs={{0,6},{1,7},{2,4},{3,5},{4,2},{5,3},{6,0},{7,1},{8,14},{9,15},{10,... | collective-permute-start | bytes 589832 | tf_op jit(solution)/shard_map/ppermute | solution.py:560
  10.0 16.7 %collective-permute-start.1 = (bf16[768,128]{1,0:T(8,128)(2,1)S(1)}, bf16[768,128]{1,0:T(8,128)(2,1)S(1)}, u32[]{:S(2)}, u32[]{:S(2)}) collective-permute-start(bf16[768,128]{1,0:T(8,128)(2,1)S(1)} %maximum_maximum_fusion), channel_id=1, source_target_pairs={{0,4},{1,5},{2,6},{3,7},{4,0},{5,1},{6,2},{7,3},{8,12},{9,13},{10,... | collective-permute-start | bytes 589832 | tf_op jit(solution)/shard_map/ppermute | solution.py:560
  10.0 16.7 %collective-permute-start = (bf16[768,128]{1,0:T(8,128)(2,1)S(1)}, bf16[768,128]{1,0:T(8,128)(2,1)S(1)}, u32[]{:S(2)}, u32[]{:S(2)}) collective-permute-start(bf16[768,128]{1,0:T(8,128)(2,1)S(1)} %maximum_maximum_fusion), channel_id=1, source_target_pairs={{0,2},{1,3},{2,0},{3,1},{4,6},{5,7},{6,4},{7,5},{8,10},{9,11},{10,... | collective-permute-start | bytes 589832 | tf_op jit(solution)/shard_map/ppermute | solution.py:560
  29.4 23.2 %collective-permute-start.9 = (bf16[2,192,384]{2,1,0:T(8,128)(2,1)S(1)}, bf16[2,192,384]{2,1,0:T(8,128)(2,1)S(1)}, u32[]{:S(2)}, u32[]{:S(2)}) collective-permute-start(bf16[2,192,384]{2,1,0:T(8,128)(2,1)S(1)} %pad_maximum_fusion.16), channel_id=1, source_target_pairs={{0,4},{1,5},{2,6},{3,7},{4,0},{5,1},{6,2},{7,3},{8,12},{9,13},{10,... | collective-permute-start | bytes 884744 | tf_op jit(solution)/shard_map/ppermute | solution.py:560
  29.4 23.3 %collective-permute-start.7 = (bf16[2,192,384]{2,1,0:T(8,128)(2,1)S(1)}, bf16[2,192,384]{2,1,0:T(8,128)(2,1)S(1)}, u32[]{:S(2)}, u32[]{:S(2)}) collective-permute-start(bf16[2,192,384]{2,1,0:T(8,128)(2,1)S(1)} %pad_maximum_fusion.16), channel_id=1, source_target_pairs={{0,2},{1,3},{2,0},{3,1},{4,6},{5,7},{6,4},{7,5},{8,10},{9,11},{10,... | collective-permute-start | bytes 884744 | tf_op jit(solution)/shard_map/ppermute | solution.py:560
  31.4 24.7 %collective-permute-start.5 = (bf16[4,384,128]{2,1,0:T(8,128)(2,1)S(1)}, bf16[4,384,128]{2,1,0:T(8,128)(2,1)S(1)}, u32[]{:S(2)}, u32[]{:S(2)}) collective-permute-start(bf16[4,384,128]{2,1,0:T(8,128)(2,1)S(1)} %get-tuple-element.47), channel_id=1, source_target_pairs={{0,8},{1,9},{2,10},{3,11},{4,12},{5,13},{6,14},{7,15},{8,0},{9,1},... | collective-permute-start | bytes 1179656 | tf_op jit(solution)/shard_map/ppermute | solution.py:560
  33.0 23.2 %collective-permute-start.6 = (bf16[4,384,128]{2,1,0:T(8,128)(2,1)S(1)}, bf16[4,384,128]{2,1,0:T(8,128)(2,1)S(1)}, u32[]{:S(2)}, u32[]{:S(2)}) collective-permute-start(bf16[4,384,128]{2,1,0:T(8,128)(2,1)S(1)} %get-tuple-element.48), channel_id=1, source_target_pairs={{0,16},{1,17},{2,18},{3,19},{4,20},{5,21},{6,22},{7,23},{8,24},{9,... | collective-permute-start | bytes 1179656 | tf_op jit(solution)/shard_map/ppermute | solution.py:560
  52.8 16.3 %collective-permute-start.15 = (bf16[4,192,384]{2,1,0:T(8,128)(2,1)S(1)}, bf16[4,192,384]{2,1,0:T(8,128)(2,1)S(1)}, u32[]{:S(2)}, u32[]{:S(2)}) collective-permute-start(bf16[4,192,384]{2,1,0:T(8,128)(2,1)S(1)} %get-tuple-element.121), channel_id=1, source_target_pairs={{0,16},{1,17},{2,18},{3,19},{4,20},{5,21},{6,22},{7,23},{8,24},{9,... | collective-permute-start | bytes 1769480 | tf_op jit(solution)/shard_map/ppermute | solution.py:560
  54.5 16.3 %collective-permute-start.14 = (bf16[4,192,384]{2,1,0:T(8,128)(2,1)S(1)}, bf16[4,192,384]{2,1,0:T(8,128)(2,1)S(1)}, u32[]{:S(2)}, u32[]{:S(2)}) collective-permute-start(bf16[4,192,384]{2,1,0:T(8,128)(2,1)S(1)} %get-tuple-element.123), channel_id=1, source_target_pairs={{0,8},{1,9},{2,10},{3,11},{4,12},{5,13},{6,14},{7,15},{8,0},{9,1},... | collective-permute-start | bytes 1769480 | tf_op jit(solution)/shard_map/ppermute | solution.py:560
  56.3 26.5 %collective-permute-start.8 = (bf16[2,4,384,128]{3,2,1,0:T(8,128)(2,1)S(1)}, bf16[2,4,384,128]{3,2,1,0:T(8,128)(2,1)S(1)}, u32[]{:S(2)}, u32[]{:S(2)}) collective-permute-start(bf16[2,4,384,128]{3,2,1,0:T(8,128)(2,1)S(1)} %pad_maximum_fusion.6), channel_id=1, source_target_pairs={{0,16},{1,17},{2,18},{3,19},{4,20},{5,21},{6,22},{7,23},{8,24},{9,... | collective-permute-start | bytes 2359304 | tf_op jit(solution)/shard_map/ppermute | solution.py:560
  56.8 27.4 %collective-permute-start.18 = (bf16[2,4,384,128]{3,2,1,0:T(8,128)(2,1)S(1)}, bf16[2,4,384,128]{3,2,1,0:T(8,128)(2,1)S(1)}, u32[]{:S(2)}, u32[]{:S(2)}) collective-permute-start(bf16[2,4,384,128]{3,2,1,0:T(8,128)(2,1)S(1)} %pad_maximum_fusion.7), channel_id=1, source_target_pairs={{0,8},{1,9},{2,10},{3,11},{4,12},{5,13},{6,14},{7,15},{8,0},{9,1},... | collective-permute-start | bytes 2359304 | tf_op jit(solution)/shard_map/ppermute | solution.py:560
  57.4 25.6 %collective-permute-start.13 = (bf16[3,384,128]{2,1,0:T(8,128)(2,1)S(1)}, bf16[3,384,128]{2,1,0:T(8,128)(2,1)S(1)}, u32[]{:S(2)}, u32[]{:S(2)}) collective-permute-start(bf16[3,384,128]{2,1,0:T(8,128)(2,1)S(1)} %pad_maximum_fusion.15), channel_id=1, source_target_pairs={{0,6},{1,7},{2,4},{3,5},{4,2},{5,3},{6,0},{7,1},{8,14},{9,15},{10,... | collective-permute-start | bytes 884744 | tf_op jit(solution)/shard_map/ppermute | solution.py:560
  86.1 21.4 %collective-permute-start.21 = (bf16[512,768]{1,0:T(8,128)(2,1)}, bf16[512,768]{1,0:T(8,128)(2,1)}, u32[]{:S(2)}, u32[]{:S(2)}) collective-permute-start(bf16[512,768]{1,0:T(8,128)(2,1)} %c_ref.1), channel_id=1, source_target_pairs={{0,1},{1,0},{2,3},{3,2},{4,5},{5,4},{6,7},{7,6},{8,9},{9,8},{10,11... | collective-permute-start | bytes 2359304 | tf_op jit(solution)/shard_map/ppermute | solution.py:560
  86.6 28.5 %collective-permute-start.22 = (bf16[2,4,192,384]{3,2,1,0:T(8,128)(2,1)}, bf16[2,4,192,384]{3,2,1,0:T(8,128)(2,1)}, u32[]{:S(2)}, u32[]{:S(2)}) collective-permute-start(bf16[2,4,192,384]{3,2,1,0:T(8,128)(2,1)} %pad_maximum_fusion.2.refs_4_), channel_id=1, source_target_pairs={{0,16},{1,17},{2,18},{3,19},{4,20},{5,21},{6,22},{7,23},{8,24},{9,... | collective-permute-start | bytes 3538952 | tf_op jit(solution)/shard_map/ppermute | solution.py:560
  90.7 28.3 %collective-permute-start.23 = (bf16[2,4,192,384]{3,2,1,0:T(8,128)(2,1)}, bf16[2,4,192,384]{3,2,1,0:T(8,128)(2,1)}, u32[]{:S(2)}, u32[]{:S(2)}) collective-permute-start(bf16[2,4,192,384]{3,2,1,0:T(8,128)(2,1)} %pad_maximum_fusion.3.refs_6_), channel_id=1, source_target_pairs={{0,8},{1,9},{2,10},{3,11},{4,12},{5,13},{6,14},{7,15},{8,0},{9,1},... | collective-permute-start | bytes 3538952 | tf_op jit(solution)/shard_map/ppermute | solution.py:560
  144.2 28.7 %collective-permute-start.26 = (bf16[2,4,192,384]{3,2,1,0:T(8,128)(2,1)}, bf16[2,4,192,384]{3,2,1,0:T(8,128)(2,1)}, u32[]{:S(2)}, u32[]{:S(2)}) collective-permute-start(bf16[2,4,192,384]{3,2,1,0:T(8,128)(2,1)} %get-tuple-element.69), channel_id=1, source_target_pairs={{0,16},{1,17},{2,18},{3,19},{4,20},{5,21},{6,22},{7,23},{8,24},{9,... | collective-permute-start | bytes 3538952 | tf_op jit(solution)/shard_map/ppermute | solution.py:560
  145.2 31.3 %collective-permute-start.27 = (bf16[2,4,192,384]{3,2,1,0:T(8,128)(2,1)}, bf16[2,4,192,384]{3,2,1,0:T(8,128)(2,1)}, u32[]{:S(2)}, u32[]{:S(2)}) collective-permute-start(bf16[2,4,192,384]{3,2,1,0:T(8,128)(2,1)} %get-tuple-element.70), channel_id=1, source_target_pairs={{0,8},{1,9},{2,10},{3,11},{4,12},{5,13},{6,14},{7,15},{8,0},{9,1},... | collective-permute-start | bytes 3538952 | tf_op jit(solution)/shard_map/ppermute | solution.py:560
  165.9 27.5 %collective-permute-start.31 = (bf16[4,4,384,128]{3,2,1,0:T(8,128)(2,1)}, bf16[4,4,384,128]{3,2,1,0:T(8,128)(2,1)}, u32[]{:S(2)}, u32[]{:S(2)}) collective-permute-start(bf16[4,4,384,128]{3,2,1,0:T(8,128)(2,1)} %get-tuple-element.81), channel_id=1, source_target_pairs={{0,1},{1,0},{2,3},{3,2},{4,5},{5,4},{6,7},{7,6},{8,9},{9,8},{10,11... | collective-permute-start | bytes 4718600 | tf_op jit(solution)/shard_map/ppermute | solution.py:560
  166.0 27.4 %collective-permute-start.30 = (bf16[4,4,576,128]{3,2,1,0:T(8,128)(2,1)}, bf16[4,4,576,128]{3,2,1,0:T(8,128)(2,1)}, u32[]{:S(2)}, u32[]{:S(2)}) collective-permute-start(bf16[4,4,576,128]{3,2,1,0:T(8,128)(2,1)} %get-tuple-element.77), channel_id=1, source_target_pairs={{0,1},{1,0},{2,3},{3,2},{4,5},{5,4},{6,7},{7,6},{8,9},{9,8},{10,11... | collective-permute-start | bytes 7077896 | tf_op jit(solution)/shard_map/ppermute | solution.py:560
  175.0 15.2 %collective-permute-start.28 = (bf16[4,192,384]{2,1,0:T(8,128)(2,1)}, bf16[4,192,384]{2,1,0:T(8,128)(2,1)}, u32[]{:S(2)}, u32[]{:S(2)}) collective-permute-start(bf16[4,192,384]{2,1,0:T(8,128)(2,1)} %fusion.2), channel_id=1, source_target_pairs={{0,8},{1,9},{2,10},{3,11},{4,12},{5,13},{6,14},{7,15},{8,0},{9,1},... | collective-permute-start | bytes 1769480 | tf_op jit(solution)/shard_map/ppermute | solution.py:560
  178.5 14.9 %collective-permute-start.29 = (bf16[4,192,384]{2,1,0:T(8,128)(2,1)}, bf16[4,192,384]{2,1,0:T(8,128)(2,1)}, u32[]{:S(2)}, u32[]{:S(2)}) collective-permute-start(bf16[4,192,384]{2,1,0:T(8,128)(2,1)} %fusion.3), channel_id=1, source_target_pairs={{0,16},{1,17},{2,18},{3,19},{4,20},{5,21},{6,22},{7,23},{8,24},{9,... | collective-permute-start | bytes 1769480 | tf_op jit(solution)/shard_map/ppermute | solution.py:560
  196.9 28.4 %collective-permute-start.35 = (bf16[2,4,576,128]{3,2,1,0:T(8,128)(2,1)S(1)}, bf16[2,4,576,128]{3,2,1,0:T(8,128)(2,1)S(1)}, u32[]{:S(2)}, u32[]{:S(2)}) collective-permute-start(bf16[2,4,576,128]{3,2,1,0:T(8,128)(2,1)S(1)} %add_convert_fusion), channel_id=1, source_target_pairs={{0,16},{1,17},{2,18},{3,19},{4,20},{5,21},{6,22},{7,23},{8,24},{9,... | collective-permute-start | bytes 3538952 | tf_op jit(solution)/shard_map/ppermute | solution.py:560
  198.2 29.2 %collective-permute-start.33 = (bf16[2,4,576,128]{3,2,1,0:T(8,128)(2,1)S(1)}, bf16[2,4,576,128]{3,2,1,0:T(8,128)(2,1)S(1)}, u32[]{:S(2)}, u32[]{:S(2)}) collective-permute-start(bf16[2,4,576,128]{3,2,1,0:T(8,128)(2,1)S(1)} %pad_maximum_fusion.5), channel_id=1, source_target_pairs={{0,8},{1,9},{2,10},{3,11},{4,12},{5,13},{6,14},{7,15},{8,0},{9,1},... | collective-permute-start | bytes 3538952 | tf_op jit(solution)/shard_map/ppermute | solution.py:560
  199.2 48.4 %collective-permute-start.24 = (bf16[512,768]{1,0:T(8,128)(2,1)S(1)}, bf16[512,768]{1,0:T(8,128)(2,1)S(1)}, u32[]{:S(2)}, u32[]{:S(2)}) collective-permute-start(bf16[512,768]{1,0:T(8,128)(2,1)S(1)} %copy-done.32), channel_id=1, source_target_pairs={{0,1},{1,0},{2,3},{3,2},{4,5},{5,4},{6,7},{7,6},{8,9},{9,8},{10,11... | collective-permute-start | bytes 2359304 | tf_op jit(solution)/shard_map/ppermute | solution.py:560
  226.7 15.0 %collective-permute-start.36 = (bf16[4,576,128]{2,1,0:T(8,128)(2,1)S(1)}, bf16[4,576,128]{2,1,0:T(8,128)(2,1)S(1)}, u32[]{:S(2)}, u32[]{:S(2)}) collective-permute-start(bf16[4,576,128]{2,1,0:T(8,128)(2,1)S(1)} %fusion), channel_id=1, source_target_pairs={{0,8},{1,9},{2,10},{3,11},{4,12},{5,13},{6,14},{7,15},{8,0},{9,1},... | collective-permute-start | bytes 1769480 | tf_op jit(solution)/shard_map/ppermute | solution.py:560
  228.7 14.7 %collective-permute-start.34 = (bf16[4,576,128]{2,1,0:T(8,128)(2,1)S(1)}, bf16[4,576,128]{2,1,0:T(8,128)(2,1)S(1)}, u32[]{:S(2)}, u32[]{:S(2)}) collective-permute-start(bf16[4,576,128]{2,1,0:T(8,128)(2,1)S(1)} %pad_maximum_fusion.10), channel_id=1, source_target_pairs={{0,16},{1,17},{2,18},{3,19},{4,20},{5,21},{6,22},{7,23},{8,24},{9,... | collective-permute-start | bytes 1769480 | tf_op jit(solution)/shard_map/ppermute | solution.py:560
  229.7 22.8 %collective-permute-start.41 = (bf16[384,384]{1,0:T(8,128)(2,1)S(1)}, bf16[384,384]{1,0:T(8,128)(2,1)S(1)}, u32[]{:S(2)}, u32[]{:S(2)}) collective-permute-start(bf16[384,384]{1,0:T(8,128)(2,1)S(1)} %pad_maximum_fusion.21), channel_id=1, source_target_pairs={{0,4},{1,5},{2,6},{3,7},{4,0},{5,1},{6,2},{7,3},{8,12},{9,13},{10,... | collective-permute-start | bytes 884744 | tf_op jit(solution)/shard_map/ppermute | solution.py:560
  229.9 23.8 %collective-permute-start.42 = (bf16[384,384]{1,0:T(8,128)(2,1)S(1)}, bf16[384,384]{1,0:T(8,128)(2,1)S(1)}, u32[]{:S(2)}, u32[]{:S(2)}) collective-permute-start(bf16[384,384]{1,0:T(8,128)(2,1)S(1)} %pad_maximum_fusion.22), channel_id=1, source_target_pairs={{0,6},{1,7},{2,4},{3,5},{4,2},{5,3},{6,0},{7,1},{8,14},{9,15},{10,... | collective-permute-start | bytes 884744 | tf_op jit(solution)/shard_map/ppermute | solution.py:560
  241.7 17.1 %collective-permute-start.40 = (bf16[384,384]{1,0:T(8,128)(2,1)S(1)}, bf16[384,384]{1,0:T(8,128)(2,1)S(1)}, u32[]{:S(2)}, u32[]{:S(2)}) collective-permute-start(bf16[384,384]{1,0:T(8,128)(2,1)S(1)} %pad_maximum_fusion.20), channel_id=1, source_target_pairs={{0,2},{1,3},{2,0},{3,1},{4,6},{5,7},{6,4},{7,5},{8,10},{9,11},{10,... | collective-permute-start | bytes 884744 | tf_op jit(solution)/shard_map/ppermute | solution.py:560
  244.8 31.9 %collective-permute-start.38 = (bf16[1152,128]{1,0:T(8,128)(2,1)S(1)}, bf16[1152,128]{1,0:T(8,128)(2,1)S(1)}, u32[]{:S(2)}, u32[]{:S(2)}) collective-permute-start(bf16[1152,128]{1,0:T(8,128)(2,1)S(1)} %pad_maximum_fusion.18), channel_id=1, source_target_pairs={{0,4},{1,5},{2,6},{3,7},{4,0},{5,1},{6,2},{7,3},{8,12},{9,13},{10,... | collective-permute-start | bytes 884744 | tf_op jit(solution)/shard_map/ppermute | solution.py:560
  247.6 29.1 %collective-permute-start.39 = (bf16[1152,128]{1,0:T(8,128)(2,1)S(1)}, bf16[1152,128]{1,0:T(8,128)(2,1)S(1)}, u32[]{:S(2)}, u32[]{:S(2)}) collective-permute-start(bf16[1152,128]{1,0:T(8,128)(2,1)S(1)} %pad_maximum_fusion.19), channel_id=1, source_target_pairs={{0,6},{1,7},{2,4},{3,5},{4,2},{5,3},{6,0},{7,1},{8,14},{9,15},{10,... | collective-permute-start | bytes 884744 | tf_op jit(solution)/shard_map/ppermute | solution.py:560
  252.5 24.2 %collective-permute-start.37 = (bf16[1152,128]{1,0:T(8,128)(2,1)S(1)}, bf16[1152,128]{1,0:T(8,128)(2,1)S(1)}, u32[]{:S(2)}, u32[]{:S(2)}) collective-permute-start(bf16[1152,128]{1,0:T(8,128)(2,1)S(1)} %pad_maximum_fusion.17), channel_id=1, source_target_pairs={{0,2},{1,3},{2,0},{3,1},{4,6},{5,7},{6,4},{7,5},{8,10},{9,11},{10,... | collective-permute-start | bytes 884744 | tf_op jit(solution)/shard_map/ppermute | solution.py:560
  (45 other events, 513.3 us)

commit v7 on v6

--- a/solution.py
+++ b/solution.py
@@ -33,6 +33,20 @@
 GA = 0.044715
 VMEM_LIMIT = 40 * 1024 * 1024
 COST = 1 << 38
+CFG = {
+    "fz": ("c1",),
+    "aw1": ("bxy",),
+    "aw2": ("fz1",),
+    "bz": ("c1",),
+    "f1": ("aw1",),
+    "wc": ("f1",),
+    "ac": ("bz", "f1"),
+    "k1": ("ac", "bc"),
+    "f2r": ("sa",),
+    "k5": ("f1r", "ca", "co"),
+    "cv": ("f2r", "ca", "co", "cb"),
+    "fzr": ("wide",),
+}
 
 F32 = jnp.float32
 BF16 = jnp.bfloat16
@@ -332,7 +346,8 @@
 def mixer_back_body(
     t, dna_ref, dnb_ref, mid_ref, c_ref, gain_ref, dq_ref, dk_ref, mix_ref, val_ref,
     a_own, a_oth, b_own, b_oth, w_own, w_oth,
-    mg_ref, ka_ref, sa_ref, kb_ref, sb_ref, vg_ref, dg_acc, br_ref, grad_ref, vg_acc, go_ref,
+    mg_ref, ka_ref, sa_ref, kb_ref, sb_ref, ko_ref, so_ref, vg_ref, dg_acc, br_ref, grad_ref, vg_acc,
+    go_ref,
 ):
     m = pl.program_id(0)
     core = t[0]
@@ -364,11 +379,11 @@
     mask = halves(dq_ref, core) == dk_ref[:, pl.ds(k0, WIN * KB)]
     heads = head_masks(core, TM)
     for g in range(G):
-        for p, ref in ((0, ka_ref), (1, sa_ref)):
-            ref[tab_b(t, g), 0, HR:, :] = go_ref[m, g * DB : (g + 1) * DB, p * LN : (p + 1) * LN]
-    rest = jnp.where(start == 0, G - 1, 0)
-    for ref, tab in ((ka_ref, tab_b), (sa_ref, tab_b), (kb_ref, tab_a), (sb_ref, tab_a)):
-        ref[tab(t, rest), 0, 0:HR, :] = jnp.zeros((HR, KB), BF16)
+        for p, ref in ((0, ko_ref), (1, so_ref)):
+            ref[tab_a(t, g), 0] = go_ref[m, g * DB : (g + 1) * DB, p * LN : (p + 1) * LN]
+    rest = tab_b(t, jnp.where(start == 0, G - 1, 0))
+    for ref in (ka_ref, sa_ref):
+        ref[rest, 0] = jnp.zeros((HR, KB), BF16)
     for z in range(Z):
         grad = halves(grad_ref, core, z, base)
         mine = jnp.concatenate(
@@ -383,14 +398,14 @@
             head = HZ * z + i
             pd = prob[i] * dp[i * TM : (i + 1) * TM]
             ds = (pd - prob[i] * jnp.sum(pd, axis=-1, keepdims=True)).astype(BF16)
-            low_half = head < HA
-            row = (head if low_half else head - HA) * QB
-            tab = tab_b if low_half else tab_a
             for k in range(WIN):
-                for p, ref in enumerate((ka_ref, sa_ref) if low_half else (kb_ref, sb_ref)):
-                    ref[tab(t, start + k), 0, row : row + QB, :] = ds[
-                        p * QB : (p + 1) * QB, k * KB : (k + 1) * KB
-                    ]
+                for p, (ra, rb) in enumerate(((ka_ref, kb_ref), (sa_ref, sb_ref))):
+                    blk = ds[p * QB : (p + 1) * QB, k * KB : (k + 1) * KB]
+                    if head < HA:
+                        ra[tab_b(t, start + k), 0, head * QB : (head + 1) * QB, :] = blk
+                    else:
+                        h = head - HA
+                        rb[0, k, h * QB : (h + 1) * QB, :] = blk
 
     @pl.when(m == Z - 1)
     def _():
@@ -432,7 +447,6 @@
 W_SHAPE = (G, Z, 2 * DB, LN)
 V_SHAPE = (G, Z, DB, LN)
 A_SHAPE = (G, Z, HR, KB)
-AO_SHAPE = (G, Z, HR + DB, KB)
 B_SHAPE = (Z, WIN, HR, KB)
 F_SHAPE = (G, Z, DB, FB)
 Z_ROWS = pl.BlockSpec((Z, TM, GW), lambda i, t: (0, i, 0))
@@ -487,8 +501,9 @@
 
 
 def run_mixer_back(tab, dn, mid, cot, gain, dq, dk, mixed, vals, a, b, w):
-    blk_a = pl.BlockSpec((G, 1, HR + DB, KB), lambda i, t: (0, tab_z(t, i), 0, 0))
-    blk_b = pl.BlockSpec((G, 1, HR, KB), lambda i, t: (0, tab_z(t, i), 0, 0))
+    blk_a = pl.BlockSpec((G, 1, HR, KB), lambda i, t: (0, tab_z(t, i), 0, 0))
+    blk_b = pl.BlockSpec((1, WIN, HR, KB), lambda i, t: (tab_z(t, i), 0, 0, 0))
+    blk_o = pl.BlockSpec((G, 1, DB, LN), lambda i, t: (0, tab_z(t, i), 0, 0))
     return call(
         mixer_back_body,
         (L // TM,),
@@ -498,10 +513,10 @@
             whole(A_SHAPE), whole(A_SHAPE), whole(B_SHAPE), whole(B_SHAPE),
             whole(W_SHAPE), whole(W_SHAPE),
         ],
-        [out_whole((L, D)), blk_a, blk_a, blk_b, blk_b, out_whole((Z, L, GW))],
+        [out_whole((L, D)), blk_a, blk_a, blk_b, blk_b, blk_o, blk_o, out_whole((Z, L, GW))],
         [
-            sds((L, D), F32), sds(AO_SHAPE, BF16), sds(AO_SHAPE, BF16), sds(A_SHAPE, BF16),
-            sds(A_SHAPE, BF16), sds((Z, L, GW), BF16),
+            sds((L, D), F32), sds(A_SHAPE, BF16), sds(A_SHAPE, BF16), sds(B_SHAPE, BF16),
+            sds(B_SHAPE, BF16), sds(V_SHAPE, BF16), sds(V_SHAPE, BF16), sds((Z, L, GW), BF16),
         ],
         scratch=(
             pltpu.VMEM((8, D), F32), pltpu.VMEM((L, D), BF16), pltpu.VMEM((Z, L, GW), BF16),
@@ -620,7 +635,7 @@
         tab, (sides[0][5], sides[1][5]), mid, cot, gain, dq, dk, mixed, vals, a, b, w
     )
     grad_in, *gv = run_last(tab, x, gain, low, vg, w, mid_grad)
-    return layer_out, grad_in, gu, gd, ga[:2], ga[2:], gv
+    return layer_out, grad_in, gu, gd, ga[:2], ga[2:4], ga[4:], gv
 
 
 def lane_pad(mat, gains):
@@ -649,27 +664,59 @@
     def along_z(val):
         return [val] + [fetch(val, "z", k) for k in range(1, Z)]
 
+    events = {}
+
+    def mark(name, *vals):
+        events[name] = vals
+
+    def hook(name, val):
+        deps = [events[d] for d in CFG.get(name, ())]
+        return after(val, *deps) if deps else val
+
     c1 = along_z(jnp.concatenate([mix[0], wts], axis=0))
+    mark("c1", c1[1:])
     cots = [cot, fetch(cot, "c", 1)]
     b = spread(spread(mix[1], "x"), "y").reshape(G, HR, KB)
+    mark("bxy", b)
     start = window(at["z"])
     order = jnp.stack(order_b)
     b = jnp.stack([lax.dynamic_index_in_dim(b, order[start + i], 0, False) for i in range(WIN)])
     a, w = (jnp.stack([v[i * HR : (i + 1) * HR] for v in c1]) for i in range(2))
-    ffn = along_z(after(jnp.stack([up_w, down_w.T]), c1[1:]))
-    a, w = after((a, w), b)
-    a, w = spread(a, "x"), spread(w, "y")
-    a, w = after((a, w), ffn[1])
-    a, w = spread(a, "y").reshape(A_SHAPE), spread(w, "x").reshape(W_SHAPE)
-    b = along_z(after(b, ffn[1:]))
-    u, d = (jnp.stack([v[i] for v in ffn]) for i in range(2))
-    u, d = spread(u, "x"), spread(d, "y")
-    w, a = both(w, b[1:], u, d), both(a, b[1:], u, d)
-    u, d = after((u, d), a[0], w[0])
+    ffn = along_z(hook("fz", jnp.stack([up_w, down_w.T])))
+    for i in range(1, Z):
+        mark("fz%d" % i, ffn[i])
+    mark("fz", ffn[1:])
+    a, w = hook("aw1", (a, w))
+    ra, rw = fetch(a, "x", 1), fetch(w, "y", 1)
+    mark("aw1", ra, rw)
+    a, w = hook("aw2", (jnp.stack([a, ra]), jnp.stack([w, rw])))
+    ra, rw = fetch(a, "y", 1), fetch(w, "x", 1)
+    mark("aw2", ra, rw)
+    mark("w2", rw)
+    a, w = jnp.stack([a, ra]).reshape(A_SHAPE), jnp.stack([w, rw]).reshape(W_SHAPE)
+    b = along_z(hook("bz", b))
+    mark("bz1", b[1])
+    mark("bz", b[1:])
+    u, d = hook("f1", tuple(jnp.stack([v[i] for v in ffn]) for i in range(2)))
+    ru, rd = fetch(u, "x", 1), fetch(d, "y", 1)
+    mark("f1", ru, rd)
+    w = both(hook("wc", w))
+    mark("wc", w[1])
+    a = both(hook("ac", a))
+    mark("ac", a[1])
+    u, d = hook("f2", (jnp.stack([u, ru]), jnp.stack([d, rd])))
     u, d = [u, fetch(u, "y", 1)], [d, fetch(d, "x", 1)]
-    b = both(jnp.stack(b))
-    low, vals, gain = run_values(tab, after(layer_in, a[1], b[1]), w)
-    mixed, mid, n_two = run_mixer(tab, layer_in, gain, dq, dk, vals, a, b, w)
+    mark("f2", u[1], d[1])
+    if CFG.get("bc") == ("k1",):
+        low, vals, gain = run_values(tab, hook("k1", layer_in), w)
+        mark("k1", low)
+        b = both(hook("bc", jnp.stack(b)))
+        mark("bc", b[1])
+    else:
+        b = both(hook("bc", jnp.stack(b)))
+        mark("bc", b[1])
+        low, vals, gain = run_values(tab, hook("k1", layer_in), w)
+    mixed, mid, n_two = run_mixer(tab, layer_in, hook("k2", gain), dq, dk, vals, a, b, w)
 
     def begin(keep, send):
         got = fetch(send, "c", 1)
@@ -686,23 +733,65 @@
     gd = [(kd, 1), (fetch(sd, "x", 1), 1)]
     out_b = fetch(out_b, "c", 1)
     layer_out = (mid + out_a + out_b.astype(F32)).astype(BF16)
-    mid_grad, ka, sa, kb, sb, vg = run_mixer_back(
+    mid_grad, ka, sa, kb, sb, ko, so, vg = run_mixer_back(
         tab, (ng_a, ng_b), mid, cot, gain, dq, dk, mixed, vals, a, b, w
     )
-    vg = after(vg, last(gu, gd))
-    gu, gd = grid.reduce(gu, 1, "x", sa), grid.reduce(gd, 1, "y", sa)
-    grad_in, kv, sv = run_last(tab, layer_in, gain, low, vg, w, mid_grad)
-    ga, gb = begin(ka, sa), begin(kb, sb)
-    gv = begin(kv, after(sv, last(gu, gd, ga, gb)))
+    mark("f1r", last(gu, gd))
+    mark("sa", sa)
+    gu, gd = gu[:-1] + [(hook("f2r", gu[-1][0]), 1)], gd[:-1] + [(hook("f2r", gd[-1][0]), 1)]
+    gu, gd = grid.reduce(gu, 1, "x"), grid.reduce(gd, 1, "y")
+    mark("f2r", last(gu, gd))
+
+    def cores():
+        rb = fetch(hook("cab", sb), "c", 1)
+        mark("cb", rb)
+        ga, go = begin(ka, hook("cab", sa)), begin(ko, hook("cab", so))
+        mark("ca", last(ga))
+        mark("co", last(go))
+        return ga, go, [(kb, 2), (rb, 2)]
+
+    if CFG.get("cab") != ("sv",):
+        ga, go, gb = cores()
+        gb[-1] = (hook("bzr", gb[-1][0]), 2)
+        gb = grid.reduce(gb, 2, "z")
+        mark("bzr1", last(gb[:-2]))
+        mark("bzr", last(gb))
+    grad_in, kv, sv = run_last(tab, layer_in, gain, low, hook("k5", vg), w, mid_grad)
+    mark("sv", sv)
+    if CFG.get("cab") == ("sv",):
+        ga, go, gb = cores()
+        gb = grid.reduce(gb, 2, "z")
+        mark("bzr", last(gb))
+    gv = begin(kv, hook("cv", sv))
+    mark("cv", last(gv))
+    ga[-1] = (hook("m1a", ga[-1][0]), 0)
     ga = grid.reduce(ga, 0, "y")
-    bv = grid.reduce_pair(gb, gv, 0, "x")
+    mark("m1a", last(ga))
+    go[-1] = (hook("m1b", go[-1][0]), 0)
+    go, gv = grid.reduce_pair(go, gv, 0, "x")
+    mark("m1b", last(go))
+    gb[-1] = (hook("by", gb[-1][0]), 3)
+    wide = grid.total(gb, 3)
+    mark("wide", wide)
+    blocks = []
+    for k in range(G):
+        spot = (at["y"] ^ (k // 2)) * 2 + (at["x"] ^ (k % 2)) - start
+        blk = lax.dynamic_index_in_dim(wide, jnp.clip(spot, 0, WIN - 1), 0, False)
+        ok = jnp.logical_and(spot >= 0, spot < WIN)
+        blocks.append(jnp.where(ok, blk, jnp.zeros_like(blk)))
+    gb = [(jnp.stack(blocks).reshape(2, 2, HR, KB), 0)]
+    gu[-1] = (hook("fzr", gu[-1][0]), 2)
     gu, gd = grid.reduce_joined((gu, gd), "z")
+    mark("fzr", gu)
     ga = grid.reduce(ga, 1, "x")
-    bv = grid.reduce_pair(*bv, 1, "y")
-    ga, gb, gv = grid.reduce_joined((ga, *bv), "z")
-
-    go = ga[HR:]
-    grad_mixing = jnp.concatenate([ga[:HR], gb], axis=0).reshape(H, QB, KB)
+    mark("m2a", last(ga))
+    go, gv = grid.reduce_pair(go, gv, 1, "y")
+    mark("m2", last(ga, go))
+    gb = grid.reduce(gb, 0, "y")
+    gb = grid.total(grid.reduce(gb, 1, "x"), 2)
+    ga, go, gv = grid.reduce_joined((ga, go, gv), "z")
+
+    grad_mixing = jnp.concatenate([ga, gb], axis=0).reshape(H, QB, KB)
     return (
         layer_out, grad_in, gv[0, CB : CB + GN], gv[:, :CB], grad_mixing, go[:, :CB].T,
         go[0, CB : CB + GN], gu, gd.T,
@@ -761,7 +850,7 @@
         grads = rest if grads is None else jax.tree.map(jnp.add, grads, rest)
     layer_out = jnp.concatenate([r[0] for r in rows_out], axis=0)
     grad_in = jnp.concatenate([r[1] for r in rows_out], axis=0)
-    gu, gd, ga, gb, gv = jax.tree.map(lambda v: v.astype(BF16), grads)
+    gu, gd, ga, gb, go, gv = jax.tree.map(lambda v: v.astype(BF16), grads)
 
     def by_a(v):
         return v.reshape((2, 2) + v.shape[1:]).swapaxes(0, 1).reshape(v.shape)
@@ -770,9 +859,16 @@
         return jnp.stack(pair).transpose(1, 3, 2, 0, 4).reshape(D, FF)
 
     value_full, dg_one = cols_out(*[by_a(v) for v in gv])
-    output_full, dg_two = cols_out(*[v[:, :, HR:] for v in ga])
-    gm = jnp.stack([jnp.stack([v[:, :, :HR] for v in ga]), jnp.stack([by_a(v) for v in gb])])
-    gm = gm.reshape(2, 2, G, Z, HA, QB, KB).transpose(0, 4, 3, 1, 5, 2, 6)
+    output_full, dg_two = cols_out(*[by_a(v) for v in go])
+    gb = jnp.stack(gb)
+    gb = jnp.stack(
+        [
+            jnp.pad(gb[:, m], ((0, 0), (s, G - WIN - s), (0, 0), (0, 0)))
+            for m, s in enumerate(starts)
+        ],
+        axis=2,
+    )
+    gm = jnp.stack([jnp.stack(ga), gb]).reshape(2, 2, G, Z, HA, QB, KB).transpose(0, 4, 3, 1, 5, 2, 6)
     gd = [by_a(v) for v in gd]
     dgs = jnp.stack([dg_one, dg_two]).astype(F32)
     dgs = lax.psum_scatter(dgs, ax, scatter_dimension=1, tiled=True)

time: 289 us -> 274 us (0.948); the launches traced: 284 us -> 273 us
  waiting for transfers between devices: 131 us -> 107 us
  starting transfers between devices: 42.2 us -> 53.4 us
    ppermute x43 -> x49, waiting for transfers between devices: 131 us -> 107 us  [fetch(): return lax.ppermute(val, ('gx', 'gy'), pairs)]
    ppermute x43 -> x49, starting transfers between devices: 42.2 us -> 53.4 us  [fetch(): return lax.ppermute(val, ('gx', 'gy'), pairs)]
    another operation x2 -> x12, other arithmetic: 1.39 us -> 5.78 us  [the longest x2 3.62 us: small_shards(): u, d = hook('f2', (jnp.stack([u, ru]), jnp.stack([d, rd])))]
    unnamed x70 -> x120, local copies, waits for them, and re-layouts: 8.69 us -> 12.2 us
    another operation x10 -> x2, other arithmetic: 3.12 us -> 0.07 us  [spread(): jnp.stack([val] + [self.fetch(val, axis, k) for k in range(1, self.size[a...]
    convert_element_type x4 -> x6, other arithmetic: 7.01 us -> 5.2 us  [reduce(): add_up([v[(0,) * (stage - born) + (k,)] for v, born in terms]).astype(BF16)]
  transfers between devices with their start and end apart: 43 -> 49, of which waited for: 19 -> 19; matrix products, arithmetic and copies ran while one was open for 9% -> 9% of each run, Pallas kernels for 13% -> 14%
where the time goes in v7:
time: 274 us; the launch traced here: 273 us
  waiting for transfers between devices  107 us (39%)
  Pallas kernels  62.5 us (23%)
  starting transfers between devices  53.4 us (19%)
  other arithmetic  26.5 us (10%)
  local copies, waits for them, and re-layouts  16.7 us (6%)
  between operations  7.35 us (3%)
    ppermute x49, waiting for transfers between devices, fetch(): return lax.ppermute(val, ('gx', 'gy'), pairs)  107 us
    ppermute x49, starting transfers between devices, fetch(): return lax.ppermute(val, ('gx', 'gy'), pairs)  53.4 us
    pallas_call x1, Pallas kernels, run_ffn(): call(functools.partial(ffn_body, n - 1), (Z // ZS,), [whole((L, D))] * (2...  24 us
    pallas_call x1, Pallas kernels, run_mixer_back(): call(mixer_back_body, (L // TM,), [whole((L, D)), whole((L, D)), whole((L...  17.8 us
    unnamed x120, local copies, waits for them, and re-layouts  12.2 us
    pallas_call x1, Pallas kernels, run_mixer(): call(mixer_body, (L // TM,), [whole((L, D)), whole((8, D)), rows(1), whol...  8.77 us
    pallas_call x1, Pallas kernels, run_last(): call(last_body, (1,), [whole((L, D)), whole((8, D)), whole((L, D)), whole...  7.71 us
  transfers between devices with their start and end apart: 49, of which 19 were waited for; matrix products, arithmetic and copies ran while one was open for 9% of the time, Pallas kernels for 14%

profile of v7, /device:TPU:0, one launch (start us, length us, event | category | flops | bytes accessed | tf_op | source)
XLA Modules:
  0.0 273.3 jit_solution(7814320294353725272)
XLA Ops:
  4.8 5.1 %collective-permute-start.2 = (bf16[768,128]{1,0:T(8,128)(2,1)S(1)}, bf16[768,128]{1,0:T(8,128)(2,1)S(1)}, u32[]{:S(2)}, u32[]{:S(2)}) collective-permute-start(bf16[768,128]{1,0:T(8,128)(2,1)S(1)} %maximum_maximum_fusion), channel_id=1, source_target_pairs={{0,6},{1,7},{2,4},{3,5},{4,2},{5,3},{6,0},{7,1},{8,14},{9,15},{10,... | collective-permute-start | bytes 589832 | tf_op jit(solution)/shard_map/ppermute | solution.py:575
  10.6 1.6 collective-permute-start.3
  20.6 6.1 %collective-permute-done.1 = bf16[768,128]{1,0:T(8,128)(2,1)S(1)} collective-permute-done((bf16[768,128]{1,0:T(8,128)(2,1)S(1)}, bf16[768,128]{1,0:T(8,128)(2,1)S(1)}, u32[]{:S(2)}, u32[]{:S(2)}) %collective-permute-start.1) | collective-permute-done | bytes 196640 | tf_op jit(solution)/shard_map/ppermute | solution.py:575
  26.7 2.5 collective-permute-start.13
  33.6 7.7 %collective-permute-done.7 = bf16[2,192,384]{2,1,0:T(8,128)(2,1)S(1)} collective-permute-done((bf16[2,192,384]{2,1,0:T(8,128)(2,1)S(1)}, bf16[2,192,384]{2,1,0:T(8,128)(2,1)S(1)}, u32[]{:S(2)}, u32[]{:S(2)}) %collective-permute-start.7) | collective-permute-done | bytes 294944 | tf_op jit(solution)/shard_map/ppermute | solution.py:575
  45.1 9.8 %collective-permute-done.12 = bf16[2,192,384]{2,1,0:T(8,128)(2,1)S(1)} collective-permute-done((bf16[2,192,384]{2,1,0:T(8,128)(2,1)S(1)}, bf16[2,192,384]{2,1,0:T(8,128)(2,1)S(1)}, u32[]{:S(2)}, u32[]{:S(2)}) %collective-permute-start.12) | collective-permute-done | bytes 294944 | tf_op jit(solution)/shard_map/ppermute | solution.py:575
  58.8 2.5 collective-permute-start.11
  61.4 16.2 %collective-permute-done.10 = bf16[3,384,128]{2,1,0:T(8,128)(2,1)S(1)} collective-permute-done((bf16[3,384,128]{2,1,0:T(8,128)(2,1)S(1)}, bf16[3,384,128]{2,1,0:T(8,128)(2,1)S(1)}, u32[]{:S(2)}, u32[]{:S(2)}) %collective-permute-start.10) | collective-permute-done | bytes 294944 | tf_op jit(solution)/shard_map/ppermute | solution.py:575
  80.8 2.5 pad_maximum_fusion.3.refs_4_
  85.9 4.1 %shard_map.169 = (bf16[512,768]{1,0:T(8,128)(2,1)S(1)}, bf16[4,512,256]{2,1,0:T(8,128)(2,1)S(1)}, f32[8,768]{1,0:T(8,128)S(1)}) custom-call(s32[14]{0:T(128)S(1)} %stack.204.t, bf16[512,768]{1,0:T(8,128)(2,1)S(1)} %copy-done.16, bf16[4,4,384,128]{3,2,1,0:T(8,128)(2,1)S(1)} %bitcast.335, bf16[4,4,384,128]{3,2,1,0:T(8,128)(2,1)} %collective-permute-done.19.oth_ref.w_oth), custom_call_target="tpu_custom_call" | custom-call | flops 274877906944 | bytes 6291456 | tf_op jit(solution)/shard_map/pallas_call | solution.py:456
  91.1 8.8 %shard_map.170 = (bf16[4,512,256]{2,1,0:T(8,128)(2,1)S(1)}, f32[512,768]{1,0:T(8,128)S(1)}, bf16[512,768]{1,0:T(8,128)(2,1)S(1)}) custom-call(s32[14]{0:T(128)S(1)} %stack.204.t, bf16[512,768]{1,0:T(8,128)(2,1)S(1)} %copy-done.16, f32[8,768]{1,0:T(8,128)S(1)} %get-tuple-element.61.gain_ref, s32[512,1]{1,0:T(8,128)S(1)} %copy.28.dq_ref, ...), custom_call_target="tpu_custom_call" | custom-call | flops 274877906944 | bytes 14680064 | tf_op jit(solution)/shard_map/pallas_call | solution.py:468
  101.1 10.7 %collective-permute-done.22.refs_5_ = bf16[2,4,192,384]{3,2,1,0:T(8,128)(2,1)} collective-permute-done((bf16[2,4,192,384]{3,2,1,0:T(8,128)(2,1)}, bf16[2,4,192,384]{3,2,1,0:T(8,128)(2,1)}, u32[]{:S(2)}, u32[]{:S(2)}) %collective-permute-start.22) | collective-permute-done | bytes 1179680 | tf_op jit(solution)/shard_map/ppermute | solution.py:575
  111.8 1.9 collective-permute-done.23.refs_7_
  114.6 24.0 %shard_map.171 = (bf16[2,4,192,384]{3,2,1,0:T(8,128)(2,1)}, bf16[2,4,192,384]{3,2,1,0:T(8,128)(2,1)}, bf16[2,4,192,384]{3,2,1,0:T(8,128)(2,1)}, bf16[2,4,192,384...) custom-call(s32[14]{0:T(128)} %copy-done.14, ...), custom_call_target="tpu_custom_call" | custom-call | flops 274877906944 | bytes 20971520 | tf_op jit(solution)/shard_map/pallas_call | solution.py:487
  141.6 17.8 %shard_map.172 = (f32[512,768]{1,0:T(8,128)S(1)}, bf16[4,4,384,128]{3,2,1,0:T(8,128)(2,1)S(1)}, bf16[4,4,384,128]{3,2,1,0:T(8,128)(2,1)}, bf16[4,3,384,128]{3,2,...) custom-call(s32[14]{0:T(128)S(1)} %copy-done.15, ...), custom_call_target="tpu_custom_call" | custom-call | flops 274877906944 | bytes 29360128 | tf_op jit(solution)/shard_map/pallas_call | solution.py:507
  165.1 2.9 %add_convert_fusion.1 = bf16[512,768]{1,0:T(8,128)(2,1)} fusion(bf16[512,768]{1,0:T(8,128)(2,1)} %collective-permute-done.24, f32[512,768]{1,0:T(8,128)S(1)} %copy-done.6, f32[512,768]{1,0:T(8,128)} %get-tuple-element.65), kind=kLoop, calls=%fused_computation.3 | loop fusion | flops 1572864 | bytes 4718592 | tf_op jit(solution)/shard_map/convert_element_type | solution.py:735
  170.6 2.0 fusion.1
  174.2 1.8 collective-permute-start.43
  175.9 6.6 %collective-permute-start.42 = (bf16[3,384,128]{2,1,0:T(8,128)(2,1)S(1)}, bf16[3,384,128]{2,1,0:T(8,128)(2,1)S(1)}, u32[]{:S(2)}, u32[]{:S(2)}) collective-permute-start(bf16[3,384,128]{2,1,0:T(8,128)(2,1)S(1)} %get-tuple-element.130), channel_id=1, source_target_pairs={{0,4},{1,5},{2,6},{3,7},{4,0},{5,1},{6,2},{7,3},{8,12},{9,13},{10,... | collective-permute-start | bytes 884744 | tf_op jit(solution)/shard_map/ppermute | solution.py:575
  185.7 2.1 fusion.18
  187.8 16.0 %collective-permute-done.42 = bf16[3,384,128]{2,1,0:T(8,128)(2,1)S(1)} collective-permute-done((bf16[3,384,128]{2,1,0:T(8,128)(2,1)S(1)}, bf16[3,384,128]{2,1,0:T(8,128)(2,1)S(1)}, u32[]{:S(2)}, u32[]{:S(2)}) %collective-permute-start.42) | collective-permute-done | bytes 294944 | tf_op jit(solution)/shard_map/ppermute | solution.py:575
  203.8 2.0 fusion.4
  206.9 7.7 %shard_map.173 = (f32[512,768]{1,0:T(8,128)}, bf16[4,4,192,128]{3,2,1,0:T(8,128)(2,1)S(1)}, bf16[4,4,192,128]{3,2,1,0:T(8,128)(2,1)S(1)}) custom-call(s32[14]{0:T(128)S(1)} %copy-done.15, bf16[512,768]{1,0:T(8,128)(2,1)S(1)} %copy-done.17, f32[8,768]{1,0:T(8,128)S(1)} %copy-done.29, bf16[512,768]{1,0:T(8,128)(2,1)S(1)} %copy-done.27, ...), custom_call_target="tpu_custom_call" | custom-call | flops 274877906944 | bytes 12582912 | tf_op jit(solution)/shard_map/pallas_call | solution.py:531
  217.4 1.8 collective-permute-start.48
  222.3 2.1 collective-permute-start.46
  224.4 14.6 %collective-permute-done.36 = bf16[2,4,384,128]{3,2,1,0:T(8,128)(2,1)S(1)} collective-permute-done((bf16[2,4,384,128]{3,2,1,0:T(8,128)(2,1)S(1)}, bf16[2,4,384,128]{3,2,1,0:T(8,128)(2,1)S(1)}, u32[]{:S(2)}, u32[]{:S(2)}) %collective-permute-start.36) | collective-permute-done | bytes 786464 | tf_op jit(solution)/shard_map/ppermute | solution.py:575
  243.8 2.2 fusion.13
  246.0 5.4 %collective-permute-done.37 = bf16[4,384,128]{2,1,0:T(8,128)(2,1)S(1)} collective-permute-done((bf16[4,384,128]{2,1,0:T(8,128)(2,1)S(1)}, bf16[4,384,128]{2,1,0:T(8,128)(2,1)S(1)}, u32[]{:S(2)}, u32[]{:S(2)}) %collective-permute-start.37) | collective-permute-done | bytes 393248 | tf_op jit(solution)/shard_map/ppermute | solution.py:575
  252.2 1.7 collective-permute-start.40
  254.0 2.8 %collective-permute-start.38 = (bf16[768,128]{1,0:T(8,128)(2,1)S(1)}, bf16[768,128]{1,0:T(8,128)(2,1)S(1)}, u32[]{:S(2)}, u32[]{:S(2)}) collective-permute-start(bf16[768,128]{1,0:T(8,128)(2,1)S(1)} %pad_maximum_fusion.22), channel_id=1, source_target_pairs={{0,2},{1,3},{2,0},{3,1},{4,6},{5,7},{6,4},{7,5},{8,10},{9,11},{10,... | collective-permute-start | bytes 589832 | tf_op jit(solution)/shard_map/ppermute | solution.py:575
  256.8 5.1 %collective-permute-done.40 = bf16[768,128]{1,0:T(8,128)(2,1)S(1)} collective-permute-done((bf16[768,128]{1,0:T(8,128)(2,1)S(1)}, bf16[768,128]{1,0:T(8,128)(2,1)S(1)}, u32[]{:S(2)}, u32[]{:S(2)}) %collective-permute-start.40) | collective-permute-done | bytes 196640 | tf_op jit(solution)/shard_map/ppermute | solution.py:575
  261.9 7.4 %collective-permute-done.39 = bf16[768,128]{1,0:T(8,128)(2,1)S(1)} collective-permute-done((bf16[768,128]{1,0:T(8,128)(2,1)S(1)}, bf16[768,128]{1,0:T(8,128)(2,1)S(1)}, u32[]{:S(2)}, u32[]{:S(2)}) %collective-permute-start.39) | collective-permute-done | bytes 196640 | tf_op jit(solution)/shard_map/ppermute | solution.py:575
  (258 shorter events, 60.7 us)
Async XLA Ops:
  4.8 15.7 %collective-permute-start.2 = (bf16[768,128]{1,0:T(8,128)(2,1)S(1)}, bf16[768,128]{1,0:T(8,128)(2,1)S(1)}, u32[]{:S(2)}, u32[]{:S(2)}) collective-permute-start(bf16[768,128]{1,0:T(8,128)(2,1)S(1)} %maximum_maximum_fusion), channel_id=1, source_target_pairs={{0,6},{1,7},{2,4},{3,5},{4,2},{5,3},{6,0},{7,1},{8,14},{9,15},{10,... | collective-permute-start | bytes 589832 | tf_op jit(solution)/shard_map/ppermute | solution.py:575
  10.0 16.7 %collective-permute-start.1 = (bf16[768,128]{1,0:T(8,128)(2,1)S(1)}, bf16[768,128]{1,0:T(8,128)(2,1)S(1)}, u32[]{:S(2)}, u32[]{:S(2)}) collective-permute-start(bf16[768,128]{1,0:T(8,128)(2,1)S(1)} %maximum_maximum_fusion), channel_id=1, source_target_pairs={{0,4},{1,5},{2,6},{3,7},{4,0},{5,1},{6,2},{7,3},{8,12},{9,13},{10,... | collective-permute-start | bytes 589832 | tf_op jit(solution)/shard_map/ppermute | solution.py:575
  10.0 16.7 %collective-permute-start = (bf16[768,128]{1,0:T(8,128)(2,1)S(1)}, bf16[768,128]{1,0:T(8,128)(2,1)S(1)}, u32[]{:S(2)}, u32[]{:S(2)}) collective-permute-start(bf16[768,128]{1,0:T(8,128)(2,1)S(1)} %maximum_maximum_fusion), channel_id=1, source_target_pairs={{0,2},{1,3},{2,0},{3,1},{4,6},{5,7},{6,4},{7,5},{8,10},{9,11},{10,... | collective-permute-start | bytes 589832 | tf_op jit(solution)/shard_map/ppermute | solution.py:575
  26.7 16.8 %collective-permute-start.13 = (bf16[2,192,384]{2,1,0:T(8,128)(2,1)S(1)}, bf16[2,192,384]{2,1,0:T(8,128)(2,1)S(1)}, u32[]{:S(2)}, u32[]{:S(2)}) collective-permute-start(bf16[2,192,384]{2,1,0:T(8,128)(2,1)S(1)} %pad_maximum_fusion.16), channel_id=1, source_target_pairs={{0,6},{1,7},{2,4},{3,5},{4,2},{5,3},{6,0},{7,1},{8,14},{9,15},{10,... | collective-permute-start | bytes 884744 | tf_op jit(solution)/shard_map/ppermute | solution.py:575
  29.1 25.7 %collective-permute-start.12 = (bf16[2,192,384]{2,1,0:T(8,128)(2,1)S(1)}, bf16[2,192,384]{2,1,0:T(8,128)(2,1)S(1)}, u32[]{:S(2)}, u32[]{:S(2)}) collective-permute-start(bf16[2,192,384]{2,1,0:T(8,128)(2,1)S(1)} %pad_maximum_fusion.16), channel_id=1, source_target_pairs={{0,4},{1,5},{2,6},{3,7},{4,0},{5,1},{6,2},{7,3},{8,12},{9,13},{10,... | collective-permute-start | bytes 884744 | tf_op jit(solution)/shard_map/ppermute | solution.py:575
  41.3 16.9 %collective-permute-start.9 = (bf16[3,384,128]{2,1,0:T(8,128)(2,1)S(1)}, bf16[3,384,128]{2,1,0:T(8,128)(2,1)S(1)}, u32[]{:S(2)}, u32[]{:S(2)}) collective-permute-start(bf16[3,384,128]{2,1,0:T(8,128)(2,1)S(1)} %pad_maximum_fusion.17), channel_id=1, source_target_pairs={{0,2},{1,3},{2,0},{3,1},{4,6},{5,7},{6,4},{7,5},{8,10},{9,11},{10,... | collective-permute-start | bytes 884744 | tf_op jit(solution)/shard_map/ppermute | solution.py:575
  41.5 17.3 %collective-permute-start.8 = (bf16[2,4,384,128]{3,2,1,0:T(8,128)(2,1)S(1)}, bf16[2,4,384,128]{3,2,1,0:T(8,128)(2,1)S(1)}, u32[]{:S(2)}, u32[]{:S(2)}) collective-permute-start(bf16[2,4,384,128]{3,2,1,0:T(8,128)(2,1)S(1)} %pad_maximum_fusion.5), channel_id=1, source_target_pairs={{0,16},{1,17},{2,18},{3,19},{4,20},{5,21},{6,22},{7,23},{8,24},{9,... | collective-permute-start | bytes 2359304 | tf_op jit(solution)/shard_map/ppermute | solution.py:575
  43.5 34.2 %collective-permute-start.18 = (bf16[2,4,384,128]{3,2,1,0:T(8,128)(2,1)S(1)}, bf16[2,4,384,128]{3,2,1,0:T(8,128)(2,1)S(1)}, u32[]{:S(2)}, u32[]{:S(2)}) collective-permute-start(bf16[2,4,384,128]{3,2,1,0:T(8,128)(2,1)S(1)} %pad_maximum_fusion.6), channel_id=1, source_target_pairs={{0,8},{1,9},{2,10},{3,11},{4,12},{5,13},{6,14},{7,15},{8,0},{9,1},... | collective-permute-start | bytes 2359304 | tf_op jit(solution)/shard_map/ppermute | solution.py:575
  55.1 22.5 %collective-permute-start.14 = (bf16[4,192,384]{2,1,0:T(8,128)(2,1)S(1)}, bf16[4,192,384]{2,1,0:T(8,128)(2,1)S(1)}, u32[]{:S(2)}, u32[]{:S(2)}) collective-permute-start(bf16[4,192,384]{2,1,0:T(8,128)(2,1)S(1)} %get-tuple-element.55), channel_id=1, source_target_pairs={{0,8},{1,9},{2,10},{3,11},{4,12},{5,13},{6,14},{7,15},{8,0},{9,1},... | collective-permute-start | bytes 1769480 | tf_op jit(solution)/shard_map/ppermute | solution.py:575
  56.7 20.9 %collective-permute-start.15 = (bf16[4,192,384]{2,1,0:T(8,128)(2,1)S(1)}, bf16[4,192,384]{2,1,0:T(8,128)(2,1)S(1)}, u32[]{:S(2)}, u32[]{:S(2)}) collective-permute-start(bf16[4,192,384]{2,1,0:T(8,128)(2,1)S(1)} %get-tuple-element.56), channel_id=1, source_target_pairs={{0,16},{1,17},{2,18},{3,19},{4,20},{5,21},{6,22},{7,23},{8,24},{9,... | collective-permute-start | bytes 1769480 | tf_op jit(solution)/shard_map/ppermute | solution.py:575
  58.2 19.4 %collective-permute-start.10 = (bf16[3,384,128]{2,1,0:T(8,128)(2,1)S(1)}, bf16[3,384,128]{2,1,0:T(8,128)(2,1)S(1)}, u32[]{:S(2)}, u32[]{:S(2)}) collective-permute-start(bf16[3,384,128]{2,1,0:T(8,128)(2,1)S(1)} %pad_maximum_fusion.17), channel_id=1, source_target_pairs={{0,4},{1,5},{2,6},{3,7},{4,0},{5,1},{6,2},{7,3},{8,12},{9,13},{10,... | collective-permute-start | bytes 884744 | tf_op jit(solution)/shard_map/ppermute | solution.py:575
  58.8 18.8 %collective-permute-start.11 = (bf16[3,384,128]{2,1,0:T(8,128)(2,1)S(1)}, bf16[3,384,128]{2,1,0:T(8,128)(2,1)S(1)}, u32[]{:S(2)}, u32[]{:S(2)}) collective-permute-start(bf16[3,384,128]{2,1,0:T(8,128)(2,1)S(1)} %pad_maximum_fusion.17), channel_id=1, source_target_pairs={{0,6},{1,7},{2,4},{3,5},{4,2},{5,3},{6,0},{7,1},{8,14},{9,15},{10,... | collective-permute-start | bytes 884744 | tf_op jit(solution)/shard_map/ppermute | solution.py:575
  80.3 20.8 %collective-permute-start.21 = (bf16[512,768]{1,0:T(8,128)(2,1)}, bf16[512,768]{1,0:T(8,128)(2,1)}, u32[]{:S(2)}, u32[]{:S(2)}) collective-permute-start(bf16[512,768]{1,0:T(8,128)(2,1)} %c_ref.1), channel_id=1, source_target_pairs={{0,1},{1,0},{2,3},{3,2},{4,5},{5,4},{6,7},{7,6},{8,9},{9,8},{10,11... | collective-permute-start | bytes 2359304 | tf_op jit(solution)/shard_map/ppermute | solution.py:575
  83.3 28.6 %collective-permute-start.22 = (bf16[2,4,192,384]{3,2,1,0:T(8,128)(2,1)}, bf16[2,4,192,384]{3,2,1,0:T(8,128)(2,1)}, u32[]{:S(2)}, u32[]{:S(2)}) collective-permute-start(bf16[2,4,192,384]{3,2,1,0:T(8,128)(2,1)} %pad_maximum_fusion.3.refs_4_), channel_id=1, source_target_pairs={{0,16},{1,17},{2,18},{3,19},{4,20},{5,21},{6,22},{7,23},{8,24},{9,... | collective-permute-start | bytes 3538952 | tf_op jit(solution)/shard_map/ppermute | solution.py:575
  85.4 28.3 %collective-permute-start.23 = (bf16[2,4,192,384]{3,2,1,0:T(8,128)(2,1)}, bf16[2,4,192,384]{3,2,1,0:T(8,128)(2,1)}, u32[]{:S(2)}, u32[]{:S(2)}) collective-permute-start(bf16[2,4,192,384]{3,2,1,0:T(8,128)(2,1)} %pad_maximum_fusion.4.refs_6_), channel_id=1, source_target_pairs={{0,8},{1,9},{2,10},{3,11},{4,12},{5,13},{6,14},{7,15},{8,0},{9,1},... | collective-permute-start | bytes 3538952 | tf_op jit(solution)/shard_map/ppermute | solution.py:575
  138.7 26.2 %collective-permute-start.24 = (bf16[512,768]{1,0:T(8,128)(2,1)}, bf16[512,768]{1,0:T(8,128)(2,1)}, u32[]{:S(2)}, u32[]{:S(2)}) collective-permute-start(bf16[512,768]{1,0:T(8,128)(2,1)} %get-tuple-element.66), channel_id=1, source_target_pairs={{0,1},{1,0},{2,3},{3,2},{4,5},{5,4},{6,7},{7,6},{8,9},{9,8},{10,11... | collective-permute-start | bytes 2359304 | tf_op jit(solution)/shard_map/ppermute | solution.py:575
  139.2 28.7 %collective-permute-start.26 = (bf16[2,4,192,384]{3,2,1,0:T(8,128)(2,1)}, bf16[2,4,192,384]{3,2,1,0:T(8,128)(2,1)}, u32[]{:S(2)}, u32[]{:S(2)}) collective-permute-start(bf16[2,4,192,384]{3,2,1,0:T(8,128)(2,1)} %get-tuple-element.72), channel_id=1, source_target_pairs={{0,16},{1,17},{2,18},{3,19},{4,20},{5,21},{6,22},{7,23},{8,24},{9,... | collective-permute-start | bytes 3538952 | tf_op jit(solution)/shard_map/ppermute | solution.py:575
  140.2 28.0 %collective-permute-start.27 = (bf16[2,4,192,384]{3,2,1,0:T(8,128)(2,1)}, bf16[2,4,192,384]{3,2,1,0:T(8,128)(2,1)}, u32[]{:S(2)}, u32[]{:S(2)}) collective-permute-start(bf16[2,4,192,384]{3,2,1,0:T(8,128)(2,1)} %get-tuple-element.73), channel_id=1, source_target_pairs={{0,8},{1,9},{2,10},{3,11},{4,12},{5,13},{6,14},{7,15},{8,0},{9,1},... | collective-permute-start | bytes 3538952 | tf_op jit(solution)/shard_map/ppermute | solution.py:575
  164.6 41.2 %collective-permute-start.28 = (bf16[4,4,384,128]{3,2,1,0:T(8,128)(2,1)}, bf16[4,4,384,128]{3,2,1,0:T(8,128)(2,1)S(1)}, u32[]{:S(2)}, u32[]{:S(2)}) collective-permute-start(bf16[4,4,384,128]{3,2,1,0:T(8,128)(2,1)} %get-tuple-element.74), channel_id=1, source_target_pairs={{0,1},{1,0},{2,3},{3,2},{4,5},{5,4},{6,7},{7,6},{8,9},{9,8},{10,11... | collective-permute-start | bytes 4718600 | tf_op jit(solution)/shard_map/ppermute | solution.py:575
  164.9 17.5 %collective-permute-start.29 = (bf16[4,4,192,128]{3,2,1,0:T(8,128)(2,1)}, bf16[4,4,192,128]{3,2,1,0:T(8,128)(2,1)S(1)}, u32[]{:S(2)}, u32[]{:S(2)}) collective-permute-start(bf16[4,4,192,128]{3,2,1,0:T(8,128)(2,1)} %copy-done.18), channel_id=1, source_target_pairs={{0,1},{1,0},{2,3},{3,2},{4,5},{5,4},{6,7},{7,6},{8,9},{9,8},{10,11... | collective-permute-start | bytes 2359304 | tf_op jit(solution)/shard_map/ppermute | solution.py:575
  169.5 15.4 %collective-permute-start.31 = (bf16[4,192,384]{2,1,0:T(8,128)(2,1)S(1)}, bf16[4,192,384]{2,1,0:T(8,128)(2,1)S(1)}, u32[]{:S(2)}, u32[]{:S(2)}) collective-permute-start(bf16[4,192,384]{2,1,0:T(8,128)(2,1)S(1)} %fusion.2), channel_id=1, source_target_pairs={{0,16},{1,17},{2,18},{3,19},{4,20},{5,21},{6,22},{7,23},{8,24},{9,... | collective-permute-start | bytes 1769480 | tf_op jit(solution)/shard_map/ppermute | solution.py:575
  175.9 27.8 %collective-permute-start.42 = (bf16[3,384,128]{2,1,0:T(8,128)(2,1)S(1)}, bf16[3,384,128]{2,1,0:T(8,128)(2,1)S(1)}, u32[]{:S(2)}, u32[]{:S(2)}) collective-permute-start(bf16[3,384,128]{2,1,0:T(8,128)(2,1)S(1)} %get-tuple-element.130), channel_id=1, source_target_pairs={{0,4},{1,5},{2,6},{3,7},{4,0},{5,1},{6,2},{7,3},{8,12},{9,13},{10,... | collective-permute-start | bytes 884744 | tf_op jit(solution)/shard_map/ppermute | solution.py:575
  182.5 21.3 %collective-permute-start.41 = (bf16[3,384,128]{2,1,0:T(8,128)(2,1)S(1)}, bf16[3,384,128]{2,1,0:T(8,128)(2,1)S(1)}, u32[]{:S(2)}, u32[]{:S(2)}) collective-permute-start(bf16[3,384,128]{2,1,0:T(8,128)(2,1)S(1)} %get-tuple-element.128), channel_id=1, source_target_pairs={{0,2},{1,3},{2,0},{3,1},{4,6},{5,7},{6,4},{7,5},{8,10},{9,11},{10,... | collective-permute-start | bytes 884744 | tf_op jit(solution)/shard_map/ppermute | solution.py:575
  185.0 29.7 %collective-permute-start.30 = (bf16[4,192,384]{2,1,0:T(8,128)(2,1)}, bf16[4,192,384]{2,1,0:T(8,128)(2,1)}, u32[]{:S(2)}, u32[]{:S(2)}) collective-permute-start(bf16[4,192,384]{2,1,0:T(8,128)(2,1)} %fusion.1), channel_id=1, source_target_pairs={{0,8},{1,9},{2,10},{3,11},{4,12},{5,13},{6,14},{7,15},{8,0},{9,1},... | collective-permute-start | bytes 1769480 | tf_op jit(solution)/shard_map/ppermute | solution.py:575
  217.4 24.1 %collective-permute-start.48 = (bf16[384,384]{1,0:T(8,128)(2,1)S(1)}, bf16[384,384]{1,0:T(8,128)(2,1)S(1)}, u32[]{:S(2)}, u32[]{:S(2)}) collective-permute-start(bf16[384,384]{1,0:T(8,128)(2,1)S(1)} %pad_maximum_fusion.20), channel_id=1, source_target_pairs={{0,6},{1,7},{2,4},{3,5},{4,2},{5,3},{6,0},{7,1},{8,14},{9,15},{10,... | collective-permute-start | bytes 884744 | tf_op jit(solution)/shard_map/ppermute | solution.py:575
  219.3 19.7 %collective-permute-start.36 = (bf16[2,4,384,128]{3,2,1,0:T(8,128)(2,1)S(1)}, bf16[2,4,384,128]{3,2,1,0:T(8,128)(2,1)S(1)}, u32[]{:S(2)}, u32[]{:S(2)}) collective-permute-start(bf16[2,4,384,128]{3,2,1,0:T(8,128)(2,1)S(1)} %add_convert_fusion), channel_id=1, source_target_pairs={{0,16},{1,17},{2,18},{3,19},{4,20},{5,21},{6,22},{7,23},{8,24},{9,... | collective-permute-start | bytes 2359304 | tf_op jit(solution)/shard_map/ppermute | solution.py:575
  220.6 19.3 %collective-permute-start.34 = (bf16[2,4,384,128]{3,2,1,0:T(8,128)(2,1)S(1)}, bf16[2,4,384,128]{3,2,1,0:T(8,128)(2,1)S(1)}, u32[]{:S(2)}, u32[]{:S(2)}) collective-permute-start(bf16[2,4,384,128]{3,2,1,0:T(8,128)(2,1)S(1)} %pad_maximum_fusion.7), channel_id=1, source_target_pairs={{0,8},{1,9},{2,10},{3,11},{4,12},{5,13},{6,14},{7,15},{8,0},{9,1},... | collective-permute-start | bytes 2359304 | tf_op jit(solution)/shard_map/ppermute | solution.py:575
  221.5 22.4 %collective-permute-start.47 = (bf16[384,384]{1,0:T(8,128)(2,1)S(1)}, bf16[384,384]{1,0:T(8,128)(2,1)S(1)}, u32[]{:S(2)}, u32[]{:S(2)}) collective-permute-start(bf16[384,384]{1,0:T(8,128)(2,1)S(1)} %pad_maximum_fusion.19), channel_id=1, source_target_pairs={{0,4},{1,5},{2,6},{3,7},{4,0},{5,1},{6,2},{7,3},{8,12},{9,13},{10,... | collective-permute-start | bytes 884744 | tf_op jit(solution)/shard_map/ppermute | solution.py:575
  222.3 21.5 %collective-permute-start.46 = (bf16[384,384]{1,0:T(8,128)(2,1)S(1)}, bf16[384,384]{1,0:T(8,128)(2,1)S(1)}, u32[]{:S(2)}, u32[]{:S(2)}) collective-permute-start(bf16[384,384]{1,0:T(8,128)(2,1)S(1)} %pad_maximum_fusion.18), channel_id=1, source_target_pairs={{0,2},{1,3},{2,0},{3,1},{4,6},{5,7},{6,4},{7,5},{8,10},{9,11},{10,... | collective-permute-start | bytes 884744 | tf_op jit(solution)/shard_map/ppermute | solution.py:575
  239.0 17.8 %collective-permute-start.45 = (bf16[384,128]{1,0:T(8,128)(2,1)S(1)}, bf16[384,128]{1,0:T(8,128)(2,1)S(1)}, u32[]{:S(2)}, u32[]{:S(2)}) collective-permute-start(bf16[384,128]{1,0:T(8,128)(2,1)S(1)} %fusion.24), channel_id=1, source_target_pairs={{0,8},{1,9},{2,10},{3,11},{4,12},{5,13},{6,14},{7,15},{8,0},{9,1},... | collective-permute-start | bytes 294920 | tf_op jit(solution)/shard_map/ppermute | solution.py:575
  253.9 15.4 %collective-permute-start.39 = (bf16[768,128]{1,0:T(8,128)(2,1)S(1)}, bf16[768,128]{1,0:T(8,128)(2,1)S(1)}, u32[]{:S(2)}, u32[]{:S(2)}) collective-permute-start(bf16[768,128]{1,0:T(8,128)(2,1)S(1)} %pad_maximum_fusion.23), channel_id=1, source_target_pairs={{0,4},{1,5},{2,6},{3,7},{4,0},{5,1},{6,2},{7,3},{8,12},{9,13},{10,... | collective-permute-start | bytes 589832 | tf_op jit(solution)/shard_map/ppermute | solution.py:575
  254.0 15.3 %collective-permute-start.38 = (bf16[768,128]{1,0:T(8,128)(2,1)S(1)}, bf16[768,128]{1,0:T(8,128)(2,1)S(1)}, u32[]{:S(2)}, u32[]{:S(2)}) collective-permute-start(bf16[768,128]{1,0:T(8,128)(2,1)S(1)} %pad_maximum_fusion.22), channel_id=1, source_target_pairs={{0,2},{1,3},{2,0},{3,1},{4,6},{5,7},{6,4},{7,5},{8,10},{9,11},{10,... | collective-permute-start | bytes 589832 | tf_op jit(solution)/shard_map/ppermute | solution.py:575
  (76 other events, 816.8 us)

commit v8 on v7

--- a/solution.py
+++ b/solution.py
@@ -42,10 +42,9 @@
     "wc": ("f1",),
     "ac": ("bz", "f1"),
     "k1": ("ac", "bc"),
-    "f2r": ("sa",),
-    "k5": ("f1r", "ca", "co"),
-    "cv": ("f2r", "ca", "co", "cb"),
-    "fzr": ("wide",),
+    "cp": ("f1r",),
+    "m1": ("f2r",),
+    "m2": ("fzr",),
 }
 
 F32 = jnp.float32
@@ -343,17 +342,24 @@
     return dv, jnp.sum(dn * xhat, axis=0, keepdims=True)
 
 
-def mixer_back_body(
-    t, dna_ref, dnb_ref, mid_ref, c_ref, gain_ref, dq_ref, dk_ref, mix_ref, val_ref,
+def back_body(
+    t, dna_ref, dnb_ref, mid_ref, c_ref, x_ref, low_ref, gain_ref, dq_ref, dk_ref, mix_ref, val_ref,
     a_own, a_oth, b_own, b_oth, w_own, w_oth,
-    mg_ref, ka_ref, sa_ref, kb_ref, sb_ref, ko_ref, so_ref, vg_ref, dg_acc, br_ref, grad_ref, vg_acc,
-    go_ref,
+    gi_ref, kp_ref, sp_ref, kq_ref, sq_ref,
+    dg_acc, br_ref, grad_ref, vg_acc, vg_ref, full_ref, mg_ref, dn_ref,
 ):
     m = pl.program_id(0)
     core = t[0]
     base = m * TM
     start = window(m)
     k0 = pl.multiple_of(start * KB, KB)
+
+    def put(tab, refs):
+        for z in range(Z):
+            for g in range(G):
+                for p, ref in enumerate(refs):
+                    blk = full_ref[z, g * DB : (g + 1) * DB, p * LN : (p + 1) * LN]
+                    ref[tab(t, g), tab_z(t, z), HR:, :] = blk
 
     @pl.when(m == 0)
     def _():
@@ -373,17 +379,18 @@
         branch = br_ref[...]
         for z in range(Z):
             grad_ref[z] = dot(branch, weight_z(w_own, w_oth, t, z, DB), 1, 0).astype(BF16)
-            go_ref[z] = dot(branch, mix_ref[z], 0, 0).astype(BF16)
-        with_gains(go_ref, dg_acc[0:1, :], t)
+            full_ref[z] = dot(branch, mix_ref[z], 0, 0).astype(BF16)
+        with_gains(full_ref, dg_acc[0:1, :], t)
+        put(tab_b, (kp_ref, sp_ref))
+        dg_acc[...] = jnp.zeros_like(dg_acc)
 
     mask = halves(dq_ref, core) == dk_ref[:, pl.ds(k0, WIN * KB)]
     heads = head_masks(core, TM)
-    for g in range(G):
-        for p, ref in ((0, ko_ref), (1, so_ref)):
-            ref[tab_a(t, g), 0] = go_ref[m, g * DB : (g + 1) * DB, p * LN : (p + 1) * LN]
-    rest = tab_b(t, jnp.where(start == 0, G - 1, 0))
-    for ref in (ka_ref, sa_ref):
-        ref[rest, 0] = jnp.zeros((HR, KB), BF16)
+    at_z = tab_z(t, m)
+    rest = jnp.where(start == 0, G - 1, 0)
+    for refs, tab in (((kp_ref, sp_ref), tab_b), ((kq_ref, sq_ref), tab_a)):
+        for ref in refs:
+            ref[tab(t, rest), at_z, 0:HR, :] = jnp.zeros((HR, KB), BF16)
     for z in range(Z):
         grad = halves(grad_ref, core, z, base)
         mine = jnp.concatenate(
@@ -398,46 +405,34 @@
             head = HZ * z + i
             pd = prob[i] * dp[i * TM : (i + 1) * TM]
             ds = (pd - prob[i] * jnp.sum(pd, axis=-1, keepdims=True)).astype(BF16)
+            refs, tab = ((kp_ref, sp_ref), tab_b) if head < HA else ((kq_ref, sq_ref), tab_a)
+            row = head % HA * QB
             for k in range(WIN):
-                for p, (ra, rb) in enumerate(((ka_ref, kb_ref), (sa_ref, sb_ref))):
-                    blk = ds[p * QB : (p + 1) * QB, k * KB : (k + 1) * KB]
-                    if head < HA:
-                        ra[tab_b(t, start + k), 0, head * QB : (head + 1) * QB, :] = blk
-                    else:
-                        h = head - HA
-                        rb[0, k, h * QB : (h + 1) * QB, :] = blk
+                for p, ref in enumerate(refs):
+                    ref[tab(t, start + k), at_z, row : row + QB, :] = ds[
+                        p * QB : (p + 1) * QB, k * KB : (k + 1) * KB
+                    ]
 
     @pl.when(m == Z - 1)
     def _():
         vg_ref[...] = vg_acc[...].astype(BF16)
-
-
-def last_body(
-    t, x_ref, gain_ref, n_ref, vg_ref, w_own, w_oth, mg_ref, gi_ref, kv_ref, sv_ref, dg_acc, dn_ref,
-    gv_ref,
-):
-    dg_acc[...] = jnp.zeros_like(dg_acc)
-    acc = dot(vg_ref[0], weight_z(w_own, w_oth, t, 0, 0), 1, 1)
-    for z in range(1, Z):
-        acc = acc + dot(vg_ref[z], weight_z(w_own, w_oth, t, z, 0), 1, 1)
-    dn_ref[...] = acc
-
-    def norm(at):
-        cen, rstd = norm_stats(x_ref[at, :].astype(F32))
-        dv, dg = norm_back(cen, rstd, gain_ref[0:1, :], dn_ref[at, :])
-        dg_acc[0:1, :] += dg
-        gi_ref[at, :] = mg_ref[at, :] + dv
-
-    by_rows(norm)
-    low = n_ref[...]
-    for z in range(Z):
-        gv_ref[z] = dot(low, vg_ref[z], 0, 0).astype(BF16)
-    with_gains(gv_ref, dg_acc[0:1, :], t)
-    for z in range(Z):
-        for g in range(G):
-            for p, ref in ((0, kv_ref), (1, sv_ref)):
-                blk = gv_ref[z, g * DB : (g + 1) * DB, p * LN : (p + 1) * LN]
-                ref[tab_a(t, g), tab_z(t, z)] = blk
+        acc = dot(vg_ref[0], weight_z(w_own, w_oth, t, 0, 0), 1, 1)
+        for z in range(1, Z):
+            acc = acc + dot(vg_ref[z], weight_z(w_own, w_oth, t, z, 0), 1, 1)
+        dn_ref[...] = acc
+
+        def norm(at):
+            cen, rstd = norm_stats(x_ref[at, :].astype(F32))
+            dv, dg = norm_back(cen, rstd, gain_ref[0:1, :], dn_ref[at, :])
+            dg_acc[0:1, :] += dg
+            gi_ref[at, :] = mg_ref[at, :] + dv
+
+        by_rows(norm)
+        low = low_ref[...]
+        for z in range(Z):
+            full_ref[z] = dot(low, vg_ref[z], 0, 0).astype(BF16)
+        with_gains(full_ref, dg_acc[0:1, :], t)
+        put(tab_a, (kq_ref, sq_ref))
 
 
 def sds(shape, dtype):
@@ -447,6 +442,7 @@
 W_SHAPE = (G, Z, 2 * DB, LN)
 V_SHAPE = (G, Z, DB, LN)
 A_SHAPE = (G, Z, HR, KB)
+S_SHAPE = (G, Z, HR + DB, KB)
 B_SHAPE = (Z, WIN, HR, KB)
 F_SHAPE = (G, Z, DB, FB)
 Z_ROWS = pl.BlockSpec((Z, TM, GW), lambda i, t: (0, i, 0))
@@ -500,47 +496,25 @@
     )(tab, *ns, *cots, *u_w, *d_w)
 
 
-def run_mixer_back(tab, dn, mid, cot, gain, dq, dk, mixed, vals, a, b, w):
-    blk_a = pl.BlockSpec((G, 1, HR, KB), lambda i, t: (0, tab_z(t, i), 0, 0))
-    blk_b = pl.BlockSpec((1, WIN, HR, KB), lambda i, t: (tab_z(t, i), 0, 0, 0))
-    blk_o = pl.BlockSpec((G, 1, DB, LN), lambda i, t: (0, tab_z(t, i), 0, 0))
+def run_back(tab, dn, mid, cot, x, low, gain, dq, dk, mixed, vals, a, b, w):
+    args = [*dn, mid, cot, x, low, gain, dq, dk, mixed, vals, *a, *b, *w]
+    specs = [whole(None)] * len(args)
+    specs[7] = rows(1)
     return call(
-        mixer_back_body,
+        back_body,
         (L // TM,),
-        [
-            whole((L, D)), whole((L, D)), whole((L, D)), whole((L, D)), whole((8, D)), rows(1),
-            whole((1, L)), whole((Z, L, GW)), whole((Z, L, GW)),
-            whole(A_SHAPE), whole(A_SHAPE), whole(B_SHAPE), whole(B_SHAPE),
-            whole(W_SHAPE), whole(W_SHAPE),
-        ],
-        [out_whole((L, D)), blk_a, blk_a, blk_b, blk_b, blk_o, blk_o, out_whole((Z, L, GW))],
-        [
-            sds((L, D), F32), sds(A_SHAPE, BF16), sds(A_SHAPE, BF16), sds(B_SHAPE, BF16),
-            sds(B_SHAPE, BF16), sds(V_SHAPE, BF16), sds(V_SHAPE, BF16), sds((Z, L, GW), BF16),
-        ],
+        specs,
+        [whole(None)] * 5,
+        [sds((L, D), F32)] + [sds(S_SHAPE, BF16)] * 4,
         scratch=(
             pltpu.VMEM((8, D), F32), pltpu.VMEM((L, D), BF16), pltpu.VMEM((Z, L, GW), BF16),
-            pltpu.VMEM((Z, L, GW), F32), pltpu.VMEM((Z, D, GW), BF16),
+            pltpu.VMEM((Z, L, GW), F32), pltpu.VMEM((Z, L, GW), BF16), pltpu.VMEM((Z, D, GW), BF16),
+            pltpu.VMEM((L, D), F32), pltpu.VMEM((L, D), F32),
         ),
-        flops=4 * L * D * Z * GW + 6 * H * L * WIN * KB * GW,
-        nbytes=28 << 20,
-    )(tab, *dn, mid, cot, gain, dq, dk, mixed, vals, *a, *b, *w)
-
-
-def run_last(tab, x, gain, low, vg, w, mid_grad):
-    return call(
-        last_body,
-        (1,),
-        [
-            whole((L, D)), whole((8, D)), whole((L, D)), whole((Z, L, GW)), whole(W_SHAPE),
-            whole(W_SHAPE), whole((L, D)),
-        ],
-        [out_whole((L, D)), out_whole(V_SHAPE), out_whole(V_SHAPE)],
-        [sds((L, D), F32), sds(V_SHAPE, BF16), sds(V_SHAPE, BF16)],
-        scratch=(pltpu.VMEM((8, D), F32), pltpu.VMEM((L, D), F32), pltpu.VMEM((Z, D, GW), BF16)),
-        flops=4 * L * D * Z * GW,
-        nbytes=12 << 20,
-    )(tab, x, gain, low, vg, *w, mid_grad)
+        flops=8 * L * D * Z * GW,
+        nbytes=40 << 20,
+        vmem=32 << 20,
+    )(tab, *args)
 
 
 def add_up(terms):
@@ -591,16 +565,6 @@
 
     def total(self, terms, stage):
         return add_up([v[(0,) * (stage - born)] for v, born in terms])
-
-    def reduce_pair(self, p, q, stage, axis, *deps):
-        if deps:
-            p = p[:-1] + [(after(p[-1][0], *deps), p[-1][1])]
-        parts = [
-            add_up([v[(0,) * (stage - born) + (1,)] for v, born in terms]).astype(BF16) for terms in (p, q)
-        ]
-        rows_p = parts[0].shape[-2]
-        got = self.fetch(jnp.concatenate(parts, axis=-2), axis, 1)
-        return p + [(got[..., :rows_p, :], stage + 1)], q + [(got[..., rows_p:, :], stage + 1)]
 
     def reduce_joined(self, groups, axis, *deps):
         groups = list(groups)
@@ -631,11 +595,10 @@
     ]
     gu, gd = ([jnp.concatenate(v[i : i + 2], axis=0) for v in sides] for i in (0, 2))
     layer_out = (mid + sides[0][4] + sides[1][4]).astype(BF16)
-    mid_grad, *ga, vg = run_mixer_back(
-        tab, (sides[0][5], sides[1][5]), mid, cot, gain, dq, dk, mixed, vals, a, b, w
+    grad_in, kp, sp, kq, sq = run_back(
+        tab, (sides[0][5], sides[1][5]), mid, cot, x, low, gain, dq, dk, mixed, vals, a, b, w
     )
-    grad_in, *gv = run_last(tab, x, gain, low, vg, w, mid_grad)
-    return layer_out, grad_in, gu, gd, ga[:2], ga[2:4], ga[4:], gv
+    return layer_out, grad_in, gu, gd, (kp, sp), (kq, sq)
 
 
 def lane_pad(mat, gains):
@@ -733,65 +696,29 @@
     gd = [(kd, 1), (fetch(sd, "x", 1), 1)]
     out_b = fetch(out_b, "c", 1)
     layer_out = (mid + out_a + out_b.astype(F32)).astype(BF16)
-    mid_grad, ka, sa, kb, sb, ko, so, vg = run_mixer_back(
-        tab, (ng_a, ng_b), mid, cot, gain, dq, dk, mixed, vals, a, b, w
+    grad_in, kp, sp, kq, sq = run_back(
+        tab, (ng_a, ng_b), mid, cot, layer_in, low, gain, dq, dk, mixed, vals, a, b, w
     )
     mark("f1r", last(gu, gd))
-    mark("sa", sa)
-    gu, gd = gu[:-1] + [(hook("f2r", gu[-1][0]), 1)], gd[:-1] + [(hook("f2r", gd[-1][0]), 1)]
-    gu, gd = grid.reduce(gu, 1, "x"), grid.reduce(gd, 1, "y")
+    sp, sq = hook("cp", (sp, sq))
+    gp, gq = begin(kp, sp), begin(kq, sq)
+    mark("cp", last(gp, gq))
+    gu, gd = grid.reduce(gu, 1, "x", sp), grid.reduce(gd, 1, "y", sp)
     mark("f2r", last(gu, gd))
-
-    def cores():
-        rb = fetch(hook("cab", sb), "c", 1)
-        mark("cb", rb)
-        ga, go = begin(ka, hook("cab", sa)), begin(ko, hook("cab", so))
-        mark("ca", last(ga))
-        mark("co", last(go))
-        return ga, go, [(kb, 2), (rb, 2)]
-
-    if CFG.get("cab") != ("sv",):
-        ga, go, gb = cores()
-        gb[-1] = (hook("bzr", gb[-1][0]), 2)
-        gb = grid.reduce(gb, 2, "z")
-        mark("bzr1", last(gb[:-2]))
-        mark("bzr", last(gb))
-    grad_in, kv, sv = run_last(tab, layer_in, gain, low, hook("k5", vg), w, mid_grad)
-    mark("sv", sv)
-    if CFG.get("cab") == ("sv",):
-        ga, go, gb = cores()
-        gb = grid.reduce(gb, 2, "z")
-        mark("bzr", last(gb))
-    gv = begin(kv, hook("cv", sv))
-    mark("cv", last(gv))
-    ga[-1] = (hook("m1a", ga[-1][0]), 0)
-    ga = grid.reduce(ga, 0, "y")
-    mark("m1a", last(ga))
-    go[-1] = (hook("m1b", go[-1][0]), 0)
-    go, gv = grid.reduce_pair(go, gv, 0, "x")
-    mark("m1b", last(go))
-    gb[-1] = (hook("by", gb[-1][0]), 3)
-    wide = grid.total(gb, 3)
-    mark("wide", wide)
-    blocks = []
-    for k in range(G):
-        spot = (at["y"] ^ (k // 2)) * 2 + (at["x"] ^ (k % 2)) - start
-        blk = lax.dynamic_index_in_dim(wide, jnp.clip(spot, 0, WIN - 1), 0, False)
-        ok = jnp.logical_and(spot >= 0, spot < WIN)
-        blocks.append(jnp.where(ok, blk, jnp.zeros_like(blk)))
-    gb = [(jnp.stack(blocks).reshape(2, 2, HR, KB), 0)]
+    gp[-1] = (hook("m1", gp[-1][0]), 0)
+    gp, gq = grid.reduce(gp, 0, "y"), grid.reduce(gq, 0, "x")
+    mark("m1", last(gp, gq))
     gu[-1] = (hook("fzr", gu[-1][0]), 2)
     gu, gd = grid.reduce_joined((gu, gd), "z")
     mark("fzr", gu)
-    ga = grid.reduce(ga, 1, "x")
-    mark("m2a", last(ga))
-    go, gv = grid.reduce_pair(go, gv, 1, "y")
-    mark("m2", last(ga, go))
-    gb = grid.reduce(gb, 0, "y")
-    gb = grid.total(grid.reduce(gb, 1, "x"), 2)
-    ga, go, gv = grid.reduce_joined((ga, go, gv), "z")
-
-    grad_mixing = jnp.concatenate([ga, gb], axis=0).reshape(H, QB, KB)
+    gp[-1] = (hook("m2", gp[-1][0]), 1)
+    gq[-1] = (hook("m2", gq[-1][0]), 1)
+    gp, gq = grid.reduce(gp, 1, "x"), grid.reduce(gq, 1, "y")
+    mark("m2", last(gp, gq))
+    gp, gq = grid.reduce_joined((gp, gq), "z")
+
+    go, gv = gp[HR:], gq[HR:]
+    grad_mixing = jnp.concatenate([gp[:HR], gq[:HR]], axis=0).reshape(H, QB, KB)
     return (
         layer_out, grad_in, gv[0, CB : CB + GN], gv[:, :CB], grad_mixing, go[:, :CB].T,
         go[0, CB : CB + GN], gu, gd.T,
@@ -850,7 +777,7 @@
         grads = rest if grads is None else jax.tree.map(jnp.add, grads, rest)
     layer_out = jnp.concatenate([r[0] for r in rows_out], axis=0)
     grad_in = jnp.concatenate([r[1] for r in rows_out], axis=0)
-    gu, gd, ga, gb, go, gv = jax.tree.map(lambda v: v.astype(BF16), grads)
+    gu, gd, gp, gq = jax.tree.map(lambda v: v.astype(BF16), grads)
 
     def by_a(v):
         return v.reshape((2, 2) + v.shape[1:]).swapaxes(0, 1).reshape(v.shape)
@@ -858,17 +785,11 @@
     def ffn_out(pair):
         return jnp.stack(pair).transpose(1, 3, 2, 0, 4).reshape(D, FF)
 
-    value_full, dg_one = cols_out(*[by_a(v) for v in gv])
-    output_full, dg_two = cols_out(*[by_a(v) for v in go])
-    gb = jnp.stack(gb)
-    gb = jnp.stack(
-        [
-            jnp.pad(gb[:, m], ((0, 0), (s, G - WIN - s), (0, 0), (0, 0)))
-            for m, s in enumerate(starts)
-        ],
-        axis=2,
-    )
-    gm = jnp.stack([jnp.stack(ga), gb]).reshape(2, 2, G, Z, HA, QB, KB).transpose(0, 4, 3, 1, 5, 2, 6)
+    value_full, dg_one = cols_out(*[by_a(v[:, :, HR:]) for v in gq])
+    output_full, dg_two = cols_out(*[v[:, :, HR:] for v in gp])
+    ga = jnp.stack([v[:, :, :HR] for v in gp])
+    gb = jnp.stack([by_a(v[:, :, :HR]) for v in gq])
+    gm = jnp.stack([ga, gb]).reshape(2, 2, G, Z, HA, QB, KB).transpose(0, 4, 3, 1, 5, 2, 6)
     gd = [by_a(v) for v in gd]
     dgs = jnp.stack([dg_one, dg_two]).astype(F32)
     dgs = lax.psum_scatter(dgs, ax, scatter_dimension=1, tiled=True)

time: 274 us -> 266 us (0.971)
  waiting for transfers between devices: 107 us -> 117 us
  other arithmetic: 26.5 us -> 17.7 us
  local copies, waits for them, and re-layouts: 16.7 us -> 9.86 us
  Pallas kernels: 62.5 us -> 59 us
    ppermute x49 -> x42, waiting for transfers between devices: 107 us -> 117 us  [fetch(): return lax.ppermute(val, ('gx', 'gy'), pairs)]
    unnamed x120 -> x60, local copies, waits for them, and re-layouts: 12.2 us -> 4.64 us
    pallas_call x2 -> x1, Pallas kernels: 25.5 us -> 22 us  [run_back(): call(back_body, (L // TM,), specs, [whole(None)] * 5, [sds((L, D), F32)]...]
    add x4 -> x1, other arithmetic: 3.25 us -> 0.26 us  [add_up(): total = total + term.astype(F32)]
    ppermute x49 -> x42, starting transfers between devices: 53.4 us -> 52.8 us  [fetch(): return lax.ppermute(val, ('gx', 'gy'), pairs)]
  transfers between devices with their start and end apart: 49 -> 42, of which waited for: 19 -> 19; matrix products, arithmetic and copies ran while one was open for 9% -> 6% of each run, Pallas kernels for 14% -> 13%
where the time goes in v8:
time: 266 us; the launch traced here: 264 us
  waiting for transfers between devices  117 us (44%)
  Pallas kernels  59 us (22%)
  starting transfers between devices  52.8 us (20%)
  other arithmetic  17.7 us (7%)
  local copies, waits for them, and re-layouts  9.86 us (4%)
  between operations  7.12 us (3%)
    ppermute x42, waiting for transfers between devices, fetch(): return lax.ppermute(val, ('gx', 'gy'), pairs)  117 us
    ppermute x42, starting transfers between devices, fetch(): return lax.ppermute(val, ('gx', 'gy'), pairs)  52.8 us
    pallas_call x1, Pallas kernels, run_ffn(): call(functools.partial(ffn_body, n - 1), (Z // ZS,), [whole((L, D))] * (2...  24.1 us
    pallas_call x1, Pallas kernels, run_back(): call(back_body, (L // TM,), specs, [whole(None)] * 5, [sds((L, D), F32)]...  22 us
    pallas_call x1, Pallas kernels, run_mixer(): call(mixer_body, (L // TM,), [whole((L, D)), whole((8, D)), rows(1), whol...  8.74 us
  transfers between devices with their start and end apart: 42, of which 19 were waited for; matrix products, arithmetic and copies ran while one was open for 6% of the time, Pallas kernels for 13%

profile of v8, /device:TPU:0, one launch (start us, length us, event | category | flops | bytes accessed | tf_op | source)
XLA Modules:
  0.0 263.6 jit_solution(6029832070989808300)
XLA Ops:
  4.8 5.1 %collective-permute-start.2 = (bf16[768,128]{1,0:T(8,128)(2,1)S(1)}, bf16[768,128]{1,0:T(8,128)(2,1)S(1)}, u32[]{:S(2)}, u32[]{:S(2)}) collective-permute-start(bf16[768,128]{1,0:T(8,128)(2,1)S(1)} %maximum_maximum_fusion), channel_id=1, source_target_pairs={{0,6},{1,7},{2,4},{3,5},{4,2},{5,3},{6,0},{7,1},{8,14},{9,15},{10,... | collective-permute-start | bytes 589832 | tf_op jit(solution)/shard_map/ppermute | solution.py:549
  10.6 1.6 collective-permute-start.3
  19.0 1.6 collective-permute-start.4
  20.6 6.1 %collective-permute-done.1 = bf16[768,128]{1,0:T(8,128)(2,1)S(1)} collective-permute-done((bf16[768,128]{1,0:T(8,128)(2,1)S(1)}, bf16[768,128]{1,0:T(8,128)(2,1)S(1)}, u32[]{:S(2)}, u32[]{:S(2)}) %collective-permute-start.1) | collective-permute-done | bytes 196640 | tf_op jit(solution)/shard_map/ppermute | solution.py:549
  26.7 2.7 %collective-permute-start.13 = (bf16[2,192,384]{2,1,0:T(8,128)(2,1)S(1)}, bf16[2,192,384]{2,1,0:T(8,128)(2,1)S(1)}, u32[]{:S(2)}, u32[]{:S(2)}) collective-permute-start(bf16[2,192,384]{2,1,0:T(8,128)(2,1)S(1)} %pad_maximum_fusion.13), channel_id=1, source_target_pairs={{0,6},{1,7},{2,4},{3,5},{4,2},{5,3},{6,0},{7,1},{8,14},{9,15},{10,... | collective-permute-start | bytes 884744 | tf_op jit(solution)/shard_map/ppermute | solution.py:549
  29.4 1.7 collective-permute-start.7
  31.3 1.6 collective-permute-start.5
  34.5 12.8 %collective-permute-done.7 = bf16[2,192,384]{2,1,0:T(8,128)(2,1)S(1)} collective-permute-done((bf16[2,192,384]{2,1,0:T(8,128)(2,1)S(1)}, bf16[2,192,384]{2,1,0:T(8,128)(2,1)S(1)}, u32[]{:S(2)}, u32[]{:S(2)}) %collective-permute-start.7) | collective-permute-done | bytes 294944 | tf_op jit(solution)/shard_map/ppermute | solution.py:549
  49.0 1.6 collective-permute-start.8
  52.2 9.0 %collective-permute-done.12 = bf16[2,192,384]{2,1,0:T(8,128)(2,1)S(1)} collective-permute-done((bf16[2,192,384]{2,1,0:T(8,128)(2,1)S(1)}, bf16[2,192,384]{2,1,0:T(8,128)(2,1)S(1)}, u32[]{:S(2)}, u32[]{:S(2)}) %collective-permute-start.12) | collective-permute-done | bytes 294944 | tf_op jit(solution)/shard_map/ppermute | solution.py:549
  64.5 1.8 collective-permute-start.10
  66.3 3.3 %collective-permute-done.8 = bf16[2,4,384,128]{3,2,1,0:T(8,128)(2,1)S(1)} collective-permute-done((bf16[2,4,384,128]{3,2,1,0:T(8,128)(2,1)S(1)}, bf16[2,4,384,128]{3,2,1,0:T(8,128)(2,1)S(1)}, u32[]{:S(2)}, u32[]{:S(2)}) %collective-permute-start.8) | collective-permute-done | bytes 786464 | tf_op jit(solution)/shard_map/ppermute | solution.py:549
  69.6 1.6 collective-permute-start.9
  71.3 7.0 %collective-permute-done.10 = bf16[3,384,128]{2,1,0:T(8,128)(2,1)S(1)} collective-permute-done((bf16[3,384,128]{2,1,0:T(8,128)(2,1)S(1)}, bf16[3,384,128]{2,1,0:T(8,128)(2,1)S(1)}, u32[]{:S(2)}, u32[]{:S(2)}) %collective-permute-start.10) | collective-permute-done | bytes 294944 | tf_op jit(solution)/shard_map/ppermute | solution.py:549
  78.3 1.6 collective-permute-done.9
  83.4 2.5 pad_maximum_fusion.4.refs_6_
  89.4 4.2 %shard_map.169 = (bf16[512,768]{1,0:T(8,128)(2,1)S(1)}, bf16[4,512,256]{2,1,0:T(8,128)(2,1)S(1)}, f32[8,768]{1,0:T(8,128)S(1)}) custom-call(s32[14]{0:T(128)S(1)} %stack.195.t, bf16[512,768]{1,0:T(8,128)(2,1)S(1)} %copy-done.6, bf16[4,4,384,128]{3,2,1,0:T(8,128)(2,1)S(1)} %bitcast.239, bf16[4,4,384,128]{3,2,1,0:T(8,128)(2,1)} %collective-permute-done.19.oth_ref.w_oth), custom_call_target="tpu_custom_call" | custom-call | flops 274877906944 | bytes 6291456 | tf_op jit(solution)/shard_map/pallas_call | solution.py:452
  93.7 8.7 %shard_map.170 = (bf16[4,512,256]{2,1,0:T(8,128)(2,1)S(1)}, f32[512,768]{1,0:T(8,128)S(1)}, bf16[512,768]{1,0:T(8,128)(2,1)S(1)}) custom-call(s32[14]{0:T(128)S(1)} %stack.195.t, bf16[512,768]{1,0:T(8,128)(2,1)S(1)} %copy-done.6, f32[8,768]{1,0:T(8,128)S(1)} %get-tuple-element.57.gain_ref, s32[512,1]{1,0:T(8,128)S(1)} %copy.28.dq_ref, ...), custom_call_target="tpu_custom_call" | custom-call | flops 274877906944 | bytes 14680064 | tf_op jit(solution)/shard_map/pallas_call | solution.py:464
  102.5 12.0 %collective-permute-done.23.refs_7_ = bf16[2,4,192,384]{3,2,1,0:T(8,128)(2,1)} collective-permute-done((bf16[2,4,192,384]{3,2,1,0:T(8,128)(2,1)}, bf16[2,4,192,384]{3,2,1,0:T(8,128)(2,1)}, u32[]{:S(2)}, u32[]{:S(2)}) %collective-permute-start.23) | collective-permute-done | bytes 1179680 | tf_op jit(solution)/shard_map/ppermute | solution.py:549
  114.5 2.4 collective-permute-done.22.refs_5_
  117.9 24.1 %shard_map.171 = (bf16[2,4,192,384]{3,2,1,0:T(8,128)(2,1)}, bf16[2,4,192,384]{3,2,1,0:T(8,128)(2,1)}, bf16[2,4,192,384]{3,2,1,0:T(8,128)(2,1)}, bf16[2,4,192,384...) custom-call(s32[14]{0:T(128)} %copy-done.4, ...), custom_call_target="tpu_custom_call" | custom-call | flops 274877906944 | bytes 20971520 | tf_op jit(solution)/shard_map/pallas_call | solution.py:483
  146.0 22.0 %shard_map.172 = (f32[512,768]{1,0:T(8,128)}, bf16[4,4,576,128]{3,2,1,0:T(8,128)(2,1)S(1)}, bf16[4,4,576,128]{3,2,1,0:T(8,128)(2,1)S(1)}, bf16[4,4,576,128]{3,2,1,0:T(8,128)(2,1)}, bf16[4,4,576,128]{3,2,1,0:T(8,128)(2,1)}) custom-call(s32[14]{0:T(128)S(1)} %copy-done.5, f32[512,768]{1,0:T(8,128)S(1)} %copy-done.9, ...), custom_call_target="tpu_custom_call" | custom-call | flops 274877906944 | bytes 41943040 | tf_op jit(solution)/shard_map/pallas_call | solution.py:503
  168.0 2.7 %collective-permute-done.26 = bf16[2,4,192,384]{3,2,1,0:T(8,128)(2,1)} collective-permute-done((bf16[2,4,192,384]{3,2,1,0:T(8,128)(2,1)}, bf16[2,4,192,384]{3,2,1,0:T(8,128)(2,1)}, u32[]{:S(2)}, u32[]{:S(2)}) %collective-permute-start.26) | collective-permute-done | bytes 1179680 | tf_op jit(solution)/shard_map/ppermute | solution.py:549
  176.6 11.8 %collective-permute-done.31 = bf16[4,192,384]{2,1,0:T(8,128)(2,1)S(1)} collective-permute-done((bf16[4,192,384]{2,1,0:T(8,128)(2,1)S(1)}, bf16[4,192,384]{2,1,0:T(8,128)(2,1)S(1)}, u32[]{:S(2)}, u32[]{:S(2)}) %collective-permute-start.31) | collective-permute-done | bytes 589856 | tf_op jit(solution)/shard_map/ppermute | solution.py:549
  194.5 1.7 collective-permute-start.33
  196.2 2.0 collective-permute-start.34
  198.3 18.0 %collective-permute-done.33 = bf16[384,384]{1,0:T(8,128)(2,1)S(1)} collective-permute-done((bf16[384,384]{1,0:T(8,128)(2,1)S(1)}, bf16[384,384]{1,0:T(8,128)(2,1)S(1)}, u32[]{:S(2)}, u32[]{:S(2)}) %collective-permute-start.33) | collective-permute-done | bytes 294944 | tf_op jit(solution)/shard_map/ppermute | solution.py:549
  216.8 2.0 fusion.8
  221.6 11.0 %collective-permute-done.35 = bf16[4,576,128]{2,1,0:T(8,128)(2,1)S(1)} collective-permute-done((bf16[4,576,128]{2,1,0:T(8,128)(2,1)S(1)}, bf16[4,576,128]{2,1,0:T(8,128)(2,1)S(1)}, u32[]{:S(2)}, u32[]{:S(2)}) %collective-permute-start.35) | collective-permute-done | bytes 589856 | tf_op jit(solution)/shard_map/ppermute | solution.py:549
  233.5 7.1 %collective-permute-start.40 = (bf16[1152,128]{1,0:T(8,128)(2,1)S(1)}, bf16[1152,128]{1,0:T(8,128)(2,1)S(1)}, u32[]{:S(2)}, u32[]{:S(2)}) collective-permute-start(bf16[1152,128]{1,0:T(8,128)(2,1)S(1)} %pad_maximum_fusion.19), channel_id=1, source_target_pairs={{0,4},{1,5},{2,6},{3,7},{4,0},{5,1},{6,2},{7,3},{8,12},{9,13},{10,... | collective-permute-start | bytes 884744 | tf_op jit(solution)/shard_map/ppermute | solution.py:549
  240.6 2.0 collective-permute-start.41
  244.0 16.0 %collective-permute-done.40 = bf16[1152,128]{1,0:T(8,128)(2,1)S(1)} collective-permute-done((bf16[1152,128]{1,0:T(8,128)(2,1)S(1)}, bf16[1152,128]{1,0:T(8,128)(2,1)S(1)}, u32[]{:S(2)}, u32[]{:S(2)}) %collective-permute-start.40) | collective-permute-done | bytes 294944 | tf_op jit(solution)/shard_map/ppermute | solution.py:549
  (174 shorter events, 47.3 us)
Async XLA Ops:
  4.8 15.7 %collective-permute-start.2 = (bf16[768,128]{1,0:T(8,128)(2,1)S(1)}, bf16[768,128]{1,0:T(8,128)(2,1)S(1)}, u32[]{:S(2)}, u32[]{:S(2)}) collective-permute-start(bf16[768,128]{1,0:T(8,128)(2,1)S(1)} %maximum_maximum_fusion), channel_id=1, source_target_pairs={{0,6},{1,7},{2,4},{3,5},{4,2},{5,3},{6,0},{7,1},{8,14},{9,15},{10,... | collective-permute-start | bytes 589832 | tf_op jit(solution)/shard_map/ppermute | solution.py:549
  10.0 16.7 %collective-permute-start.1 = (bf16[768,128]{1,0:T(8,128)(2,1)S(1)}, bf16[768,128]{1,0:T(8,128)(2,1)S(1)}, u32[]{:S(2)}, u32[]{:S(2)}) collective-permute-start(bf16[768,128]{1,0:T(8,128)(2,1)S(1)} %maximum_maximum_fusion), channel_id=1, source_target_pairs={{0,4},{1,5},{2,6},{3,7},{4,0},{5,1},{6,2},{7,3},{8,12},{9,13},{10,... | collective-permute-start | bytes 589832 | tf_op jit(solution)/shard_map/ppermute | solution.py:549
  10.0 16.7 %collective-permute-start = (bf16[768,128]{1,0:T(8,128)(2,1)S(1)}, bf16[768,128]{1,0:T(8,128)(2,1)S(1)}, u32[]{:S(2)}, u32[]{:S(2)}) collective-permute-start(bf16[768,128]{1,0:T(8,128)(2,1)S(1)} %maximum_maximum_fusion), channel_id=1, source_target_pairs={{0,2},{1,3},{2,0},{3,1},{4,6},{5,7},{6,4},{7,5},{8,10},{9,11},{10,... | collective-permute-start | bytes 589832 | tf_op jit(solution)/shard_map/ppermute | solution.py:549
  26.7 23.9 %collective-permute-start.13 = (bf16[2,192,384]{2,1,0:T(8,128)(2,1)S(1)}, bf16[2,192,384]{2,1,0:T(8,128)(2,1)S(1)}, u32[]{:S(2)}, u32[]{:S(2)}) collective-permute-start(bf16[2,192,384]{2,1,0:T(8,128)(2,1)S(1)} %pad_maximum_fusion.13), channel_id=1, source_target_pairs={{0,6},{1,7},{2,4},{3,5},{4,2},{5,3},{6,0},{7,1},{8,14},{9,15},{10,... | collective-permute-start | bytes 884744 | tf_op jit(solution)/shard_map/ppermute | solution.py:549
  29.4 31.8 %collective-permute-start.12 = (bf16[2,192,384]{2,1,0:T(8,128)(2,1)S(1)}, bf16[2,192,384]{2,1,0:T(8,128)(2,1)S(1)}, u32[]{:S(2)}, u32[]{:S(2)}) collective-permute-start(bf16[2,192,384]{2,1,0:T(8,128)(2,1)S(1)} %pad_maximum_fusion.13), channel_id=1, source_target_pairs={{0,4},{1,5},{2,6},{3,7},{4,0},{5,1},{6,2},{7,3},{8,12},{9,13},{10,... | collective-permute-start | bytes 884744 | tf_op jit(solution)/shard_map/ppermute | solution.py:549
  29.4 17.9 %collective-permute-start.7 = (bf16[2,192,384]{2,1,0:T(8,128)(2,1)S(1)}, bf16[2,192,384]{2,1,0:T(8,128)(2,1)S(1)}, u32[]{:S(2)}, u32[]{:S(2)}) collective-permute-start(bf16[2,192,384]{2,1,0:T(8,128)(2,1)S(1)} %pad_maximum_fusion.13), channel_id=1, source_target_pairs={{0,2},{1,3},{2,0},{3,1},{4,6},{5,7},{6,4},{7,5},{8,10},{9,11},{10,... | collective-permute-start | bytes 884744 | tf_op jit(solution)/shard_map/ppermute | solution.py:549
  31.3 17.5 %collective-permute-start.5 = (bf16[4,384,128]{2,1,0:T(8,128)(2,1)S(1)}, bf16[4,384,128]{2,1,0:T(8,128)(2,1)S(1)}, u32[]{:S(2)}, u32[]{:S(2)}) collective-permute-start(bf16[4,384,128]{2,1,0:T(8,128)(2,1)S(1)} %get-tuple-element.46), channel_id=1, source_target_pairs={{0,8},{1,9},{2,10},{3,11},{4,12},{5,13},{6,14},{7,15},{8,0},{9,1},... | collective-permute-start | bytes 1179656 | tf_op jit(solution)/shard_map/ppermute | solution.py:549
  32.9 16.0 %collective-permute-start.6 = (bf16[4,384,128]{2,1,0:T(8,128)(2,1)S(1)}, bf16[4,384,128]{2,1,0:T(8,128)(2,1)S(1)}, u32[]{:S(2)}, u32[]{:S(2)}) collective-permute-start(bf16[4,384,128]{2,1,0:T(8,128)(2,1)S(1)} %get-tuple-element.47), channel_id=1, source_target_pairs={{0,16},{1,17},{2,18},{3,19},{4,20},{5,21},{6,22},{7,23},{8,24},{9,... | collective-permute-start | bytes 1179656 | tf_op jit(solution)/shard_map/ppermute | solution.py:549
  47.3 17.3 %collective-permute-start.11 = (bf16[3,384,128]{2,1,0:T(8,128)(2,1)S(1)}, bf16[3,384,128]{2,1,0:T(8,128)(2,1)S(1)}, u32[]{:S(2)}, u32[]{:S(2)}) collective-permute-start(bf16[3,384,128]{2,1,0:T(8,128)(2,1)S(1)} %pad_maximum_fusion.14), channel_id=1, source_target_pairs={{0,6},{1,7},{2,4},{3,5},{4,2},{5,3},{6,0},{7,1},{8,14},{9,15},{10,... | collective-permute-start | bytes 884744 | tf_op jit(solution)/shard_map/ppermute | solution.py:549
  49.0 20.5 %collective-permute-start.8 = (bf16[2,4,384,128]{3,2,1,0:T(8,128)(2,1)S(1)}, bf16[2,4,384,128]{3,2,1,0:T(8,128)(2,1)S(1)}, u32[]{:S(2)}, u32[]{:S(2)}) collective-permute-start(bf16[2,4,384,128]{3,2,1,0:T(8,128)(2,1)S(1)} %pad_maximum_fusion.5), channel_id=1, source_target_pairs={{0,16},{1,17},{2,18},{3,19},{4,20},{5,21},{6,22},{7,23},{8,24},{9,... | collective-permute-start | bytes 2359304 | tf_op jit(solution)/shard_map/ppermute | solution.py:549
  50.6 30.0 %collective-permute-start.18 = (bf16[2,4,384,128]{3,2,1,0:T(8,128)(2,1)S(1)}, bf16[2,4,384,128]{3,2,1,0:T(8,128)(2,1)S(1)}, u32[]{:S(2)}, u32[]{:S(2)}) collective-permute-start(bf16[2,4,384,128]{3,2,1,0:T(8,128)(2,1)S(1)} %pad_maximum_fusion.6), channel_id=1, source_target_pairs={{0,8},{1,9},{2,10},{3,11},{4,12},{5,13},{6,14},{7,15},{8,0},{9,1},... | collective-permute-start | bytes 2359304 | tf_op jit(solution)/shard_map/ppermute | solution.py:549
  61.4 19.1 %collective-permute-start.14 = (bf16[4,192,384]{2,1,0:T(8,128)(2,1)S(1)}, bf16[4,192,384]{2,1,0:T(8,128)(2,1)S(1)}, u32[]{:S(2)}, u32[]{:S(2)}) collective-permute-start(bf16[4,192,384]{2,1,0:T(8,128)(2,1)S(1)} %get-tuple-element.51), channel_id=1, source_target_pairs={{0,8},{1,9},{2,10},{3,11},{4,12},{5,13},{6,14},{7,15},{8,0},{9,1},... | collective-permute-start | bytes 1769480 | tf_op jit(solution)/shard_map/ppermute | solution.py:549
  63.0 17.5 %collective-permute-start.15 = (bf16[4,192,384]{2,1,0:T(8,128)(2,1)S(1)}, bf16[4,192,384]{2,1,0:T(8,128)(2,1)S(1)}, u32[]{:S(2)}, u32[]{:S(2)}) collective-permute-start(bf16[4,192,384]{2,1,0:T(8,128)(2,1)S(1)} %get-tuple-element.52), channel_id=1, source_target_pairs={{0,16},{1,17},{2,18},{3,19},{4,20},{5,21},{6,22},{7,23},{8,24},{9,... | collective-permute-start | bytes 1769480 | tf_op jit(solution)/shard_map/ppermute | solution.py:549
  83.0 19.5 %collective-permute-start.21 = (bf16[512,768]{1,0:T(8,128)(2,1)}, bf16[512,768]{1,0:T(8,128)(2,1)}, u32[]{:S(2)}, u32[]{:S(2)}) collective-permute-start(bf16[512,768]{1,0:T(8,128)(2,1)} %c_ref.1), channel_id=1, source_target_pairs={{0,1},{1,0},{2,3},{3,2},{4,5},{5,4},{6,7},{7,6},{8,9},{9,8},{10,11... | collective-permute-start | bytes 2359304 | tf_op jit(solution)/shard_map/ppermute | solution.py:549
  85.9 28.6 %collective-permute-start.23 = (bf16[2,4,192,384]{3,2,1,0:T(8,128)(2,1)}, bf16[2,4,192,384]{3,2,1,0:T(8,128)(2,1)}, u32[]{:S(2)}, u32[]{:S(2)}) collective-permute-start(bf16[2,4,192,384]{3,2,1,0:T(8,128)(2,1)} %pad_maximum_fusion.4.refs_6_), channel_id=1, source_target_pairs={{0,8},{1,9},{2,10},{3,11},{4,12},{5,13},{6,14},{7,15},{8,0},{9,1},... | collective-permute-start | bytes 3538952 | tf_op jit(solution)/shard_map/ppermute | solution.py:549
  88.6 28.3 %collective-permute-start.22 = (bf16[2,4,192,384]{3,2,1,0:T(8,128)(2,1)}, bf16[2,4,192,384]{3,2,1,0:T(8,128)(2,1)}, u32[]{:S(2)}, u32[]{:S(2)}) collective-permute-start(bf16[2,4,192,384]{3,2,1,0:T(8,128)(2,1)} %pad_maximum_fusion.3.refs_4_), channel_id=1, source_target_pairs={{0,16},{1,17},{2,18},{3,19},{4,20},{5,21},{6,22},{7,23},{8,24},{9,... | collective-permute-start | bytes 3538952 | tf_op jit(solution)/shard_map/ppermute | solution.py:549
  102.4 14.5 %collective-permute-start.20 = (bf16[512,768]{1,0:T(8,128)(2,1)S(1)}, bf16[512,768]{1,0:T(8,128)(2,1)S(1)}, u32[]{:S(2)}, u32[]{:S(2)}) collective-permute-start(bf16[512,768]{1,0:T(8,128)(2,1)S(1)} %get-tuple-element.60.refs_0_), channel_id=1, source_target_pairs={{0,1},{1,0},{2,3},{3,2},{4,5},{5,4},{6,7},{7,6},{8,9},{9,8},{10,11... | collective-permute-start | bytes 2359304 | tf_op jit(solution)/shard_map/ppermute | solution.py:549
  142.0 28.7 %collective-permute-start.26 = (bf16[2,4,192,384]{3,2,1,0:T(8,128)(2,1)}, bf16[2,4,192,384]{3,2,1,0:T(8,128)(2,1)}, u32[]{:S(2)}, u32[]{:S(2)}) collective-permute-start(bf16[2,4,192,384]{3,2,1,0:T(8,128)(2,1)} %get-tuple-element.71), channel_id=1, source_target_pairs={{0,16},{1,17},{2,18},{3,19},{4,20},{5,21},{6,22},{7,23},{8,24},{9,... | collective-permute-start | bytes 3538952 | tf_op jit(solution)/shard_map/ppermute | solution.py:549
  143.0 28.4 %collective-permute-start.27 = (bf16[2,4,192,384]{3,2,1,0:T(8,128)(2,1)}, bf16[2,4,192,384]{3,2,1,0:T(8,128)(2,1)}, u32[]{:S(2)}, u32[]{:S(2)}) collective-permute-start(bf16[2,4,192,384]{3,2,1,0:T(8,128)(2,1)} %get-tuple-element.72), channel_id=1, source_target_pairs={{0,8},{1,9},{2,10},{3,11},{4,12},{5,13},{6,14},{7,15},{8,0},{9,1},... | collective-permute-start | bytes 3538952 | tf_op jit(solution)/shard_map/ppermute | solution.py:549
  171.3 20.4 %collective-permute-start.28 = (bf16[4,4,576,128]{3,2,1,0:T(8,128)(2,1)}, bf16[4,4,576,128]{3,2,1,0:T(8,128)(2,1)S(1)}, u32[]{:S(2)}, u32[]{:S(2)}) collective-permute-start(bf16[4,4,576,128]{3,2,1,0:T(8,128)(2,1)} %get-tuple-element.73), channel_id=1, source_target_pairs={{0,1},{1,0},{2,3},{3,2},{4,5},{5,4},{6,7},{7,6},{8,9},{9,8},{10,11... | collective-permute-start | bytes 7077896 | tf_op jit(solution)/shard_map/ppermute | solution.py:549
  171.3 21.9 %collective-permute-start.36 = (bf16[4,4,576,128]{3,2,1,0:T(8,128)(2,1)S(1)}, bf16[4,4,576,128]{3,2,1,0:T(8,128)(2,1)S(1)}, u32[]{:S(2)}, u32[]{:S(2)}) collective-permute-start(bf16[4,4,576,128]{3,2,1,0:T(8,128)(2,1)S(1)} %get-tuple-element.75), channel_id=1, source_target_pairs={{0,1},{1,0},{2,3},{3,2},{4,5},{5,4},{6,7},{7,6},{8,9},{9,8},{10,11... | collective-permute-start | bytes 7077896 | tf_op jit(solution)/shard_map/ppermute | solution.py:549
  173.0 15.3 %collective-permute-start.31 = (bf16[4,192,384]{2,1,0:T(8,128)(2,1)S(1)}, bf16[4,192,384]{2,1,0:T(8,128)(2,1)S(1)}, u32[]{:S(2)}, u32[]{:S(2)}) collective-permute-start(bf16[4,192,384]{2,1,0:T(8,128)(2,1)S(1)} %fusion.4), channel_id=1, source_target_pairs={{0,16},{1,17},{2,18},{3,19},{4,20},{5,21},{6,22},{7,23},{8,24},{9,... | collective-permute-start | bytes 1769480 | tf_op jit(solution)/shard_map/ppermute | solution.py:549
  175.5 15.0 %collective-permute-start.30 = (bf16[4,192,384]{2,1,0:T(8,128)(2,1)S(1)}, bf16[4,192,384]{2,1,0:T(8,128)(2,1)S(1)}, u32[]{:S(2)}, u32[]{:S(2)}) collective-permute-start(bf16[4,192,384]{2,1,0:T(8,128)(2,1)S(1)} %fusion.3), channel_id=1, source_target_pairs={{0,8},{1,9},{2,10},{3,11},{4,12},{5,13},{6,14},{7,15},{8,0},{9,1},... | collective-permute-start | bytes 1769480 | tf_op jit(solution)/shard_map/ppermute | solution.py:549
  192.1 26.8 %collective-permute-start.29 = (bf16[2,4,576,128]{3,2,1,0:T(8,128)(2,1)S(1)}, bf16[2,4,576,128]{3,2,1,0:T(8,128)(2,1)S(1)}, u32[]{:S(2)}, u32[]{:S(2)}) collective-permute-start(bf16[2,4,576,128]{3,2,1,0:T(8,128)(2,1)S(1)} %add_convert_fusion), channel_id=1, source_target_pairs={{0,8},{1,9},{2,10},{3,11},{4,12},{5,13},{6,14},{7,15},{8,0},{9,1},... | collective-permute-start | bytes 3538952 | tf_op jit(solution)/shard_map/ppermute | solution.py:549
  193.5 26.8 %collective-permute-start.37 = (bf16[2,4,576,128]{3,2,1,0:T(8,128)(2,1)S(1)}, bf16[2,4,576,128]{3,2,1,0:T(8,128)(2,1)S(1)}, u32[]{:S(2)}, u32[]{:S(2)}) collective-permute-start(bf16[2,4,576,128]{3,2,1,0:T(8,128)(2,1)S(1)} %fusion), channel_id=1, source_target_pairs={{0,16},{1,17},{2,18},{3,19},{4,20},{5,21},{6,22},{7,23},{8,24},{9,... | collective-permute-start | bytes 3538952 | tf_op jit(solution)/shard_map/ppermute | solution.py:549
  194.5 21.8 %collective-permute-start.33 = (bf16[384,384]{1,0:T(8,128)(2,1)S(1)}, bf16[384,384]{1,0:T(8,128)(2,1)S(1)}, u32[]{:S(2)}, u32[]{:S(2)}) collective-permute-start(bf16[384,384]{1,0:T(8,128)(2,1)S(1)} %pad_maximum_fusion.16), channel_id=1, source_target_pairs={{0,4},{1,5},{2,6},{3,7},{4,0},{5,1},{6,2},{7,3},{8,12},{9,13},{10,... | collective-permute-start | bytes 884744 | tf_op jit(solution)/shard_map/ppermute | solution.py:549
  196.2 20.1 %collective-permute-start.34 = (bf16[384,384]{1,0:T(8,128)(2,1)S(1)}, bf16[384,384]{1,0:T(8,128)(2,1)S(1)}, u32[]{:S(2)}, u32[]{:S(2)}) collective-permute-start(bf16[384,384]{1,0:T(8,128)(2,1)S(1)} %pad_maximum_fusion.17), channel_id=1, source_target_pairs={{0,6},{1,7},{2,4},{3,5},{4,2},{5,3},{6,0},{7,1},{8,14},{9,15},{10,... | collective-permute-start | bytes 884744 | tf_op jit(solution)/shard_map/ppermute | solution.py:549
  198.2 18.6 %collective-permute-start.32 = (bf16[384,384]{1,0:T(8,128)(2,1)S(1)}, bf16[384,384]{1,0:T(8,128)(2,1)S(1)}, u32[]{:S(2)}, u32[]{:S(2)}) collective-permute-start(bf16[384,384]{1,0:T(8,128)(2,1)S(1)} %pad_maximum_fusion.15), channel_id=1, source_target_pairs={{0,2},{1,3},{2,0},{3,1},{4,6},{5,7},{6,4},{7,5},{8,10},{9,11},{10,... | collective-permute-start | bytes 884744 | tf_op jit(solution)/shard_map/ppermute | solution.py:549
  221.6 21.1 %collective-permute-start.24 = (bf16[512,768]{1,0:T(8,128)(2,1)S(1)}, bf16[512,768]{1,0:T(8,128)(2,1)S(1)}, u32[]{:S(2)}, u32[]{:S(2)}) collective-permute-start(bf16[512,768]{1,0:T(8,128)(2,1)S(1)} %copy-done.27), channel_id=1, source_target_pairs={{0,1},{1,0},{2,3},{3,2},{4,5},{5,4},{6,7},{7,6},{8,9},{9,8},{10,11... | collective-permute-start | bytes 2359304 | tf_op jit(solution)/shard_map/ppermute | solution.py:549
  233.5 26.5 %collective-permute-start.40 = (bf16[1152,128]{1,0:T(8,128)(2,1)S(1)}, bf16[1152,128]{1,0:T(8,128)(2,1)S(1)}, u32[]{:S(2)}, u32[]{:S(2)}) collective-permute-start(bf16[1152,128]{1,0:T(8,128)(2,1)S(1)} %pad_maximum_fusion.19), channel_id=1, source_target_pairs={{0,4},{1,5},{2,6},{3,7},{4,0},{5,1},{6,2},{7,3},{8,12},{9,13},{10,... | collective-permute-start | bytes 884744 | tf_op jit(solution)/shard_map/ppermute | solution.py:549
  240.6 19.3 %collective-permute-start.41 = (bf16[1152,128]{1,0:T(8,128)(2,1)S(1)}, bf16[1152,128]{1,0:T(8,128)(2,1)S(1)}, u32[]{:S(2)}, u32[]{:S(2)}) collective-permute-start(bf16[1152,128]{1,0:T(8,128)(2,1)S(1)} %pad_maximum_fusion.20), channel_id=1, source_target_pairs={{0,6},{1,7},{2,4},{3,5},{4,2},{5,3},{6,0},{7,1},{8,14},{9,15},{10,... | collective-permute-start | bytes 884744 | tf_op jit(solution)/shard_map/ppermute | solution.py:549
  242.7 17.3 %collective-permute-start.39 = (bf16[1152,128]{1,0:T(8,128)(2,1)S(1)}, bf16[1152,128]{1,0:T(8,128)(2,1)S(1)}, u32[]{:S(2)}, u32[]{:S(2)}) collective-permute-start(bf16[1152,128]{1,0:T(8,128)(2,1)S(1)} %pad_maximum_fusion.18), channel_id=1, source_target_pairs={{0,2},{1,3},{2,0},{3,1},{4,6},{5,7},{6,4},{7,5},{8,10},{9,11},{10,... | collective-permute-start | bytes 884744 | tf_op jit(solution)/shard_map/ppermute | solution.py:549
  (39 other events, 515.7 us)

commit v9 on v8

--- a/solution.py
+++ b/solution.py
@@ -32,7 +32,7 @@
 GC = 0.7978845608
 GA = 0.044715
 VMEM_LIMIT = 40 * 1024 * 1024
-COST = 1 << 38
+COST = 1
 CFG = {
     "fz": ("c1",),
     "aw1": ("bxy",),

time: 266 us -> 261 us (0.981)
  other arithmetic: 17.7 us -> 11 us
  local copies, waits for them, and re-layouts: 9.86 us -> 15.8 us
  waiting for transfers between devices: 117 us -> 114 us
    unnamed x60 -> x46, local copies, waits for them, and re-layouts: 4.64 us -> 10.5 us
    ppermute x42, waiting for transfers between devices: 117 us -> 114 us  [fetch(): return lax.ppermute(val, ('gx', 'gy'), pairs)]
  transfers between devices with their start and end apart: 42 -> 42, of which waited for: 19 -> 21; matrix products, arithmetic and copies ran while one was open for 6% -> 4% of each run, Pallas kernels for 13% -> 13%
where the time goes in v9:
time: 261 us; the launch traced here: 259 us
  waiting for transfers between devices  114 us (44%)
  Pallas kernels  58.6 us (22%)
  starting transfers between devices  53.1 us (20%)
  local copies, waits for them, and re-layouts  15.8 us (6%)
  other arithmetic  11 us (4%)
  between operations  6.96 us (3%)
    ppermute x42, waiting for transfers between devices, fetch(): return lax.ppermute(val, ('gx', 'gy'), pairs)  114 us
    ppermute x42, starting transfers between devices, fetch(): return lax.ppermute(val, ('gx', 'gy'), pairs)  53.1 us
    pallas_call x1, Pallas kernels, run_ffn(): call(functools.partial(ffn_body, n - 1), (Z // ZS,), [whole((L, D))] * (2...  23.9 us
    pallas_call x1, Pallas kernels, run_back(): call(back_body, (L // TM,), specs, [whole(None)] * 5, [sds((L, D), F32)]...  21.8 us
    unnamed x46, local copies, waits for them, and re-layouts  10.5 us
    pallas_call x1, Pallas kernels, run_mixer(): call(mixer_body, (L // TM,), [whole((L, D)), whole((8, D)), rows(1), whol...  8.69 us
  transfers between devices with their start and end apart: 42, of which 21 were waited for; matrix products, arithmetic and copies ran while one was open for 4% of the time, Pallas kernels for 13%

profile of v9, /device:TPU:0, one launch (start us, length us, event | category | flops | bytes accessed | tf_op | source)
XLA Modules:
  0.0 259.3 jit_solution(17385282172359114712)
XLA Ops:
  4.8 5.1 %collective-permute-start.2 = (bf16[768,128]{1,0:T(8,128)(2,1)S(1)}, bf16[768,128]{1,0:T(8,128)(2,1)S(1)}, u32[]{:S(2)}, u32[]{:S(2)}) collective-permute-start(bf16[768,128]{1,0:T(8,128)(2,1)S(1)} %maximum_maximum_fusion), channel_id=1, source_target_pairs={{0,6},{1,7},{2,4},{3,5},{4,2},{5,3},{6,0},{7,1},{8,14},{9,15},{10,... | collective-permute-start | bytes 589832 | tf_op jit(solution)/shard_map/ppermute | solution.py:549
  10.6 1.6 collective-permute-start.3
  19.0 1.6 collective-permute-start.4
  20.6 6.1 %collective-permute-done.1 = bf16[768,128]{1,0:T(8,128)(2,1)S(1)} collective-permute-done((bf16[768,128]{1,0:T(8,128)(2,1)S(1)}, bf16[768,128]{1,0:T(8,128)(2,1)S(1)}, u32[]{:S(2)}, u32[]{:S(2)}) %collective-permute-start.1) | collective-permute-done | bytes 196640 | tf_op jit(solution)/shard_map/ppermute | solution.py:549
  26.7 2.7 %collective-permute-start.13 = (bf16[2,192,384]{2,1,0:T(8,128)(2,1)S(1)}, bf16[2,192,384]{2,1,0:T(8,128)(2,1)S(1)}, u32[]{:S(2)}, u32[]{:S(2)}) collective-permute-start(bf16[2,192,384]{2,1,0:T(8,128)(2,1)S(1)} %pad_maximum_fusion.13), channel_id=1, source_target_pairs={{0,6},{1,7},{2,4},{3,5},{4,2},{5,3},{6,0},{7,1},{8,14},{9,15},{10,... | collective-permute-start | bytes 884744 | tf_op jit(solution)/shard_map/ppermute | solution.py:549
  29.4 1.7 collective-permute-start.7
  31.3 1.6 collective-permute-start.5
  34.5 12.8 %collective-permute-done.7 = bf16[2,192,384]{2,1,0:T(8,128)(2,1)S(1)} collective-permute-done((bf16[2,192,384]{2,1,0:T(8,128)(2,1)S(1)}, bf16[2,192,384]{2,1,0:T(8,128)(2,1)S(1)}, u32[]{:S(2)}, u32[]{:S(2)}) %collective-permute-start.7) | collective-permute-done | bytes 294944 | tf_op jit(solution)/shard_map/ppermute | solution.py:549
  49.0 1.6 collective-permute-start.8
  50.6 1.6 collective-permute-start.18
  52.2 9.0 %collective-permute-done.12 = bf16[2,192,384]{2,1,0:T(8,128)(2,1)S(1)} collective-permute-done((bf16[2,192,384]{2,1,0:T(8,128)(2,1)S(1)}, bf16[2,192,384]{2,1,0:T(8,128)(2,1)S(1)}, u32[]{:S(2)}, u32[]{:S(2)}) %collective-permute-start.12) | collective-permute-done | bytes 294944 | tf_op jit(solution)/shard_map/ppermute | solution.py:549
  61.4 1.6 collective-permute-start.14
  64.5 1.8 collective-permute-start.10
  66.3 3.3 %collective-permute-done.8 = bf16[2,4,384,128]{3,2,1,0:T(8,128)(2,1)S(1)} collective-permute-done((bf16[2,4,384,128]{3,2,1,0:T(8,128)(2,1)S(1)}, bf16[2,4,384,128]{3,2,1,0:T(8,128)(2,1)S(1)}, u32[]{:S(2)}, u32[]{:S(2)}) %collective-permute-start.8) | collective-permute-done | bytes 786464 | tf_op jit(solution)/shard_map/ppermute | solution.py:549
  69.6 1.6 collective-permute-start.9
  71.3 7.0 %collective-permute-done.10 = bf16[3,384,128]{2,1,0:T(8,128)(2,1)S(1)} collective-permute-done((bf16[3,384,128]{2,1,0:T(8,128)(2,1)S(1)}, bf16[3,384,128]{2,1,0:T(8,128)(2,1)S(1)}, u32[]{:S(2)}, u32[]{:S(2)}) %collective-permute-start.10) | collective-permute-done | bytes 294944 | tf_op jit(solution)/shard_map/ppermute | solution.py:549
  78.3 1.6 collective-permute-done.9
  89.1 4.1 %shard_map.169 = (bf16[512,768]{1,0:T(8,128)(2,1)S(1)}, bf16[4,512,256]{2,1,0:T(8,128)(2,1)S(1)}, f32[8,768]{1,0:T(8,128)S(1)}) custom-call(s32[14]{0:T(128)S(1)} %stack.195.t, bf16[512,768]{1,0:T(8,128)(2,1)S(1)} %copy-done.2, bf16[4,4,384,128]{3,2,1,0:T(8,128)(2,1)S(1)} %bitcast.233, bf16[4,4,384,128]{3,2,1,0:T(8,128)(2,1)} %collective-permute-done.19.oth_ref.w_oth), custom_call_target="tpu_custom_call" | custom-call | flops 1 | bytes 6291456 | tf_op jit(solution)/shard_map/pallas_call | solution.py:452
  94.2 8.7 %shard_map.170 = (bf16[4,512,256]{2,1,0:T(8,128)(2,1)S(1)}, f32[512,768]{1,0:T(8,128)S(1)}, bf16[512,768]{1,0:T(8,128)(2,1)S(1)}) custom-call(s32[14]{0:T(128)S(1)} %stack.195.t, bf16[512,768]{1,0:T(8,128)(2,1)S(1)} %copy-done.2, f32[8,768]{1,0:T(8,128)S(1)} %get-tuple-element.57.gain_ref, s32[512,1]{1,0:T(8,128)S(1)} %copy.28.dq_ref, ...), custom_call_target="tpu_custom_call" | custom-call | flops 1 | bytes 14680064 | tf_op jit(solution)/shard_map/pallas_call | solution.py:464
  105.0 7.3 %collective-permute-done.23.refs_7_ = bf16[2,4,192,384]{3,2,1,0:T(8,128)(2,1)} collective-permute-done((bf16[2,4,192,384]{3,2,1,0:T(8,128)(2,1)}, bf16[2,4,192,384]{3,2,1,0:T(8,128)(2,1)}, u32[]{:S(2)}, u32[]{:S(2)}) %collective-permute-start.23) | collective-permute-done | bytes 1179680 | tf_op jit(solution)/shard_map/ppermute | solution.py:549
  112.3 2.4 collective-permute-done.22.refs_5_
  115.5 23.9 %shard_map.171 = (bf16[2,4,192,384]{3,2,1,0:T(8,128)(2,1)}, bf16[2,4,192,384]{3,2,1,0:T(8,128)(2,1)}, bf16[2,4,192,384]{3,2,1,0:T(8,128)(2,1)}, bf16[2,4,192,384...) custom-call(s32[14]{0:T(128)} %copy-done.11, ...), custom_call_target="tpu_custom_call" | custom-call | flops 1 | bytes 20971520 | tf_op jit(solution)/shard_map/pallas_call | solution.py:483
  140.9 2.5 collective-permute-done.25.dnb_ref
  147.1 21.8 %shard_map.172 = (f32[512,768]{1,0:T(8,128)}, bf16[4,4,576,128]{3,2,1,0:T(8,128)(2,1)S(1)}, bf16[4,4,576,128]{3,2,1,0:T(8,128)(2,1)S(1)}, bf16[4,4,576,128]{3,2,1,0:T(8,128)(2,1)}, bf16[4,4,576,128]{3,2,1,0:T(8,128)(2,1)}) custom-call(s32[14]{0:T(128)S(1)} %copy-done.12, f32[512,768]{1,0:T(8,128)S(1)} %copy-done.5, ...), custom_call_target="tpu_custom_call" | custom-call | flops 1 | bytes 41943040 | tf_op jit(solution)/shard_map/pallas_call | solution.py:503
  172.6 12.5 %collective-permute-done.31 = bf16[4,192,384]{2,1,0:T(8,128)(2,1)S(1)} collective-permute-done((bf16[4,192,384]{2,1,0:T(8,128)(2,1)S(1)}, bf16[4,192,384]{2,1,0:T(8,128)(2,1)S(1)}, u32[]{:S(2)}, u32[]{:S(2)}) %collective-permute-start.31) | collective-permute-done | bytes 589856 | tf_op jit(solution)/shard_map/ppermute | solution.py:549
  190.2 2.1 collective-permute-start.33
  192.3 2.0 collective-permute-start.34
  194.4 18.3 %collective-permute-done.33 = bf16[384,384]{1,0:T(8,128)(2,1)S(1)} collective-permute-done((bf16[384,384]{1,0:T(8,128)(2,1)S(1)}, bf16[384,384]{1,0:T(8,128)(2,1)S(1)}, u32[]{:S(2)}, u32[]{:S(2)}) %collective-permute-start.33) | collective-permute-done | bytes 294944 | tf_op jit(solution)/shard_map/ppermute | solution.py:549
  217.6 11.0 %collective-permute-done.35 = bf16[4,576,128]{2,1,0:T(8,128)(2,1)S(1)} collective-permute-done((bf16[4,576,128]{2,1,0:T(8,128)(2,1)S(1)}, bf16[4,576,128]{2,1,0:T(8,128)(2,1)S(1)}, u32[]{:S(2)}, u32[]{:S(2)}) %collective-permute-start.35) | collective-permute-done | bytes 589856 | tf_op jit(solution)/shard_map/ppermute | solution.py:549
  229.8 5.7 %collective-permute-start.40 = (bf16[1152,128]{1,0:T(8,128)(2,1)S(1)}, bf16[1152,128]{1,0:T(8,128)(2,1)S(1)}, u32[]{:S(2)}, u32[]{:S(2)}) collective-permute-start(bf16[1152,128]{1,0:T(8,128)(2,1)S(1)} %pad_maximum_fusion.19), channel_id=1, source_target_pairs={{0,4},{1,5},{2,6},{3,7},{4,0},{5,1},{6,2},{7,3},{8,12},{9,13},{10,... | collective-permute-start | bytes 884744 | tf_op jit(solution)/shard_map/ppermute | solution.py:549
  235.5 2.4 collective-permute-start.41
  239.2 16.4 %collective-permute-done.40 = bf16[1152,128]{1,0:T(8,128)(2,1)S(1)} collective-permute-done((bf16[1152,128]{1,0:T(8,128)(2,1)S(1)}, bf16[1152,128]{1,0:T(8,128)(2,1)S(1)}, u32[]{:S(2)}, u32[]{:S(2)}) %collective-permute-start.40) | collective-permute-done | bytes 294944 | tf_op jit(solution)/shard_map/ppermute | solution.py:549
  (160 shorter events, 49.2 us)
Async XLA Ops:
  4.8 15.7 %collective-permute-start.2 = (bf16[768,128]{1,0:T(8,128)(2,1)S(1)}, bf16[768,128]{1,0:T(8,128)(2,1)S(1)}, u32[]{:S(2)}, u32[]{:S(2)}) collective-permute-start(bf16[768,128]{1,0:T(8,128)(2,1)S(1)} %maximum_maximum_fusion), channel_id=1, source_target_pairs={{0,6},{1,7},{2,4},{3,5},{4,2},{5,3},{6,0},{7,1},{8,14},{9,15},{10,... | collective-permute-start | bytes 589832 | tf_op jit(solution)/shard_map/ppermute | solution.py:549
  10.0 16.7 %collective-permute-start.1 = (bf16[768,128]{1,0:T(8,128)(2,1)S(1)}, bf16[768,128]{1,0:T(8,128)(2,1)S(1)}, u32[]{:S(2)}, u32[]{:S(2)}) collective-permute-start(bf16[768,128]{1,0:T(8,128)(2,1)S(1)} %maximum_maximum_fusion), channel_id=1, source_target_pairs={{0,4},{1,5},{2,6},{3,7},{4,0},{5,1},{6,2},{7,3},{8,12},{9,13},{10,... | collective-permute-start | bytes 589832 | tf_op jit(solution)/shard_map/ppermute | solution.py:549
  10.0 16.7 %collective-permute-start = (bf16[768,128]{1,0:T(8,128)(2,1)S(1)}, bf16[768,128]{1,0:T(8,128)(2,1)S(1)}, u32[]{:S(2)}, u32[]{:S(2)}) collective-permute-start(bf16[768,128]{1,0:T(8,128)(2,1)S(1)} %maximum_maximum_fusion), channel_id=1, source_target_pairs={{0,2},{1,3},{2,0},{3,1},{4,6},{5,7},{6,4},{7,5},{8,10},{9,11},{10,... | collective-permute-start | bytes 589832 | tf_op jit(solution)/shard_map/ppermute | solution.py:549
  26.7 23.9 %collective-permute-start.13 = (bf16[2,192,384]{2,1,0:T(8,128)(2,1)S(1)}, bf16[2,192,384]{2,1,0:T(8,128)(2,1)S(1)}, u32[]{:S(2)}, u32[]{:S(2)}) collective-permute-start(bf16[2,192,384]{2,1,0:T(8,128)(2,1)S(1)} %pad_maximum_fusion.13), channel_id=1, source_target_pairs={{0,6},{1,7},{2,4},{3,5},{4,2},{5,3},{6,0},{7,1},{8,14},{9,15},{10,... | collective-permute-start | bytes 884744 | tf_op jit(solution)/shard_map/ppermute | solution.py:549
  29.4 31.8 %collective-permute-start.12 = (bf16[2,192,384]{2,1,0:T(8,128)(2,1)S(1)}, bf16[2,192,384]{2,1,0:T(8,128)(2,1)S(1)}, u32[]{:S(2)}, u32[]{:S(2)}) collective-permute-start(bf16[2,192,384]{2,1,0:T(8,128)(2,1)S(1)} %pad_maximum_fusion.13), channel_id=1, source_target_pairs={{0,4},{1,5},{2,6},{3,7},{4,0},{5,1},{6,2},{7,3},{8,12},{9,13},{10,... | collective-permute-start | bytes 884744 | tf_op jit(solution)/shard_map/ppermute | solution.py:549
  29.4 17.9 %collective-permute-start.7 = (bf16[2,192,384]{2,1,0:T(8,128)(2,1)S(1)}, bf16[2,192,384]{2,1,0:T(8,128)(2,1)S(1)}, u32[]{:S(2)}, u32[]{:S(2)}) collective-permute-start(bf16[2,192,384]{2,1,0:T(8,128)(2,1)S(1)} %pad_maximum_fusion.13), channel_id=1, source_target_pairs={{0,2},{1,3},{2,0},{3,1},{4,6},{5,7},{6,4},{7,5},{8,10},{9,11},{10,... | collective-permute-start | bytes 884744 | tf_op jit(solution)/shard_map/ppermute | solution.py:549
  31.3 17.5 %collective-permute-start.5 = (bf16[4,384,128]{2,1,0:T(8,128)(2,1)S(1)}, bf16[4,384,128]{2,1,0:T(8,128)(2,1)S(1)}, u32[]{:S(2)}, u32[]{:S(2)}) collective-permute-start(bf16[4,384,128]{2,1,0:T(8,128)(2,1)S(1)} %get-tuple-element.46), channel_id=1, source_target_pairs={{0,8},{1,9},{2,10},{3,11},{4,12},{5,13},{6,14},{7,15},{8,0},{9,1},... | collective-permute-start | bytes 1179656 | tf_op jit(solution)/shard_map/ppermute | solution.py:549
  32.9 16.0 %collective-permute-start.6 = (bf16[4,384,128]{2,1,0:T(8,128)(2,1)S(1)}, bf16[4,384,128]{2,1,0:T(8,128)(2,1)S(1)}, u32[]{:S(2)}, u32[]{:S(2)}) collective-permute-start(bf16[4,384,128]{2,1,0:T(8,128)(2,1)S(1)} %get-tuple-element.47), channel_id=1, source_target_pairs={{0,16},{1,17},{2,18},{3,19},{4,20},{5,21},{6,22},{7,23},{8,24},{9,... | collective-permute-start | bytes 1179656 | tf_op jit(solution)/shard_map/ppermute | solution.py:549
  47.3 17.2 %collective-permute-start.11 = (bf16[3,384,128]{2,1,0:T(8,128)(2,1)S(1)}, bf16[3,384,128]{2,1,0:T(8,128)(2,1)S(1)}, u32[]{:S(2)}, u32[]{:S(2)}) collective-permute-start(bf16[3,384,128]{2,1,0:T(8,128)(2,1)S(1)} %pad_maximum_fusion.14), channel_id=1, source_target_pairs={{0,6},{1,7},{2,4},{3,5},{4,2},{5,3},{6,0},{7,1},{8,14},{9,15},{10,... | collective-permute-start | bytes 884744 | tf_op jit(solution)/shard_map/ppermute | solution.py:549
  49.0 20.5 %collective-permute-start.8 = (bf16[2,4,384,128]{3,2,1,0:T(8,128)(2,1)S(1)}, bf16[2,4,384,128]{3,2,1,0:T(8,128)(2,1)S(1)}, u32[]{:S(2)}, u32[]{:S(2)}) collective-permute-start(bf16[2,4,384,128]{3,2,1,0:T(8,128)(2,1)S(1)} %pad_maximum_fusion.5), channel_id=1, source_target_pairs={{0,16},{1,17},{2,18},{3,19},{4,20},{5,21},{6,22},{7,23},{8,24},{9,... | collective-permute-start | bytes 2359304 | tf_op jit(solution)/shard_map/ppermute | solution.py:549
  50.6 29.9 %collective-permute-start.18 = (bf16[2,4,384,128]{3,2,1,0:T(8,128)(2,1)S(1)}, bf16[2,4,384,128]{3,2,1,0:T(8,128)(2,1)S(1)}, u32[]{:S(2)}, u32[]{:S(2)}) collective-permute-start(bf16[2,4,384,128]{3,2,1,0:T(8,128)(2,1)S(1)} %pad_maximum_fusion.6), channel_id=1, source_target_pairs={{0,8},{1,9},{2,10},{3,11},{4,12},{5,13},{6,14},{7,15},{8,0},{9,1},... | collective-permute-start | bytes 2359304 | tf_op jit(solution)/shard_map/ppermute | solution.py:549
  61.4 19.1 %collective-permute-start.14 = (bf16[4,192,384]{2,1,0:T(8,128)(2,1)S(1)}, bf16[4,192,384]{2,1,0:T(8,128)(2,1)S(1)}, u32[]{:S(2)}, u32[]{:S(2)}) collective-permute-start(bf16[4,192,384]{2,1,0:T(8,128)(2,1)S(1)} %get-tuple-element.51), channel_id=1, source_target_pairs={{0,8},{1,9},{2,10},{3,11},{4,12},{5,13},{6,14},{7,15},{8,0},{9,1},... | collective-permute-start | bytes 1769480 | tf_op jit(solution)/shard_map/ppermute | solution.py:549
  63.0 17.5 %collective-permute-start.15 = (bf16[4,192,384]{2,1,0:T(8,128)(2,1)S(1)}, bf16[4,192,384]{2,1,0:T(8,128)(2,1)S(1)}, u32[]{:S(2)}, u32[]{:S(2)}) collective-permute-start(bf16[4,192,384]{2,1,0:T(8,128)(2,1)S(1)} %get-tuple-element.52), channel_id=1, source_target_pairs={{0,16},{1,17},{2,18},{3,19},{4,20},{5,21},{6,22},{7,23},{8,24},{9,... | collective-permute-start | bytes 1769480 | tf_op jit(solution)/shard_map/ppermute | solution.py:549
  83.6 28.7 %collective-permute-start.23 = (bf16[2,4,192,384]{3,2,1,0:T(8,128)(2,1)}, bf16[2,4,192,384]{3,2,1,0:T(8,128)(2,1)}, u32[]{:S(2)}, u32[]{:S(2)}) collective-permute-start(bf16[2,4,192,384]{3,2,1,0:T(8,128)(2,1)} %pad_maximum_fusion.4.refs_6_), channel_id=1, source_target_pairs={{0,8},{1,9},{2,10},{3,11},{4,12},{5,13},{6,14},{7,15},{8,0},{9,1},... | collective-permute-start | bytes 3538952 | tf_op jit(solution)/shard_map/ppermute | solution.py:549
  86.2 28.4 %collective-permute-start.22 = (bf16[2,4,192,384]{3,2,1,0:T(8,128)(2,1)}, bf16[2,4,192,384]{3,2,1,0:T(8,128)(2,1)}, u32[]{:S(2)}, u32[]{:S(2)}) collective-permute-start(bf16[2,4,192,384]{3,2,1,0:T(8,128)(2,1)} %pad_maximum_fusion.3.refs_4_), channel_id=1, source_target_pairs={{0,16},{1,17},{2,18},{3,19},{4,20},{5,21},{6,22},{7,23},{8,24},{9,... | collective-permute-start | bytes 3538952 | tf_op jit(solution)/shard_map/ppermute | solution.py:549
  87.6 17.3 %collective-permute-start.21 = (bf16[512,768]{1,0:T(8,128)(2,1)}, bf16[512,768]{1,0:T(8,128)(2,1)}, u32[]{:S(2)}, u32[]{:S(2)}) collective-permute-start(bf16[512,768]{1,0:T(8,128)(2,1)} %c_ref.1), channel_id=1, source_target_pairs={{0,1},{1,0},{2,3},{3,2},{4,5},{5,4},{6,7},{7,6},{8,9},{9,8},{10,11... | collective-permute-start | bytes 2359304 | tf_op jit(solution)/shard_map/ppermute | solution.py:549
  139.5 29.5 %collective-permute-start.26 = (bf16[2,4,192,384]{3,2,1,0:T(8,128)(2,1)}, bf16[2,4,192,384]{3,2,1,0:T(8,128)(2,1)S(1)}, u32[]{:S(2)}, u32[]{:S(2)}) collective-permute-start(bf16[2,4,192,384]{3,2,1,0:T(8,128)(2,1)} %get-tuple-element.71), channel_id=1, source_target_pairs={{0,16},{1,17},{2,18},{3,19},{4,20},{5,21},{6,22},{7,23},{8,24},{9,... | collective-permute-start | bytes 3538952 | tf_op jit(solution)/shard_map/ppermute | solution.py:549
  140.4 28.6 %collective-permute-start.27 = (bf16[2,4,192,384]{3,2,1,0:T(8,128)(2,1)}, bf16[2,4,192,384]{3,2,1,0:T(8,128)(2,1)S(1)}, u32[]{:S(2)}, u32[]{:S(2)}) collective-permute-start(bf16[2,4,192,384]{3,2,1,0:T(8,128)(2,1)} %get-tuple-element.72), channel_id=1, source_target_pairs={{0,8},{1,9},{2,10},{3,11},{4,12},{5,13},{6,14},{7,15},{8,0},{9,1},... | collective-permute-start | bytes 3538952 | tf_op jit(solution)/shard_map/ppermute | solution.py:549
  168.9 17.4 %collective-permute-start.28 = (bf16[4,4,576,128]{3,2,1,0:T(8,128)(2,1)}, bf16[4,4,576,128]{3,2,1,0:T(8,128)(2,1)S(1)}, u32[]{:S(2)}, u32[]{:S(2)}) collective-permute-start(bf16[4,4,576,128]{3,2,1,0:T(8,128)(2,1)} %get-tuple-element.73), channel_id=1, source_target_pairs={{0,1},{1,0},{2,3},{3,2},{4,5},{5,4},{6,7},{7,6},{8,9},{9,8},{10,11... | collective-permute-start | bytes 7077896 | tf_op jit(solution)/shard_map/ppermute | solution.py:549
  169.1 19.5 %collective-permute-start.36 = (bf16[4,4,576,128]{3,2,1,0:T(8,128)(2,1)S(1)}, bf16[4,4,576,128]{3,2,1,0:T(8,128)(2,1)S(1)}, u32[]{:S(2)}, u32[]{:S(2)}) collective-permute-start(bf16[4,4,576,128]{3,2,1,0:T(8,128)(2,1)S(1)} %get-tuple-element.75), channel_id=1, source_target_pairs={{0,1},{1,0},{2,3},{3,2},{4,5},{5,4},{6,7},{7,6},{8,9},{9,8},{10,11... | collective-permute-start | bytes 7077896 | tf_op jit(solution)/shard_map/ppermute | solution.py:549
  169.7 15.4 %collective-permute-start.31 = (bf16[4,192,384]{2,1,0:T(8,128)(2,1)S(1)}, bf16[4,192,384]{2,1,0:T(8,128)(2,1)S(1)}, u32[]{:S(2)}, u32[]{:S(2)}) collective-permute-start(bf16[4,192,384]{2,1,0:T(8,128)(2,1)S(1)} %fusion.4), channel_id=1, source_target_pairs={{0,16},{1,17},{2,18},{3,19},{4,20},{5,21},{6,22},{7,23},{8,24},{9,... | collective-permute-start | bytes 1769480 | tf_op jit(solution)/shard_map/ppermute | solution.py:549
  171.1 15.1 %collective-permute-start.30 = (bf16[4,192,384]{2,1,0:T(8,128)(2,1)S(1)}, bf16[4,192,384]{2,1,0:T(8,128)(2,1)S(1)}, u32[]{:S(2)}, u32[]{:S(2)}) collective-permute-start(bf16[4,192,384]{2,1,0:T(8,128)(2,1)S(1)} %fusion.3), channel_id=1, source_target_pairs={{0,8},{1,9},{2,10},{3,11},{4,12},{5,13},{6,14},{7,15},{8,0},{9,1},... | collective-permute-start | bytes 1769480 | tf_op jit(solution)/shard_map/ppermute | solution.py:549
  187.1 27.2 %collective-permute-start.29 = (bf16[2,4,576,128]{3,2,1,0:T(8,128)(2,1)S(1)}, bf16[2,4,576,128]{3,2,1,0:T(8,128)(2,1)S(1)}, u32[]{:S(2)}, u32[]{:S(2)}) collective-permute-start(bf16[2,4,576,128]{3,2,1,0:T(8,128)(2,1)S(1)} %add_convert_fusion), channel_id=1, source_target_pairs={{0,8},{1,9},{2,10},{3,11},{4,12},{5,13},{6,14},{7,15},{8,0},{9,1},... | collective-permute-start | bytes 3538952 | tf_op jit(solution)/shard_map/ppermute | solution.py:549
  189.0 27.2 %collective-permute-start.37 = (bf16[2,4,576,128]{3,2,1,0:T(8,128)(2,1)S(1)}, bf16[2,4,576,128]{3,2,1,0:T(8,128)(2,1)S(1)}, u32[]{:S(2)}, u32[]{:S(2)}) collective-permute-start(bf16[2,4,576,128]{3,2,1,0:T(8,128)(2,1)S(1)} %fusion), channel_id=1, source_target_pairs={{0,16},{1,17},{2,18},{3,19},{4,20},{5,21},{6,22},{7,23},{8,24},{9,... | collective-permute-start | bytes 3538952 | tf_op jit(solution)/shard_map/ppermute | solution.py:549
  190.2 22.5 %collective-permute-start.33 = (bf16[384,384]{1,0:T(8,128)(2,1)S(1)}, bf16[384,384]{1,0:T(8,128)(2,1)S(1)}, u32[]{:S(2)}, u32[]{:S(2)}) collective-permute-start(bf16[384,384]{1,0:T(8,128)(2,1)S(1)} %pad_maximum_fusion.16), channel_id=1, source_target_pairs={{0,4},{1,5},{2,6},{3,7},{4,0},{5,1},{6,2},{7,3},{8,12},{9,13},{10,... | collective-permute-start | bytes 884744 | tf_op jit(solution)/shard_map/ppermute | solution.py:549
  192.3 20.4 %collective-permute-start.34 = (bf16[384,384]{1,0:T(8,128)(2,1)S(1)}, bf16[384,384]{1,0:T(8,128)(2,1)S(1)}, u32[]{:S(2)}, u32[]{:S(2)}) collective-permute-start(bf16[384,384]{1,0:T(8,128)(2,1)S(1)} %pad_maximum_fusion.17), channel_id=1, source_target_pairs={{0,6},{1,7},{2,4},{3,5},{4,2},{5,3},{6,0},{7,1},{8,14},{9,15},{10,... | collective-permute-start | bytes 884744 | tf_op jit(solution)/shard_map/ppermute | solution.py:549
  194.4 18.7 %collective-permute-start.32 = (bf16[384,384]{1,0:T(8,128)(2,1)S(1)}, bf16[384,384]{1,0:T(8,128)(2,1)S(1)}, u32[]{:S(2)}, u32[]{:S(2)}) collective-permute-start(bf16[384,384]{1,0:T(8,128)(2,1)S(1)} %pad_maximum_fusion.15), channel_id=1, source_target_pairs={{0,2},{1,3},{2,0},{3,1},{4,6},{5,7},{6,4},{7,5},{8,10},{9,11},{10,... | collective-permute-start | bytes 884744 | tf_op jit(solution)/shard_map/ppermute | solution.py:549
  214.6 14.0 %collective-permute-start.35 = (bf16[4,576,128]{2,1,0:T(8,128)(2,1)S(1)}, bf16[4,576,128]{2,1,0:T(8,128)(2,1)S(1)}, u32[]{:S(2)}, u32[]{:S(2)}) collective-permute-start(bf16[4,576,128]{2,1,0:T(8,128)(2,1)S(1)} %fusion.2), channel_id=1, source_target_pairs={{0,16},{1,17},{2,18},{3,19},{4,20},{5,21},{6,22},{7,23},{8,24},{9,... | collective-permute-start | bytes 1769480 | tf_op jit(solution)/shard_map/ppermute | solution.py:549
  217.6 20.4 %collective-permute-start.24 = (bf16[512,768]{1,0:T(8,128)(2,1)S(1)}, bf16[512,768]{1,0:T(8,128)(2,1)S(1)}, u32[]{:S(2)}, u32[]{:S(2)}) collective-permute-start(bf16[512,768]{1,0:T(8,128)(2,1)S(1)} %copy-done.21), channel_id=1, source_target_pairs={{0,1},{1,0},{2,3},{3,2},{4,5},{5,4},{6,7},{7,6},{8,9},{9,8},{10,11... | collective-permute-start | bytes 2359304 | tf_op jit(solution)/shard_map/ppermute | solution.py:549
  229.8 25.8 %collective-permute-start.40 = (bf16[1152,128]{1,0:T(8,128)(2,1)S(1)}, bf16[1152,128]{1,0:T(8,128)(2,1)S(1)}, u32[]{:S(2)}, u32[]{:S(2)}) collective-permute-start(bf16[1152,128]{1,0:T(8,128)(2,1)S(1)} %pad_maximum_fusion.19), channel_id=1, source_target_pairs={{0,4},{1,5},{2,6},{3,7},{4,0},{5,1},{6,2},{7,3},{8,12},{9,13},{10,... | collective-permute-start | bytes 884744 | tf_op jit(solution)/shard_map/ppermute | solution.py:549
  235.5 20.1 %collective-permute-start.41 = (bf16[1152,128]{1,0:T(8,128)(2,1)S(1)}, bf16[1152,128]{1,0:T(8,128)(2,1)S(1)}, u32[]{:S(2)}, u32[]{:S(2)}) collective-permute-start(bf16[1152,128]{1,0:T(8,128)(2,1)S(1)} %pad_maximum_fusion.20), channel_id=1, source_target_pairs={{0,6},{1,7},{2,4},{3,5},{4,2},{5,3},{6,0},{7,1},{8,14},{9,15},{10,... | collective-permute-start | bytes 884744 | tf_op jit(solution)/shard_map/ppermute | solution.py:549
  237.9 17.7 %collective-permute-start.39 = (bf16[1152,128]{1,0:T(8,128)(2,1)S(1)}, bf16[1152,128]{1,0:T(8,128)(2,1)S(1)}, u32[]{:S(2)}, u32[]{:S(2)}) collective-permute-start(bf16[1152,128]{1,0:T(8,128)(2,1)S(1)} %pad_maximum_fusion.18), channel_id=1, source_target_pairs={{0,2},{1,3},{2,0},{3,1},{4,6},{5,7},{6,4},{7,5},{8,10},{9,11},{10,... | collective-permute-start | bytes 884744 | tf_op jit(solution)/shard_map/ppermute | solution.py:549
  (32 other events, 401.3 us)

commit v10 on v9

--- a/solution.py
+++ b/solution.py
@@ -39,12 +39,13 @@
     "aw2": ("fz1",),
     "bz": ("c1",),
     "f1": ("aw1",),
-    "wc": ("f1",),
+    "wc": ("bz", "f1"),
     "ac": ("bz", "f1"),
     "k1": ("ac", "bc"),
     "cp": ("f1r",),
     "m1": ("f2r",),
     "m2": ("fzr",),
+    "f2": ("aw2",),
 }
 
 F32 = jnp.float32

time: 261 us -> 261 us (level)
  starting transfers between devices: 53.1 us -> 50.4 us
    ppermute x42, starting transfers between devices: 53.1 us -> 50.4 us  [fetch(): return lax.ppermute(val, ('gx', 'gy'), pairs)]
  transfers between devices with their start and end apart: 42 -> 42, of which waited for: 21 -> 20; matrix products, arithmetic and copies ran while one was open for 4% -> 4% of each run, Pallas kernels for 13% -> 13%
where the time goes in v10:
time: 261 us; the launch traced here: 258 us
  waiting for transfers between devices  115 us (44%)
  Pallas kernels  58.6 us (22%)
  starting transfers between devices  50.4 us (19%)
  local copies, waits for them, and re-layouts  16.1 us (6%)
  other arithmetic  11 us (4%)
  between operations  6.96 us (3%)
    ppermute x42, waiting for transfers between devices, fetch(): return lax.ppermute(val, ('gx', 'gy'), pairs)  115 us
    ppermute x42, starting transfers between devices, fetch(): return lax.ppermute(val, ('gx', 'gy'), pairs)  50.4 us
    pallas_call x1, Pallas kernels, run_ffn(): call(functools.partial(ffn_body, n - 1), (Z // ZS,), [whole((L, D))] * (2...  23.9 us
    pallas_call x1, Pallas kernels, run_back(): call(back_body, (L // TM,), specs, [whole(None)] * 5, [sds((L, D), F32)]...  21.8 us
    unnamed x46, local copies, waits for them, and re-layouts  10.9 us
    pallas_call x1, Pallas kernels, run_mixer(): call(mixer_body, (L // TM,), [whole((L, D)), whole((8, D)), rows(1), whol...  8.69 us
  transfers between devices with their start and end apart: 42, of which 20 were waited for; matrix products, arithmetic and copies ran while one was open for 4% of the time, Pallas kernels for 13%

profile of v10, /device:TPU:0, one launch (start us, length us, event | category | flops | bytes accessed | tf_op | source)
XLA Modules:
  0.0 258.3 jit_solution(8010127275434400360)
XLA Ops:
  4.8 5.1 %collective-permute-start.2 = (bf16[768,128]{1,0:T(8,128)(2,1)S(1)}, bf16[768,128]{1,0:T(8,128)(2,1)S(1)}, u32[]{:S(2)}, u32[]{:S(2)}) collective-permute-start(bf16[768,128]{1,0:T(8,128)(2,1)S(1)} %maximum_maximum_fusion), channel_id=1, source_target_pairs={{0,6},{1,7},{2,4},{3,5},{4,2},{5,3},{6,0},{7,1},{8,14},{9,15},{10,... | collective-permute-start | bytes 589832 | tf_op jit(solution)/shard_map/ppermute | solution.py:550
  10.6 1.6 collective-permute-start.3
  19.0 1.6 collective-permute-start.4
  20.6 6.1 %collective-permute-done.1 = bf16[768,128]{1,0:T(8,128)(2,1)S(1)} collective-permute-done((bf16[768,128]{1,0:T(8,128)(2,1)S(1)}, bf16[768,128]{1,0:T(8,128)(2,1)S(1)}, u32[]{:S(2)}, u32[]{:S(2)}) %collective-permute-start.1) | collective-permute-done | bytes 196640 | tf_op jit(solution)/shard_map/ppermute | solution.py:550
  26.7 2.7 %collective-permute-start.13 = (bf16[2,192,384]{2,1,0:T(8,128)(2,1)S(1)}, bf16[2,192,384]{2,1,0:T(8,128)(2,1)S(1)}, u32[]{:S(2)}, u32[]{:S(2)}) collective-permute-start(bf16[2,192,384]{2,1,0:T(8,128)(2,1)S(1)} %pad_maximum_fusion.13), channel_id=1, source_target_pairs={{0,6},{1,7},{2,4},{3,5},{4,2},{5,3},{6,0},{7,1},{8,14},{9,15},{10,... | collective-permute-start | bytes 884744 | tf_op jit(solution)/shard_map/ppermute | solution.py:550
  29.4 1.7 collective-permute-start.7
  31.3 1.6 collective-permute-start.5
  34.5 12.8 %collective-permute-done.7 = bf16[2,192,384]{2,1,0:T(8,128)(2,1)S(1)} collective-permute-done((bf16[2,192,384]{2,1,0:T(8,128)(2,1)S(1)}, bf16[2,192,384]{2,1,0:T(8,128)(2,1)S(1)}, u32[]{:S(2)}, u32[]{:S(2)}) %collective-permute-start.7) | collective-permute-done | bytes 294944 | tf_op jit(solution)/shard_map/ppermute | solution.py:550
  47.3 1.5 collective-permute-start.11
  49.0 1.6 collective-permute-start.8
  50.6 1.6 collective-permute-start.18
  52.2 9.0 %collective-permute-done.12 = bf16[2,192,384]{2,1,0:T(8,128)(2,1)S(1)} collective-permute-done((bf16[2,192,384]{2,1,0:T(8,128)(2,1)S(1)}, bf16[2,192,384]{2,1,0:T(8,128)(2,1)S(1)}, u32[]{:S(2)}, u32[]{:S(2)}) %collective-permute-start.12) | collective-permute-done | bytes 294944 | tf_op jit(solution)/shard_map/ppermute | solution.py:550
  61.4 1.6 collective-permute-start.14
  64.5 1.8 collective-permute-start.10
  66.3 3.3 %collective-permute-done.8 = bf16[2,4,384,128]{3,2,1,0:T(8,128)(2,1)S(1)} collective-permute-done((bf16[2,4,384,128]{3,2,1,0:T(8,128)(2,1)S(1)}, bf16[2,4,384,128]{3,2,1,0:T(8,128)(2,1)S(1)}, u32[]{:S(2)}, u32[]{:S(2)}) %collective-permute-start.8) | collective-permute-done | bytes 786464 | tf_op jit(solution)/shard_map/ppermute | solution.py:550
  69.6 1.6 collective-permute-start.9
  71.3 7.0 %collective-permute-done.10 = bf16[3,384,128]{2,1,0:T(8,128)(2,1)S(1)} collective-permute-done((bf16[3,384,128]{2,1,0:T(8,128)(2,1)S(1)}, bf16[3,384,128]{2,1,0:T(8,128)(2,1)S(1)}, u32[]{:S(2)}, u32[]{:S(2)}) %collective-permute-start.10) | collective-permute-done | bytes 294944 | tf_op jit(solution)/shard_map/ppermute | solution.py:550
  78.3 1.6 collective-permute-done.9
  89.1 4.1 %shard_map.169 = (bf16[512,768]{1,0:T(8,128)(2,1)S(1)}, bf16[4,512,256]{2,1,0:T(8,128)(2,1)S(1)}, f32[8,768]{1,0:T(8,128)S(1)}) custom-call(s32[14]{0:T(128)S(1)} %stack.195.t, bf16[512,768]{1,0:T(8,128)(2,1)S(1)} %copy-done.2, bf16[4,4,384,128]{3,2,1,0:T(8,128)(2,1)S(1)} %bitcast.233, bf16[4,4,384,128]{3,2,1,0:T(8,128)(2,1)} %collective-permute-done.19.oth_ref.w_oth), custom_call_target="tpu_custom_call" | custom-call | flops 1 | bytes 6291456 | tf_op jit(solution)/shard_map/pallas_call | solution.py:453
  94.2 8.7 %shard_map.170 = (bf16[4,512,256]{2,1,0:T(8,128)(2,1)S(1)}, f32[512,768]{1,0:T(8,128)S(1)}, bf16[512,768]{1,0:T(8,128)(2,1)S(1)}) custom-call(s32[14]{0:T(128)S(1)} %stack.195.t, bf16[512,768]{1,0:T(8,128)(2,1)S(1)} %copy-done.2, f32[8,768]{1,0:T(8,128)S(1)} %get-tuple-element.59.gain_ref, s32[512,1]{1,0:T(8,128)S(1)} %copy.28.dq_ref, ...), custom_call_target="tpu_custom_call" | custom-call | flops 1 | bytes 14680064 | tf_op jit(solution)/shard_map/pallas_call | solution.py:465
  105.0 8.5 %collective-permute-done.22.refs_5_ = bf16[2,4,192,384]{3,2,1,0:T(8,128)(2,1)} collective-permute-done((bf16[2,4,192,384]{3,2,1,0:T(8,128)(2,1)}, bf16[2,4,192,384]{3,2,1,0:T(8,128)(2,1)}, u32[]{:S(2)}, u32[]{:S(2)}) %collective-permute-start.22) | collective-permute-done | bytes 1179680 | tf_op jit(solution)/shard_map/ppermute | solution.py:550
  114.9 23.9 %shard_map.171 = (bf16[2,4,192,384]{3,2,1,0:T(8,128)(2,1)}, bf16[2,4,192,384]{3,2,1,0:T(8,128)(2,1)}, bf16[2,4,192,384]{3,2,1,0:T(8,128)(2,1)}, bf16[2,4,192,384...) custom-call(s32[14]{0:T(128)} %copy-done.11, ...), custom_call_target="tpu_custom_call" | custom-call | flops 1 | bytes 20971520 | tf_op jit(solution)/shard_map/pallas_call | solution.py:484
  141.6 2.5 collective-permute-done.25.dnb_ref
  147.7 21.8 %shard_map.172 = (f32[512,768]{1,0:T(8,128)}, bf16[4,4,576,128]{3,2,1,0:T(8,128)(2,1)S(1)}, bf16[4,4,576,128]{3,2,1,0:T(8,128)(2,1)S(1)}, bf16[4,4,576,128]{3,2,1,0:T(8,128)(2,1)}, bf16[4,4,576,128]{3,2,1,0:T(8,128)(2,1)}) custom-call(s32[14]{0:T(128)S(1)} %copy-done.12, f32[512,768]{1,0:T(8,128)S(1)} %copy-done.5, ...), custom_call_target="tpu_custom_call" | custom-call | flops 1 | bytes 41943040 | tf_op jit(solution)/shard_map/pallas_call | solution.py:504
  172.0 13.8 %collective-permute-done.31 = bf16[4,192,384]{2,1,0:T(8,128)(2,1)S(1)} collective-permute-done((bf16[4,192,384]{2,1,0:T(8,128)(2,1)S(1)}, bf16[4,192,384]{2,1,0:T(8,128)(2,1)S(1)}, u32[]{:S(2)}, u32[]{:S(2)}) %collective-permute-start.31) | collective-permute-done | bytes 589856 | tf_op jit(solution)/shard_map/ppermute | solution.py:550
  189.6 1.7 collective-permute-start.33
  191.3 2.0 collective-permute-start.34
  193.5 18.3 %collective-permute-done.33 = bf16[384,384]{1,0:T(8,128)(2,1)S(1)} collective-permute-done((bf16[384,384]{1,0:T(8,128)(2,1)S(1)}, bf16[384,384]{1,0:T(8,128)(2,1)S(1)}, u32[]{:S(2)}, u32[]{:S(2)}) %collective-permute-start.33) | collective-permute-done | bytes 294944 | tf_op jit(solution)/shard_map/ppermute | solution.py:550
  217.6 11.2 %collective-permute-done.35 = bf16[4,576,128]{2,1,0:T(8,128)(2,1)S(1)} collective-permute-done((bf16[4,576,128]{2,1,0:T(8,128)(2,1)S(1)}, bf16[4,576,128]{2,1,0:T(8,128)(2,1)S(1)}, u32[]{:S(2)}, u32[]{:S(2)}) %collective-permute-start.35) | collective-permute-done | bytes 589856 | tf_op jit(solution)/shard_map/ppermute | solution.py:550
  230.0 5.2 %collective-permute-start.40 = (bf16[1152,128]{1,0:T(8,128)(2,1)S(1)}, bf16[1152,128]{1,0:T(8,128)(2,1)S(1)}, u32[]{:S(2)}, u32[]{:S(2)}) collective-permute-start(bf16[1152,128]{1,0:T(8,128)(2,1)S(1)} %pad_maximum_fusion.19), channel_id=1, source_target_pairs={{0,4},{1,5},{2,6},{3,7},{4,0},{5,1},{6,2},{7,3},{8,12},{9,13},{10,... | collective-permute-start | bytes 884744 | tf_op jit(solution)/shard_map/ppermute | solution.py:550
  235.3 2.0 collective-permute-start.41
  238.5 16.1 %collective-permute-done.40 = bf16[1152,128]{1,0:T(8,128)(2,1)S(1)} collective-permute-done((bf16[1152,128]{1,0:T(8,128)(2,1)S(1)}, bf16[1152,128]{1,0:T(8,128)(2,1)S(1)}, u32[]{:S(2)}, u32[]{:S(2)}) %collective-permute-start.40) | collective-permute-done | bytes 294944 | tf_op jit(solution)/shard_map/ppermute | solution.py:550
  (160 shorter events, 47.9 us)
Async XLA Ops:
  4.8 15.7 %collective-permute-start.2 = (bf16[768,128]{1,0:T(8,128)(2,1)S(1)}, bf16[768,128]{1,0:T(8,128)(2,1)S(1)}, u32[]{:S(2)}, u32[]{:S(2)}) collective-permute-start(bf16[768,128]{1,0:T(8,128)(2,1)S(1)} %maximum_maximum_fusion), channel_id=1, source_target_pairs={{0,6},{1,7},{2,4},{3,5},{4,2},{5,3},{6,0},{7,1},{8,14},{9,15},{10,... | collective-permute-start | bytes 589832 | tf_op jit(solution)/shard_map/ppermute | solution.py:550
  10.0 16.7 %collective-permute-start.1 = (bf16[768,128]{1,0:T(8,128)(2,1)S(1)}, bf16[768,128]{1,0:T(8,128)(2,1)S(1)}, u32[]{:S(2)}, u32[]{:S(2)}) collective-permute-start(bf16[768,128]{1,0:T(8,128)(2,1)S(1)} %maximum_maximum_fusion), channel_id=1, source_target_pairs={{0,4},{1,5},{2,6},{3,7},{4,0},{5,1},{6,2},{7,3},{8,12},{9,13},{10,... | collective-permute-start | bytes 589832 | tf_op jit(solution)/shard_map/ppermute | solution.py:550
  10.0 16.7 %collective-permute-start = (bf16[768,128]{1,0:T(8,128)(2,1)S(1)}, bf16[768,128]{1,0:T(8,128)(2,1)S(1)}, u32[]{:S(2)}, u32[]{:S(2)}) collective-permute-start(bf16[768,128]{1,0:T(8,128)(2,1)S(1)} %maximum_maximum_fusion), channel_id=1, source_target_pairs={{0,2},{1,3},{2,0},{3,1},{4,6},{5,7},{6,4},{7,5},{8,10},{9,11},{10,... | collective-permute-start | bytes 589832 | tf_op jit(solution)/shard_map/ppermute | solution.py:550
  26.7 23.9 %collective-permute-start.13 = (bf16[2,192,384]{2,1,0:T(8,128)(2,1)S(1)}, bf16[2,192,384]{2,1,0:T(8,128)(2,1)S(1)}, u32[]{:S(2)}, u32[]{:S(2)}) collective-permute-start(bf16[2,192,384]{2,1,0:T(8,128)(2,1)S(1)} %pad_maximum_fusion.13), channel_id=1, source_target_pairs={{0,6},{1,7},{2,4},{3,5},{4,2},{5,3},{6,0},{7,1},{8,14},{9,15},{10,... | collective-permute-start | bytes 884744 | tf_op jit(solution)/shard_map/ppermute | solution.py:550
  29.4 31.8 %collective-permute-start.12 = (bf16[2,192,384]{2,1,0:T(8,128)(2,1)S(1)}, bf16[2,192,384]{2,1,0:T(8,128)(2,1)S(1)}, u32[]{:S(2)}, u32[]{:S(2)}) collective-permute-start(bf16[2,192,384]{2,1,0:T(8,128)(2,1)S(1)} %pad_maximum_fusion.13), channel_id=1, source_target_pairs={{0,4},{1,5},{2,6},{3,7},{4,0},{5,1},{6,2},{7,3},{8,12},{9,13},{10,... | collective-permute-start | bytes 884744 | tf_op jit(solution)/shard_map/ppermute | solution.py:550
  29.4 17.9 %collective-permute-start.7 = (bf16[2,192,384]{2,1,0:T(8,128)(2,1)S(1)}, bf16[2,192,384]{2,1,0:T(8,128)(2,1)S(1)}, u32[]{:S(2)}, u32[]{:S(2)}) collective-permute-start(bf16[2,192,384]{2,1,0:T(8,128)(2,1)S(1)} %pad_maximum_fusion.13), channel_id=1, source_target_pairs={{0,2},{1,3},{2,0},{3,1},{4,6},{5,7},{6,4},{7,5},{8,10},{9,11},{10,... | collective-permute-start | bytes 884744 | tf_op jit(solution)/shard_map/ppermute | solution.py:550
  31.3 17.5 %collective-permute-start.5 = (bf16[4,384,128]{2,1,0:T(8,128)(2,1)S(1)}, bf16[4,384,128]{2,1,0:T(8,128)(2,1)S(1)}, u32[]{:S(2)}, u32[]{:S(2)}) collective-permute-start(bf16[4,384,128]{2,1,0:T(8,128)(2,1)S(1)} %get-tuple-element.48), channel_id=1, source_target_pairs={{0,8},{1,9},{2,10},{3,11},{4,12},{5,13},{6,14},{7,15},{8,0},{9,1},... | collective-permute-start | bytes 1179656 | tf_op jit(solution)/shard_map/ppermute | solution.py:550
  32.9 16.0 %collective-permute-start.6 = (bf16[4,384,128]{2,1,0:T(8,128)(2,1)S(1)}, bf16[4,384,128]{2,1,0:T(8,128)(2,1)S(1)}, u32[]{:S(2)}, u32[]{:S(2)}) collective-permute-start(bf16[4,384,128]{2,1,0:T(8,128)(2,1)S(1)} %get-tuple-element.49), channel_id=1, source_target_pairs={{0,16},{1,17},{2,18},{3,19},{4,20},{5,21},{6,22},{7,23},{8,24},{9,... | collective-permute-start | bytes 1179656 | tf_op jit(solution)/shard_map/ppermute | solution.py:550
  47.3 17.2 %collective-permute-start.11 = (bf16[3,384,128]{2,1,0:T(8,128)(2,1)S(1)}, bf16[3,384,128]{2,1,0:T(8,128)(2,1)S(1)}, u32[]{:S(2)}, u32[]{:S(2)}) collective-permute-start(bf16[3,384,128]{2,1,0:T(8,128)(2,1)S(1)} %pad_maximum_fusion.14), channel_id=1, source_target_pairs={{0,6},{1,7},{2,4},{3,5},{4,2},{5,3},{6,0},{7,1},{8,14},{9,15},{10,... | collective-permute-start | bytes 884744 | tf_op jit(solution)/shard_map/ppermute | solution.py:550
  49.0 20.5 %collective-permute-start.8 = (bf16[2,4,384,128]{3,2,1,0:T(8,128)(2,1)S(1)}, bf16[2,4,384,128]{3,2,1,0:T(8,128)(2,1)S(1)}, u32[]{:S(2)}, u32[]{:S(2)}) collective-permute-start(bf16[2,4,384,128]{3,2,1,0:T(8,128)(2,1)S(1)} %pad_maximum_fusion.5), channel_id=1, source_target_pairs={{0,16},{1,17},{2,18},{3,19},{4,20},{5,21},{6,22},{7,23},{8,24},{9,... | collective-permute-start | bytes 2359304 | tf_op jit(solution)/shard_map/ppermute | solution.py:550
  50.6 29.9 %collective-permute-start.18 = (bf16[2,4,384,128]{3,2,1,0:T(8,128)(2,1)S(1)}, bf16[2,4,384,128]{3,2,1,0:T(8,128)(2,1)S(1)}, u32[]{:S(2)}, u32[]{:S(2)}) collective-permute-start(bf16[2,4,384,128]{3,2,1,0:T(8,128)(2,1)S(1)} %pad_maximum_fusion.6), channel_id=1, source_target_pairs={{0,8},{1,9},{2,10},{3,11},{4,12},{5,13},{6,14},{7,15},{8,0},{9,1},... | collective-permute-start | bytes 2359304 | tf_op jit(solution)/shard_map/ppermute | solution.py:550
  61.4 19.1 %collective-permute-start.14 = (bf16[4,192,384]{2,1,0:T(8,128)(2,1)S(1)}, bf16[4,192,384]{2,1,0:T(8,128)(2,1)S(1)}, u32[]{:S(2)}, u32[]{:S(2)}) collective-permute-start(bf16[4,192,384]{2,1,0:T(8,128)(2,1)S(1)} %get-tuple-element.53), channel_id=1, source_target_pairs={{0,8},{1,9},{2,10},{3,11},{4,12},{5,13},{6,14},{7,15},{8,0},{9,1},... | collective-permute-start | bytes 1769480 | tf_op jit(solution)/shard_map/ppermute | solution.py:550
  63.0 17.5 %collective-permute-start.15 = (bf16[4,192,384]{2,1,0:T(8,128)(2,1)S(1)}, bf16[4,192,384]{2,1,0:T(8,128)(2,1)S(1)}, u32[]{:S(2)}, u32[]{:S(2)}) collective-permute-start(bf16[4,192,384]{2,1,0:T(8,128)(2,1)S(1)} %get-tuple-element.54), channel_id=1, source_target_pairs={{0,16},{1,17},{2,18},{3,19},{4,20},{5,21},{6,22},{7,23},{8,24},{9,... | collective-permute-start | bytes 1769480 | tf_op jit(solution)/shard_map/ppermute | solution.py:550
  64.5 13.8 %collective-permute-start.10 = (bf16[3,384,128]{2,1,0:T(8,128)(2,1)S(1)}, bf16[3,384,128]{2,1,0:T(8,128)(2,1)S(1)}, u32[]{:S(2)}, u32[]{:S(2)}) collective-permute-start(bf16[3,384,128]{2,1,0:T(8,128)(2,1)S(1)} %pad_maximum_fusion.14), channel_id=1, source_target_pairs={{0,4},{1,5},{2,6},{3,7},{4,0},{5,1},{6,2},{7,3},{8,12},{9,13},{10,... | collective-permute-start | bytes 884744 | tf_op jit(solution)/shard_map/ppermute | solution.py:550
  84.7 28.7 %collective-permute-start.22 = (bf16[2,4,192,384]{3,2,1,0:T(8,128)(2,1)}, bf16[2,4,192,384]{3,2,1,0:T(8,128)(2,1)}, u32[]{:S(2)}, u32[]{:S(2)}) collective-permute-start(bf16[2,4,192,384]{3,2,1,0:T(8,128)(2,1)} %pad_maximum_fusion.3.refs_4_), channel_id=1, source_target_pairs={{0,16},{1,17},{2,18},{3,19},{4,20},{5,21},{6,22},{7,23},{8,24},{9,... | collective-permute-start | bytes 3538952 | tf_op jit(solution)/shard_map/ppermute | solution.py:550
  85.6 28.4 %collective-permute-start.23 = (bf16[2,4,192,384]{3,2,1,0:T(8,128)(2,1)}, bf16[2,4,192,384]{3,2,1,0:T(8,128)(2,1)}, u32[]{:S(2)}, u32[]{:S(2)}) collective-permute-start(bf16[2,4,192,384]{3,2,1,0:T(8,128)(2,1)} %pad_maximum_fusion.4.refs_6_), channel_id=1, source_target_pairs={{0,8},{1,9},{2,10},{3,11},{4,12},{5,13},{6,14},{7,15},{8,0},{9,1},... | collective-permute-start | bytes 3538952 | tf_op jit(solution)/shard_map/ppermute | solution.py:550
  87.6 17.3 %collective-permute-start.21 = (bf16[512,768]{1,0:T(8,128)(2,1)}, bf16[512,768]{1,0:T(8,128)(2,1)}, u32[]{:S(2)}, u32[]{:S(2)}) collective-permute-start(bf16[512,768]{1,0:T(8,128)(2,1)} %c_ref.1), channel_id=1, source_target_pairs={{0,1},{1,0},{2,3},{3,2},{4,5},{5,4},{6,7},{7,6},{8,9},{9,8},{10,11... | collective-permute-start | bytes 2359304 | tf_op jit(solution)/shard_map/ppermute | solution.py:550
  138.8 30.8 %collective-permute-start.26 = (bf16[2,4,192,384]{3,2,1,0:T(8,128)(2,1)}, bf16[2,4,192,384]{3,2,1,0:T(8,128)(2,1)S(1)}, u32[]{:S(2)}, u32[]{:S(2)}) collective-permute-start(bf16[2,4,192,384]{3,2,1,0:T(8,128)(2,1)} %get-tuple-element.75), channel_id=1, source_target_pairs={{0,16},{1,17},{2,18},{3,19},{4,20},{5,21},{6,22},{7,23},{8,24},{9,... | collective-permute-start | bytes 3538952 | tf_op jit(solution)/shard_map/ppermute | solution.py:550
  140.1 29.5 %collective-permute-start.27 = (bf16[2,4,192,384]{3,2,1,0:T(8,128)(2,1)}, bf16[2,4,192,384]{3,2,1,0:T(8,128)(2,1)S(1)}, u32[]{:S(2)}, u32[]{:S(2)}) collective-permute-start(bf16[2,4,192,384]{3,2,1,0:T(8,128)(2,1)} %get-tuple-element.76), channel_id=1, source_target_pairs={{0,8},{1,9},{2,10},{3,11},{4,12},{5,13},{6,14},{7,15},{8,0},{9,1},... | collective-permute-start | bytes 3538952 | tf_op jit(solution)/shard_map/ppermute | solution.py:550
  169.6 17.1 %collective-permute-start.28 = (bf16[4,4,576,128]{3,2,1,0:T(8,128)(2,1)}, bf16[4,4,576,128]{3,2,1,0:T(8,128)(2,1)S(1)}, u32[]{:S(2)}, u32[]{:S(2)}) collective-permute-start(bf16[4,4,576,128]{3,2,1,0:T(8,128)(2,1)} %get-tuple-element.77), channel_id=1, source_target_pairs={{0,1},{1,0},{2,3},{3,2},{4,5},{5,4},{6,7},{7,6},{8,9},{9,8},{10,11... | collective-permute-start | bytes 7077896 | tf_op jit(solution)/shard_map/ppermute | solution.py:550
  169.8 18.5 %collective-permute-start.36 = (bf16[4,4,576,128]{3,2,1,0:T(8,128)(2,1)S(1)}, bf16[4,4,576,128]{3,2,1,0:T(8,128)(2,1)S(1)}, u32[]{:S(2)}, u32[]{:S(2)}) collective-permute-start(bf16[4,4,576,128]{3,2,1,0:T(8,128)(2,1)S(1)} %get-tuple-element.79), channel_id=1, source_target_pairs={{0,1},{1,0},{2,3},{3,2},{4,5},{5,4},{6,7},{7,6},{8,9},{9,8},{10,11... | collective-permute-start | bytes 7077896 | tf_op jit(solution)/shard_map/ppermute | solution.py:550
  170.3 15.4 %collective-permute-start.31 = (bf16[4,192,384]{2,1,0:T(8,128)(2,1)S(1)}, bf16[4,192,384]{2,1,0:T(8,128)(2,1)S(1)}, u32[]{:S(2)}, u32[]{:S(2)}) collective-permute-start(bf16[4,192,384]{2,1,0:T(8,128)(2,1)S(1)} %fusion.4), channel_id=1, source_target_pairs={{0,16},{1,17},{2,18},{3,19},{4,20},{5,21},{6,22},{7,23},{8,24},{9,... | collective-permute-start | bytes 1769480 | tf_op jit(solution)/shard_map/ppermute | solution.py:550
  171.4 15.1 %collective-permute-start.30 = (bf16[4,192,384]{2,1,0:T(8,128)(2,1)S(1)}, bf16[4,192,384]{2,1,0:T(8,128)(2,1)S(1)}, u32[]{:S(2)}, u32[]{:S(2)}) collective-permute-start(bf16[4,192,384]{2,1,0:T(8,128)(2,1)S(1)} %fusion.3), channel_id=1, source_target_pairs={{0,8},{1,9},{2,10},{3,11},{4,12},{5,13},{6,14},{7,15},{8,0},{9,1},... | collective-permute-start | bytes 1769480 | tf_op jit(solution)/shard_map/ppermute | solution.py:550
  187.7 27.2 %collective-permute-start.29 = (bf16[2,4,576,128]{3,2,1,0:T(8,128)(2,1)S(1)}, bf16[2,4,576,128]{3,2,1,0:T(8,128)(2,1)S(1)}, u32[]{:S(2)}, u32[]{:S(2)}) collective-permute-start(bf16[2,4,576,128]{3,2,1,0:T(8,128)(2,1)S(1)} %add_convert_fusion), channel_id=1, source_target_pairs={{0,8},{1,9},{2,10},{3,11},{4,12},{5,13},{6,14},{7,15},{8,0},{9,1},... | collective-permute-start | bytes 3538952 | tf_op jit(solution)/shard_map/ppermute | solution.py:550
  188.6 27.5 %collective-permute-start.37 = (bf16[2,4,576,128]{3,2,1,0:T(8,128)(2,1)S(1)}, bf16[2,4,576,128]{3,2,1,0:T(8,128)(2,1)S(1)}, u32[]{:S(2)}, u32[]{:S(2)}) collective-permute-start(bf16[2,4,576,128]{3,2,1,0:T(8,128)(2,1)S(1)} %fusion), channel_id=1, source_target_pairs={{0,16},{1,17},{2,18},{3,19},{4,20},{5,21},{6,22},{7,23},{8,24},{9,... | collective-permute-start | bytes 3538952 | tf_op jit(solution)/shard_map/ppermute | solution.py:550
  189.6 22.1 %collective-permute-start.33 = (bf16[384,384]{1,0:T(8,128)(2,1)S(1)}, bf16[384,384]{1,0:T(8,128)(2,1)S(1)}, u32[]{:S(2)}, u32[]{:S(2)}) collective-permute-start(bf16[384,384]{1,0:T(8,128)(2,1)S(1)} %pad_maximum_fusion.16), channel_id=1, source_target_pairs={{0,4},{1,5},{2,6},{3,7},{4,0},{5,1},{6,2},{7,3},{8,12},{9,13},{10,... | collective-permute-start | bytes 884744 | tf_op jit(solution)/shard_map/ppermute | solution.py:550
  191.3 20.4 %collective-permute-start.34 = (bf16[384,384]{1,0:T(8,128)(2,1)S(1)}, bf16[384,384]{1,0:T(8,128)(2,1)S(1)}, u32[]{:S(2)}, u32[]{:S(2)}) collective-permute-start(bf16[384,384]{1,0:T(8,128)(2,1)S(1)} %pad_maximum_fusion.17), channel_id=1, source_target_pairs={{0,6},{1,7},{2,4},{3,5},{4,2},{5,3},{6,0},{7,1},{8,14},{9,15},{10,... | collective-permute-start | bytes 884744 | tf_op jit(solution)/shard_map/ppermute | solution.py:550
  193.4 19.0 %collective-permute-start.32 = (bf16[384,384]{1,0:T(8,128)(2,1)S(1)}, bf16[384,384]{1,0:T(8,128)(2,1)S(1)}, u32[]{:S(2)}, u32[]{:S(2)}) collective-permute-start(bf16[384,384]{1,0:T(8,128)(2,1)S(1)} %pad_maximum_fusion.15), channel_id=1, source_target_pairs={{0,2},{1,3},{2,0},{3,1},{4,6},{5,7},{6,4},{7,5},{8,10},{9,11},{10,... | collective-permute-start | bytes 884744 | tf_op jit(solution)/shard_map/ppermute | solution.py:550
  217.6 19.7 %collective-permute-start.24 = (bf16[512,768]{1,0:T(8,128)(2,1)S(1)}, bf16[512,768]{1,0:T(8,128)(2,1)S(1)}, u32[]{:S(2)}, u32[]{:S(2)}) collective-permute-start(bf16[512,768]{1,0:T(8,128)(2,1)S(1)} %copy-done.21), channel_id=1, source_target_pairs={{0,1},{1,0},{2,3},{3,2},{4,5},{5,4},{6,7},{7,6},{8,9},{9,8},{10,11... | collective-permute-start | bytes 2359304 | tf_op jit(solution)/shard_map/ppermute | solution.py:550
  230.0 24.6 %collective-permute-start.40 = (bf16[1152,128]{1,0:T(8,128)(2,1)S(1)}, bf16[1152,128]{1,0:T(8,128)(2,1)S(1)}, u32[]{:S(2)}, u32[]{:S(2)}) collective-permute-start(bf16[1152,128]{1,0:T(8,128)(2,1)S(1)} %pad_maximum_fusion.19), channel_id=1, source_target_pairs={{0,4},{1,5},{2,6},{3,7},{4,0},{5,1},{6,2},{7,3},{8,12},{9,13},{10,... | collective-permute-start | bytes 884744 | tf_op jit(solution)/shard_map/ppermute | solution.py:550
  235.3 19.4 %collective-permute-start.41 = (bf16[1152,128]{1,0:T(8,128)(2,1)S(1)}, bf16[1152,128]{1,0:T(8,128)(2,1)S(1)}, u32[]{:S(2)}, u32[]{:S(2)}) collective-permute-start(bf16[1152,128]{1,0:T(8,128)(2,1)S(1)} %pad_maximum_fusion.20), channel_id=1, source_target_pairs={{0,6},{1,7},{2,4},{3,5},{4,2},{5,3},{6,0},{7,1},{8,14},{9,15},{10,... | collective-permute-start | bytes 884744 | tf_op jit(solution)/shard_map/ppermute | solution.py:550
  237.3 17.4 %collective-permute-start.39 = (bf16[1152,128]{1,0:T(8,128)(2,1)S(1)}, bf16[1152,128]{1,0:T(8,128)(2,1)S(1)}, u32[]{:S(2)}, u32[]{:S(2)}) collective-permute-start(bf16[1152,128]{1,0:T(8,128)(2,1)S(1)} %pad_maximum_fusion.18), channel_id=1, source_target_pairs={{0,2},{1,3},{2,0},{3,1},{4,6},{5,7},{6,4},{7,5},{8,10},{9,11},{10,... | collective-permute-start | bytes 884744 | tf_op jit(solution)/shard_map/ppermute | solution.py:550
  (32 other events, 401.7 us)
